TPU v7x, 32 devices: a whole 2x2x4 slice. The times are simulated.
32 devices in a mesh: section: 2 (over x), img: 4 (over z), ch: 4 (over y, core).
Axes of the slice: x: 2, y: 2, z: 4, core: 2. Of those that a mesh axis runs over, the one named last changes fastest.
Arguments:
- pixels: bfloat16 [8, 32, 28, 640], P('img', 'ch'), may hold values from -6 to 6
- first_gain: float32 [640], replicated, may hold values from 0.25 to 1.75
- first_shift: float32 [640], replicated, may hold values from -3 to 3
- first_kernel: bfloat16 [3, 3, 640, 640], P(None, None, 'img'), may hold values from -0.078125 to 0.078125
- projection: bfloat16 [640, 2560], P('img'), may hold values from -0.25 to 0.25
- second_gain: float32 [2560], replicated, may hold values from 0.25 to 1.75
- second_shift: float32 [2560], replicated, may hold values from -3 to 3
- second_kernel: bfloat16 [3, 3, 2560, 2560], P(None, None, ('img', 'ch')), may hold values from -0.0390625 to 0.0390625
Outputs:
- section_outputs: bfloat16 [2, 8, 16, 14, 2560], P('section', 'img', 'ch')
All inputs are finite; a program needn't handle non-finite values.
Results may differ from a plain program's by a relative error of at most 0.013.
Values may be sent and summed in bfloat16 or wider, within the bound.
No kernel may reach another device: no remote copies, remote signals or barrier semaphores. Data moves between devices by JAX's collectives and lax.ppermute only.
A program may use at most 128 MiB of HBM per device.

v0:
```python
import functools

import jax
import jax.numpy as jnp
from jax import lax
from jax.experimental import pallas as pl
from jax.experimental.pallas import tpu as pltpu
from jax.sharding import PartitionSpec as P


BF16 = jnp.bfloat16
F32 = jnp.float32


def swap(array, axis, k, unit=1):
    count = lax.axis_size(axis)
    return lax.ppermute(array, axis, [(i, i ^ (k * unit)) for i in range(count)])


def resident(array):
    return pltpu.with_memory_space_constraint(array, pltpu.VMEM)


def pick(stack, index):
    return lax.dynamic_index_in_dim(stack, index, 0, keepdims=False)


def whole(memory_space=pltpu.VMEM):
    return pl.BlockSpec(memory_space=memory_space)


def unfold_kernel(pairs, imgs, ocols, kd, ids, gains, shifts, *refs):
    own, other = refs[:pairs], refs[pairs : 2 * pairs]
    out_own, out_other, centre, border, strip = refs[2 * pairs :]
    y, core, group = ids[4], ids[5], ids[6]
    gain, shift = gains[pl.ds(group, 1), :], shifts[pl.ds(group, 1), :]
    px = own[0].shape[1]
    first = core == 0
    base = 24

    def halves(value):
        normed = jax.nn.relu(value.astype(F32) * gain + shift).astype(BF16).astype(F32)
        low, high = normed[:, :kd], normed[:, kd:]
        return jnp.where(first, low, high), jnp.where(first, high, low)

    border[0] = jnp.zeros(border.shape[1:], F32)
    border[pairs + 1] = jnp.zeros(border.shape[1:], F32)
    for k in range(pairs):
        place = jnp.bitwise_xor(y, k)
        for i in range(imgs):
            for half, value in enumerate(halves(own[k][i])):
                centre[place, i, half] = value
            for half, value in enumerate(halves(other[k][i])):
                border[place + 1, i, half, 0] = value[:ocols]
                border[place + 1, i, half, 1] = value[px - ocols :]
    at = lax.broadcasted_iota(jnp.int32, (px, kd), 0) % ocols
    left, right = at == 0, at == ocols - 1
    shift_up = jnp.where(first, 0, 1)
    strip[...] = jnp.zeros(strip.shape, F32)
    for k in range(pairs):
        place = jnp.bitwise_xor(y, k)
        for half, out in enumerate((out_own, out_other)):
            for i in range(0, imgs, 2):
                for m in range(2):
                    strip[m, base : base + px] = centre[place, i + m, half]
                    strip[m, base - ocols : base] = border[place + shift_up, i + m, half, 1]
                    strip[m, base + px : base + px + ocols] = border[place + 1 + shift_up, i + m, half, 0]
                for tap in range(9):
                    dy, dx = tap // 3 - 1, tap % 3 - 1
                    off = base + dy * ocols + dx
                    values = [strip[m, off : off + px] for m in range(2)]
                    if dx == -1:
                        values = [jnp.where(left, 0.0, v) for v in values]
                    if dx == 1:
                        values = [jnp.where(right, 0.0, v) for v in values]
                    row = (k * imgs + i) * px
                    out[row : row + 2 * px, tap * kd : (tap + 1) * kd] = jnp.concatenate(values).astype(BF16)


def unfold(ids, gain, shift, own, other, ocols):
    pairs = len(own)
    imgs, px, kc = own[0].shape
    kd = kc // 2
    rows = pairs * imgs * px
    lanes = -(-kd // 128) * 128
    need = 8 * pairs * imgs * px * lanes + 256 * (pairs + 2) * imgs * lanes
    need += 36 * rows * kd + 8 * pairs * imgs * px * lanes
    return pl.pallas_call(
        functools.partial(unfold_kernel, pairs, imgs, ocols, kd),
        out_shape=[pltpu.VMEM((rows, 9 * kd), BF16)] * 2,
        in_specs=[whole(pltpu.SMEM)] + [whole()] * (2 + 2 * pairs),
        out_specs=[whole()] * 2,
        scratch_shapes=[
            pltpu.VMEM((pairs, imgs, 2, px, kd), F32),
            pltpu.VMEM((pairs + 2, imgs, 2, 2, ocols, kd), F32),
            pltpu.VMEM((2, 24 + px + 24, kd), F32),
        ],
        name="unfold",
        compiler_params=pltpu.CompilerParams(vmem_limit_bytes=min(60 << 20, (2 << 20) + 2 * need)),
        cost_estimate=pl.CostEstimate(flops=20 * rows * 9 * kd, bytes_accessed=8 * rows * 9 * kd, transcendentals=0),
    )(ids, gain, shift, *own, *other)


def mix_kernel(first, step, a_own, a_other, w_own, w_other, out):
    count = out.shape[1]
    for at in range(0, count, step):
        cut = slice(first + at, first + at + step)
        value = jnp.dot(a_own[...], w_own[:, cut], preferred_element_type=F32)
        value = value + jnp.dot(a_other[...], w_other[:, cut], preferred_element_type=F32)
        out[:, at : at + step] = value.astype(BF16)


def mix(a_own, a_other, w_own, w_other, first, count):
    rows, deep = a_own.shape
    return pl.pallas_call(
        functools.partial(mix_kernel, first, count),
        out_shape=jax.ShapeDtypeStruct((rows, count), BF16),
        in_specs=[whole()] * 4,
        out_specs=whole(),
        name="mix",
        compiler_params=pltpu.CompilerParams(vmem_limit_bytes=8 << 20),
        cost_estimate=pl.CostEstimate(
            flops=4 * rows * deep * count, bytes_accessed=2 * rows * count, transcendentals=0
        ),
    )(a_own, a_other, w_own, w_other)


def packing(rows, colp, c1):
    main = c1 // 128
    rest = c1 - main * 128
    fit = 128 // rest if rest else 1
    deep = -(-rows // fit) if rest else 0
    return main, rest, deep, main * rows * colp + deep * colp


def pack_kernel(groups, per, c1, colp, ids, pixels, above, below, gain, shift, *refs):
    outs, mean, held, pair = refs[:groups], refs[groups], refs[groups + 1], refs[groups + 2]
    sec, z, ch, last = ids[0], ids[1], ids[2], ids[3]
    _, rows, cols, depth = pixels.shape
    main, rest, deep, size = packing(rows + 2, colp, c1)
    scale, offset = gain[...], shift[...]
    filler = jnp.zeros((colp - cols, depth), F32)
    for p in range(per):
        for r in range(rows + 2):
            if r == 0:
                value = above[p, 0].astype(F32)
            elif r == rows + 1:
                value = below[p, 0].astype(F32)
            else:
                value = pixels[sec * per + p, r - 1].astype(F32)
            if 1 <= r <= rows:
                i, half = (r - 1) // 2, cols // 2
                for t in range(depth // 128):
                    lanes = slice(t * 128, (t + 1) * 128)
                    if r % 2 == 1:
                        pair[t] = value[:, lanes]
                    else:
                        pair[t] = pair[t] + value[:, lanes]
                        both = pair.at[t]
                        total = both[pl.ds(0, half, stride=2), :] + both[pl.ds(1, half, stride=2), :]
                        mean[p, i * half : (i + 1) * half, lanes] = total * 0.25
            value = jax.nn.relu(value * scale + offset)
            if r == 0:
                value = jnp.where(ch == 0, 0.0, value)
            if r == rows + 1:
                value = jnp.where(ch == last, 0.0, value)
            value = jnp.concatenate([value, filler]).astype(BF16)
            for g in range(groups):
                for m in range(main):
                    at = p * size + (m * (rows + 2) + r) * colp
                    lane = g * c1 + m * 128
                    held[g, at : at + colp, :] = value[:, lane : lane + 128]
                if rest:
                    at = p * size + main * (rows + 2) * colp + (r % deep) * colp
                    lane = g * c1 + main * 128
                    into = (r // deep) * rest
                    held[g, at : at + colp, into : into + rest] = value[:, lane : lane + rest]
    for k in range(groups):
        outs[k][...] = held[jnp.bitwise_xor(z, k)]


def pack(ids, pixels, above, below, gain, shift, groups, per, colp):
    _, rows, cols, depth = pixels.shape
    c1 = depth // groups
    size = packing(rows + 2, colp, c1)[3]
    block = jax.ShapeDtypeStruct((per * size, 128), BF16)
    half = jax.ShapeDtypeStruct((per, rows * cols // 4, depth), F32)
    return pl.pallas_call(
        functools.partial(pack_kernel, groups, per, c1, colp),
        out_shape=[block] * groups + [half],
        in_specs=[whole(pltpu.SMEM)] + [whole()] * 5,
        out_specs=[whole()] * (groups + 1),
        scratch_shapes=[pltpu.VMEM((groups, per * size, 128), BF16), pltpu.VMEM((depth // 128, cols, 128), F32)],
        name="pack",
        compiler_params=pltpu.CompilerParams(vmem_limit_bytes=8 << 20),
        cost_estimate=pl.CostEstimate(
            flops=4 * rows * cols * depth, bytes_accessed=6 * rows * cols * depth, transcendentals=0
        ),
    )(ids, pixels, above, below, gain, shift)


def stage_kernel(groups, per, rows, cols, colp, c1, *refs):
    blocks, kernel = refs[:groups], refs[groups]
    outs = refs[groups + 1 : 2 * groups + 1]
    flat, taps, squeezed = refs[2 * groups + 1 :]
    main, rest, deep, size = packing(rows + 2, colp, c1)
    tiles = main + (1 if rest else 0)
    orows, ocols = rows // 2, cols // 2
    base, wide = 8, (rows + 2) * colp
    half = colp // 2
    flat[...] = jnp.zeros(flat.shape, F32)
    for k in range(groups):
        for p in range(per):
            for t in range(tiles):
                lanes = 128 if t < main else rest
                if t < main:
                    at = p * size + t * wide
                    flat[t, base : base + wide, :] = blocks[k][at : at + wide, :].astype(F32)
                else:
                    for r in range(rows + 2):
                        at = p * size + main * wide + (r % deep) * colp
                        lane = (r // deep) * rest
                        flat[t, base + r * colp : base + (r + 1) * colp, 0:rest] = blocks[k][
                            at : at + colp, lane : lane + rest
                        ].astype(F32)
                span = (rows + 1) * colp + base + 8
                tall = flat[t, 0:span, :] + flat[t, colp : colp + span, :]
                flat[tiles, 0:span, :] = tall
                both = flat[tiles, 0 : span - 8, :] + flat[tiles, 1 : span - 7, :]
                flat[tiles + 1, 0 : span - 8, :] = both * 0.25
                plane = flat.at[tiles + 1]
                for tap in range(9):
                    ty, tx = tap // 3, tap % 3
                    for i in range(orows):
                        q = base + (2 * i + ty) * colp + tx - 1
                        value = plane[pl.ds(q, half, stride=2), :].astype(BF16)
                        row = ((k * per + p) * orows + i) * half
                        taps[tap, row : row + half, t * 128 : t * 128 + lanes] = value[:, :lanes]
    total = jnp.dot(taps[0], kernel[0], preferred_element_type=F32)
    for tap in range(1, 9):
        total = total + jnp.dot(taps[tap], kernel[tap], preferred_element_type=F32)
    for k in range(groups):
        for p in range(per):
            for i in range(orows):
                row = ((k * per + p) * orows + i) * half
                at = (p * orows + i) * ocols
                squeezed[at : at + ocols, :] = total[row : row + ocols]
        outs[k][...] = squeezed[...].astype(outs[k].dtype)


def stage(blocks, kernel, per, rows, cols, colp):
    groups = len(blocks)
    taps, c1, depth = kernel.shape
    tiles = -(-c1 // 128)
    px = per * rows * cols // 4
    count = groups * per * (rows // 2) * (colp // 2)
    return pl.pallas_call(
        functools.partial(stage_kernel, groups, per, rows, cols, colp, c1),
        out_shape=[jax.ShapeDtypeStruct((px, depth), F32)]
        + [jax.ShapeDtypeStruct((px, depth), BF16)] * (groups - 1),
        in_specs=[whole()] * (groups + 1),
        out_specs=[whole()] * groups,
        scratch_shapes=[
            pltpu.VMEM((tiles + 2, (rows + 3) * colp + 32, 128), F32),
            pltpu.VMEM((taps, count, c1), BF16),
            pltpu.VMEM((px, depth), F32),
        ],
        name="stage",
        compiler_params=pltpu.CompilerParams(vmem_limit_bytes=12 << 20),
        cost_estimate=pl.CostEstimate(
            flops=2 * count * taps * c1 * depth, bytes_accessed=4 * groups * px * depth, transcendentals=0
        ),
    )(*blocks, kernel)


def sum_images(value, groups):
    k = 1
    while k < groups:
        sent = value.astype(BF16)
        value = value[0::2].astype(F32) + swap(sent[1::2], "img", k).astype(F32)
        k *= 2
    return value[0]


def sum_pairs(value, pairs):
    k = 1
    while k < pairs:
        sent = value.astype(BF16)
        value = value[0::2].astype(F32) + swap(sent[1::2], "ch", k, 2).astype(F32)
        k *= 2
    return value[0]


def cross(stack_of, index, count):
    return [pick(stack_of, index ^ i) for i in range(count)]


def body(pixels, first_gain, first_shift, first_kernel, projection, second_gain, second_shift, second_kernel):
    sec = lax.axis_index("section")
    z = lax.axis_index("img")
    ch = lax.axis_index("ch")
    sections = lax.axis_size("section")
    groups = lax.axis_size("img")
    shards = lax.axis_size("ch")
    pairs = shards // 2
    y, core = ch // 2, ch % 2
    per = pixels.shape[0] // sections
    _, rows, cols, depth = pixels.shape
    orows, ocols = rows // 2, cols // 2
    wide = second_gain.shape[0]
    slab = wide // groups
    kc = slab // pairs
    kd = kc // 2
    c1 = depth // groups

    other_kernel = swap(second_kernel, "ch", 1)

    colp = -(-(cols + 2) // 16) * 16
    tails = lax.dynamic_slice_in_dim(pixels[:, -1:], sec * per, per, 0)
    heads = lax.dynamic_slice_in_dim(pixels[:, :1], sec * per, per, 0)
    above = lax.ppermute(tails, "ch", [(i, i + 1) for i in range(shards - 1)])
    below = lax.ppermute(heads, "ch", [(i + 1, i) for i in range(shards - 1)])
    ids = jnp.stack([sec, z, ch, jnp.int32(shards - 1), y, core, z * pairs + y]).astype(jnp.int32)
    *blocks, mean = pack(
        ids, pixels, above, below, first_gain.reshape(1, -1), first_shift.reshape(1, -1), groups, per, colp
    )
    got = [blocks[0]] + [swap(blocks[k], "img", k) for k in range(1, groups)]

    part_rows = c1 // shards
    projection, mean = lax.optimization_barrier((projection, mean))
    mine_rows = lax.dynamic_slice_in_dim(projection, ch * part_rows, part_rows, 0)
    proj_parts = mine_rows.reshape(part_rows, groups, slab).transpose(1, 0, 2)
    proj_rel = [pick(proj_parts, z)] + [swap(pick(proj_parts, z ^ k), "img", k) for k in range(1, groups)]
    proj_abs = jnp.stack(cross(jnp.stack(proj_rel), z, groups))
    proj_pairs = [proj_abs] + [swap(proj_abs, "ch", k, 2) for k in range(1, pairs)]
    proj_pairs = jnp.stack(cross(jnp.stack(proj_pairs), y, pairs), axis=1)
    proj_twin = swap(proj_pairs, "ch", 1)
    proj_cores = jnp.where(core == 0, jnp.stack([proj_pairs, proj_twin], 2), jnp.stack([proj_twin, proj_pairs], 2))
    proj_slab = proj_cores.reshape(depth, slab)

    total, *sent = stage(got, first_kernel.reshape(9, c1, depth), per, rows, cols, colp)
    for k in range(1, groups):
        total = total + swap(sent[k - 1], "img", k).astype(F32)
    pooled = (total + mean.reshape(total.shape)).astype(BF16)
    pooled_all = jnp.stack([pooled] + [swap(pooled, "img", k) for k in range(1, groups)])
    px = per * orows * ocols
    projected = jnp.dot(
        pooled_all.reshape(groups * px, depth), proj_slab, preferred_element_type=F32
    ).astype(BF16)

    back = projected.reshape(groups, px, slab)
    back_rel = jnp.stack([back[0]] + [swap(back[k], "img", k) for k in range(1, groups)])
    mine_projected = jnp.concatenate([pick(back_rel, z ^ i) for i in range(groups)], axis=1)
    far_projected = lax.ppermute(mine_projected, "section", [(1, 0)])

    imgs = groups * per
    out_px = orows * ocols
    by_pair = projected.reshape(groups * px, pairs, kc).transpose(1, 0, 2)
    chip = [pick(by_pair, y)]
    chip += [swap(pick(by_pair, y ^ k), "ch", k, 2) for k in range(1, pairs)]
    twin = [swap(part, "ch", 1) for part in chip]
    a_own, a_other = unfold(
        ids,
        second_gain.reshape(groups * pairs, kc),
        second_shift.reshape(groups * pairs, kc),
        [c.reshape(imgs, out_px, kc) for c in chip],
        [c.reshape(imgs, out_px, kc) for c in twin],
        ocols,
    )
    w_own = resident(second_kernel.reshape(9 * kd, wide))
    w_other = resident(other_kernel.reshape(9 * kd, wide))

    unit = wide // 10
    outs, fars = [], []
    first = 0
    for j, n in enumerate((2 * unit, 3 * unit, 3 * unit, 2 * unit)):
        value = mix(a_own, a_other, w_own, w_other, first, n)
        value = value.reshape(pairs, groups, px, n)
        if j % 2 == 0:
            total = sum_pairs(value, pairs)
            total = sum_images(total, groups)
        else:
            total = sum_images(value.swapaxes(0, 1), groups)
            total = sum_pairs(total, pairs)
        done = (total + mine_projected[:, first : first + n].astype(F32)).astype(BF16)
        first += n
        outs.append(done)
        fars.append(lax.ppermute(done, "section", [(0, 1)]))
    block = jnp.concatenate(outs, axis=-1)
    far_block = jnp.concatenate(fars, axis=-1)
    first = jnp.stack([mine_projected, far_projected])
    second = jnp.stack([far_block, block])
    final = jnp.where(sec == 0, first, second)
    return final.reshape(1, sections * per, orows, ocols, wide)


def solution(mesh):
    placed = (
        P("img", "ch", None, None),
        P(),
        P(),
        P(None, None, "img", None),
        P("img", None),
        P(),
        P(),
        P(None, None, ("img", "ch"), None),
    )

    return jax.shard_map(
        body,
        mesh=mesh,
        in_specs=placed,
        out_specs=P("section", "img", "ch", None, None),
        check_vma=False,
    )
```

profile of v0, /device:TPU:0, one launch (start us, length us, event | category | flops | bytes accessed | tf_op | source)
XLA Modules:
  0.0 147.2 jit_solution(3164439005116531528)
XLA Ops:
  1.8 2.0 %collective-permute-start = (bf16[1,1,28,640]{3,2,1,0:T(8,128)(2,1)S(1)}, bf16[1,1,28,640]{3,2,1,0:T(8,128)(2,1)S(1)}, u32[]{:S(2)}, u32[]{:S(2)}) collective-permute-start(bf16[1,1,28,640]{3,2,1,0:T(8,128)(2,1)S(1)} %constant_dynamic-slice_fusion.15), channel_id=1, source_target_pairs={{0,1},{1,2},{2,3},{4,5},{5,6},{6,7},{8,9},{9,10},{10,11},{12,13},{... | collective-permute-start | bytes 107528 | tf_op jit(solution)/shard_map/ppermute | solution.py:321
  3.8 1.3 collective-permute-start.1
  5.3 7.0 %collective-permute-done.above = bf16[1,1,28,640]{3,2,1,0:T(8,128)(2,1)S(1)} collective-permute-done((bf16[1,1,28,640]{3,2,1,0:T(8,128)(2,1)S(1)}, bf16[1,1,28,640]{3,2,1,0:T(8,128)(2,1)S(1)}, u32[]{:S(2)}, u32[]{:S(2)}) %collective-permute-start) | collective-permute-done | bytes 35872 | tf_op jit(solution)/shard_map/ppermute | solution.py:321
  13.8 3.0 %collective-permute-start.11 = (bf16[40,640]{1,0:T(8,128)(2,1)S(1)}, bf16[40,640]{1,0:T(8,128)(2,1)S(1)}, u32[]{:S(2)}, u32[]{:S(2)}) collective-permute-start(bf16[40,640]{1,0:T(8,128)(2,1)S(1)} %bitcast.179), channel_id=1, source_target_pairs={{0,4},{4,0},{8,12},{12,8},{1,5},{5,1},{9,13},{13,9},{2,6},{6,2},{1... | collective-permute-start | bytes 153608 | tf_op jit(solution)/shard_map/ppermute | solution.py:17
  16.8 2.7 %collective-permute-start.12 = (bf16[40,640]{1,0:T(8,128)(2,1)S(1)}, bf16[40,640]{1,0:T(8,128)(2,1)S(1)}, u32[]{:S(2)}, u32[]{:S(2)}) collective-permute-start(bf16[40,640]{1,0:T(8,128)(2,1)S(1)} %bitcast.180), channel_id=1, source_target_pairs={{0,8},{4,12},{8,0},{12,4},{1,9},{5,13},{9,1},{13,5},{2,10},{6,14},... | collective-permute-start | bytes 153608 | tf_op jit(solution)/shard_map/ppermute | solution.py:17
  19.5 3.1 %collective-permute-done.12 = bf16[40,640]{1,0:T(8,128)(2,1)S(1)} collective-permute-done((bf16[40,640]{1,0:T(8,128)(2,1)S(1)}, bf16[40,640]{1,0:T(8,128)(2,1)S(1)}, u32[]{:S(2)}, u32[]{:S(2)}) %collective-permute-start.12) | collective-permute-done | bytes 51232 | tf_op jit(solution)/shard_map/ppermute | solution.py:17
  22.7 2.7 %collective-permute-done.13 = bf16[40,640]{1,0:T(8,128)(2,1)S(1)} collective-permute-done((bf16[40,640]{1,0:T(8,128)(2,1)S(1)}, bf16[40,640]{1,0:T(8,128)(2,1)S(1)}, u32[]{:S(2)}, u32[]{:S(2)}) %collective-permute-start.13) | collective-permute-done | bytes 51232 | tf_op jit(solution)/shard_map/ppermute | solution.py:17
  26.3 1.5 %collective-permute-start.14 = (bf16[4,40,640]{2,1,0:T(8,128)(2,1)}, bf16[4,40,640]{2,1,0:T(8,128)(2,1)}, u32[]{:S(2)}, u32[]{:S(2)}) collective-permute-start(bf16[4,40,640]{2,1,0:T(8,128)(2,1)} %get-tuple-element.55), channel_id=1, source_target_pairs={{0,2},{1,3},{2,0},{3,1},{4,6},{5,7},{6,4},{7,5},{8,10},{9,11},{10,... | collective-permute-start | bytes 614408 | tf_op jit(solution)/shard_map/ppermute | solution.py:17
  27.8 1.7 %collective-permute-start.3 = (bf16[416,128]{1,0:T(8,128)(2,1)S(1)}, bf16[416,128]{1,0:T(8,128)(2,1)S(1)}, u32[]{:S(2)}, u32[]{:S(2)}) collective-permute-start(bf16[416,128]{1,0:T(8,128)(2,1)S(1)} %get-tuple-element.20), channel_id=1, source_target_pairs={{0,8},{4,12},{8,0},{12,4},{1,9},{5,13},{9,1},{13,5},{2,10},{6,14},... | collective-permute-start | bytes 319496 | tf_op jit(solution)/shard_map/ppermute | solution.py:17
  29.5 2.7 %collective-permute-start.4 = (bf16[416,128]{1,0:T(8,128)(2,1)S(1)}, bf16[416,128]{1,0:T(8,128)(2,1)S(1)}, u32[]{:S(2)}, u32[]{:S(2)}) collective-permute-start(bf16[416,128]{1,0:T(8,128)(2,1)S(1)} %get-tuple-element.21), channel_id=1, source_target_pairs={{0,12},{4,8},{8,4},{12,0},{1,13},{5,9},{9,5},{13,1},{2,14},{6,10},... | collective-permute-start | bytes 319496 | tf_op jit(solution)/shard_map/ppermute | solution.py:17
  32.2 1.5 collective-permute-done.2.refs_1_
  33.7 3.9 %collective-permute-done.3.refs_2_ = bf16[416,128]{1,0:T(8,128)(2,1)S(1)} collective-permute-done((bf16[416,128]{1,0:T(8,128)(2,1)S(1)}, bf16[416,128]{1,0:T(8,128)(2,1)S(1)}, u32[]{:S(2)}, u32[]{:S(2)}) %collective-permute-start.3) | collective-permute-done | bytes 106528 | tf_op jit(solution)/shard_map/ppermute | solution.py:17
  37.5 1.6 %stage.1 = (f32[56,640]{1,0:T(8,128)S(1)}, bf16[56,640]{1,0:T(8,128)(2,1)S(1)}, bf16[56,640]{1,0:T(8,128)(2,1)S(1)}, bf16[56,640]{1,0:T(8,128)(2,1)S(1)}) custom-call(bf16[416,128]{1,0:T(8,128)(2,1)S(1)} %get-tuple-element.18.refs_0_, bf16[416,128]{1,0:T(8,128)(2,1)S(1)} %collective-permute-done.2.refs_1_, ...), custom_call_target="tpu_custom_call" | custom-call | flops 471859200 | bytes 573440 | tf_op jit(solution)/shard_map/stage/pallas_call | solution.py:257
  39.1 1.8 %collective-permute-start.5 = (bf16[56,640]{1,0:T(8,128)(2,1)S(1)}, bf16[56,640]{1,0:T(8,128)(2,1)S(1)}, u32[]{:S(2)}, u32[]{:S(2)}) collective-permute-start(bf16[56,640]{1,0:T(8,128)(2,1)S(1)} %get-tuple-element.23), channel_id=1, source_target_pairs={{0,4},{4,0},{8,12},{12,8},{1,5},{5,1},{9,13},{13,9},{2,6},{6,2},{1... | collective-permute-start | bytes 215048 | tf_op jit(solution)/shard_map/ppermute | solution.py:17
  41.1 2.4 %collective-permute-start.7 = (bf16[56,640]{1,0:T(8,128)(2,1)S(1)}, bf16[56,640]{1,0:T(8,128)(2,1)S(1)}, u32[]{:S(2)}, u32[]{:S(2)}) collective-permute-start(bf16[56,640]{1,0:T(8,128)(2,1)S(1)} %get-tuple-element.25), channel_id=1, source_target_pairs={{0,12},{4,8},{8,4},{12,0},{1,13},{5,9},{9,5},{13,1},{2,14},{6,10},... | collective-permute-start | bytes 215048 | tf_op jit(solution)/shard_map/ppermute | solution.py:17
  45.0 2.6 %collective-permute-done.6 = bf16[56,640]{1,0:T(8,128)(2,1)S(1)} collective-permute-done((bf16[56,640]{1,0:T(8,128)(2,1)S(1)}, bf16[56,640]{1,0:T(8,128)(2,1)S(1)}, u32[]{:S(2)}, u32[]{:S(2)}) %collective-permute-start.6) | collective-permute-done | bytes 71712 | tf_op jit(solution)/shard_map/ppermute | solution.py:17
  47.7 1.4 collective-permute-start.9
  49.0 2.4 %collective-permute-start.10 = (bf16[56,640]{1,0:T(8,128)(2,1)S(1)}, bf16[56,640]{1,0:T(8,128)(2,1)S(1)}, u32[]{:S(2)}, u32[]{:S(2)}) collective-permute-start(bf16[56,640]{1,0:T(8,128)(2,1)S(1)} %fusion.13), channel_id=1, source_target_pairs={{0,12},{4,8},{8,4},{12,0},{1,13},{5,9},{9,5},{13,1},{2,14},{6,10},... | collective-permute-start | bytes 215048 | tf_op jit(solution)/shard_map/ppermute | solution.py:17
  51.4 1.5 %collective-permute-done.9 = bf16[56,640]{1,0:T(8,128)(2,1)S(1)} collective-permute-done((bf16[56,640]{1,0:T(8,128)(2,1)S(1)}, bf16[56,640]{1,0:T(8,128)(2,1)S(1)}, u32[]{:S(2)}, u32[]{:S(2)}) %collective-permute-start.9) | collective-permute-done | bytes 71712 | tf_op jit(solution)/shard_map/ppermute | solution.py:17
  53.0 2.3 %collective-permute-done.10 = bf16[56,640]{1,0:T(8,128)(2,1)S(1)} collective-permute-done((bf16[56,640]{1,0:T(8,128)(2,1)S(1)}, bf16[56,640]{1,0:T(8,128)(2,1)S(1)}, u32[]{:S(2)}, u32[]{:S(2)}) %collective-permute-start.10) | collective-permute-done | bytes 71712 | tf_op jit(solution)/shard_map/ppermute | solution.py:17
  56.1 1.3 maximum_select_fusion
  58.6 2.0 %collective-permute-start.17 = (bf16[56,640]{1,0:T(8,128)(2,1)S(1)}, bf16[56,640]{1,0:T(8,128)(2,1)S(1)}, u32[]{:S(2)}, u32[]{:S(2)}) collective-permute-start(bf16[56,640]{1,0:T(8,128)(2,1)S(1)} %get-tuple-element.53), channel_id=1, source_target_pairs={{0,8},{4,12},{8,0},{12,4},{1,9},{5,13},{9,1},{13,5},{2,10},{6,14},... | collective-permute-start | bytes 215048 | tf_op jit(solution)/shard_map/ppermute | solution.py:17
  60.6 1.9 %collective-permute-start.18 = (bf16[56,640]{1,0:T(8,128)(2,1)S(1)}, bf16[56,640]{1,0:T(8,128)(2,1)S(1)}, u32[]{:S(2)}, u32[]{:S(2)}) collective-permute-start(bf16[56,640]{1,0:T(8,128)(2,1)S(1)} %get-tuple-element.52), channel_id=1, source_target_pairs={{0,12},{4,8},{8,4},{12,0},{1,13},{5,9},{9,5},{13,1},{2,14},{6,10},... | collective-permute-start | bytes 215048 | tf_op jit(solution)/shard_map/ppermute | solution.py:17
  63.9 2.9 %collective-permute-done.18 = bf16[56,640]{1,0:T(8,128)(2,1)S(1)} collective-permute-done((bf16[56,640]{1,0:T(8,128)(2,1)S(1)}, bf16[56,640]{1,0:T(8,128)(2,1)S(1)}, u32[]{:S(2)}, u32[]{:S(2)}) %collective-permute-start.18) | collective-permute-done | bytes 71712 | tf_op jit(solution)/shard_map/ppermute | solution.py:17
  67.6 1.5 collective-permute-start.19
  71.2 3.0 %unfold.1 = (bf16[448,1440]{1,0:T(8,128)(2,1)S(1)}, bf16[448,1440]{1,0:T(8,128)(2,1)S(1)}) custom-call(s32[7]{0:T(128)S(1)} %stack.122.ids, f32[8,320]{1,0:T(8,128)S(1)} %reshape.192.gains, f32[8,320]{1,0:T(8,128)S(1)} %reshape.193.shifts, bf16[4,56,320]{2,1,0:T(8,128)(2,1)S(1)} %bitcast.142, bf16[4,56,320]{2,1,0:T(8,128)(2,1)S(1)} %bitcast.143, ...), custom_call_target="tpu_custom_call" | custom-call | flops 12902400 | bytes 5160960 | tf_op jit(solution)/shard_map/unfold/pallas_call | solution.py:88
  74.3 1.2 copy-done.2
  77.5 3.1 %copy-done.1 = bf16[3,3,160,2560]{3,2,1,0:T(8,128)(2,1)S(1)} copy-done((bf16[3,3,160,2560]{3,2,1,0:T(8,128)(2,1)S(1)}, bf16[3,3,160,2560]{3,2,1,0:T(8,128)(2,1)}, u32[]{:S(2)}) %copy-start.1) | copy-done | bytes 7372824
  80.6 1.3 copy-done.3
  81.9 4.7 %mix.4 = bf16[448,512]{1,0:T(8,128)(2,1)S(1)} custom-call(bf16[448,1440]{1,0:T(8,128)(2,1)S(1)} %get-tuple-element.29.a_own, bf16[448,1440]{1,0:T(8,128)(2,1)S(1)} %copy-done.3, bf16[1440,2560]{1,0:T(8,128)(2,1)S(1)} %bitcast.133, bf16[1440,2560]{1,0:T(8,128)(2,1)} %bitcast.39.w_other), custom_call_target="tpu_custom_call" | custom-call | flops 1321205760 | bytes 458752 | tf_op jit(solution)/shard_map/mix/pallas_call | solution.py:115
  86.6 5.5 %mix.5 = bf16[448,768]{1,0:T(8,128)(2,1)S(1)} custom-call(bf16[448,1440]{1,0:T(8,128)(2,1)S(1)} %get-tuple-element.29.a_own, bf16[448,1440]{1,0:T(8,128)(2,1)S(1)} %copy-done.3, bf16[1440,2560]{1,0:T(8,128)(2,1)S(1)} %bitcast.134, bf16[1440,2560]{1,0:T(8,128)(2,1)} %bitcast.39.w_other), custom_call_target="tpu_custom_call" | custom-call | flops 1981808640 | bytes 688128 | tf_op jit(solution)/shard_map/mix/pallas_call | solution.py:115
  92.2 5.5 %mix.6 = bf16[448,768]{1,0:T(8,128)(2,1)S(1)} custom-call(bf16[448,1440]{1,0:T(8,128)(2,1)S(1)} %get-tuple-element.29.a_own, bf16[448,1440]{1,0:T(8,128)(2,1)S(1)} %copy-done.3, bf16[1440,2560]{1,0:T(8,128)(2,1)S(1)} %bitcast.135, bf16[1440,2560]{1,0:T(8,128)(2,1)} %bitcast.39.w_other), custom_call_target="tpu_custom_call" | custom-call | flops 1981808640 | bytes 688128 | tf_op jit(solution)/shard_map/mix/pallas_call | solution.py:115
  98.6 1.6 %collective-permute-start.32 = (bf16[1,4,56,768]{3,2,1,0:T(8,128)(2,1)S(1)}, bf16[1,4,56,768]{3,2,1,0:T(8,128)(2,1)S(1)}, u32[]{:S(2)}, u32[]{:S(2)}) collective-permute-start(bf16[1,4,56,768]{3,2,1,0:T(8,128)(2,1)S(1)} %bitcast.166), channel_id=1, source_target_pairs={{0,2},{1,3},{2,0},{3,1},{4,6},{5,7},{6,4},{7,5},{8,10},{9,11},{10,... | collective-permute-start | bytes 1032200 | tf_op jit(solution)/shard_map/ppermute | solution.py:17
  100.1 4.7 %mix.7 = bf16[448,512]{1,0:T(8,128)(2,1)S(1)} custom-call(bf16[448,1440]{1,0:T(8,128)(2,1)S(1)} %get-tuple-element.29.a_own, bf16[448,1440]{1,0:T(8,128)(2,1)S(1)} %copy-done.4, bf16[1440,2560]{1,0:T(8,128)(2,1)S(1)} %bitcast.138, bf16[1440,2560]{1,0:T(8,128)(2,1)} %bitcast.39.w_other), custom_call_target="tpu_custom_call" | custom-call | flops 1321205760 | bytes 458752 | tf_op jit(solution)/shard_map/mix/pallas_call | solution.py:115
  104.9 2.1 %collective-permute-start.36 = (bf16[2,2,56,512]{3,2,1,0:T(8,128)(2,1)S(1)}, bf16[2,2,56,512]{3,2,1,0:T(8,128)(2,1)S(1)}, u32[]{:S(2)}, u32[]{:S(2)}) collective-permute-start(bf16[2,2,56,512]{3,2,1,0:T(8,128)(2,1)S(1)} %slice.179), channel_id=1, source_target_pairs={{0,4},{4,0},{8,12},{12,8},{1,5},{5,1},{9,13},{13,9},{2,6},{6,2},{1... | collective-permute-start | bytes 688136 | tf_op jit(solution)/shard_map/ppermute | solution.py:17
  107.2 6.2 %collective-permute-done.36 = bf16[2,2,56,512]{3,2,1,0:T(8,128)(2,1)S(1)} collective-permute-done((bf16[2,2,56,512]{3,2,1,0:T(8,128)(2,1)S(1)}, bf16[2,2,56,512]{3,2,1,0:T(8,128)(2,1)S(1)}, u32[]{:S(2)}, u32[]{:S(2)}) %collective-permute-start.36) | collective-permute-done | bytes 229408 | tf_op jit(solution)/shard_map/ppermute | solution.py:17
  114.6 2.2 %collective-permute-start.26 = (bf16[1,56,512]{2,1,0:T(8,128)(2,1)S(1)}, bf16[1,56,512]{2,1,0:T(8,128)(2,1)S(1)}, u32[]{:S(2)}, u32[]{:S(2)}) collective-permute-start(bf16[1,56,512]{2,1,0:T(8,128)(2,1)S(1)} %slice.265), channel_id=1, source_target_pairs={{0,8},{4,12},{8,0},{12,4},{1,9},{5,13},{9,1},{13,5},{2,10},{6,14},... | collective-permute-start | bytes 172040 | tf_op jit(solution)/shard_map/ppermute | solution.py:17
  117.9 1.8 %collective-permute-start.33 = (bf16[2,56,768]{2,1,0:T(8,128)(2,1)S(1)}, bf16[2,56,768]{2,1,0:T(8,128)(2,1)S(1)}, u32[]{:S(2)}, u32[]{:S(2)}) collective-permute-start(bf16[2,56,768]{2,1,0:T(8,128)(2,1)S(1)} %slice.174), channel_id=1, source_target_pairs={{0,4},{4,0},{8,12},{12,8},{1,5},{5,1},{9,13},{13,9},{2,6},{6,2},{1... | collective-permute-start | bytes 516104 | tf_op jit(solution)/shard_map/ppermute | solution.py:17
  119.7 6.3 %collective-permute-done.37 = bf16[1,2,56,512]{3,2,1,0:T(8,128)(2,1)S(1)} collective-permute-done((bf16[1,2,56,512]{3,2,1,0:T(8,128)(2,1)S(1)}, bf16[1,2,56,512]{3,2,1,0:T(8,128)(2,1)S(1)}, u32[]{:S(2)}, u32[]{:S(2)}) %collective-permute-start.37) | collective-permute-done | bytes 114720 | tf_op jit(solution)/shard_map/ppermute | solution.py:17
  126.0 1.5 %collective-permute-start.38 = (bf16[1,56,512]{2,1,0:T(8,128)(2,1)S(1)}, bf16[1,56,512]{2,1,0:T(8,128)(2,1)S(1)}, u32[]{:S(2)}, u32[]{:S(2)}) collective-permute-start(bf16[1,56,512]{2,1,0:T(8,128)(2,1)S(1)} %fusion.22), channel_id=1, source_target_pairs={{0,2},{1,3},{2,0},{3,1},{4,6},{5,7},{6,4},{7,5},{8,10},{9,11},{10,... | collective-permute-start | bytes 172040 | tf_op jit(solution)/shard_map/ppermute | solution.py:17
  127.5 4.8 %collective-permute-start.27 = (bf16[56,512]{1,0:T(8,128)(2,1)S(1)}, bf16[56,512]{1,0:T(8,128)(2,1)S(1)}, u32[]{:S(2)}, u32[]{:S(2)}) collective-permute-start(bf16[56,512]{1,0:T(8,128)(2,1)S(1)} %fusion.20), channel_id=1, source_target_pairs={{0,16},{1,17},{2,18},{3,19},{4,20},{5,21},{6,22},{7,23},{8,24},{9,... | collective-permute-start | bytes 172040 | tf_op jit(solution)/shard_map/ppermute | solution.py:388
  132.4 2.8 %collective-permute-start.39 = (bf16[56,512]{1,0:T(8,128)(2,1)S(1)}, bf16[56,512]{1,0:T(8,128)(2,1)S(1)}, u32[]{:S(2)}, u32[]{:S(2)}) collective-permute-start(bf16[56,512]{1,0:T(8,128)(2,1)S(1)} %fusion.17), channel_id=1, source_target_pairs={{0,16},{1,17},{2,18},{3,19},{4,20},{5,21},{6,22},{7,23},{8,24},{9,... | collective-permute-start | bytes 172040 | tf_op jit(solution)/shard_map/ppermute | solution.py:388
  135.2 1.4 collective-permute-start.30
  136.8 3.0 %collective-permute-done.30 = bf16[1,56,768]{2,1,0:T(8,128)(2,1)S(1)} collective-permute-done((bf16[1,56,768]{2,1,0:T(8,128)(2,1)S(1)}, bf16[1,56,768]{2,1,0:T(8,128)(2,1)S(1)}, u32[]{:S(2)}, u32[]{:S(2)}) %collective-permute-start.30) | collective-permute-done | bytes 86048 | tf_op jit(solution)/shard_map/ppermute | solution.py:17
  139.8 1.4 collective-permute-start.31
  142.2 1.3 collective-permute-start.35
  143.7 1.9 %collective-permute-done.35 = bf16[56,768]{1,0:T(8,128)(2,1)S(1)} collective-permute-done((bf16[56,768]{1,0:T(8,128)(2,1)S(1)}, bf16[56,768]{1,0:T(8,128)(2,1)S(1)}, u32[]{:S(2)}, u32[]{:S(2)}) %collective-permute-start.35) | collective-permute-done | bytes 86048 | tf_op jit(solution)/shard_map/ppermute | solution.py:388
  145.9 1.3 copy.35
  (140 shorter events, 19.4 us)
Async XLA Ops:
  0.0 13.2 %copy-start = (bf16[160,2560]{1,0:T(8,128)(2,1)S(1)}, bf16[160,2560]{1,0:T(8,128)(2,1)}, u32[]{:S(2)}) copy-start(bf16[160,2560]{1,0:T(8,128)(2,1)} %param.12) | copy-start | bytes 2457604
  0.0 77.5 %collective-permute-start.23 = (bf16[3,3,160,2560]{3,2,1,0:T(8,128)(2,1)}, bf16[3,3,160,2560]{3,2,1,0:T(8,128)(2,1)}, u32[]{:S(2)}, u32[]{:S(2)}) collective-permute-start(bf16[3,3,160,2560]{3,2,1,0:T(8,128)(2,1)} %param.15), channel_id=1, source_target_pairs={{0,1},{1,0},{2,3},{3,2},{4,5},{5,4},{6,7},{7,6},{8,9},{9,8},{10,11... | collective-permute-start | bytes 22118408 | tf_op jit(solution)/shard_map/ppermute | solution.py:17
  1.8 10.5 %collective-permute-start = (bf16[1,1,28,640]{3,2,1,0:T(8,128)(2,1)S(1)}, bf16[1,1,28,640]{3,2,1,0:T(8,128)(2,1)S(1)}, u32[]{:S(2)}, u32[]{:S(2)}) collective-permute-start(bf16[1,1,28,640]{3,2,1,0:T(8,128)(2,1)S(1)} %constant_dynamic-slice_fusion.15), channel_id=1, source_target_pairs={{0,1},{1,2},{2,3},{4,5},{5,6},{6,7},{8,9},{9,10},{10,11},{12,13},{... | collective-permute-start | bytes 107528 | tf_op jit(solution)/shard_map/ppermute | solution.py:321
  3.8 8.5 %collective-permute-start.1 = (bf16[1,1,28,640]{3,2,1,0:T(8,128)(2,1)S(1)}, bf16[1,1,28,640]{3,2,1,0:T(8,128)(2,1)S(1)}, u32[]{:S(2)}, u32[]{:S(2)}) collective-permute-start(bf16[1,1,28,640]{3,2,1,0:T(8,128)(2,1)S(1)} %constant_dynamic-slice_fusion.14), channel_id=1, source_target_pairs={{1,0},{2,1},{3,2},{5,4},{6,5},{7,6},{9,8},{10,9},{11,10},{13,12},{... | collective-permute-start | bytes 107528 | tf_op jit(solution)/shard_map/ppermute | solution.py:322
  13.3 24.2 %copy-start.5 = (bf16[3,3,160,640]{3,2,1,0:T(8,128)(2,1)S(1)}, bf16[3,3,160,640]{3,2,1,0:T(8,128)(2,1)}, u32[]{:S(2)}) copy-start(bf16[3,3,160,640]{3,2,1,0:T(8,128)(2,1)} %param.11) | copy-start | bytes 5529604
  13.8 5.8 %collective-permute-start.11 = (bf16[40,640]{1,0:T(8,128)(2,1)S(1)}, bf16[40,640]{1,0:T(8,128)(2,1)S(1)}, u32[]{:S(2)}, u32[]{:S(2)}) collective-permute-start(bf16[40,640]{1,0:T(8,128)(2,1)S(1)} %bitcast.179), channel_id=1, source_target_pairs={{0,4},{4,0},{8,12},{12,8},{1,5},{5,1},{9,13},{13,9},{2,6},{6,2},{1... | collective-permute-start | bytes 153608 | tf_op jit(solution)/shard_map/ppermute | solution.py:17
  16.8 5.9 %collective-permute-start.12 = (bf16[40,640]{1,0:T(8,128)(2,1)S(1)}, bf16[40,640]{1,0:T(8,128)(2,1)S(1)}, u32[]{:S(2)}, u32[]{:S(2)}) collective-permute-start(bf16[40,640]{1,0:T(8,128)(2,1)S(1)} %bitcast.180), channel_id=1, source_target_pairs={{0,8},{4,12},{8,0},{12,4},{1,9},{5,13},{9,1},{13,5},{2,10},{6,14},... | collective-permute-start | bytes 153608 | tf_op jit(solution)/shard_map/ppermute | solution.py:17
  19.4 6.0 %collective-permute-start.13 = (bf16[40,640]{1,0:T(8,128)(2,1)S(1)}, bf16[40,640]{1,0:T(8,128)(2,1)S(1)}, u32[]{:S(2)}, u32[]{:S(2)}) collective-permute-start(bf16[40,640]{1,0:T(8,128)(2,1)S(1)} %bitcast.181), channel_id=1, source_target_pairs={{0,12},{4,8},{8,4},{12,0},{1,13},{5,9},{9,5},{13,1},{2,14},{6,10},... | collective-permute-start | bytes 153608 | tf_op jit(solution)/shard_map/ppermute | solution.py:17
  26.3 17.2 %collective-permute-start.14 = (bf16[4,40,640]{2,1,0:T(8,128)(2,1)}, bf16[4,40,640]{2,1,0:T(8,128)(2,1)}, u32[]{:S(2)}, u32[]{:S(2)}) collective-permute-start(bf16[4,40,640]{2,1,0:T(8,128)(2,1)} %get-tuple-element.55), channel_id=1, source_target_pairs={{0,2},{1,3},{2,0},{3,1},{4,6},{5,7},{6,4},{7,5},{8,10},{9,11},{10,... | collective-permute-start | bytes 614408 | tf_op jit(solution)/shard_map/ppermute | solution.py:17
  27.8 5.8 %collective-permute-start.2 = (bf16[416,128]{1,0:T(8,128)(2,1)S(1)}, bf16[416,128]{1,0:T(8,128)(2,1)S(1)}, u32[]{:S(2)}, u32[]{:S(2)}) collective-permute-start(bf16[416,128]{1,0:T(8,128)(2,1)S(1)} %get-tuple-element.19), channel_id=1, source_target_pairs={{0,4},{4,0},{8,12},{12,8},{1,5},{5,1},{9,13},{13,9},{2,6},{6,2},{1... | collective-permute-start | bytes 319496 | tf_op jit(solution)/shard_map/ppermute | solution.py:17
  27.8 9.7 %collective-permute-start.3 = (bf16[416,128]{1,0:T(8,128)(2,1)S(1)}, bf16[416,128]{1,0:T(8,128)(2,1)S(1)}, u32[]{:S(2)}, u32[]{:S(2)}) collective-permute-start(bf16[416,128]{1,0:T(8,128)(2,1)S(1)} %get-tuple-element.20), channel_id=1, source_target_pairs={{0,8},{4,12},{8,0},{12,4},{1,9},{5,13},{9,1},{13,5},{2,10},{6,14},... | collective-permute-start | bytes 319496 | tf_op jit(solution)/shard_map/ppermute | solution.py:17
  29.5 8.1 %collective-permute-start.4 = (bf16[416,128]{1,0:T(8,128)(2,1)S(1)}, bf16[416,128]{1,0:T(8,128)(2,1)S(1)}, u32[]{:S(2)}, u32[]{:S(2)}) collective-permute-start(bf16[416,128]{1,0:T(8,128)(2,1)S(1)} %get-tuple-element.21), channel_id=1, source_target_pairs={{0,12},{4,8},{8,4},{12,0},{1,13},{5,9},{9,5},{13,1},{2,14},{6,10},... | collective-permute-start | bytes 319496 | tf_op jit(solution)/shard_map/ppermute | solution.py:17
  32.2 11.3 %copy-start.6 = (bf16[1,4,40,640]{3,2,1,0:T(8,128)(2,1)S(1)}, bf16[1,4,40,640]{3,2,1,0:T(8,128)(2,1)}, u32[]{:S(2)}) copy-start(bf16[1,4,40,640]{3,2,1,0:T(8,128)(2,1)} %get-tuple-element.56) | copy-start | bytes 614404
  39.1 5.9 %collective-permute-start.5 = (bf16[56,640]{1,0:T(8,128)(2,1)S(1)}, bf16[56,640]{1,0:T(8,128)(2,1)S(1)}, u32[]{:S(2)}, u32[]{:S(2)}) collective-permute-start(bf16[56,640]{1,0:T(8,128)(2,1)S(1)} %get-tuple-element.23), channel_id=1, source_target_pairs={{0,4},{4,0},{8,12},{12,8},{1,5},{5,1},{9,13},{13,9},{2,6},{6,2},{1... | collective-permute-start | bytes 215048 | tf_op jit(solution)/shard_map/ppermute | solution.py:17
  40.9 6.8 %collective-permute-start.6 = (bf16[56,640]{1,0:T(8,128)(2,1)S(1)}, bf16[56,640]{1,0:T(8,128)(2,1)S(1)}, u32[]{:S(2)}, u32[]{:S(2)}) collective-permute-start(bf16[56,640]{1,0:T(8,128)(2,1)S(1)} %get-tuple-element.24), channel_id=1, source_target_pairs={{0,8},{4,12},{8,0},{12,4},{1,9},{5,13},{9,1},{13,5},{2,10},{6,14},... | collective-permute-start | bytes 215048 | tf_op jit(solution)/shard_map/ppermute | solution.py:17
  41.1 6.5 %collective-permute-start.7 = (bf16[56,640]{1,0:T(8,128)(2,1)S(1)}, bf16[56,640]{1,0:T(8,128)(2,1)S(1)}, u32[]{:S(2)}, u32[]{:S(2)}) collective-permute-start(bf16[56,640]{1,0:T(8,128)(2,1)S(1)} %get-tuple-element.25), channel_id=1, source_target_pairs={{0,12},{4,8},{8,4},{12,0},{1,13},{5,9},{9,5},{13,1},{2,14},{6,10},... | collective-permute-start | bytes 215048 | tf_op jit(solution)/shard_map/ppermute | solution.py:17
  44.7 11.4 %collective-permute-start.15 = (bf16[4,2,40,640]{3,2,1,0:T(8,128)(2,1)S(1)}, bf16[4,2,40,640]{3,2,1,0:T(8,128)(2,1)}, u32[]{:S(2)}, u32[]{:S(2)}) collective-permute-start(bf16[4,2,40,640]{3,2,1,0:T(8,128)(2,1)S(1)} %get-tuple-element.42), channel_id=1, source_target_pairs={{0,1},{1,0},{2,3},{3,2},{4,5},{5,4},{6,7},{7,6},{8,9},{9,8},{10,11... | collective-permute-start | bytes 1228808 | tf_op jit(solution)/shard_map/ppermute | solution.py:17
  47.7 5.3 %collective-permute-start.9 = (bf16[56,640]{1,0:T(8,128)(2,1)S(1)}, bf16[56,640]{1,0:T(8,128)(2,1)S(1)}, u32[]{:S(2)}, u32[]{:S(2)}) collective-permute-start(bf16[56,640]{1,0:T(8,128)(2,1)S(1)} %fusion.13), channel_id=1, source_target_pairs={{0,8},{4,12},{8,0},{12,4},{1,9},{5,13},{9,1},{13,5},{2,10},{6,14},... | collective-permute-start | bytes 215048 | tf_op jit(solution)/shard_map/ppermute | solution.py:17
  49.0 6.2 %collective-permute-start.10 = (bf16[56,640]{1,0:T(8,128)(2,1)S(1)}, bf16[56,640]{1,0:T(8,128)(2,1)S(1)}, u32[]{:S(2)}, u32[]{:S(2)}) collective-permute-start(bf16[56,640]{1,0:T(8,128)(2,1)S(1)} %fusion.13), channel_id=1, source_target_pairs={{0,12},{4,8},{8,4},{12,0},{1,13},{5,9},{9,5},{13,1},{2,14},{6,10},... | collective-permute-start | bytes 215048 | tf_op jit(solution)/shard_map/ppermute | solution.py:17
  51.4 4.6 %collective-permute-start.8 = (bf16[56,640]{1,0:T(8,128)(2,1)S(1)}, bf16[56,640]{1,0:T(8,128)(2,1)S(1)}, u32[]{:S(2)}, u32[]{:S(2)}) collective-permute-start(bf16[56,640]{1,0:T(8,128)(2,1)S(1)} %fusion.13), channel_id=1, source_target_pairs={{0,4},{4,0},{8,12},{12,8},{1,5},{5,1},{9,13},{13,9},{2,6},{6,2},{1... | collective-permute-start | bytes 215048 | tf_op jit(solution)/shard_map/ppermute | solution.py:17
  58.1 11.6 %copy-start.8 = (f32[2560]{0:T(1024)S(1)}, f32[2560]{0:T(1024)}, u32[]{:S(2)}) copy-start(f32[2560]{0:T(1024)} %param.13) | copy-start | bytes 30724
  58.1 11.7 %copy-start.9 = (f32[2560]{0:T(1024)S(1)}, f32[2560]{0:T(1024)}, u32[]{:S(2)}) copy-start(f32[2560]{0:T(1024)} %param.14) | copy-start | bytes 30724
  58.1 5.1 %collective-permute-start.16 = (bf16[56,640]{1,0:T(8,128)(2,1)S(1)}, bf16[56,640]{1,0:T(8,128)(2,1)S(1)}, u32[]{:S(2)}, u32[]{:S(2)}) collective-permute-start(bf16[56,640]{1,0:T(8,128)(2,1)S(1)} %get-tuple-element.54), channel_id=1, source_target_pairs={{0,4},{4,0},{8,12},{12,8},{1,5},{5,1},{9,13},{13,9},{2,6},{6,2},{1... | collective-permute-start | bytes 215048 | tf_op jit(solution)/shard_map/ppermute | solution.py:17
  58.6 5.2 %collective-permute-start.17 = (bf16[56,640]{1,0:T(8,128)(2,1)S(1)}, bf16[56,640]{1,0:T(8,128)(2,1)S(1)}, u32[]{:S(2)}, u32[]{:S(2)}) collective-permute-start(bf16[56,640]{1,0:T(8,128)(2,1)S(1)} %get-tuple-element.53), channel_id=1, source_target_pairs={{0,8},{4,12},{8,0},{12,4},{1,9},{5,13},{9,1},{13,5},{2,10},{6,14},... | collective-permute-start | bytes 215048 | tf_op jit(solution)/shard_map/ppermute | solution.py:17
  60.6 6.1 %collective-permute-start.18 = (bf16[56,640]{1,0:T(8,128)(2,1)S(1)}, bf16[56,640]{1,0:T(8,128)(2,1)S(1)}, u32[]{:S(2)}, u32[]{:S(2)}) collective-permute-start(bf16[56,640]{1,0:T(8,128)(2,1)S(1)} %get-tuple-element.52), channel_id=1, source_target_pairs={{0,12},{4,8},{8,4},{12,0},{1,13},{5,9},{9,5},{13,1},{2,14},{6,10},... | collective-permute-start | bytes 215048 | tf_op jit(solution)/shard_map/ppermute | solution.py:17
  62.6 6.6 %collective-permute-start.20 = (bf16[224,320]{0,1:T(8,128)(2,1)S(1)}, bf16[224,320]{0,1:T(8,128)(2,1)S(1)}, u32[]{:S(2)}, u32[]{:S(2)}) collective-permute-start(bf16[224,320]{0,1:T(8,128)(2,1)S(1)} %get-tuple-element.45), channel_id=1, source_target_pairs={{0,2},{1,3},{2,0},{3,1},{4,6},{5,7},{6,4},{7,5},{8,10},{9,11},{10,... | collective-permute-start | bytes 430088 | tf_op jit(solution)/shard_map/ppermute | solution.py:17
  67.6 8.8 %collective-permute-start.19 = (bf16[56,2560]{1,0:T(8,128)(2,1)}, bf16[56,2560]{1,0:T(8,128)(2,1)}, u32[]{:S(2)}, u32[]{:S(2)}) collective-permute-start(bf16[56,2560]{1,0:T(8,128)(2,1)} %pad_maximum_fusion.3), channel_id=1, source_target_pairs={{16,0},{17,1},{18,2},{19,3},{20,4},{21,5},{22,6},{23,7},{24,8},{25... | collective-permute-start | bytes 860168 | tf_op jit(solution)/shard_map/ppermute | solution.py:354
  69.1 1.8 %collective-permute-start.21 = (bf16[224,320]{0,1:T(8,128)(2,1)S(1)}, bf16[224,320]{0,1:T(8,128)(2,1)S(1)}, u32[]{:S(2)}, u32[]{:S(2)}) collective-permute-start(bf16[224,320]{0,1:T(8,128)(2,1)S(1)} %bitcast.165), channel_id=1, source_target_pairs={{0,1},{1,0},{2,3},{3,2},{4,5},{5,4},{6,7},{7,6},{8,9},{9,8},{10,11... | collective-permute-start | bytes 430088 | tf_op jit(solution)/shard_map/ppermute | solution.py:17
  69.2 1.9 %collective-permute-start.22 = (bf16[224,320]{0,1:T(8,128)(2,1)S(1)}, bf16[224,320]{0,1:T(8,128)(2,1)S(1)}, u32[]{:S(2)}, u32[]{:S(2)}) collective-permute-start(bf16[224,320]{0,1:T(8,128)(2,1)S(1)} %collective-permute-done.20), channel_id=1, source_target_pairs={{0,1},{1,0},{2,3},{3,2},{4,5},{5,4},{6,7},{7,6},{8,9},{9,8},{10,11... | collective-permute-start | bytes 430088 | tf_op jit(solution)/shard_map/ppermute | solution.py:17
  86.6 13.5 %slice-start = ((s8[7372800]{0:T(1024)(128)(4,1)}), s8[4194304]{0:T(1024)(128)(4,1)S(1)}, s32[]{:S(2)}) async-start(s8[7372800]{0:T(1024)(128)(4,1)} %bitcast.136), calls=%async_computation | async-start | bytes 8388608
  92.2 8.0 %slice-start.1 = ((s8[7372800]{0:T(1024)(128)(4,1)}), s8[3178496]{0:T(1024)(128)(4,1)S(1)}, s32[]{:S(2)}) async-start(s8[7372800]{0:T(1024)(128)(4,1)} %bitcast.136), calls=%async_computation.1 | async-start | bytes 6356992
  97.8 9.2 %collective-permute-start.24 = (bf16[1,4,56,512]{3,2,1,0:T(8,128)(2,1)S(1)}, bf16[1,4,56,512]{3,2,1,0:T(8,128)(2,1)S(1)}, u32[]{:S(2)}, u32[]{:S(2)}) collective-permute-start(bf16[1,4,56,512]{3,2,1,0:T(8,128)(2,1)S(1)} %bitcast.168), channel_id=1, source_target_pairs={{0,2},{1,3},{2,0},{3,1},{4,6},{5,7},{6,4},{7,5},{8,10},{9,11},{10,... | collective-permute-start | bytes 688136 | tf_op jit(solution)/shard_map/ppermute | solution.py:17
  98.4 18.4 %collective-permute-start.28 = (bf16[2,2,56,768]{3,2,1,0:T(8,128)(2,1)S(1)}, bf16[2,2,56,768]{3,2,1,0:T(8,128)(2,1)S(1)}, u32[]{:S(2)}, u32[]{:S(2)}) collective-permute-start(bf16[2,2,56,768]{3,2,1,0:T(8,128)(2,1)S(1)} %slice.162), channel_id=1, source_target_pairs={{0,4},{4,0},{8,12},{12,8},{1,5},{5,1},{9,13},{13,9},{2,6},{6,2},{1... | collective-permute-start | bytes 1032200 | tf_op jit(solution)/shard_map/ppermute | solution.py:17
  98.6 19.3 %collective-permute-start.32 = (bf16[1,4,56,768]{3,2,1,0:T(8,128)(2,1)S(1)}, bf16[1,4,56,768]{3,2,1,0:T(8,128)(2,1)S(1)}, u32[]{:S(2)}, u32[]{:S(2)}) collective-permute-start(bf16[1,4,56,768]{3,2,1,0:T(8,128)(2,1)S(1)} %bitcast.166), channel_id=1, source_target_pairs={{0,2},{1,3},{2,0},{3,1},{4,6},{5,7},{6,4},{7,5},{8,10},{9,11},{10,... | collective-permute-start | bytes 1032200 | tf_op jit(solution)/shard_map/ppermute | solution.py:17
  104.9 8.5 %collective-permute-start.36 = (bf16[2,2,56,512]{3,2,1,0:T(8,128)(2,1)S(1)}, bf16[2,2,56,512]{3,2,1,0:T(8,128)(2,1)S(1)}, u32[]{:S(2)}, u32[]{:S(2)}) collective-permute-start(bf16[2,2,56,512]{3,2,1,0:T(8,128)(2,1)S(1)} %slice.179), channel_id=1, source_target_pairs={{0,4},{4,0},{8,12},{12,8},{1,5},{5,1},{9,13},{13,9},{2,6},{6,2},{1... | collective-permute-start | bytes 688136 | tf_op jit(solution)/shard_map/ppermute | solution.py:17
  107.1 7.5 %collective-permute-start.25 = (bf16[2,56,512]{2,1,0:T(8,128)(2,1)S(1)}, bf16[2,56,512]{2,1,0:T(8,128)(2,1)S(1)}, u32[]{:S(2)}, u32[]{:S(2)}) collective-permute-start(bf16[2,56,512]{2,1,0:T(8,128)(2,1)S(1)} %slice.157), channel_id=1, source_target_pairs={{0,4},{4,0},{8,12},{12,8},{1,5},{5,1},{9,13},{13,9},{2,6},{6,2},{1... | collective-permute-start | bytes 344072 | tf_op jit(solution)/shard_map/ppermute | solution.py:17
  113.5 12.5 %collective-permute-start.37 = (bf16[1,2,56,512]{3,2,1,0:T(8,128)(2,1)S(1)}, bf16[1,2,56,512]{3,2,1,0:T(8,128)(2,1)S(1)}, u32[]{:S(2)}, u32[]{:S(2)}) collective-permute-start(bf16[1,2,56,512]{3,2,1,0:T(8,128)(2,1)S(1)} %slice.263), channel_id=1, source_target_pairs={{0,8},{4,12},{8,0},{12,4},{1,9},{5,13},{9,1},{13,5},{2,10},{6,14},... | collective-permute-start | bytes 344072 | tf_op jit(solution)/shard_map/ppermute | solution.py:17
  114.6 12.9 %collective-permute-start.26 = (bf16[1,56,512]{2,1,0:T(8,128)(2,1)S(1)}, bf16[1,56,512]{2,1,0:T(8,128)(2,1)S(1)}, u32[]{:S(2)}, u32[]{:S(2)}) collective-permute-start(bf16[1,56,512]{2,1,0:T(8,128)(2,1)S(1)} %slice.265), channel_id=1, source_target_pairs={{0,8},{4,12},{8,0},{12,4},{1,9},{5,13},{9,1},{13,5},{2,10},{6,14},... | collective-permute-start | bytes 172040 | tf_op jit(solution)/shard_map/ppermute | solution.py:17
  116.9 18.3 %collective-permute-start.29 = (bf16[1,2,56,768]{3,2,1,0:T(8,128)(2,1)S(1)}, bf16[1,2,56,768]{3,2,1,0:T(8,128)(2,1)S(1)}, u32[]{:S(2)}, u32[]{:S(2)}) collective-permute-start(bf16[1,2,56,768]{3,2,1,0:T(8,128)(2,1)S(1)} %slice.262), channel_id=1, source_target_pairs={{0,8},{4,12},{8,0},{12,4},{1,9},{5,13},{9,1},{13,5},{2,10},{6,14},... | collective-permute-start | bytes 516104 | tf_op jit(solution)/shard_map/ppermute | solution.py:17
  117.9 18.8 %collective-permute-start.33 = (bf16[2,56,768]{2,1,0:T(8,128)(2,1)S(1)}, bf16[2,56,768]{2,1,0:T(8,128)(2,1)S(1)}, u32[]{:S(2)}, u32[]{:S(2)}) collective-permute-start(bf16[2,56,768]{2,1,0:T(8,128)(2,1)S(1)} %slice.174), channel_id=1, source_target_pairs={{0,4},{4,0},{8,12},{12,8},{1,5},{5,1},{9,13},{13,9},{2,6},{6,2},{1... | collective-permute-start | bytes 516104 | tf_op jit(solution)/shard_map/ppermute | solution.py:17
  126.0 6.4 %collective-permute-start.38 = (bf16[1,56,512]{2,1,0:T(8,128)(2,1)S(1)}, bf16[1,56,512]{2,1,0:T(8,128)(2,1)S(1)}, u32[]{:S(2)}, u32[]{:S(2)}) collective-permute-start(bf16[1,56,512]{2,1,0:T(8,128)(2,1)S(1)} %fusion.22), channel_id=1, source_target_pairs={{0,2},{1,3},{2,0},{3,1},{4,6},{5,7},{6,4},{7,5},{8,10},{9,11},{10,... | collective-permute-start | bytes 172040 | tf_op jit(solution)/shard_map/ppermute | solution.py:17
  127.5 16.1 %collective-permute-start.27 = (bf16[56,512]{1,0:T(8,128)(2,1)S(1)}, bf16[56,512]{1,0:T(8,128)(2,1)S(1)}, u32[]{:S(2)}, u32[]{:S(2)}) collective-permute-start(bf16[56,512]{1,0:T(8,128)(2,1)S(1)} %fusion.20), channel_id=1, source_target_pairs={{0,16},{1,17},{2,18},{3,19},{4,20},{5,21},{6,22},{7,23},{8,24},{9,... | collective-permute-start | bytes 172040 | tf_op jit(solution)/shard_map/ppermute | solution.py:388
  132.4 11.3 %collective-permute-start.39 = (bf16[56,512]{1,0:T(8,128)(2,1)S(1)}, bf16[56,512]{1,0:T(8,128)(2,1)S(1)}, u32[]{:S(2)}, u32[]{:S(2)}) collective-permute-start(bf16[56,512]{1,0:T(8,128)(2,1)S(1)} %fusion.17), channel_id=1, source_target_pairs={{0,16},{1,17},{2,18},{3,19},{4,20},{5,21},{6,22},{7,23},{8,24},{9,... | collective-permute-start | bytes 172040 | tf_op jit(solution)/shard_map/ppermute | solution.py:388
  135.2 4.6 %collective-permute-start.30 = (bf16[1,56,768]{2,1,0:T(8,128)(2,1)S(1)}, bf16[1,56,768]{2,1,0:T(8,128)(2,1)S(1)}, u32[]{:S(2)}, u32[]{:S(2)}) collective-permute-start(bf16[1,56,768]{2,1,0:T(8,128)(2,1)S(1)} %fusion.21), channel_id=1, source_target_pairs={{0,2},{1,3},{2,0},{3,1},{4,6},{5,7},{6,4},{7,5},{8,10},{9,11},{10,... | collective-permute-start | bytes 258056 | tf_op jit(solution)/shard_map/ppermute | solution.py:17
  136.7 5.4 %collective-permute-start.34 = (bf16[1,56,768]{2,1,0:T(8,128)(2,1)S(1)}, bf16[1,56,768]{2,1,0:T(8,128)(2,1)S(1)}, u32[]{:S(2)}, u32[]{:S(2)}) collective-permute-start(bf16[1,56,768]{2,1,0:T(8,128)(2,1)S(1)} %slice.264), channel_id=1, source_target_pairs={{0,8},{4,12},{8,0},{12,4},{1,9},{5,13},{9,1},{13,5},{2,10},{6,14},... | collective-permute-start | bytes 258056 | tf_op jit(solution)/shard_map/ppermute | solution.py:17
  139.8 5.9 %copy-start.7 = (bf16[1,1,4,14,640]{4,3,2,1,0:T(8,128)(2,1)S(1)}, bf16[1,1,4,14,640]{4,3,2,1,0:T(8,128)(2,1)}, u32[]{:S(2)}) copy-start(bf16[1,1,4,14,640]{4,3,2,1,0:T(8,128)(2,1)} %concatenate.43) | copy-start | bytes 215044
  139.8 3.8 %collective-permute-start.31 = (bf16[56,768]{1,0:T(8,128)(2,1)S(1)}, bf16[56,768]{1,0:T(8,128)(2,1)S(1)}, u32[]{:S(2)}, u32[]{:S(2)}) collective-permute-start(bf16[56,768]{1,0:T(8,128)(2,1)S(1)} %fusion.12), channel_id=1, source_target_pairs={{0,16},{1,17},{2,18},{3,19},{4,20},{5,21},{6,22},{7,23},{8,24},{9,... | collective-permute-start | bytes 258056 | tf_op jit(solution)/shard_map/ppermute | solution.py:388
  142.2 3.4 %collective-permute-start.35 = (bf16[56,768]{1,0:T(8,128)(2,1)S(1)}, bf16[56,768]{1,0:T(8,128)(2,1)S(1)}, u32[]{:S(2)}, u32[]{:S(2)}) collective-permute-start(bf16[56,768]{1,0:T(8,128)(2,1)S(1)} %fusion.8), channel_id=1, source_target_pairs={{0,16},{1,17},{2,18},{3,19},{4,20},{5,21},{6,22},{7,23},{8,24},{9,... | collective-permute-start | bytes 258056 | tf_op jit(solution)/shard_map/ppermute | solution.py:388
  (6 other events, 17.6 us)
where the time goes:
time: 148 us; the launch traced here: 147 us
  starting transfers between devices  54.3 us (37%)
  waiting for transfers between devices  48.7 us (33%)
  Pallas kernels  25.9 us (18%)
  local copies, waits for them, and re-layouts  12 us (8%)
  other arithmetic  4.98 us (3%)
    ppermute x33, starting transfers between devices, swap(): return lax.ppermute(array, axis, [(i, i ^ k * unit) for i in range(count)])  39.3 us
    ppermute x33, waiting for transfers between devices, swap(): return lax.ppermute(array, axis, [(i, i ^ k * unit) for i in range(count)])  38.7 us
    pallas_call x4, Pallas kernels, mix(): pl.pallas_call(functools.partial(mix_kernel, first, count), out_shape=jax...  20.4 us
    ppermute x4, starting transfers between devices, body(): fars.append(lax.ppermute(done, 'section', [(0, 1)]))  10.3 us
    ppermute x1, waiting for transfers between devices, body(): above = lax.ppermute(tails, 'ch', [(i, i + 1) for i in range(shards - 1)])  6.97 us
    unnamed x33, local copies, waits for them, and re-layouts  6.81 us
    pallas_call x1, Pallas kernels, unfold(): pl.pallas_call(functools.partial(unfold_kernel, pairs, imgs, ocols, kd),...  3.03 us
  transfers between devices with their start and end apart: 40, of which 19 were waited for; matrix products, arithmetic and copies ran while one was open for 7% of the time, Pallas kernels for 7%

commit v1 on v0

--- a/solution.py
+++ b/solution.py
@@ -15,10 +15,6 @@
 def swap(array, axis, k, unit=1):
     count = lax.axis_size(axis)
     return lax.ppermute(array, axis, [(i, i ^ (k * unit)) for i in range(count)])
-
-
-def resident(array):
-    return pltpu.with_memory_space_constraint(array, pltpu.VMEM)
 
 
 def pick(stack, index):
@@ -101,28 +97,141 @@
     )(ids, gain, shift, *own, *other)
 
 
-def mix_kernel(first, step, a_own, a_other, w_own, w_other, out):
-    count = out.shape[1]
-    for at in range(0, count, step):
-        cut = slice(first + at, first + at + step)
-        value = jnp.dot(a_own[...], w_own[:, cut], preferred_element_type=F32)
-        value = value + jnp.dot(a_other[...], w_other[:, cut], preferred_element_type=F32)
-        out[:, at : at + step] = value.astype(BF16)
-
-
-def mix(a_own, a_other, w_own, w_other, first, count):
-    rows, deep = a_own.shape
-    return pl.pallas_call(
-        functools.partial(mix_kernel, first, count),
-        out_shape=jax.ShapeDtypeStruct((rows, count), BF16),
-        in_specs=[whole()] * 4,
-        out_specs=whole(),
+def copy_rows(out, value, rows, px):
+    for i, row in enumerate(rows):
+        out[i * px : (i + 1) * px, :] = value[row * px : (row + 1) * px].astype(out.dtype)
+
+
+def mix_kernel(rows, px, a_own, a_other, w_own, w_other, sent, kept):
+    value = jnp.dot(a_own[...], w_own[...], preferred_element_type=F32)
+    value = value + jnp.dot(a_other[...], w_other[...], preferred_element_type=F32)
+    copy_rows(sent, value, rows[0], px)
+    copy_rows(kept, value, rows[1], px)
+
+
+def mix(a_own, a_other, w_own, w_other, first, count, step, rows, px):
+    total, deep = a_own.shape
+    weight = pl.BlockSpec((deep, step), lambda i: (0, first // step + i))
+    sizes = [len(r) * px for r in rows]
+    return pl.pallas_call(
+        functools.partial(mix_kernel, rows, px),
+        grid=(count // step,),
+        out_shape=[
+            jax.ShapeDtypeStruct((sizes[0], count), BF16),
+            jax.ShapeDtypeStruct((sizes[1], count), F32),
+        ],
+        in_specs=[whole()] * 2 + [weight] * 2,
+        out_specs=[pl.BlockSpec((size, step), lambda i: (0, i)) for size in sizes],
         name="mix",
-        compiler_params=pltpu.CompilerParams(vmem_limit_bytes=8 << 20),
+        compiler_params=pltpu.CompilerParams(vmem_limit_bytes=16 << 20),
         cost_estimate=pl.CostEstimate(
-            flops=4 * rows * deep * count, bytes_accessed=2 * rows * count, transcendentals=0
+            flops=4 * total * deep * count,
+            bytes_accessed=4 * deep * count + 3 * total * count,
+            transcendentals=0,
         ),
     )(a_own, a_other, w_own, w_other)
+
+
+def merge_kernel(rows, px, kept, came, *outs):
+    value = kept[...] + came[...].astype(F32)
+    for out, some in zip(outs, rows):
+        copy_rows(out, value, some, px)
+
+
+def merge(kept, came, rows, px):
+    count = kept.shape[1]
+    return pl.pallas_call(
+        functools.partial(merge_kernel, rows, px),
+        out_shape=[jax.ShapeDtypeStruct((len(r) * px, count), t) for r, t in zip(rows, (BF16, F32))],
+        in_specs=[whole()] * 2,
+        out_specs=[whole()] * 2,
+        name="merge",
+        compiler_params=pltpu.CompilerParams(vmem_limit_bytes=10 << 20),
+        cost_estimate=pl.CostEstimate(flops=kept.size, bytes_accessed=10 * kept.size, transcendentals=0),
+    )(kept, came)
+
+
+def finish_kernel(first, kept, came, extra, out):
+    count = kept.shape[1]
+    value = kept[...] + came[...].astype(F32) + extra[:, first : first + count].astype(F32)
+    out[...] = value.astype(BF16)
+
+
+def finish(kept, came, extra, first):
+    return pl.pallas_call(
+        functools.partial(finish_kernel, first),
+        out_shape=jax.ShapeDtypeStruct(kept.shape, BF16),
+        in_specs=[whole()] * 3,
+        out_specs=whole(),
+        name="finish",
+        compiler_params=pltpu.CompilerParams(vmem_limit_bytes=6 << 20),
+        cost_estimate=pl.CostEstimate(flops=2 * kept.size, bytes_accessed=10 * kept.size, transcendentals=0),
+    )(kept, came, extra)
+
+
+def join_kernel(*refs):
+    for i, ref in enumerate(refs[:-1]):
+        refs[-1][i] = ref[...]
+
+
+def join(parts):
+    return pl.pallas_call(
+        join_kernel,
+        out_shape=jax.ShapeDtypeStruct((len(parts),) + parts[0].shape, parts[0].dtype),
+        in_specs=[whole()] * len(parts),
+        out_specs=whole(),
+        name="join",
+        compiler_params=pltpu.CompilerParams(vmem_limit_bytes=6 << 20),
+    )(*parts)
+
+
+def project_kernel(groups, pairs, ids, *refs):
+    pooled = refs[:groups]
+    own, twin = refs[groups : groups + pairs], refs[groups + pairs : groups + 2 * pairs]
+    backs = refs[groups + 2 * pairs : 2 * groups + 2 * pairs]
+    parts = refs[2 * groups + 2 * pairs : 2 * groups + 3 * pairs]
+    weight, held = refs[2 * groups + 3 * pairs :]
+    z, y, core = ids[1], ids[4], ids[5]
+    px, depth = pooled[0].shape
+    for k in range(groups):
+        for j in range(pairs):
+            for half, source in enumerate((own, twin)):
+                place = (jnp.bitwise_xor(z, k) * pairs + jnp.bitwise_xor(y, j)) * 2 + jnp.bitwise_xor(core, half)
+                weight[place] = source[j][k].astype(F32)
+    slab = weight[...].reshape(depth, weight.shape[2]).astype(BF16)
+    kc = weight.shape[2] // pairs
+    rows = jnp.concatenate([ref[...].astype(F32) for ref in pooled]).astype(BF16)
+    value = jnp.dot(rows, slab, preferred_element_type=F32)
+    for k in range(groups):
+        backs[k][...] = value[k * px : (k + 1) * px].astype(BF16)
+    for j in range(pairs):
+        held[j] = value[:, j * kc : (j + 1) * kc].astype(BF16)
+    for j in range(pairs):
+        parts[j][...] = held[jnp.bitwise_xor(y, j)]
+
+
+def project(ids, pooled, own, twin):
+    groups, pairs = len(pooled), len(own)
+    px, depth = pooled[0].shape
+    _, deep, slab = own[0].shape
+    kc = slab // pairs
+    back = jax.ShapeDtypeStruct((px, slab), BF16)
+    part = jax.ShapeDtypeStruct((groups * px, kc), BF16)
+    return pl.pallas_call(
+        functools.partial(project_kernel, groups, pairs),
+        out_shape=[back] * groups + [part] * pairs,
+        in_specs=[whole(pltpu.SMEM)] + [whole()] * (groups + 2 * pairs),
+        out_specs=[whole()] * (groups + pairs),
+        scratch_shapes=[
+            pltpu.VMEM((groups * pairs * 2, deep, slab), F32),
+            pltpu.VMEM((pairs, groups * px, kc), BF16),
+        ],
+        name="project",
+        compiler_params=pltpu.CompilerParams(vmem_limit_bytes=14 << 20),
+        cost_estimate=pl.CostEstimate(
+            flops=2 * groups * px * depth * slab, bytes_accessed=4 * depth * slab, transcendentals=0
+        ),
+    )(ids, *pooled, *own, *twin)
 
 
 def packing(rows, colp, c1):
@@ -133,8 +242,10 @@
     return main, rest, deep, main * rows * colp + deep * colp
 
 
-def pack_kernel(groups, per, c1, colp, ids, pixels, above, below, gain, shift, *refs):
-    outs, mean, held, pair = refs[:groups], refs[groups], refs[groups + 1], refs[groups + 2]
+def pack_kernel(groups, per, c1, colp, ids, pixels, above, below, gain, shift, projection, *refs):
+    outs, mean = refs[:groups], refs[groups]
+    cuts = refs[groups + 1 : 2 * groups + 1]
+    held, pair, strip = refs[2 * groups + 1 :]
     sec, z, ch, last = ids[0], ids[1], ids[2], ids[3]
     _, rows, cols, depth = pixels.shape
     main, rest, deep, size = packing(rows + 2, colp, c1)
@@ -177,26 +288,38 @@
                     held[g, at : at + colp, into : into + rest] = value[:, lane : lane + rest]
     for k in range(groups):
         outs[k][...] = held[jnp.bitwise_xor(z, k)]
-
-
-def pack(ids, pixels, above, below, gain, shift, groups, per, colp):
+    deep, slab = cuts[0].shape
+    for i in range(c1 // deep):
+        for g in range(groups):
+            strip[i, g] = projection[i * deep : (i + 1) * deep, g * slab : (g + 1) * slab].astype(F32)
+    for k in range(groups):
+        cuts[k][...] = strip[ch, jnp.bitwise_xor(z, k)].astype(BF16)
+
+
+def pack(ids, pixels, above, below, gain, shift, projection, groups, shards, per, colp):
     _, rows, cols, depth = pixels.shape
     c1 = depth // groups
     size = packing(rows + 2, colp, c1)[3]
     block = jax.ShapeDtypeStruct((per * size, 128), BF16)
     half = jax.ShapeDtypeStruct((per, rows * cols // 4, depth), F32)
+    deep, slab = c1 // shards, projection.shape[1] // groups
+    cut = jax.ShapeDtypeStruct((deep, slab), BF16)
     return pl.pallas_call(
         functools.partial(pack_kernel, groups, per, c1, colp),
-        out_shape=[block] * groups + [half],
-        in_specs=[whole(pltpu.SMEM)] + [whole()] * 5,
-        out_specs=[whole()] * (groups + 1),
-        scratch_shapes=[pltpu.VMEM((groups, per * size, 128), BF16), pltpu.VMEM((depth // 128, cols, 128), F32)],
+        out_shape=[block] * groups + [half] + [cut] * groups,
+        in_specs=[whole(pltpu.SMEM)] + [whole()] * 6,
+        out_specs=[whole()] * (2 * groups + 1),
+        scratch_shapes=[
+            pltpu.VMEM((groups, per * size, 128), BF16),
+            pltpu.VMEM((depth // 128, cols, 128), F32),
+            pltpu.VMEM((shards, groups, deep, slab), F32),
+        ],
         name="pack",
-        compiler_params=pltpu.CompilerParams(vmem_limit_bytes=8 << 20),
+        compiler_params=pltpu.CompilerParams(vmem_limit_bytes=14 << 20),
         cost_estimate=pl.CostEstimate(
             flops=4 * rows * cols * depth, bytes_accessed=6 * rows * cols * depth, transcendentals=0
         ),
-    )(ids, pixels, above, below, gain, shift)
+    )(ids, pixels, above, below, gain, shift, projection)
 
 
 def stage_kernel(groups, per, rows, cols, colp, c1, *refs):
@@ -273,28 +396,6 @@
     )(*blocks, kernel)
 
 
-def sum_images(value, groups):
-    k = 1
-    while k < groups:
-        sent = value.astype(BF16)
-        value = value[0::2].astype(F32) + swap(sent[1::2], "img", k).astype(F32)
-        k *= 2
-    return value[0]
-
-
-def sum_pairs(value, pairs):
-    k = 1
-    while k < pairs:
-        sent = value.astype(BF16)
-        value = value[0::2].astype(F32) + swap(sent[1::2], "ch", k, 2).astype(F32)
-        k *= 2
-    return value[0]
-
-
-def cross(stack_of, index, count):
-    return [pick(stack_of, index ^ i) for i in range(count)]
-
-
 def body(pixels, first_gain, first_shift, first_kernel, projection, second_gain, second_shift, second_kernel):
     sec = lax.axis_index("section")
     z = lax.axis_index("img")
@@ -321,44 +422,40 @@
     above = lax.ppermute(tails, "ch", [(i, i + 1) for i in range(shards - 1)])
     below = lax.ppermute(heads, "ch", [(i + 1, i) for i in range(shards - 1)])
     ids = jnp.stack([sec, z, ch, jnp.int32(shards - 1), y, core, z * pairs + y]).astype(jnp.int32)
-    *blocks, mean = pack(
-        ids, pixels, above, below, first_gain.reshape(1, -1), first_shift.reshape(1, -1), groups, per, colp
+    packed = pack(
+        ids,
+        pixels,
+        above,
+        below,
+        first_gain.reshape(1, -1),
+        first_shift.reshape(1, -1),
+        projection,
+        groups,
+        shards,
+        per,
+        colp,
     )
+    blocks, mean, cuts = packed[:groups], packed[groups], packed[groups + 1 :]
     got = [blocks[0]] + [swap(blocks[k], "img", k) for k in range(1, groups)]
 
-    part_rows = c1 // shards
-    projection, mean = lax.optimization_barrier((projection, mean))
-    mine_rows = lax.dynamic_slice_in_dim(projection, ch * part_rows, part_rows, 0)
-    proj_parts = mine_rows.reshape(part_rows, groups, slab).transpose(1, 0, 2)
-    proj_rel = [pick(proj_parts, z)] + [swap(pick(proj_parts, z ^ k), "img", k) for k in range(1, groups)]
-    proj_abs = jnp.stack(cross(jnp.stack(proj_rel), z, groups))
-    proj_pairs = [proj_abs] + [swap(proj_abs, "ch", k, 2) for k in range(1, pairs)]
-    proj_pairs = jnp.stack(cross(jnp.stack(proj_pairs), y, pairs), axis=1)
-    proj_twin = swap(proj_pairs, "ch", 1)
-    proj_cores = jnp.where(core == 0, jnp.stack([proj_pairs, proj_twin], 2), jnp.stack([proj_twin, proj_pairs], 2))
-    proj_slab = proj_cores.reshape(depth, slab)
+    proj_z = join([cuts[0]] + [swap(cuts[k], "img", k) for k in range(1, groups)])
+    proj_own = [proj_z] + [swap(proj_z, "ch", k, 2) for k in range(1, pairs)]
+    proj_twin = [swap(part, "ch", 1) for part in proj_own]
 
     total, *sent = stage(got, first_kernel.reshape(9, c1, depth), per, rows, cols, colp)
     for k in range(1, groups):
         total = total + swap(sent[k - 1], "img", k).astype(F32)
     pooled = (total + mean.reshape(total.shape)).astype(BF16)
-    pooled_all = jnp.stack([pooled] + [swap(pooled, "img", k) for k in range(1, groups)])
+    pooled_all = [pooled] + [swap(pooled, "img", k) for k in range(1, groups)]
     px = per * orows * ocols
-    projected = jnp.dot(
-        pooled_all.reshape(groups * px, depth), proj_slab, preferred_element_type=F32
-    ).astype(BF16)
-
-    back = projected.reshape(groups, px, slab)
-    back_rel = jnp.stack([back[0]] + [swap(back[k], "img", k) for k in range(1, groups)])
-    mine_projected = jnp.concatenate([pick(back_rel, z ^ i) for i in range(groups)], axis=1)
-    far_projected = lax.ppermute(mine_projected, "section", [(1, 0)])
-
     imgs = groups * per
     out_px = orows * ocols
-    by_pair = projected.reshape(groups * px, pairs, kc).transpose(1, 0, 2)
-    chip = [pick(by_pair, y)]
-    chip += [swap(pick(by_pair, y ^ k), "ch", k, 2) for k in range(1, pairs)]
+    made = project(ids, pooled_all, proj_own, proj_twin)
+    back, chip = made[:groups], made[groups:]
+
+    chip = [chip[0]] + [swap(chip[k], "ch", k, 2) for k in range(1, pairs)]
     twin = [swap(part, "ch", 1) for part in chip]
+    back = [back[0]] + [swap(back[k], "img", k) for k in range(1, groups)]
     a_own, a_other = unfold(
         ids,
         second_gain.reshape(groups * pairs, kc),
@@ -367,25 +464,42 @@
         [c.reshape(imgs, out_px, kc) for c in twin],
         ocols,
     )
-    w_own = resident(second_kernel.reshape(9 * kd, wide))
-    w_other = resident(other_kernel.reshape(9 * kd, wide))
+    w_own = second_kernel.reshape(9 * kd, wide)
+    w_other = other_kernel.reshape(9 * kd, wide)
 
     unit = wide // 10
+    plan = ((0, 2), (1, 3), (0, 3), (1, 2))
+    names = [("ch", 1 << i, 2) for i in range(pairs.bit_length() - 1)]
+    names_z = [("img", 1 << i, 1) for i in range(groups.bit_length() - 1)]
+    values, first = [], 0
+    for kind, n in plan:
+        hops = names_z + names if kind else names + names_z
+        keys = [(a, b) for a in range(pairs) for b in range(groups)]
+
+        def split(keys, hop):
+            axis, k, _ = hop
+            bit = [key[0] & k if axis == "ch" else key[1] & k for key in keys]
+            rows = ([i for i, x in enumerate(bit) if x], [i for i, x in enumerate(bit) if not x])
+            return rows, [key for key, x in zip(keys, bit) if not x]
+
+        rows, keys = split(keys, hops[0])
+        sent, kept = mix(a_own, a_other, w_own, w_other, first, n * unit, unit, rows, px)
+        for h, hop in enumerate(hops):
+            axis, k, size = hop
+            came = swap(sent, axis, k, size)
+            if h + 1 < len(hops):
+                rows, keys = split(keys, hops[h + 1])
+                sent, kept = merge(kept, came, rows, px)
+        values.append((kept, came, first, n * unit))
+        first += n * unit
+
+    back_rel = join(back)
+    mine_projected = jnp.concatenate([pick(back_rel, z ^ i) for i in range(groups)], axis=1)
+    far_projected = lax.ppermute(mine_projected, "section", [(1, 0)])
     outs, fars = [], []
-    first = 0
-    for j, n in enumerate((2 * unit, 3 * unit, 3 * unit, 2 * unit)):
-        value = mix(a_own, a_other, w_own, w_other, first, n)
-        value = value.reshape(pairs, groups, px, n)
-        if j % 2 == 0:
-            total = sum_pairs(value, pairs)
-            total = sum_images(total, groups)
-        else:
-            total = sum_images(value.swapaxes(0, 1), groups)
-            total = sum_pairs(total, pairs)
-        done = (total + mine_projected[:, first : first + n].astype(F32)).astype(BF16)
-        first += n
-        outs.append(done)
-        fars.append(lax.ppermute(done, "section", [(0, 1)]))
+    for j, (kept, came, first, n) in enumerate(values):
+        outs.append(finish(kept, came, mine_projected, first))
+        fars.append(lax.ppermute(outs[j], "section", [(0, 1)]))
     block = jnp.concatenate(outs, axis=-1)
     far_block = jnp.concatenate(fars, axis=-1)
     first = jnp.stack([mine_projected, far_projected])

time: 148 us -> 132 us (0.89)
  local copies, waits for them, and re-layouts: 12 us -> 6.21 us
  other arithmetic: 4.98 us -> 0.34 us
  Pallas kernels: 25.9 us -> 21.6 us
    pallas_call x4 -> x19, Pallas kernels: 20.4 us -> 16 us  [the longest x4 14.3 us: mix(): pl.pallas_call(functools.partial(mix_kernel, rows, px), grid=(count // st...]
    ppermute x4, starting transfers between devices: 10.3 us -> 7.28 us  [body(): fars.append(lax.ppermute(outs[j], 'section', [(0, 1)]))]
    unnamed x33 -> x15, local copies, waits for them, and re-layouts: 6.81 us -> 4.25 us
    ppermute x33 -> x34, starting transfers between devices: 39.3 us -> 41.4 us  [swap(): return lax.ppermute(array, axis, [(i, i ^ k * unit) for i in range(count)])]
    another operation x6 -> x0, other arithmetic: 2.12 us -> none  [the longest x1 1.11 us: body(): proj_pairs = jnp.stack(cross(jnp.stack(proj_pairs), y, pairs), axis=1)]
    ppermute x33 -> x34, waiting for transfers between devices: 38.7 us -> 40.7 us  [swap(): return lax.ppermute(array, axis, [(i, i ^ k * unit) for i in range(count)])]
  transfers between devices with their start and end apart: 40 -> 41, of which waited for: 19 -> 18; matrix products, arithmetic and copies ran while one was open for 7% -> 1% of each run, Pallas kernels for 7% -> 6%
where the time goes in v1:
time: 132 us
  starting transfers between devices  53.4 us (40%)
  waiting for transfers between devices  49.4 us (37%)
  Pallas kernels  21.6 us (16%)
  local copies, waits for them, and re-layouts  6.21 us (5%)
    ppermute x34, starting transfers between devices, swap(): return lax.ppermute(array, axis, [(i, i ^ k * unit) for i in range(count)])  41.4 us
    ppermute x34, waiting for transfers between devices, swap(): return lax.ppermute(array, axis, [(i, i ^ k * unit) for i in range(count)])  40.7 us
    pallas_call x4, Pallas kernels, mix(): pl.pallas_call(functools.partial(mix_kernel, rows, px), grid=(count // st...  14.3 us
    ppermute x4, starting transfers between devices, body(): fars.append(lax.ppermute(outs[j], 'section', [(0, 1)]))  7.28 us
    ppermute x1, waiting for transfers between devices, body(): above = lax.ppermute(tails, 'ch', [(i, i + 1) for i in range(shards - 1)])  6.84 us
    unnamed x15, local copies, waits for them, and re-layouts  4.25 us
    pallas_call x1, Pallas kernels, unfold(): pl.pallas_call(functools.partial(unfold_kernel, pairs, imgs, ocols, kd),...  3.03 us
  transfers between devices with their start and end apart: 41, of which 18 were waited for; matrix products, arithmetic and copies ran while one was open for 1% of the time, Pallas kernels for 6%

profile of v1, /device:TPU:0, one launch (start us, length us, event | category | flops | bytes accessed | tf_op | source)
XLA Modules:
  0.0 131.6 jit_solution(13905079003667296884)
XLA Ops:
  0.6 1.1 copy.17.pixels
  1.8 2.1 %collective-permute-start = (bf16[1,1,28,640]{3,2,1,0:T(8,128)(2,1)S(1)}, bf16[1,1,28,640]{3,2,1,0:T(8,128)(2,1)S(1)}, u32[]{:S(2)}, u32[]{:S(2)}) collective-permute-start(bf16[1,1,28,640]{3,2,1,0:T(8,128)(2,1)S(1)} %constant_dynamic-slice_fusion.5), channel_id=1, source_target_pairs={{0,1},{1,2},{2,3},{4,5},{5,6},{6,7},{8,9},{9,10},{10,11},{12,13},{... | collective-permute-start | bytes 107528 | tf_op jit(solution)/shard_map/ppermute | solution.py:422
  3.9 1.3 collective-permute-start.1
  5.4 6.8 %collective-permute-done.above = bf16[1,1,28,640]{3,2,1,0:T(8,128)(2,1)S(1)} collective-permute-done((bf16[1,1,28,640]{3,2,1,0:T(8,128)(2,1)S(1)}, bf16[1,1,28,640]{3,2,1,0:T(8,128)(2,1)S(1)}, u32[]{:S(2)}, u32[]{:S(2)}) %collective-permute-start) | collective-permute-done | bytes 35872 | tf_op jit(solution)/shard_map/ppermute | solution.py:422
  13.3 3.0 %collective-permute-start.11 = (bf16[40,640]{1,0:T(8,128)(2,1)S(1)}, bf16[40,640]{1,0:T(8,128)(2,1)S(1)}, u32[]{:S(2)}, u32[]{:S(2)}) collective-permute-start(bf16[40,640]{1,0:T(8,128)(2,1)S(1)} %get-tuple-element.60), channel_id=1, source_target_pairs={{0,4},{4,0},{8,12},{12,8},{1,5},{5,1},{9,13},{13,9},{2,6},{6,2},{1... | collective-permute-start | bytes 153608 | tf_op jit(solution)/shard_map/ppermute | solution.py:17
  16.3 2.6 %collective-permute-start.12 = (bf16[40,640]{1,0:T(8,128)(2,1)S(1)}, bf16[40,640]{1,0:T(8,128)(2,1)S(1)}, u32[]{:S(2)}, u32[]{:S(2)}) collective-permute-start(bf16[40,640]{1,0:T(8,128)(2,1)S(1)} %get-tuple-element.61), channel_id=1, source_target_pairs={{0,8},{4,12},{8,0},{12,4},{1,9},{5,13},{9,1},{13,5},{2,10},{6,14},... | collective-permute-start | bytes 153608 | tf_op jit(solution)/shard_map/ppermute | solution.py:17
  19.8 3.5 %collective-permute-start.3 = (bf16[416,128]{1,0:T(8,128)(2,1)S(1)}, bf16[416,128]{1,0:T(8,128)(2,1)S(1)}, u32[]{:S(2)}, u32[]{:S(2)}) collective-permute-start(bf16[416,128]{1,0:T(8,128)(2,1)S(1)} %get-tuple-element.52), channel_id=1, source_target_pairs={{0,8},{4,12},{8,0},{12,4},{1,9},{5,13},{9,1},{13,5},{2,10},{6,14},... | collective-permute-start | bytes 319496 | tf_op jit(solution)/shard_map/ppermute | solution.py:17
  23.3 2.3 %collective-permute-start.4 = (bf16[416,128]{1,0:T(8,128)(2,1)S(1)}, bf16[416,128]{1,0:T(8,128)(2,1)S(1)}, u32[]{:S(2)}, u32[]{:S(2)}) collective-permute-start(bf16[416,128]{1,0:T(8,128)(2,1)S(1)} %get-tuple-element.53), channel_id=1, source_target_pairs={{0,12},{4,8},{8,4},{12,0},{1,13},{5,9},{9,5},{13,1},{2,14},{6,10},... | collective-permute-start | bytes 319496 | tf_op jit(solution)/shard_map/ppermute | solution.py:17
  25.6 1.6 %collective-permute-start.14 = (bf16[4,40,640]{2,1,0:T(8,128)(2,1)S(1)}, bf16[4,40,640]{2,1,0:T(8,128)(2,1)S(1)}, u32[]{:S(2)}, u32[]{:S(2)}) collective-permute-start(bf16[4,40,640]{2,1,0:T(8,128)(2,1)S(1)} %join.2.refs_4_), channel_id=1, source_target_pairs={{0,2},{1,3},{2,0},{3,1},{4,6},{5,7},{6,4},{7,5},{8,10},{9,11},{10,... | collective-permute-start | bytes 614408 | tf_op jit(solution)/shard_map/ppermute | solution.py:17
  27.2 4.7 %collective-permute-done.3.refs_2_ = bf16[416,128]{1,0:T(8,128)(2,1)S(1)} collective-permute-done((bf16[416,128]{1,0:T(8,128)(2,1)S(1)}, bf16[416,128]{1,0:T(8,128)(2,1)S(1)}, u32[]{:S(2)}, u32[]{:S(2)}) %collective-permute-start.3) | collective-permute-done | bytes 106528 | tf_op jit(solution)/shard_map/ppermute | solution.py:17
  31.9 1.5 %stage.1 = (f32[56,640]{1,0:T(8,128)S(1)}, bf16[56,640]{1,0:T(8,128)(2,1)S(1)}, bf16[56,640]{1,0:T(8,128)(2,1)S(1)}, bf16[56,640]{1,0:T(8,128)(2,1)S(1)}) custom-call(bf16[416,128]{1,0:T(8,128)(2,1)S(1)} %get-tuple-element.50.refs_0_, bf16[416,128]{1,0:T(8,128)(2,1)S(1)} %collective-permute-done.2.refs_1_, ...), custom_call_target="tpu_custom_call" | custom-call | flops 471859200 | bytes 573440 | tf_op jit(solution)/shard_map/stage/pallas_call | solution.py:380
  33.5 1.9 %collective-permute-start.5 = (bf16[56,640]{1,0:T(8,128)(2,1)S(1)}, bf16[56,640]{1,0:T(8,128)(2,1)S(1)}, u32[]{:S(2)}, u32[]{:S(2)}) collective-permute-start(bf16[56,640]{1,0:T(8,128)(2,1)S(1)} %get-tuple-element.55), channel_id=1, source_target_pairs={{0,4},{4,0},{8,12},{12,8},{1,5},{5,1},{9,13},{13,9},{2,6},{6,2},{1... | collective-permute-start | bytes 215048 | tf_op jit(solution)/shard_map/ppermute | solution.py:17
  36.5 1.5 %collective-permute-start.7 = (bf16[56,640]{1,0:T(8,128)(2,1)S(1)}, bf16[56,640]{1,0:T(8,128)(2,1)S(1)}, u32[]{:S(2)}, u32[]{:S(2)}) collective-permute-start(bf16[56,640]{1,0:T(8,128)(2,1)S(1)} %get-tuple-element.57), channel_id=1, source_target_pairs={{0,12},{4,8},{8,4},{12,0},{1,13},{5,9},{9,5},{13,1},{2,14},{6,10},... | collective-permute-start | bytes 215048 | tf_op jit(solution)/shard_map/ppermute | solution.py:17
  39.2 4.2 %collective-permute-done.6 = bf16[56,640]{1,0:T(8,128)(2,1)S(1)} collective-permute-done((bf16[56,640]{1,0:T(8,128)(2,1)S(1)}, bf16[56,640]{1,0:T(8,128)(2,1)S(1)}, u32[]{:S(2)}, u32[]{:S(2)}) %collective-permute-start.6) | collective-permute-done | bytes 71712 | tf_op jit(solution)/shard_map/ppermute | solution.py:17
  43.4 2.5 %collective-permute-start.10 = (bf16[56,640]{1,0:T(8,128)(2,1)S(1)}, bf16[56,640]{1,0:T(8,128)(2,1)S(1)}, u32[]{:S(2)}, u32[]{:S(2)}) collective-permute-start(bf16[56,640]{1,0:T(8,128)(2,1)S(1)} %fusion.refs_0_), channel_id=1, source_target_pairs={{0,12},{4,8},{8,4},{12,0},{1,13},{5,9},{9,5},{13,1},{2,14},{6,10},... | collective-permute-start | bytes 215048 | tf_op jit(solution)/shard_map/ppermute | solution.py:17
  46.3 3.3 %collective-permute-done.10.refs_3_ = bf16[56,640]{1,0:T(8,128)(2,1)S(1)} collective-permute-done((bf16[56,640]{1,0:T(8,128)(2,1)S(1)}, bf16[56,640]{1,0:T(8,128)(2,1)S(1)}, u32[]{:S(2)}, u32[]{:S(2)}) %collective-permute-start.10) | collective-permute-done | bytes 71712 | tf_op jit(solution)/shard_map/ppermute | solution.py:17
  50.4 4.8 %collective-permute-done.9.refs_2_ = bf16[56,640]{1,0:T(8,128)(2,1)S(1)} collective-permute-done((bf16[56,640]{1,0:T(8,128)(2,1)S(1)}, bf16[56,640]{1,0:T(8,128)(2,1)S(1)}, u32[]{:S(2)}, u32[]{:S(2)}) %collective-permute-start.9) | collective-permute-done | bytes 71712 | tf_op jit(solution)/shard_map/ppermute | solution.py:17
  55.2 1.2 project.1
  56.5 1.6 %collective-permute-start.21 = (bf16[224,320]{1,0:T(8,128)(2,1)S(1)}, bf16[224,320]{1,0:T(8,128)(2,1)S(1)}, u32[]{:S(2)}, u32[]{:S(2)}) collective-permute-start(bf16[224,320]{1,0:T(8,128)(2,1)S(1)} %get-tuple-element.68), channel_id=1, source_target_pairs={{0,2},{1,3},{2,0},{3,1},{4,6},{5,7},{6,4},{7,5},{8,10},{9,11},{10,... | collective-permute-start | bytes 430088 | tf_op jit(solution)/shard_map/ppermute | solution.py:17
  58.1 2.7 %collective-permute-start.18 = (bf16[56,640]{1,0:T(8,128)(2,1)S(1)}, bf16[56,640]{1,0:T(8,128)(2,1)S(1)}, u32[]{:S(2)}, u32[]{:S(2)}) collective-permute-start(bf16[56,640]{1,0:T(8,128)(2,1)S(1)} %get-tuple-element.65), channel_id=1, source_target_pairs={{0,8},{4,12},{8,0},{12,4},{1,9},{5,13},{9,1},{13,5},{2,10},{6,14},... | collective-permute-start | bytes 215048 | tf_op jit(solution)/shard_map/ppermute | solution.py:17
  60.8 1.7 %collective-permute-start.19 = (bf16[56,640]{1,0:T(8,128)(2,1)S(1)}, bf16[56,640]{1,0:T(8,128)(2,1)S(1)}, u32[]{:S(2)}, u32[]{:S(2)}) collective-permute-start(bf16[56,640]{1,0:T(8,128)(2,1)S(1)} %get-tuple-element.66), channel_id=1, source_target_pairs={{0,12},{4,8},{8,4},{12,0},{1,13},{5,9},{9,5},{13,1},{2,14},{6,10},... | collective-permute-start | bytes 215048 | tf_op jit(solution)/shard_map/ppermute | solution.py:17
  62.4 1.3 collective-permute-done.17.refs_1_
  64.4 2.5 %collective-permute-done.19.refs_3_ = bf16[56,640]{1,0:T(8,128)(2,1)S(1)} collective-permute-done((bf16[56,640]{1,0:T(8,128)(2,1)S(1)}, bf16[56,640]{1,0:T(8,128)(2,1)S(1)}, u32[]{:S(2)}, u32[]{:S(2)}) %collective-permute-start.19) | collective-permute-done | bytes 71712 | tf_op jit(solution)/shard_map/ppermute | solution.py:17
  67.0 3.0 %unfold.1 = (bf16[448,1440]{1,0:T(8,128)(2,1)S(1)}, bf16[448,1440]{1,0:T(8,128)(2,1)S(1)}) custom-call(s32[7]{0:T(128)S(1)} %stack.43.ids, f32[8,320]{1,0:T(8,128)S(1)} %reshape.105.gains, f32[8,320]{1,0:T(8,128)S(1)} %reshape.106.shifts, bf16[4,56,320]{2,1,0:T(8,128)(2,1)S(1)} %bitcast.26, bf16[4,56,320]{2,1,0:T(8,128)(2,1)S(1)} %bitcast.27, ...), custom_call_target="tpu_custom_call" | custom-call | flops 12902400 | bytes 5160960 | tf_op jit(solution)/shard_map/unfold/pallas_call | solution.py:84
  70.0 3.1 %copy-done = bf16[3,3,160,2560]{3,2,1,0:T(8,128)(2,1)S(1)} copy-done((bf16[3,3,160,2560]{3,2,1,0:T(8,128)(2,1)S(1)}, bf16[3,3,160,2560]{3,2,1,0:T(8,128)(2,1)}, u32[]{:S(2)}) %copy-start) | copy-done | bytes 7372824
  73.1 3.0 %mix.4 = (bf16[224,512]{1,0:T(8,128)(2,1)S(1)}, f32[224,512]{1,0:T(8,128)S(1)}) custom-call(bf16[448,1440]{1,0:T(8,128)(2,1)S(1)} %get-tuple-element.69.a_own, bf16[448,1440]{1,0:T(8,128)(2,1)S(1)} %get-tuple-element.70.a_other, bf16[1440,2560]{1,0:T(8,128)(2,1)S(1)} %bitcast.21, bf16[1440,2560]{1,0:T(8,128)(2,1)} %bitcast.17.w_other), custom_call_target="tpu_custom_call" | custom-call | flops 1321205760 | bytes 3637248 | tf_op jit(solution)/shard_map/mix/pallas_call | solution.py:116
  76.1 4.2 %mix.5 = (bf16[224,768]{1,0:T(8,128)(2,1)S(1)}, f32[224,768]{1,0:T(8,128)S(1)}) custom-call(bf16[448,1440]{1,0:T(8,128)(2,1)S(1)} %get-tuple-element.69.a_own, bf16[448,1440]{1,0:T(8,128)(2,1)S(1)} %get-tuple-element.70.a_other, bf16[1440,2560]{1,0:T(8,128)(2,1)S(1)} %bitcast.22, bf16[1440,2560]{1,0:T(8,128)(2,1)} %bitcast.17.w_other), custom_call_target="tpu_custom_call" | custom-call | flops 1981808640 | bytes 5455872 | tf_op jit(solution)/shard_map/mix/pallas_call | solution.py:116
  80.3 4.2 %mix.6 = (bf16[224,768]{1,0:T(8,128)(2,1)S(1)}, f32[224,768]{1,0:T(8,128)S(1)}) custom-call(bf16[448,1440]{1,0:T(8,128)(2,1)S(1)} %get-tuple-element.69.a_own, bf16[448,1440]{1,0:T(8,128)(2,1)S(1)} %get-tuple-element.70.a_other, bf16[1440,2560]{1,0:T(8,128)(2,1)S(1)} %bitcast.23, bf16[1440,2560]{1,0:T(8,128)(2,1)} %bitcast.17.w_other), custom_call_target="tpu_custom_call" | custom-call | flops 1981808640 | bytes 5455872 | tf_op jit(solution)/shard_map/mix/pallas_call | solution.py:116
  84.5 3.0 %mix.7 = (bf16[224,512]{1,0:T(8,128)(2,1)S(1)}, f32[224,512]{1,0:T(8,128)S(1)}) custom-call(bf16[448,1440]{1,0:T(8,128)(2,1)S(1)} %get-tuple-element.69.a_own, bf16[448,1440]{1,0:T(8,128)(2,1)S(1)} %get-tuple-element.70.a_other, bf16[1440,2560]{1,0:T(8,128)(2,1)S(1)} %bitcast.24, bf16[1440,2560]{1,0:T(8,128)(2,1)} %bitcast.17.w_other), custom_call_target="tpu_custom_call" | custom-call | flops 1321205760 | bytes 3637248 | tf_op jit(solution)/shard_map/mix/pallas_call | solution.py:116
  88.1 1.5 %collective-permute-start.33 = (bf16[224,768]{1,0:T(8,128)(2,1)S(1)}, bf16[224,768]{1,0:T(8,128)(2,1)S(1)}, u32[]{:S(2)}, u32[]{:S(2)}) collective-permute-start(bf16[224,768]{1,0:T(8,128)(2,1)S(1)} %get-tuple-element.84), channel_id=1, source_target_pairs={{0,2},{1,3},{2,0},{3,1},{4,6},{5,7},{6,4},{7,5},{8,10},{9,11},{10,... | collective-permute-start | bytes 1032200 | tf_op jit(solution)/shard_map/ppermute | solution.py:17
  89.6 2.0 %collective-permute-start.37 = (bf16[224,512]{1,0:T(8,128)(2,1)S(1)}, bf16[224,512]{1,0:T(8,128)(2,1)S(1)}, u32[]{:S(2)}, u32[]{:S(2)}) collective-permute-start(bf16[224,512]{1,0:T(8,128)(2,1)S(1)} %get-tuple-element.90), channel_id=1, source_target_pairs={{0,4},{4,0},{8,12},{12,8},{1,5},{5,1},{9,13},{13,9},{2,6},{6,2},{1... | collective-permute-start | bytes 688136 | tf_op jit(solution)/shard_map/ppermute | solution.py:17
  91.6 1.3 collective-permute-start.20
  92.9 7.4 %collective-permute-done.29.came = bf16[224,768]{1,0:T(8,128)(2,1)S(1)} collective-permute-done((bf16[224,768]{1,0:T(8,128)(2,1)S(1)}, bf16[224,768]{1,0:T(8,128)(2,1)S(1)}, u32[]{:S(2)}, u32[]{:S(2)}) %collective-permute-start.29) | collective-permute-done | bytes 344096 | tf_op jit(solution)/shard_map/ppermute | solution.py:17
  101.1 1.4 %collective-permute-start.34 = (bf16[112,768]{1,0:T(8,128)(2,1)S(1)}, bf16[112,768]{1,0:T(8,128)(2,1)S(1)}, u32[]{:S(2)}, u32[]{:S(2)}) collective-permute-start(bf16[112,768]{1,0:T(8,128)(2,1)S(1)} %get-tuple-element.86), channel_id=1, source_target_pairs={{0,4},{4,0},{8,12},{12,8},{1,5},{5,1},{9,13},{13,9},{2,6},{6,2},{1... | collective-permute-start | bytes 516104 | tf_op jit(solution)/shard_map/ppermute | solution.py:17
  103.3 2.0 %collective-permute-done.37.came = bf16[224,512]{1,0:T(8,128)(2,1)S(1)} collective-permute-done((bf16[224,512]{1,0:T(8,128)(2,1)S(1)}, bf16[224,512]{1,0:T(8,128)(2,1)S(1)}, u32[]{:S(2)}, u32[]{:S(2)}) %collective-permute-start.37) | collective-permute-done | bytes 229408 | tf_op jit(solution)/shard_map/ppermute | solution.py:17
  105.3 1.8 %collective-permute-start.38 = (bf16[112,512]{1,0:T(8,128)(2,1)S(1)}, bf16[112,512]{1,0:T(8,128)(2,1)S(1)}, u32[]{:S(2)}, u32[]{:S(2)}) collective-permute-start(bf16[112,512]{1,0:T(8,128)(2,1)S(1)} %get-tuple-element.92), channel_id=1, source_target_pairs={{0,8},{4,12},{8,0},{12,4},{1,9},{5,13},{9,1},{13,5},{2,10},{6,14},... | collective-permute-start | bytes 344072 | tf_op jit(solution)/shard_map/ppermute | solution.py:17
  107.1 3.7 %collective-permute-done.30.came = bf16[112,768]{1,0:T(8,128)(2,1)S(1)} collective-permute-done((bf16[112,768]{1,0:T(8,128)(2,1)S(1)}, bf16[112,768]{1,0:T(8,128)(2,1)S(1)}, u32[]{:S(2)}, u32[]{:S(2)}) %collective-permute-start.30) | collective-permute-done | bytes 172064 | tf_op jit(solution)/shard_map/ppermute | solution.py:17
  111.7 1.1 collective-permute-done.34.came
  112.9 1.1 collective-permute-done.26.came
  114.0 1.9 %collective-permute-start.27 = (bf16[56,512]{1,0:T(8,128)(2,1)S(1)}, bf16[56,512]{1,0:T(8,128)(2,1)S(1)}, u32[]{:S(2)}, u32[]{:S(2)}) collective-permute-start(bf16[56,512]{1,0:T(8,128)(2,1)S(1)} %get-tuple-element.76), channel_id=1, source_target_pairs={{0,8},{4,12},{8,0},{12,4},{1,9},{5,13},{9,1},{13,5},{2,10},{6,14},... | collective-permute-start | bytes 172040 | tf_op jit(solution)/shard_map/ppermute | solution.py:17
  115.9 1.4 %collective-permute-start.39 = (bf16[56,512]{1,0:T(8,128)(2,1)S(1)}, bf16[56,512]{1,0:T(8,128)(2,1)S(1)}, u32[]{:S(2)}, u32[]{:S(2)}) collective-permute-start(bf16[56,512]{1,0:T(8,128)(2,1)S(1)} %get-tuple-element.94), channel_id=1, source_target_pairs={{0,2},{1,3},{2,0},{3,1},{4,6},{5,7},{6,4},{7,5},{8,10},{9,11},{10,... | collective-permute-start | bytes 172040 | tf_op jit(solution)/shard_map/ppermute | solution.py:17
  117.5 2.9 %collective-permute-done.27.came = bf16[56,512]{1,0:T(8,128)(2,1)S(1)} collective-permute-done((bf16[56,512]{1,0:T(8,128)(2,1)S(1)}, bf16[56,512]{1,0:T(8,128)(2,1)S(1)}, u32[]{:S(2)}, u32[]{:S(2)}) %collective-permute-start.27) | collective-permute-done | bytes 57376 | tf_op jit(solution)/shard_map/ppermute | solution.py:17
  120.4 3.4 %collective-permute-start.28 = (bf16[56,512]{1,0:T(8,128)(2,1)S(1)}, bf16[56,512]{1,0:T(8,128)(2,1)S(1)}, u32[]{:S(2)}, u32[]{:S(2)}) collective-permute-start(bf16[56,512]{1,0:T(8,128)(2,1)S(1)} %finish.4), channel_id=1, source_target_pairs={{0,16},{1,17},{2,18},{3,19},{4,20},{5,21},{6,22},{7,23},{8,24},{9,... | collective-permute-start | bytes 172040 | tf_op jit(solution)/shard_map/ppermute | solution.py:502
  123.9 1.3 collective-permute-start.40
  125.2 1.3 collective-permute-start.32
  126.6 1.3 collective-permute-start.36
  128.6 1.4 %collective-permute-done.36 = bf16[56,768]{1,0:T(8,128)(2,1)S(1)} collective-permute-done((bf16[56,768]{1,0:T(8,128)(2,1)S(1)}, bf16[56,768]{1,0:T(8,128)(2,1)S(1)}, u32[]{:S(2)}, u32[]{:S(2)}) %collective-permute-start.36) | collective-permute-done | bytes 86048 | tf_op jit(solution)/shard_map/ppermute | solution.py:502
  130.3 1.3 copy.18
  (93 shorter events, 11.5 us)
Async XLA Ops:
  0.0 5.3 %copy-start.5 = (f32[640]{0:T(1024)S(1)}, f32[640]{0:T(1024)}, u32[]{:S(2)}) copy-start(f32[640]{0:T(1024)} %param.9) | copy-start | bytes 7684
  0.0 5.3 %copy-start.6 = (f32[640]{0:T(1024)S(1)}, f32[640]{0:T(1024)}, u32[]{:S(2)}) copy-start(f32[640]{0:T(1024)} %param.10) | copy-start | bytes 7684
  0.0 12.2 %copy-start.2 = (bf16[160,2560]{1,0:T(8,128)(2,1)S(1)}, bf16[160,2560]{1,0:T(8,128)(2,1)}, u32[]{:S(2)}) copy-start(bf16[160,2560]{1,0:T(8,128)(2,1)} %projection.1) | copy-start | bytes 2457604
  0.0 70.0 %collective-permute-start.24 = (bf16[3,3,160,2560]{3,2,1,0:T(8,128)(2,1)}, bf16[3,3,160,2560]{3,2,1,0:T(8,128)(2,1)}, u32[]{:S(2)}, u32[]{:S(2)}) collective-permute-start(bf16[3,3,160,2560]{3,2,1,0:T(8,128)(2,1)} %param.15), channel_id=1, source_target_pairs={{0,1},{1,0},{2,3},{3,2},{4,5},{5,4},{6,7},{7,6},{8,9},{9,8},{10,11... | collective-permute-start | bytes 22118408 | tf_op jit(solution)/shard_map/ppermute | solution.py:17
  1.7 30.2 %copy-start.1 = (bf16[3,3,160,640]{3,2,1,0:T(8,128)(2,1)S(1)}, bf16[3,3,160,640]{3,2,1,0:T(8,128)(2,1)}, u32[]{:S(2)}) copy-start(bf16[3,3,160,640]{3,2,1,0:T(8,128)(2,1)} %param.11) | copy-start | bytes 5529604
  1.8 10.5 %collective-permute-start = (bf16[1,1,28,640]{3,2,1,0:T(8,128)(2,1)S(1)}, bf16[1,1,28,640]{3,2,1,0:T(8,128)(2,1)S(1)}, u32[]{:S(2)}, u32[]{:S(2)}) collective-permute-start(bf16[1,1,28,640]{3,2,1,0:T(8,128)(2,1)S(1)} %constant_dynamic-slice_fusion.5), channel_id=1, source_target_pairs={{0,1},{1,2},{2,3},{4,5},{5,6},{6,7},{8,9},{9,10},{10,11},{12,13},{... | collective-permute-start | bytes 107528 | tf_op jit(solution)/shard_map/ppermute | solution.py:422
  3.9 8.3 %collective-permute-start.1 = (bf16[1,1,28,640]{3,2,1,0:T(8,128)(2,1)S(1)}, bf16[1,1,28,640]{3,2,1,0:T(8,128)(2,1)S(1)}, u32[]{:S(2)}, u32[]{:S(2)}) collective-permute-start(bf16[1,1,28,640]{3,2,1,0:T(8,128)(2,1)S(1)} %constant_dynamic-slice_fusion.4), channel_id=1, source_target_pairs={{1,0},{2,1},{3,2},{5,4},{6,5},{7,6},{9,8},{10,9},{11,10},{13,12},{... | collective-permute-start | bytes 107528 | tf_op jit(solution)/shard_map/ppermute | solution.py:423
  13.3 6.5 %collective-permute-start.11 = (bf16[40,640]{1,0:T(8,128)(2,1)S(1)}, bf16[40,640]{1,0:T(8,128)(2,1)S(1)}, u32[]{:S(2)}, u32[]{:S(2)}) collective-permute-start(bf16[40,640]{1,0:T(8,128)(2,1)S(1)} %get-tuple-element.60), channel_id=1, source_target_pairs={{0,4},{4,0},{8,12},{12,8},{1,5},{5,1},{9,13},{13,9},{2,6},{6,2},{1... | collective-permute-start | bytes 153608 | tf_op jit(solution)/shard_map/ppermute | solution.py:17
  16.3 7.0 %collective-permute-start.12 = (bf16[40,640]{1,0:T(8,128)(2,1)S(1)}, bf16[40,640]{1,0:T(8,128)(2,1)S(1)}, u32[]{:S(2)}, u32[]{:S(2)}) collective-permute-start(bf16[40,640]{1,0:T(8,128)(2,1)S(1)} %get-tuple-element.61), channel_id=1, source_target_pairs={{0,8},{4,12},{8,0},{12,4},{1,9},{5,13},{9,1},{13,5},{2,10},{6,14},... | collective-permute-start | bytes 153608 | tf_op jit(solution)/shard_map/ppermute | solution.py:17
  18.9 6.7 %collective-permute-start.13 = (bf16[40,640]{1,0:T(8,128)(2,1)S(1)}, bf16[40,640]{1,0:T(8,128)(2,1)S(1)}, u32[]{:S(2)}, u32[]{:S(2)}) collective-permute-start(bf16[40,640]{1,0:T(8,128)(2,1)S(1)} %get-tuple-element.62), channel_id=1, source_target_pairs={{0,12},{4,8},{8,4},{12,0},{1,13},{5,9},{9,5},{13,1},{2,14},{6,10},... | collective-permute-start | bytes 153608 | tf_op jit(solution)/shard_map/ppermute | solution.py:17
  18.9 8.3 %collective-permute-start.2 = (bf16[416,128]{1,0:T(8,128)(2,1)S(1)}, bf16[416,128]{1,0:T(8,128)(2,1)S(1)}, u32[]{:S(2)}, u32[]{:S(2)}) collective-permute-start(bf16[416,128]{1,0:T(8,128)(2,1)S(1)} %get-tuple-element.51), channel_id=1, source_target_pairs={{0,4},{4,0},{8,12},{12,8},{1,5},{5,1},{9,13},{13,9},{2,6},{6,2},{1... | collective-permute-start | bytes 319496 | tf_op jit(solution)/shard_map/ppermute | solution.py:17
  19.8 12.1 %collective-permute-start.3 = (bf16[416,128]{1,0:T(8,128)(2,1)S(1)}, bf16[416,128]{1,0:T(8,128)(2,1)S(1)}, u32[]{:S(2)}, u32[]{:S(2)}) collective-permute-start(bf16[416,128]{1,0:T(8,128)(2,1)S(1)} %get-tuple-element.52), channel_id=1, source_target_pairs={{0,8},{4,12},{8,0},{12,4},{1,9},{5,13},{9,1},{13,5},{2,10},{6,14},... | collective-permute-start | bytes 319496 | tf_op jit(solution)/shard_map/ppermute | solution.py:17
  23.3 8.6 %collective-permute-start.4 = (bf16[416,128]{1,0:T(8,128)(2,1)S(1)}, bf16[416,128]{1,0:T(8,128)(2,1)S(1)}, u32[]{:S(2)}, u32[]{:S(2)}) collective-permute-start(bf16[416,128]{1,0:T(8,128)(2,1)S(1)} %get-tuple-element.53), channel_id=1, source_target_pairs={{0,12},{4,8},{8,4},{12,0},{1,13},{5,9},{9,5},{13,1},{2,14},{6,10},... | collective-permute-start | bytes 319496 | tf_op jit(solution)/shard_map/ppermute | solution.py:17
  25.6 13.1 %collective-permute-start.14 = (bf16[4,40,640]{2,1,0:T(8,128)(2,1)S(1)}, bf16[4,40,640]{2,1,0:T(8,128)(2,1)S(1)}, u32[]{:S(2)}, u32[]{:S(2)}) collective-permute-start(bf16[4,40,640]{2,1,0:T(8,128)(2,1)S(1)} %join.2.refs_4_), channel_id=1, source_target_pairs={{0,2},{1,3},{2,0},{3,1},{4,6},{5,7},{6,4},{7,5},{8,10},{9,11},{10,... | collective-permute-start | bytes 614408 | tf_op jit(solution)/shard_map/ppermute | solution.py:17
  33.5 30.7 %copy-start.3 = (f32[2560]{0:T(1024)S(1)}, f32[2560]{0:T(1024)}, u32[]{:S(2)}) copy-start(f32[2560]{0:T(1024)} %param.13) | copy-start | bytes 30724
  33.5 30.8 %copy-start.4 = (f32[2560]{0:T(1024)S(1)}, f32[2560]{0:T(1024)}, u32[]{:S(2)}) copy-start(f32[2560]{0:T(1024)} %param.14) | copy-start | bytes 30724
  33.5 5.2 %collective-permute-start.5 = (bf16[56,640]{1,0:T(8,128)(2,1)S(1)}, bf16[56,640]{1,0:T(8,128)(2,1)S(1)}, u32[]{:S(2)}, u32[]{:S(2)}) collective-permute-start(bf16[56,640]{1,0:T(8,128)(2,1)S(1)} %get-tuple-element.55), channel_id=1, source_target_pairs={{0,4},{4,0},{8,12},{12,8},{1,5},{5,1},{9,13},{13,9},{2,6},{6,2},{1... | collective-permute-start | bytes 215048 | tf_op jit(solution)/shard_map/ppermute | solution.py:17
  35.4 7.9 %collective-permute-start.6 = (bf16[56,640]{1,0:T(8,128)(2,1)S(1)}, bf16[56,640]{1,0:T(8,128)(2,1)S(1)}, u32[]{:S(2)}, u32[]{:S(2)}) collective-permute-start(bf16[56,640]{1,0:T(8,128)(2,1)S(1)} %get-tuple-element.56), channel_id=1, source_target_pairs={{0,8},{4,12},{8,0},{12,4},{1,9},{5,13},{9,1},{13,5},{2,10},{6,14},... | collective-permute-start | bytes 215048 | tf_op jit(solution)/shard_map/ppermute | solution.py:17
  36.5 6.9 %collective-permute-start.7 = (bf16[56,640]{1,0:T(8,128)(2,1)S(1)}, bf16[56,640]{1,0:T(8,128)(2,1)S(1)}, u32[]{:S(2)}, u32[]{:S(2)}) collective-permute-start(bf16[56,640]{1,0:T(8,128)(2,1)S(1)} %get-tuple-element.57), channel_id=1, source_target_pairs={{0,12},{4,8},{8,4},{12,0},{1,13},{5,9},{9,5},{13,1},{2,14},{6,10},... | collective-permute-start | bytes 215048 | tf_op jit(solution)/shard_map/ppermute | solution.py:17
  38.7 16.5 %collective-permute-start.15 = (bf16[4,40,640]{2,1,0:T(8,128)(2,1)S(1)}, bf16[4,40,640]{2,1,0:T(8,128)(2,1)S(1)}, u32[]{:S(2)}, u32[]{:S(2)}) collective-permute-start(bf16[4,40,640]{2,1,0:T(8,128)(2,1)S(1)} %join.2.refs_4_), channel_id=1, source_target_pairs={{0,1},{1,0},{2,3},{3,2},{4,5},{5,4},{6,7},{7,6},{8,9},{9,8},{10,11... | collective-permute-start | bytes 614408 | tf_op jit(solution)/shard_map/ppermute | solution.py:17
  38.7 16.5 %collective-permute-start.16 = (bf16[4,40,640]{2,1,0:T(8,128)(2,1)S(1)}, bf16[4,40,640]{2,1,0:T(8,128)(2,1)S(1)}, u32[]{:S(2)}, u32[]{:S(2)}) collective-permute-start(bf16[4,40,640]{2,1,0:T(8,128)(2,1)S(1)} %collective-permute-done.14.refs_5_), channel_id=1, source_target_pairs={{0,1},{1,0},{2,3},{3,2},{4,5},{5,4},{6,7},{7,6},{8,9},{9,8},{10,11... | collective-permute-start | bytes 614408 | tf_op jit(solution)/shard_map/ppermute | solution.py:17
  43.4 6.2 %collective-permute-start.10 = (bf16[56,640]{1,0:T(8,128)(2,1)S(1)}, bf16[56,640]{1,0:T(8,128)(2,1)S(1)}, u32[]{:S(2)}, u32[]{:S(2)}) collective-permute-start(bf16[56,640]{1,0:T(8,128)(2,1)S(1)} %fusion.refs_0_), channel_id=1, source_target_pairs={{0,12},{4,8},{8,4},{12,0},{1,13},{5,9},{9,5},{13,1},{2,14},{6,10},... | collective-permute-start | bytes 215048 | tf_op jit(solution)/shard_map/ppermute | solution.py:17
  45.9 4.5 %collective-permute-start.8 = (bf16[56,640]{1,0:T(8,128)(2,1)S(1)}, bf16[56,640]{1,0:T(8,128)(2,1)S(1)}, u32[]{:S(2)}, u32[]{:S(2)}) collective-permute-start(bf16[56,640]{1,0:T(8,128)(2,1)S(1)} %fusion.refs_0_), channel_id=1, source_target_pairs={{0,4},{4,0},{8,12},{12,8},{1,5},{5,1},{9,13},{13,9},{2,6},{6,2},{1... | collective-permute-start | bytes 215048 | tf_op jit(solution)/shard_map/ppermute | solution.py:17
  49.6 5.6 %collective-permute-start.9 = (bf16[56,640]{1,0:T(8,128)(2,1)S(1)}, bf16[56,640]{1,0:T(8,128)(2,1)S(1)}, u32[]{:S(2)}, u32[]{:S(2)}) collective-permute-start(bf16[56,640]{1,0:T(8,128)(2,1)S(1)} %fusion.refs_0_), channel_id=1, source_target_pairs={{0,8},{4,12},{8,0},{12,4},{1,9},{5,13},{9,1},{13,5},{2,10},{6,14},... | collective-permute-start | bytes 215048 | tf_op jit(solution)/shard_map/ppermute | solution.py:17
  56.5 7.2 %collective-permute-start.21 = (bf16[224,320]{1,0:T(8,128)(2,1)S(1)}, bf16[224,320]{1,0:T(8,128)(2,1)S(1)}, u32[]{:S(2)}, u32[]{:S(2)}) collective-permute-start(bf16[224,320]{1,0:T(8,128)(2,1)S(1)} %get-tuple-element.68), channel_id=1, source_target_pairs={{0,2},{1,3},{2,0},{3,1},{4,6},{5,7},{6,4},{7,5},{8,10},{9,11},{10,... | collective-permute-start | bytes 430088 | tf_op jit(solution)/shard_map/ppermute | solution.py:17
  58.0 5.6 %collective-permute-start.17 = (bf16[56,640]{1,0:T(8,128)(2,1)S(1)}, bf16[56,640]{1,0:T(8,128)(2,1)S(1)}, u32[]{:S(2)}, u32[]{:S(2)}) collective-permute-start(bf16[56,640]{1,0:T(8,128)(2,1)S(1)} %get-tuple-element.64), channel_id=1, source_target_pairs={{0,4},{4,0},{8,12},{12,8},{1,5},{5,1},{9,13},{13,9},{2,6},{6,2},{1... | collective-permute-start | bytes 215048 | tf_op jit(solution)/shard_map/ppermute | solution.py:17
  58.1 6.3 %collective-permute-start.18 = (bf16[56,640]{1,0:T(8,128)(2,1)S(1)}, bf16[56,640]{1,0:T(8,128)(2,1)S(1)}, u32[]{:S(2)}, u32[]{:S(2)}) collective-permute-start(bf16[56,640]{1,0:T(8,128)(2,1)S(1)} %get-tuple-element.65), channel_id=1, source_target_pairs={{0,8},{4,12},{8,0},{12,4},{1,9},{5,13},{9,1},{13,5},{2,10},{6,14},... | collective-permute-start | bytes 215048 | tf_op jit(solution)/shard_map/ppermute | solution.py:17
  60.8 6.1 %collective-permute-start.19 = (bf16[56,640]{1,0:T(8,128)(2,1)S(1)}, bf16[56,640]{1,0:T(8,128)(2,1)S(1)}, u32[]{:S(2)}, u32[]{:S(2)}) collective-permute-start(bf16[56,640]{1,0:T(8,128)(2,1)S(1)} %get-tuple-element.66), channel_id=1, source_target_pairs={{0,12},{4,8},{8,4},{12,0},{1,13},{5,9},{9,5},{13,1},{2,14},{6,10},... | collective-permute-start | bytes 215048 | tf_op jit(solution)/shard_map/ppermute | solution.py:17
  63.7 3.3 %collective-permute-start.22 = (bf16[224,320]{1,0:T(8,128)(2,1)S(1)}, bf16[224,320]{1,0:T(8,128)(2,1)S(1)}, u32[]{:S(2)}, u32[]{:S(2)}) collective-permute-start(bf16[224,320]{1,0:T(8,128)(2,1)S(1)} %get-tuple-element.67), channel_id=1, source_target_pairs={{0,1},{1,0},{2,3},{3,2},{4,5},{5,4},{6,7},{7,6},{8,9},{9,8},{10,11... | collective-permute-start | bytes 430088 | tf_op jit(solution)/shard_map/ppermute | solution.py:17
  63.7 3.3 %collective-permute-start.23 = (bf16[224,320]{1,0:T(8,128)(2,1)S(1)}, bf16[224,320]{1,0:T(8,128)(2,1)S(1)}, u32[]{:S(2)}, u32[]{:S(2)}) collective-permute-start(bf16[224,320]{1,0:T(8,128)(2,1)S(1)} %collective-permute-done.21), channel_id=1, source_target_pairs={{0,1},{1,0},{2,3},{3,2},{4,5},{5,4},{6,7},{7,6},{8,9},{9,8},{10,11... | collective-permute-start | bytes 430088 | tf_op jit(solution)/shard_map/ppermute | solution.py:17
  70.0 3.1 %copy-start = (bf16[3,3,160,2560]{3,2,1,0:T(8,128)(2,1)S(1)}, bf16[3,3,160,2560]{3,2,1,0:T(8,128)(2,1)}, u32[]{:S(2)}) copy-start(bf16[3,3,160,2560]{3,2,1,0:T(8,128)(2,1)} %param.15) | copy-start | bytes 22118404
  87.5 15.1 %collective-permute-start.25 = (bf16[224,512]{1,0:T(8,128)(2,1)S(1)}, bf16[224,512]{1,0:T(8,128)(2,1)S(1)}, u32[]{:S(2)}, u32[]{:S(2)}) collective-permute-start(bf16[224,512]{1,0:T(8,128)(2,1)S(1)} %get-tuple-element.72), channel_id=1, source_target_pairs={{0,2},{1,3},{2,0},{3,1},{4,6},{5,7},{6,4},{7,5},{8,10},{9,11},{10,... | collective-permute-start | bytes 688136 | tf_op jit(solution)/shard_map/ppermute | solution.py:17
  88.1 12.3 %collective-permute-start.29 = (bf16[224,768]{1,0:T(8,128)(2,1)S(1)}, bf16[224,768]{1,0:T(8,128)(2,1)S(1)}, u32[]{:S(2)}, u32[]{:S(2)}) collective-permute-start(bf16[224,768]{1,0:T(8,128)(2,1)S(1)} %get-tuple-element.78), channel_id=1, source_target_pairs={{0,4},{4,0},{8,12},{12,8},{1,5},{5,1},{9,13},{13,9},{2,6},{6,2},{1... | collective-permute-start | bytes 1032200 | tf_op jit(solution)/shard_map/ppermute | solution.py:17
  88.1 13.0 %collective-permute-start.33 = (bf16[224,768]{1,0:T(8,128)(2,1)S(1)}, bf16[224,768]{1,0:T(8,128)(2,1)S(1)}, u32[]{:S(2)}, u32[]{:S(2)}) collective-permute-start(bf16[224,768]{1,0:T(8,128)(2,1)S(1)} %get-tuple-element.84), channel_id=1, source_target_pairs={{0,2},{1,3},{2,0},{3,1},{4,6},{5,7},{6,4},{7,5},{8,10},{9,11},{10,... | collective-permute-start | bytes 1032200 | tf_op jit(solution)/shard_map/ppermute | solution.py:17
  89.6 15.7 %collective-permute-start.37 = (bf16[224,512]{1,0:T(8,128)(2,1)S(1)}, bf16[224,512]{1,0:T(8,128)(2,1)S(1)}, u32[]{:S(2)}, u32[]{:S(2)}) collective-permute-start(bf16[224,512]{1,0:T(8,128)(2,1)S(1)} %get-tuple-element.90), channel_id=1, source_target_pairs={{0,4},{4,0},{8,12},{12,8},{1,5},{5,1},{9,13},{13,9},{2,6},{6,2},{1... | collective-permute-start | bytes 688136 | tf_op jit(solution)/shard_map/ppermute | solution.py:17
  91.6 25.8 %collective-permute-start.20 = (bf16[56,2560]{1,0:T(8,128)(2,1)S(1)}, bf16[56,2560]{1,0:T(8,128)(2,1)S(1)}, u32[]{:S(2)}, u32[]{:S(2)}) collective-permute-start(bf16[56,2560]{1,0:T(8,128)(2,1)S(1)} %pad_maximum_fusion.extra), channel_id=1, source_target_pairs={{16,0},{17,1},{18,2},{19,3},{20,4},{21,5},{22,6},{23,7},{24,8},{25... | collective-permute-start | bytes 860168 | tf_op jit(solution)/shard_map/ppermute | solution.py:498
  100.4 10.5 %collective-permute-start.30 = (bf16[112,768]{1,0:T(8,128)(2,1)S(1)}, bf16[112,768]{1,0:T(8,128)(2,1)S(1)}, u32[]{:S(2)}, u32[]{:S(2)}) collective-permute-start(bf16[112,768]{1,0:T(8,128)(2,1)S(1)} %get-tuple-element.80), channel_id=1, source_target_pairs={{0,8},{4,12},{8,0},{12,4},{1,9},{5,13},{9,1},{13,5},{2,10},{6,14},... | collective-permute-start | bytes 516104 | tf_op jit(solution)/shard_map/ppermute | solution.py:17
  101.1 11.7 %collective-permute-start.34 = (bf16[112,768]{1,0:T(8,128)(2,1)S(1)}, bf16[112,768]{1,0:T(8,128)(2,1)S(1)}, u32[]{:S(2)}, u32[]{:S(2)}) collective-permute-start(bf16[112,768]{1,0:T(8,128)(2,1)S(1)} %get-tuple-element.86), channel_id=1, source_target_pairs={{0,4},{4,0},{8,12},{12,8},{1,5},{5,1},{9,13},{13,9},{2,6},{6,2},{1... | collective-permute-start | bytes 516104 | tf_op jit(solution)/shard_map/ppermute | solution.py:17
  102.6 11.4 %collective-permute-start.26 = (bf16[112,512]{1,0:T(8,128)(2,1)S(1)}, bf16[112,512]{1,0:T(8,128)(2,1)S(1)}, u32[]{:S(2)}, u32[]{:S(2)}) collective-permute-start(bf16[112,512]{1,0:T(8,128)(2,1)S(1)} %get-tuple-element.74), channel_id=1, source_target_pairs={{0,4},{4,0},{8,12},{12,8},{1,5},{5,1},{9,13},{13,9},{2,6},{6,2},{1... | collective-permute-start | bytes 344072 | tf_op jit(solution)/shard_map/ppermute | solution.py:17
  105.3 10.6 %collective-permute-start.38 = (bf16[112,512]{1,0:T(8,128)(2,1)S(1)}, bf16[112,512]{1,0:T(8,128)(2,1)S(1)}, u32[]{:S(2)}, u32[]{:S(2)}) collective-permute-start(bf16[112,512]{1,0:T(8,128)(2,1)S(1)} %get-tuple-element.92), channel_id=1, source_target_pairs={{0,8},{4,12},{8,0},{12,4},{1,9},{5,13},{9,1},{13,5},{2,10},{6,14},... | collective-permute-start | bytes 344072 | tf_op jit(solution)/shard_map/ppermute | solution.py:17
  110.9 14.3 %collective-permute-start.31 = (bf16[56,768]{1,0:T(8,128)(2,1)S(1)}, bf16[56,768]{1,0:T(8,128)(2,1)S(1)}, u32[]{:S(2)}, u32[]{:S(2)}) collective-permute-start(bf16[56,768]{1,0:T(8,128)(2,1)S(1)} %get-tuple-element.82), channel_id=1, source_target_pairs={{0,2},{1,3},{2,0},{3,1},{4,6},{5,7},{6,4},{7,5},{8,10},{9,11},{10,... | collective-permute-start | bytes 258056 | tf_op jit(solution)/shard_map/ppermute | solution.py:17
  112.8 13.7 %collective-permute-start.35 = (bf16[56,768]{1,0:T(8,128)(2,1)S(1)}, bf16[56,768]{1,0:T(8,128)(2,1)S(1)}, u32[]{:S(2)}, u32[]{:S(2)}) collective-permute-start(bf16[56,768]{1,0:T(8,128)(2,1)S(1)} %get-tuple-element.88), channel_id=1, source_target_pairs={{0,8},{4,12},{8,0},{12,4},{1,9},{5,13},{9,1},{13,5},{2,10},{6,14},... | collective-permute-start | bytes 258056 | tf_op jit(solution)/shard_map/ppermute | solution.py:17
  114.0 6.4 %collective-permute-start.27 = (bf16[56,512]{1,0:T(8,128)(2,1)S(1)}, bf16[56,512]{1,0:T(8,128)(2,1)S(1)}, u32[]{:S(2)}, u32[]{:S(2)}) collective-permute-start(bf16[56,512]{1,0:T(8,128)(2,1)S(1)} %get-tuple-element.76), channel_id=1, source_target_pairs={{0,8},{4,12},{8,0},{12,4},{1,9},{5,13},{9,1},{13,5},{2,10},{6,14},... | collective-permute-start | bytes 172040 | tf_op jit(solution)/shard_map/ppermute | solution.py:17
  115.9 7.9 %collective-permute-start.39 = (bf16[56,512]{1,0:T(8,128)(2,1)S(1)}, bf16[56,512]{1,0:T(8,128)(2,1)S(1)}, u32[]{:S(2)}, u32[]{:S(2)}) collective-permute-start(bf16[56,512]{1,0:T(8,128)(2,1)S(1)} %get-tuple-element.94), channel_id=1, source_target_pairs={{0,2},{1,3},{2,0},{3,1},{4,6},{5,7},{6,4},{7,5},{8,10},{9,11},{10,... | collective-permute-start | bytes 172040 | tf_op jit(solution)/shard_map/ppermute | solution.py:17
  120.4 7.6 %collective-permute-start.28 = (bf16[56,512]{1,0:T(8,128)(2,1)S(1)}, bf16[56,512]{1,0:T(8,128)(2,1)S(1)}, u32[]{:S(2)}, u32[]{:S(2)}) collective-permute-start(bf16[56,512]{1,0:T(8,128)(2,1)S(1)} %finish.4), channel_id=1, source_target_pairs={{0,16},{1,17},{2,18},{3,19},{4,20},{5,21},{6,22},{7,23},{8,24},{9,... | collective-permute-start | bytes 172040 | tf_op jit(solution)/shard_map/ppermute | solution.py:502
  123.9 4.1 %collective-permute-start.40 = (bf16[56,512]{1,0:T(8,128)(2,1)S(1)}, bf16[56,512]{1,0:T(8,128)(2,1)S(1)}, u32[]{:S(2)}, u32[]{:S(2)}) collective-permute-start(bf16[56,512]{1,0:T(8,128)(2,1)S(1)} %finish.7), channel_id=1, source_target_pairs={{0,16},{1,17},{2,18},{3,19},{4,20},{5,21},{6,22},{7,23},{8,24},{9,... | collective-permute-start | bytes 172040 | tf_op jit(solution)/shard_map/ppermute | solution.py:502
  125.2 3.4 %collective-permute-start.32 = (bf16[56,768]{1,0:T(8,128)(2,1)S(1)}, bf16[56,768]{1,0:T(8,128)(2,1)S(1)}, u32[]{:S(2)}, u32[]{:S(2)}) collective-permute-start(bf16[56,768]{1,0:T(8,128)(2,1)S(1)} %finish.5), channel_id=1, source_target_pairs={{0,16},{1,17},{2,18},{3,19},{4,20},{5,21},{6,22},{7,23},{8,24},{9,... | collective-permute-start | bytes 258056 | tf_op jit(solution)/shard_map/ppermute | solution.py:502
  126.6 3.4 %collective-permute-start.36 = (bf16[56,768]{1,0:T(8,128)(2,1)S(1)}, bf16[56,768]{1,0:T(8,128)(2,1)S(1)}, u32[]{:S(2)}, u32[]{:S(2)}) collective-permute-start(bf16[56,768]{1,0:T(8,128)(2,1)S(1)} %finish.6), channel_id=1, source_target_pairs={{0,16},{1,17},{2,18},{3,19},{4,20},{5,21},{6,22},{7,23},{8,24},{9,... | collective-permute-start | bytes 258056 | tf_op jit(solution)/shard_map/ppermute | solution.py:502

commit v2 on v1

--- a/solution.py
+++ b/solution.py
@@ -17,8 +17,8 @@
     return lax.ppermute(array, axis, [(i, i ^ (k * unit)) for i in range(count)])
 
 
-def pick(stack, index):
-    return lax.dynamic_index_in_dim(stack, index, 0, keepdims=False)
+def streamed(array):
+    return pltpu.with_memory_space_constraint(array, pltpu.HBM)
 
 
 def whole(memory_space=pltpu.VMEM):
@@ -151,22 +151,30 @@
     )(kept, came)
 
 
-def finish_kernel(first, kept, came, extra, out):
-    count = kept.shape[1]
-    value = kept[...] + came[...].astype(F32) + extra[:, first : first + count].astype(F32)
-    out[...] = value.astype(BF16)
-
-
-def finish(kept, came, extra, first):
-    return pl.pallas_call(
-        functools.partial(finish_kernel, first),
-        out_shape=jax.ShapeDtypeStruct(kept.shape, BF16),
-        in_specs=[whole()] * 3,
+def finish_kernel(first, count, *refs):
+    extra, out = refs[2 * count :]
+    at = 0
+    for i in range(count):
+        kept, came = refs[2 * i : 2 * i + 2]
+        n = kept.shape[1]
+        value = kept[...] + came[...].astype(F32) + extra[:, first + at : first + at + n].astype(F32)
+        out[:, at : at + n] = value.astype(BF16)
+        at += n
+
+
+def finish(parts, extra, first):
+    flat = [array for part in parts for array in part]
+    px = flat[0].shape[0]
+    wide = sum(part[0].shape[1] for part in parts)
+    return pl.pallas_call(
+        functools.partial(finish_kernel, first, len(parts)),
+        out_shape=jax.ShapeDtypeStruct((px, wide), BF16),
+        in_specs=[whole()] * (2 * len(parts) + 1),
         out_specs=whole(),
         name="finish",
         compiler_params=pltpu.CompilerParams(vmem_limit_bytes=6 << 20),
-        cost_estimate=pl.CostEstimate(flops=2 * kept.size, bytes_accessed=10 * kept.size, transcendentals=0),
-    )(kept, came, extra)
+        cost_estimate=pl.CostEstimate(flops=2 * px * wide, bytes_accessed=10 * px * wide, transcendentals=0),
+    )(*flat, extra)
 
 
 def join_kernel(*refs):
@@ -242,10 +250,91 @@
     return main, rest, deep, main * rows * colp + deep * colp
 
 
-def pack_kernel(groups, per, c1, colp, ids, pixels, above, below, gain, shift, projection, *refs):
+def cut_kernel(ids, projection, *refs):
+    cuts, strip = refs[:-1], refs[-1]
+    z, ch = ids[1], ids[2]
+    deep, slab = cuts[0].shape
+    groups = len(cuts)
+    for i in range(projection.shape[0] // deep):
+        for g in range(groups):
+            strip[i, g] = projection[i * deep : (i + 1) * deep, g * slab : (g + 1) * slab].astype(F32)
+    for k in range(groups):
+        cuts[k][...] = strip[ch, jnp.bitwise_xor(z, k)].astype(BF16)
+
+
+def cut(ids, projection, groups, shards):
+    deep, slab = projection.shape[0] // shards, projection.shape[1] // groups
+    return pl.pallas_call(
+        cut_kernel,
+        out_shape=[jax.ShapeDtypeStruct((deep, slab), BF16)] * groups,
+        in_specs=[whole(pltpu.SMEM), whole()],
+        out_specs=[whole()] * groups,
+        scratch_shapes=[pltpu.VMEM((shards, groups, deep, slab), F32)],
+        name="cut",
+        compiler_params=pltpu.CompilerParams(vmem_limit_bytes=8 << 20),
+    )(ids, projection)
+
+
+def spread_kernel(groups, ids, *refs):
+    backs, out, held = refs[:groups], refs[groups], refs[groups + 1]
+    slab = backs[0].shape[1]
+    for k in range(groups):
+        held[jnp.bitwise_xor(ids[1], k)] = backs[k][...]
+    for g in range(groups):
+        out[:, g * slab : (g + 1) * slab] = held[g]
+
+
+def spread(ids, backs):
+    px, slab = backs[0].shape
+    groups = len(backs)
+    return pl.pallas_call(
+        functools.partial(spread_kernel, groups),
+        out_shape=jax.ShapeDtypeStruct((px, groups * slab), BF16),
+        in_specs=[whole(pltpu.SMEM)] + [whole()] * groups,
+        out_specs=whole(),
+        scratch_shapes=[pltpu.VMEM((groups, px, slab), BF16)],
+        name="spread",
+        compiler_params=pltpu.CompilerParams(vmem_limit_bytes=6 << 20),
+    )(ids, *backs)
+
+
+def final_kernel(parts, per, orows, ocols, ids, mine, far_mine, *refs):
+    own, far = refs[:parts], refs[parts : 2 * parts]
+    out, held = refs[2 * parts :]
+    first = ids[0] == 0
+    for half in range(2):
+        at = 0
+        for i in range(parts):
+            count = own[i].shape[1]
+            for lane in range(0, count, 128):
+                here = slice(lane, lane + 128)
+                there = slice(at + lane, at + lane + 128)
+                a = mine[:, there] if half == 0 else far_mine[:, there]
+                b = far[i][:, here] if half == 0 else own[i][:, here]
+                held[...] = jnp.where(first, a.astype(F32), b.astype(F32))
+                for p in range(per):
+                    for c in range(ocols):
+                        some = held[pl.ds(p * orows * ocols + c, orows, stride=ocols), :]
+                        out[half * per + p, c, :, there] = some.astype(BF16)
+            at += count
+
+
+def final(ids, mine, far_mine, own, far, per, orows, ocols):
+    wide = mine.shape[1]
+    return pl.pallas_call(
+        functools.partial(final_kernel, len(own), per, orows, ocols),
+        out_shape=jax.ShapeDtypeStruct((2 * per, ocols, orows, wide), BF16),
+        in_specs=[whole(pltpu.SMEM)] + [whole()] * (2 + 2 * len(own)),
+        out_specs=whole(),
+        scratch_shapes=[pltpu.VMEM((mine.shape[0], 128), F32)],
+        name="final",
+        compiler_params=pltpu.CompilerParams(vmem_limit_bytes=10 << 20),
+    )(ids, mine, far_mine, *own, *far)
+
+
+def pack_kernel(groups, per, c1, colp, ids, pixels, above, below, gain, shift, *refs):
     outs, mean = refs[:groups], refs[groups]
-    cuts = refs[groups + 1 : 2 * groups + 1]
-    held, pair, strip = refs[2 * groups + 1 :]
+    held, pair = refs[groups + 1 :]
     sec, z, ch, last = ids[0], ids[1], ids[2], ids[3]
     _, rows, cols, depth = pixels.shape
     main, rest, deep, size = packing(rows + 2, colp, c1)
@@ -288,38 +377,29 @@
                     held[g, at : at + colp, into : into + rest] = value[:, lane : lane + rest]
     for k in range(groups):
         outs[k][...] = held[jnp.bitwise_xor(z, k)]
-    deep, slab = cuts[0].shape
-    for i in range(c1 // deep):
-        for g in range(groups):
-            strip[i, g] = projection[i * deep : (i + 1) * deep, g * slab : (g + 1) * slab].astype(F32)
-    for k in range(groups):
-        cuts[k][...] = strip[ch, jnp.bitwise_xor(z, k)].astype(BF16)
-
-
-def pack(ids, pixels, above, below, gain, shift, projection, groups, shards, per, colp):
+
+
+def pack(ids, pixels, above, below, gain, shift, groups, per, colp):
     _, rows, cols, depth = pixels.shape
     c1 = depth // groups
     size = packing(rows + 2, colp, c1)[3]
     block = jax.ShapeDtypeStruct((per * size, 128), BF16)
     half = jax.ShapeDtypeStruct((per, rows * cols // 4, depth), F32)
-    deep, slab = c1 // shards, projection.shape[1] // groups
-    cut = jax.ShapeDtypeStruct((deep, slab), BF16)
     return pl.pallas_call(
         functools.partial(pack_kernel, groups, per, c1, colp),
-        out_shape=[block] * groups + [half] + [cut] * groups,
-        in_specs=[whole(pltpu.SMEM)] + [whole()] * 6,
-        out_specs=[whole()] * (2 * groups + 1),
+        out_shape=[block] * groups + [half],
+        in_specs=[whole(pltpu.SMEM)] + [whole()] * 5,
+        out_specs=[whole()] * (groups + 1),
         scratch_shapes=[
             pltpu.VMEM((groups, per * size, 128), BF16),
             pltpu.VMEM((depth // 128, cols, 128), F32),
-            pltpu.VMEM((shards, groups, deep, slab), F32),
         ],
         name="pack",
         compiler_params=pltpu.CompilerParams(vmem_limit_bytes=14 << 20),
         cost_estimate=pl.CostEstimate(
             flops=4 * rows * cols * depth, bytes_accessed=6 * rows * cols * depth, transcendentals=0
         ),
-    )(ids, pixels, above, below, gain, shift, projection)
+    )(ids, pixels, above, below, gain, shift)
 
 
 def stage_kernel(groups, per, rows, cols, colp, c1, *refs):
@@ -416,12 +496,14 @@
 
     other_kernel = swap(second_kernel, "ch", 1)
 
+    ids = jnp.stack([sec, z, ch, jnp.int32(shards - 1), y, core, z * pairs + y]).astype(jnp.int32)
+    cuts = cut(ids, projection, groups, shards)
     colp = -(-(cols + 2) // 16) * 16
     tails = lax.dynamic_slice_in_dim(pixels[:, -1:], sec * per, per, 0)
     heads = lax.dynamic_slice_in_dim(pixels[:, :1], sec * per, per, 0)
+    pixels, tails, heads = lax.optimization_barrier((pixels, tails, heads))
     above = lax.ppermute(tails, "ch", [(i, i + 1) for i in range(shards - 1)])
     below = lax.ppermute(heads, "ch", [(i + 1, i) for i in range(shards - 1)])
-    ids = jnp.stack([sec, z, ch, jnp.int32(shards - 1), y, core, z * pairs + y]).astype(jnp.int32)
     packed = pack(
         ids,
         pixels,
@@ -429,13 +511,11 @@
         below,
         first_gain.reshape(1, -1),
         first_shift.reshape(1, -1),
-        projection,
         groups,
-        shards,
         per,
         colp,
     )
-    blocks, mean, cuts = packed[:groups], packed[groups], packed[groups + 1 :]
+    blocks, mean = packed[:groups], packed[groups]
     got = [blocks[0]] + [swap(blocks[k], "img", k) for k in range(1, groups)]
 
     proj_z = join([cuts[0]] + [swap(cuts[k], "img", k) for k in range(1, groups)])
@@ -454,7 +534,8 @@
     back, chip = made[:groups], made[groups:]
 
     chip = [chip[0]] + [swap(chip[k], "ch", k, 2) for k in range(1, pairs)]
-    twin = [swap(part, "ch", 1) for part in chip]
+    twin = [swap(chip[0], "ch", 1)]
+    twin += [swap(part, "ch", 1) for part in chip[1:]]
     back = [back[0]] + [swap(back[k], "img", k) for k in range(1, groups)]
     a_own, a_other = unfold(
         ids,
@@ -464,8 +545,8 @@
         [c.reshape(imgs, out_px, kc) for c in twin],
         ocols,
     )
-    w_own = second_kernel.reshape(9 * kd, wide)
-    w_other = other_kernel.reshape(9 * kd, wide)
+    w_own = streamed(second_kernel.reshape(9 * kd, wide))
+    w_other = streamed(other_kernel.reshape(9 * kd, wide))
 
     unit = wide // 10
     plan = ((0, 2), (1, 3), (0, 3), (1, 2))
@@ -493,19 +574,14 @@
         values.append((kept, came, first, n * unit))
         first += n * unit
 
-    back_rel = join(back)
-    mine_projected = jnp.concatenate([pick(back_rel, z ^ i) for i in range(groups)], axis=1)
+    mine_projected = spread(ids, back)
     far_projected = lax.ppermute(mine_projected, "section", [(1, 0)])
     outs, fars = [], []
-    for j, (kept, came, first, n) in enumerate(values):
-        outs.append(finish(kept, came, mine_projected, first))
+    for j, some in enumerate((values[:2], values[2:])):
+        outs.append(finish([v[:2] for v in some], mine_projected, some[0][2]))
         fars.append(lax.ppermute(outs[j], "section", [(0, 1)]))
-    block = jnp.concatenate(outs, axis=-1)
-    far_block = jnp.concatenate(fars, axis=-1)
-    first = jnp.stack([mine_projected, far_projected])
-    second = jnp.stack([far_block, block])
-    final = jnp.where(sec == 0, first, second)
-    return final.reshape(1, sections * per, orows, ocols, wide)
+    block = final(ids, mine_projected, far_projected, outs, fars, per, orows, ocols)
+    return block.transpose(0, 2, 1, 3)[None]
 
 
 def solution(mesh):

time: 132 us -> 126 us (0.955)
  waiting for transfers between devices: 49.4 us -> 43.1 us
  Pallas kernels: 21.6 us -> 25.8 us
  local copies, waits for them, and re-layouts: 6.21 us -> 3.13 us
    ppermute x1, waiting for transfers between devices: 6.84 us -> 0.01 us  [body(): above = lax.ppermute(tails, 'ch', [(i, i + 1) for i in range(shards - 1)])]
    pallas_call x4 -> x5, Pallas kernels: 0.12 us -> 3.21 us  [the longest x1 1.84 us: final(): pl.pallas_call(functools.partial(final_kernel, len(own), per, orows, ocol...]
    unnamed x15 -> x14, local copies, waits for them, and re-layouts: 4.25 us -> 1.17 us
    ppermute x4 -> x2, waiting for transfers between devices: 1.93 us -> 4.12 us  [body(): fars.append(lax.ppermute(outs[j], 'section', [(0, 1)]))]
    ppermute x34, waiting for transfers between devices: 40.7 us -> 39 us  [swap(): return lax.ppermute(array, axis, [(i, i ^ k * unit) for i in range(count)])]
    slice x1, local copies, waits for them, and re-layouts: 0.02 us -> 1.47 us  [body(): heads = lax.dynamic_slice_in_dim(pixels[:, :1], sec * per, per, 0)]
    ppermute x4 -> x2, starting transfers between devices: 7.28 us -> 6.03 us  [body(): fars.append(lax.ppermute(outs[j], 'section', [(0, 1)]))]
  transfers between devices with their start and end apart: 41 -> 39, of which waited for: 18 -> 15; matrix products, arithmetic and copies ran while one was open for 1% -> 2% of each run, Pallas kernels for 6% -> 12%
where the time goes in v2:
time: 126 us
  starting transfers between devices  53.3 us (42%)
  waiting for transfers between devices  43.1 us (34%)
  Pallas kernels  25.8 us (20%)
  local copies, waits for them, and re-layouts  3.13 us (2%)
    ppermute x34, starting transfers between devices, swap(): return lax.ppermute(array, axis, [(i, i ^ k * unit) for i in range(count)])  42.6 us
    ppermute x34, waiting for transfers between devices, swap(): return lax.ppermute(array, axis, [(i, i ^ k * unit) for i in range(count)])  39 us
    pallas_call x4, Pallas kernels, mix(): pl.pallas_call(functools.partial(mix_kernel, rows, px), grid=(count // st...  15.5 us
    ppermute x2, starting transfers between devices, body(): fars.append(lax.ppermute(outs[j], 'section', [(0, 1)]))  6.03 us
    ppermute x2, waiting for transfers between devices, body(): fars.append(lax.ppermute(outs[j], 'section', [(0, 1)]))  4.12 us
    pallas_call x1, Pallas kernels, unfold(): pl.pallas_call(functools.partial(unfold_kernel, pairs, imgs, ocols, kd),...  3.02 us
  transfers between devices with their start and end apart: 39, of which 15 were waited for; matrix products, arithmetic and copies ran while one was open for 2% of the time, Pallas kernels for 12%

profile of v2, /device:TPU:0, one launch (start us, length us, event | category | flops | bytes accessed | tf_op | source)
XLA Modules:
  0.0 125.8 jit_solution(14022223868428470152)
XLA Ops:
  0.6 1.5 %fusion.1 = (bf16[2,1,28,640]{3,1,2,0:T(2,128)(2,1)S(1)}, bf16[2,1,28,640]{3,1,2,0:T(2,128)(2,1)S(1)}) fusion(bf16[2,8,28,640]{3,1,2,0:T(8,128)(2,1)} %param.8), kind=kLoop, calls=%fused_computation.4 | loop fusion | bytes 286720 | tf_op jit(solution)/shard_map/slice | solution.py:503
  2.2 2.1 %collective-permute-start = (bf16[1,1,28,640]{3,2,1,0:T(8,128)(2,1)S(1)}, bf16[1,1,28,640]{3,2,1,0:T(8,128)(2,1)S(1)}, u32[]{:S(2)}, u32[]{:S(2)}) collective-permute-start(bf16[1,1,28,640]{3,2,1,0:T(8,128)(2,1)S(1)} %copy.13), channel_id=1, source_target_pairs={{0,1},{1,2},{2,3},{4,5},{5,6},{6,7},{8,9},{9,10},{10,11},{12,13},{... | collective-permute-start | bytes 107528 | tf_op jit(solution)/shard_map/ppermute | solution.py:505
  4.5 1.1 copy-done.1
  5.6 0.7 cut.1
  6.3 3.1 %collective-permute-start.11 = (bf16[40,640]{1,0:T(8,128)(2,1)S(1)}, bf16[40,640]{1,0:T(8,128)(2,1)S(1)}, u32[]{:S(2)}, u32[]{:S(2)}) collective-permute-start(bf16[40,640]{1,0:T(8,128)(2,1)S(1)} %get-tuple-element.66), channel_id=1, source_target_pairs={{0,4},{4,0},{8,12},{12,8},{1,5},{5,1},{9,13},{13,9},{2,6},{6,2},{1... | collective-permute-start | bytes 153608 | tf_op jit(solution)/shard_map/ppermute | solution.py:17
  9.4 2.6 %collective-permute-start.12 = (bf16[40,640]{1,0:T(8,128)(2,1)S(1)}, bf16[40,640]{1,0:T(8,128)(2,1)S(1)}, u32[]{:S(2)}, u32[]{:S(2)}) collective-permute-start(bf16[40,640]{1,0:T(8,128)(2,1)S(1)} %get-tuple-element.67), channel_id=1, source_target_pairs={{0,8},{4,12},{8,0},{12,4},{1,9},{5,13},{9,1},{13,5},{2,10},{6,14},... | collective-permute-start | bytes 153608 | tf_op jit(solution)/shard_map/ppermute | solution.py:17
  12.0 1.3 %collective-permute-start.1 = (bf16[1,1,28,640]{3,2,1,0:T(8,128)(2,1)S(1)}, bf16[1,1,28,640]{3,2,1,0:T(8,128)(2,1)S(1)}, u32[]{:S(2)}, u32[]{:S(2)}) collective-permute-start(bf16[1,1,28,640]{3,2,1,0:T(8,128)(2,1)S(1)} %copy.15), channel_id=1, source_target_pairs={{1,0},{2,1},{3,2},{5,4},{6,5},{7,6},{9,8},{10,9},{11,10},{13,12},{... | collective-permute-start | bytes 107528 | tf_op jit(solution)/shard_map/ppermute | solution.py:506
  13.3 3.6 %collective-permute-start.13 = (bf16[40,640]{1,0:T(8,128)(2,1)S(1)}, bf16[40,640]{1,0:T(8,128)(2,1)S(1)}, u32[]{:S(2)}, u32[]{:S(2)}) collective-permute-start(bf16[40,640]{1,0:T(8,128)(2,1)S(1)} %get-tuple-element.68), channel_id=1, source_target_pairs={{0,12},{4,8},{8,4},{12,0},{1,13},{5,9},{9,5},{13,1},{2,14},{6,10},... | collective-permute-start | bytes 153608 | tf_op jit(solution)/shard_map/ppermute | solution.py:17
  17.0 0.9 pack.1
  18.0 0.8 collective-permute-start.3
  18.9 3.5 %collective-permute-start.4 = (bf16[416,128]{1,0:T(8,128)(2,1)S(1)}, bf16[416,128]{1,0:T(8,128)(2,1)S(1)}, u32[]{:S(2)}, u32[]{:S(2)}) collective-permute-start(bf16[416,128]{1,0:T(8,128)(2,1)S(1)} %get-tuple-element.59), channel_id=1, source_target_pairs={{0,12},{4,8},{8,4},{12,0},{1,13},{5,9},{9,5},{13,1},{2,14},{6,10},... | collective-permute-start | bytes 319496 | tf_op jit(solution)/shard_map/ppermute | solution.py:17
  22.4 1.6 %collective-permute-start.14 = (bf16[4,40,640]{2,1,0:T(8,128)(2,1)S(1)}, bf16[4,40,640]{2,1,0:T(8,128)(2,1)S(1)}, u32[]{:S(2)}, u32[]{:S(2)}) collective-permute-start(bf16[4,40,640]{2,1,0:T(8,128)(2,1)S(1)} %join.1.refs_4_), channel_id=1, source_target_pairs={{0,2},{1,3},{2,0},{3,1},{4,6},{5,7},{6,4},{7,5},{8,10},{9,11},{10,... | collective-permute-start | bytes 614408 | tf_op jit(solution)/shard_map/ppermute | solution.py:17
  24.0 0.9 collective-permute-done.2.refs_1_
  24.9 4.2 %collective-permute-done.3.refs_2_ = bf16[416,128]{1,0:T(8,128)(2,1)S(1)} collective-permute-done((bf16[416,128]{1,0:T(8,128)(2,1)S(1)}, bf16[416,128]{1,0:T(8,128)(2,1)S(1)}, u32[]{:S(2)}, u32[]{:S(2)}) %collective-permute-start.3) | collective-permute-done | bytes 106528 | tf_op jit(solution)/shard_map/ppermute | solution.py:17
  29.1 1.5 %stage.1 = (f32[56,640]{1,0:T(8,128)S(1)}, bf16[56,640]{1,0:T(8,128)(2,1)S(1)}, bf16[56,640]{1,0:T(8,128)(2,1)S(1)}, bf16[56,640]{1,0:T(8,128)(2,1)S(1)}) custom-call(bf16[416,128]{1,0:T(8,128)(2,1)S(1)} %get-tuple-element.56.refs_0_, bf16[416,128]{1,0:T(8,128)(2,1)S(1)} %collective-permute-done.2.refs_1_, ...), custom_call_target="tpu_custom_call" | custom-call | flops 471859200 | bytes 573440 | tf_op jit(solution)/shard_map/stage/pallas_call | solution.py:460
  30.7 2.9 %collective-permute-start.5 = (bf16[56,640]{1,0:T(8,128)(2,1)S(1)}, bf16[56,640]{1,0:T(8,128)(2,1)S(1)}, u32[]{:S(2)}, u32[]{:S(2)}) collective-permute-start(bf16[56,640]{1,0:T(8,128)(2,1)S(1)} %get-tuple-element.61), channel_id=1, source_target_pairs={{0,4},{4,0},{8,12},{12,8},{1,5},{5,1},{9,13},{13,9},{2,6},{6,2},{1... | collective-permute-start | bytes 215048 | tf_op jit(solution)/shard_map/ppermute | solution.py:17
  33.9 2.1 %collective-permute-start.7 = (bf16[56,640]{1,0:T(8,128)(2,1)S(1)}, bf16[56,640]{1,0:T(8,128)(2,1)S(1)}, u32[]{:S(2)}, u32[]{:S(2)}) collective-permute-start(bf16[56,640]{1,0:T(8,128)(2,1)S(1)} %get-tuple-element.63), channel_id=1, source_target_pairs={{0,12},{4,8},{8,4},{12,0},{1,13},{5,9},{9,5},{13,1},{2,14},{6,10},... | collective-permute-start | bytes 215048 | tf_op jit(solution)/shard_map/ppermute | solution.py:17
  36.7 5.2 %collective-permute-done.6 = bf16[56,640]{1,0:T(8,128)(2,1)S(1)} collective-permute-done((bf16[56,640]{1,0:T(8,128)(2,1)S(1)}, bf16[56,640]{1,0:T(8,128)(2,1)S(1)}, u32[]{:S(2)}, u32[]{:S(2)}) %collective-permute-start.6) | collective-permute-done | bytes 71712 | tf_op jit(solution)/shard_map/ppermute | solution.py:17
  42.0 2.0 %collective-permute-start.10 = (bf16[56,640]{1,0:T(8,128)(2,1)S(1)}, bf16[56,640]{1,0:T(8,128)(2,1)S(1)}, u32[]{:S(2)}, u32[]{:S(2)}) collective-permute-start(bf16[56,640]{1,0:T(8,128)(2,1)S(1)} %fusion.refs_0_), channel_id=1, source_target_pairs={{0,12},{4,8},{8,4},{12,0},{1,13},{5,9},{9,5},{13,1},{2,14},{6,10},... | collective-permute-start | bytes 215048 | tf_op jit(solution)/shard_map/ppermute | solution.py:17
  44.5 1.9 %collective-permute-start.9 = (bf16[56,640]{1,0:T(8,128)(2,1)S(1)}, bf16[56,640]{1,0:T(8,128)(2,1)S(1)}, u32[]{:S(2)}, u32[]{:S(2)}) collective-permute-start(bf16[56,640]{1,0:T(8,128)(2,1)S(1)} %fusion.refs_0_), channel_id=1, source_target_pairs={{0,8},{4,12},{8,0},{12,4},{1,9},{5,13},{9,1},{13,5},{2,10},{6,14},... | collective-permute-start | bytes 215048 | tf_op jit(solution)/shard_map/ppermute | solution.py:17
  46.5 2.4 %collective-permute-done.10.refs_3_ = bf16[56,640]{1,0:T(8,128)(2,1)S(1)} collective-permute-done((bf16[56,640]{1,0:T(8,128)(2,1)S(1)}, bf16[56,640]{1,0:T(8,128)(2,1)S(1)}, u32[]{:S(2)}, u32[]{:S(2)}) %collective-permute-start.10) | collective-permute-done | bytes 71712 | tf_op jit(solution)/shard_map/ppermute | solution.py:17
  49.4 2.0 %collective-permute-done.9.refs_2_ = bf16[56,640]{1,0:T(8,128)(2,1)S(1)} collective-permute-done((bf16[56,640]{1,0:T(8,128)(2,1)S(1)}, bf16[56,640]{1,0:T(8,128)(2,1)S(1)}, u32[]{:S(2)}, u32[]{:S(2)}) %collective-permute-start.9) | collective-permute-done | bytes 71712 | tf_op jit(solution)/shard_map/ppermute | solution.py:17
  51.4 1.2 project.1
  52.8 5.3 %collective-permute-done.21 = bf16[224,320]{1,0:T(8,128)(2,1)S(1)} collective-permute-done((bf16[224,320]{1,0:T(8,128)(2,1)S(1)}, bf16[224,320]{1,0:T(8,128)(2,1)S(1)}, u32[]{:S(2)}, u32[]{:S(2)}) %collective-permute-start.21) | collective-permute-done | bytes 143392 | tf_op jit(solution)/shard_map/ppermute | solution.py:17
  58.2 1.2 collective-permute-done.23
  59.5 3.0 %unfold.1 = (bf16[448,1440]{1,0:T(8,128)(2,1)S(1)}, bf16[448,1440]{1,0:T(8,128)(2,1)S(1)}) custom-call(s32[7]{0:T(128)S(1)} %stack.27.ids, f32[8,320]{1,0:T(8,128)S(1)} %reshape.40.gains, f32[8,320]{1,0:T(8,128)S(1)} %reshape.41.shifts, bf16[4,56,320]{2,1,0:T(8,128)(2,1)S(1)} %bitcast.21, bf16[4,56,320]{2,1,0:T(8,128)(2,1)S(1)} %bitcast.22, ...), custom_call_target="tpu_custom_call" | custom-call | flops 12902400 | bytes 5160960 | tf_op jit(solution)/shard_map/unfold/pallas_call | solution.py:84
  62.5 4.6 %mix.6 = (bf16[224,768]{1,0:T(8,128)(2,1)S(1)}, f32[224,768]{1,0:T(8,128)S(1)}) custom-call(bf16[448,1440]{1,0:T(8,128)(2,1)S(1)} %get-tuple-element.75.a_own, bf16[448,1440]{1,0:T(8,128)(2,1)S(1)} %get-tuple-element.76.a_other, bf16[1440,2560]{1,0:T(8,128)(2,1)} %bitcast.25, bf16[1440,2560]{1,0:T(8,128)(2,1)} %bitcast.13.w_other), custom_call_target="tpu_custom_call" | custom-call | flops 1981808640 | bytes 5455872 | tf_op jit(solution)/shard_map/mix/pallas_call | solution.py:116
  67.1 4.5 %mix.5 = (bf16[224,768]{1,0:T(8,128)(2,1)S(1)}, f32[224,768]{1,0:T(8,128)S(1)}) custom-call(bf16[448,1440]{1,0:T(8,128)(2,1)S(1)} %get-tuple-element.75.a_own, bf16[448,1440]{1,0:T(8,128)(2,1)S(1)} %get-tuple-element.76.a_other, bf16[1440,2560]{1,0:T(8,128)(2,1)} %bitcast.26, bf16[1440,2560]{1,0:T(8,128)(2,1)} %bitcast.13.w_other), custom_call_target="tpu_custom_call" | custom-call | flops 1981808640 | bytes 5455872 | tf_op jit(solution)/shard_map/mix/pallas_call | solution.py:116
  71.8 3.2 %mix.7 = (bf16[224,512]{1,0:T(8,128)(2,1)S(1)}, f32[224,512]{1,0:T(8,128)S(1)}) custom-call(bf16[448,1440]{1,0:T(8,128)(2,1)S(1)} %get-tuple-element.75.a_own, bf16[448,1440]{1,0:T(8,128)(2,1)S(1)} %get-tuple-element.76.a_other, bf16[1440,2560]{1,0:T(8,128)(2,1)} %bitcast.27, bf16[1440,2560]{1,0:T(8,128)(2,1)} %bitcast.13.w_other), custom_call_target="tpu_custom_call" | custom-call | flops 1321205760 | bytes 3637248 | tf_op jit(solution)/shard_map/mix/pallas_call | solution.py:116
  75.0 2.1 %collective-permute-start.34 = (bf16[224,512]{1,0:T(8,128)(2,1)S(1)}, bf16[224,512]{1,0:T(8,128)(2,1)S(1)}, u32[]{:S(2)}, u32[]{:S(2)}) collective-permute-start(bf16[224,512]{1,0:T(8,128)(2,1)S(1)} %get-tuple-element.96), channel_id=1, source_target_pairs={{0,4},{4,0},{8,12},{12,8},{1,5},{5,1},{9,13},{13,9},{2,6},{6,2},{1... | collective-permute-start | bytes 688136 | tf_op jit(solution)/shard_map/ppermute | solution.py:17
  77.1 3.2 %mix.4 = (bf16[224,512]{1,0:T(8,128)(2,1)S(1)}, f32[224,512]{1,0:T(8,128)S(1)}) custom-call(bf16[448,1440]{1,0:T(8,128)(2,1)S(1)} %get-tuple-element.75.a_own, bf16[448,1440]{1,0:T(8,128)(2,1)S(1)} %get-tuple-element.76.a_other, bf16[1440,2560]{1,0:T(8,128)(2,1)} %bitcast.28, bf16[1440,2560]{1,0:T(8,128)(2,1)} %bitcast.13.w_other), custom_call_target="tpu_custom_call" | custom-call | flops 1321205760 | bytes 3637248 | tf_op jit(solution)/shard_map/mix/pallas_call | solution.py:116
  80.3 2.0 %collective-permute-start.25 = (bf16[224,512]{1,0:T(8,128)(2,1)S(1)}, bf16[224,512]{1,0:T(8,128)(2,1)S(1)}, u32[]{:S(2)}, u32[]{:S(2)}) collective-permute-start(bf16[224,512]{1,0:T(8,128)(2,1)S(1)} %get-tuple-element.78), channel_id=1, source_target_pairs={{0,2},{1,3},{2,0},{3,1},{4,6},{5,7},{6,4},{7,5},{8,10},{9,11},{10,... | collective-permute-start | bytes 688136 | tf_op jit(solution)/shard_map/ppermute | solution.py:17
  82.4 2.1 %collective-permute-start.32 = (bf16[112,768]{1,0:T(8,128)(2,1)S(1)}, bf16[112,768]{1,0:T(8,128)(2,1)S(1)}, u32[]{:S(2)}, u32[]{:S(2)}) collective-permute-start(bf16[112,768]{1,0:T(8,128)(2,1)S(1)} %get-tuple-element.92), channel_id=1, source_target_pairs={{0,4},{4,0},{8,12},{12,8},{1,5},{5,1},{9,13},{13,9},{2,6},{6,2},{1... | collective-permute-start | bytes 516104 | tf_op jit(solution)/shard_map/ppermute | solution.py:17
  84.5 1.0 collective-permute-start.29
  85.5 7.4 %collective-permute-done.17.refs_1_ = bf16[56,640]{1,0:T(8,128)(2,1)S(1)} collective-permute-done((bf16[56,640]{1,0:T(8,128)(2,1)S(1)}, bf16[56,640]{1,0:T(8,128)(2,1)S(1)}, u32[]{:S(2)}, u32[]{:S(2)}) %collective-permute-start.17) | collective-permute-done | bytes 71712 | tf_op jit(solution)/shard_map/ppermute | solution.py:17
  93.5 1.9 %collective-permute-start.19 = (bf16[56,640]{1,0:T(8,128)(2,1)S(1)}, bf16[56,640]{1,0:T(8,128)(2,1)S(1)}, u32[]{:S(2)}, u32[]{:S(2)}) collective-permute-start(bf16[56,640]{1,0:T(8,128)(2,1)S(1)} %get-tuple-element.72), channel_id=1, source_target_pairs={{0,12},{4,8},{8,4},{12,0},{1,13},{5,9},{9,5},{13,1},{2,14},{6,10},... | collective-permute-start | bytes 215048 | tf_op jit(solution)/shard_map/ppermute | solution.py:17
  95.5 2.1 %collective-permute-start.35 = (bf16[112,512]{1,0:T(8,128)(2,1)S(1)}, bf16[112,512]{1,0:T(8,128)(2,1)S(1)}, u32[]{:S(2)}, u32[]{:S(2)}) collective-permute-start(bf16[112,512]{1,0:T(8,128)(2,1)S(1)} %get-tuple-element.98), channel_id=1, source_target_pairs={{0,8},{4,12},{8,0},{12,4},{1,9},{5,13},{9,1},{13,5},{2,10},{6,14},... | collective-permute-start | bytes 344072 | tf_op jit(solution)/shard_map/ppermute | solution.py:17
  97.6 5.9 %collective-permute-done.18.refs_2_ = bf16[56,640]{1,0:T(8,128)(2,1)S(1)} collective-permute-done((bf16[56,640]{1,0:T(8,128)(2,1)S(1)}, bf16[56,640]{1,0:T(8,128)(2,1)S(1)}, u32[]{:S(2)}, u32[]{:S(2)}) %collective-permute-start.18) | collective-permute-done | bytes 71712 | tf_op jit(solution)/shard_map/ppermute | solution.py:17
  104.1 1.3 %collective-permute-start.20 = (bf16[56,2560]{1,0:T(8,128)(2,1)S(1)}, bf16[56,2560]{1,0:T(8,128)(2,1)S(1)}, u32[]{:S(2)}, u32[]{:S(2)}) collective-permute-start(bf16[56,2560]{1,0:T(8,128)(2,1)S(1)} %spread.1.refs_4_.mine), channel_id=1, source_target_pairs={{16,0},{17,1},{18,2},{19,3},{20,4},{21,5},{22,6},{23,7},{24,8},{25... | collective-permute-start | bytes 860168 | tf_op jit(solution)/shard_map/ppermute | solution.py:578
  105.5 2.2 %collective-permute-start.33 = (bf16[56,768]{1,0:T(8,128)(2,1)S(1)}, bf16[56,768]{1,0:T(8,128)(2,1)S(1)}, u32[]{:S(2)}, u32[]{:S(2)}) collective-permute-start(bf16[56,768]{1,0:T(8,128)(2,1)S(1)} %get-tuple-element.94), channel_id=1, source_target_pairs={{0,8},{4,12},{8,0},{12,4},{1,9},{5,13},{9,1},{13,5},{2,10},{6,14},... | collective-permute-start | bytes 258056 | tf_op jit(solution)/shard_map/ppermute | solution.py:17
  107.7 1.7 %collective-permute-start.30 = (bf16[56,768]{1,0:T(8,128)(2,1)S(1)}, bf16[56,768]{1,0:T(8,128)(2,1)S(1)}, u32[]{:S(2)}, u32[]{:S(2)}) collective-permute-start(bf16[56,768]{1,0:T(8,128)(2,1)S(1)} %get-tuple-element.88), channel_id=1, source_target_pairs={{0,2},{1,3},{2,0},{3,1},{4,6},{5,7},{6,4},{7,5},{8,10},{9,11},{10,... | collective-permute-start | bytes 258056 | tf_op jit(solution)/shard_map/ppermute | solution.py:17
  109.8 1.5 %collective-permute-done.26.came = bf16[112,512]{1,0:T(8,128)(2,1)S(1)} collective-permute-done((bf16[112,512]{1,0:T(8,128)(2,1)S(1)}, bf16[112,512]{1,0:T(8,128)(2,1)S(1)}, u32[]{:S(2)}, u32[]{:S(2)}) %collective-permute-start.26) | collective-permute-done | bytes 114720 | tf_op jit(solution)/shard_map/ppermute | solution.py:17
  111.5 2.2 %collective-permute-done.36.refs_3_ = bf16[56,512]{1,0:T(8,128)(2,1)S(1)} collective-permute-done((bf16[56,512]{1,0:T(8,128)(2,1)S(1)}, bf16[56,512]{1,0:T(8,128)(2,1)S(1)}, u32[]{:S(2)}, u32[]{:S(2)}) %collective-permute-start.36) | collective-permute-done | bytes 57376 | tf_op jit(solution)/shard_map/ppermute | solution.py:17
  113.7 4.6 %collective-permute-start.38 = (bf16[56,1280]{1,0:T(8,128)(2,1)S(1)}, bf16[56,1280]{1,0:T(8,128)(2,1)S(1)}, u32[]{:S(2)}, u32[]{:S(2)}) collective-permute-start(bf16[56,1280]{1,0:T(8,128)(2,1)S(1)} %finish.3.refs_1_), channel_id=1, source_target_pairs={{0,16},{1,17},{2,18},{3,19},{4,20},{5,21},{6,22},{7,23},{8,24},{9,... | collective-permute-start | bytes 430088 | tf_op jit(solution)/shard_map/ppermute | solution.py:582
  118.4 1.4 %collective-permute-start.37 = (bf16[56,1280]{1,0:T(8,128)(2,1)S(1)}, bf16[56,1280]{1,0:T(8,128)(2,1)S(1)}, u32[]{:S(2)}, u32[]{:S(2)}) collective-permute-start(bf16[56,1280]{1,0:T(8,128)(2,1)S(1)} %finish.2.refs_0_), channel_id=1, source_target_pairs={{0,16},{1,17},{2,18},{3,19},{4,20},{5,21},{6,22},{7,23},{8,24},{9,... | collective-permute-start | bytes 430088 | tf_op jit(solution)/shard_map/ppermute | solution.py:582
  119.9 2.5 %collective-permute-done.38.refs_3_ = bf16[56,1280]{1,0:T(8,128)(2,1)S(1)} collective-permute-done((bf16[56,1280]{1,0:T(8,128)(2,1)S(1)}, bf16[56,1280]{1,0:T(8,128)(2,1)S(1)}, u32[]{:S(2)}, u32[]{:S(2)}) %collective-permute-start.38) | collective-permute-done | bytes 143392 | tf_op jit(solution)/shard_map/ppermute | solution.py:582
  122.4 1.6 %collective-permute-done.37.refs_2_ = bf16[56,1280]{1,0:T(8,128)(2,1)S(1)} collective-permute-done((bf16[56,1280]{1,0:T(8,128)(2,1)S(1)}, bf16[56,1280]{1,0:T(8,128)(2,1)S(1)}, u32[]{:S(2)}, u32[]{:S(2)}) %collective-permute-start.37) | collective-permute-done | bytes 143392 | tf_op jit(solution)/shard_map/ppermute | solution.py:582
  124.0 1.8 %final.1 = bf16[2,14,4,2560]{3,2,1,0:T(4,128)(2,1)} custom-call(s32[7]{0:T(128)S(1)} %stack.27.ids, bf16[56,2560]{1,0:T(8,128)(2,1)S(1)} %spread.1.refs_4_.mine, bf16[56,2560]{1,0:T(8,128)(2,1)S(1)} %collective-permute-done.20.far_mine, bf16[56,1280]{1,0:T(8,128)(2,1)S(1)} %finish.2.refs_0_, bf16[56,1280]{1,0:T(8,128)(2,1)S(1)} %finish.3.refs_1_, ...), custom_call_target="tpu_custom_call" | custom-call | tf_op jit(solution)/shard_map/final/pallas_call | solution.py:324
  (77 shorter events, 5.7 us)
Async XLA Ops:
  0.0 16.8 %copy-start.2 = (bf16[2,8,28,640]{3,1,2,0:T(8,128)(2,1)S(1)}, bf16[2,8,28,640]{3,1,2,0:T(8,128)(2,1)}, u32[]{:S(2)}) copy-start(bf16[2,8,28,640]{3,1,2,0:T(8,128)(2,1)} %param.8) | copy-start | bytes 1720324
  0.0 16.9 %copy-start.5 = (f32[640]{0:T(1024)S(1)}, f32[640]{0:T(1024)}, u32[]{:S(2)}) copy-start(f32[640]{0:T(1024)} %param.9) | copy-start | bytes 7684
  0.0 16.9 %copy-start.6 = (f32[640]{0:T(1024)S(1)}, f32[640]{0:T(1024)}, u32[]{:S(2)}) copy-start(f32[640]{0:T(1024)} %param.10) | copy-start | bytes 7684
  0.0 62.5 %collective-permute-start.24 = (bf16[3,3,160,2560]{3,2,1,0:T(8,128)(2,1)}, bf16[3,3,160,2560]{3,2,1,0:T(8,128)(2,1)}, u32[]{:S(2)}, u32[]{:S(2)}) collective-permute-start(bf16[3,3,160,2560]{3,2,1,0:T(8,128)(2,1)} %param.15), channel_id=1, source_target_pairs={{0,1},{1,0},{2,3},{3,2},{4,5},{5,4},{6,7},{7,6},{8,9},{9,8},{10,11... | collective-permute-start | bytes 22118408 | tf_op jit(solution)/shard_map/ppermute | solution.py:17
  2.0 27.1 %copy-start = (bf16[3,3,160,640]{3,2,1,0:T(8,128)(2,1)S(1)}, bf16[3,3,160,640]{3,2,1,0:T(8,128)(2,1)}, u32[]{:S(2)}) copy-start(bf16[3,3,160,640]{3,2,1,0:T(8,128)(2,1)} %param.11) | copy-start | bytes 5529604
  2.2 11.0 %collective-permute-start = (bf16[1,1,28,640]{3,2,1,0:T(8,128)(2,1)S(1)}, bf16[1,1,28,640]{3,2,1,0:T(8,128)(2,1)S(1)}, u32[]{:S(2)}, u32[]{:S(2)}) collective-permute-start(bf16[1,1,28,640]{3,2,1,0:T(8,128)(2,1)S(1)} %copy.13), channel_id=1, source_target_pairs={{0,1},{1,2},{2,3},{4,5},{5,6},{6,7},{8,9},{9,10},{10,11},{12,13},{... | collective-permute-start | bytes 107528 | tf_op jit(solution)/shard_map/ppermute | solution.py:505
  4.5 1.1 copy-start.1
  6.3 11.7 %collective-permute-start.11 = (bf16[40,640]{1,0:T(8,128)(2,1)S(1)}, bf16[40,640]{1,0:T(8,128)(2,1)S(1)}, u32[]{:S(2)}, u32[]{:S(2)}) collective-permute-start(bf16[40,640]{1,0:T(8,128)(2,1)S(1)} %get-tuple-element.66), channel_id=1, source_target_pairs={{0,4},{4,0},{8,12},{12,8},{1,5},{5,1},{9,13},{13,9},{2,6},{6,2},{1... | collective-permute-start | bytes 153608 | tf_op jit(solution)/shard_map/ppermute | solution.py:17
  9.4 9.5 %collective-permute-start.12 = (bf16[40,640]{1,0:T(8,128)(2,1)S(1)}, bf16[40,640]{1,0:T(8,128)(2,1)S(1)}, u32[]{:S(2)}, u32[]{:S(2)}) collective-permute-start(bf16[40,640]{1,0:T(8,128)(2,1)S(1)} %get-tuple-element.67), channel_id=1, source_target_pairs={{0,8},{4,12},{8,0},{12,4},{1,9},{5,13},{9,1},{13,5},{2,10},{6,14},... | collective-permute-start | bytes 153608 | tf_op jit(solution)/shard_map/ppermute | solution.py:17
  12.0 5.0 %collective-permute-start.1 = (bf16[1,1,28,640]{3,2,1,0:T(8,128)(2,1)S(1)}, bf16[1,1,28,640]{3,2,1,0:T(8,128)(2,1)S(1)}, u32[]{:S(2)}, u32[]{:S(2)}) collective-permute-start(bf16[1,1,28,640]{3,2,1,0:T(8,128)(2,1)S(1)} %copy.15), channel_id=1, source_target_pairs={{1,0},{2,1},{3,2},{5,4},{6,5},{7,6},{9,8},{10,9},{11,10},{13,12},{... | collective-permute-start | bytes 107528 | tf_op jit(solution)/shard_map/ppermute | solution.py:506
  13.3 9.1 %collective-permute-start.13 = (bf16[40,640]{1,0:T(8,128)(2,1)S(1)}, bf16[40,640]{1,0:T(8,128)(2,1)S(1)}, u32[]{:S(2)}, u32[]{:S(2)}) collective-permute-start(bf16[40,640]{1,0:T(8,128)(2,1)S(1)} %get-tuple-element.68), channel_id=1, source_target_pairs={{0,12},{4,8},{8,4},{12,0},{1,13},{5,9},{9,5},{13,1},{2,14},{6,10},... | collective-permute-start | bytes 153608 | tf_op jit(solution)/shard_map/ppermute | solution.py:17
  17.9 6.9 %collective-permute-start.2 = (bf16[416,128]{1,0:T(8,128)(2,1)S(1)}, bf16[416,128]{1,0:T(8,128)(2,1)S(1)}, u32[]{:S(2)}, u32[]{:S(2)}) collective-permute-start(bf16[416,128]{1,0:T(8,128)(2,1)S(1)} %get-tuple-element.57), channel_id=1, source_target_pairs={{0,4},{4,0},{8,12},{12,8},{1,5},{5,1},{9,13},{13,9},{2,6},{6,2},{1... | collective-permute-start | bytes 319496 | tf_op jit(solution)/shard_map/ppermute | solution.py:17
  18.0 11.1 %collective-permute-start.3 = (bf16[416,128]{1,0:T(8,128)(2,1)S(1)}, bf16[416,128]{1,0:T(8,128)(2,1)S(1)}, u32[]{:S(2)}, u32[]{:S(2)}) collective-permute-start(bf16[416,128]{1,0:T(8,128)(2,1)S(1)} %get-tuple-element.58), channel_id=1, source_target_pairs={{0,8},{4,12},{8,0},{12,4},{1,9},{5,13},{9,1},{13,5},{2,10},{6,14},... | collective-permute-start | bytes 319496 | tf_op jit(solution)/shard_map/ppermute | solution.py:17
  18.9 10.3 %collective-permute-start.4 = (bf16[416,128]{1,0:T(8,128)(2,1)S(1)}, bf16[416,128]{1,0:T(8,128)(2,1)S(1)}, u32[]{:S(2)}, u32[]{:S(2)}) collective-permute-start(bf16[416,128]{1,0:T(8,128)(2,1)S(1)} %get-tuple-element.59), channel_id=1, source_target_pairs={{0,12},{4,8},{8,4},{12,0},{1,13},{5,9},{9,5},{13,1},{2,14},{6,10},... | collective-permute-start | bytes 319496 | tf_op jit(solution)/shard_map/ppermute | solution.py:17
  22.4 13.8 %collective-permute-start.14 = (bf16[4,40,640]{2,1,0:T(8,128)(2,1)S(1)}, bf16[4,40,640]{2,1,0:T(8,128)(2,1)S(1)}, u32[]{:S(2)}, u32[]{:S(2)}) collective-permute-start(bf16[4,40,640]{2,1,0:T(8,128)(2,1)S(1)} %join.1.refs_4_), channel_id=1, source_target_pairs={{0,2},{1,3},{2,0},{3,1},{4,6},{5,7},{6,4},{7,5},{8,10},{9,11},{10,... | collective-permute-start | bytes 614408 | tf_op jit(solution)/shard_map/ppermute | solution.py:17
  29.1 29.0 %copy-start.3 = (f32[2560]{0:T(1024)S(1)}, f32[2560]{0:T(1024)}, u32[]{:S(2)}) copy-start(f32[2560]{0:T(1024)} %param.13) | copy-start | bytes 30724
  29.1 29.0 %copy-start.4 = (f32[2560]{0:T(1024)S(1)}, f32[2560]{0:T(1024)}, u32[]{:S(2)}) copy-start(f32[2560]{0:T(1024)} %param.14) | copy-start | bytes 30724
  30.7 5.5 %collective-permute-start.5 = (bf16[56,640]{1,0:T(8,128)(2,1)S(1)}, bf16[56,640]{1,0:T(8,128)(2,1)S(1)}, u32[]{:S(2)}, u32[]{:S(2)}) collective-permute-start(bf16[56,640]{1,0:T(8,128)(2,1)S(1)} %get-tuple-element.61), channel_id=1, source_target_pairs={{0,4},{4,0},{8,12},{12,8},{1,5},{5,1},{9,13},{13,9},{2,6},{6,2},{1... | collective-permute-start | bytes 215048 | tf_op jit(solution)/shard_map/ppermute | solution.py:17
  33.6 8.4 %collective-permute-start.6 = (bf16[56,640]{1,0:T(8,128)(2,1)S(1)}, bf16[56,640]{1,0:T(8,128)(2,1)S(1)}, u32[]{:S(2)}, u32[]{:S(2)}) collective-permute-start(bf16[56,640]{1,0:T(8,128)(2,1)S(1)} %get-tuple-element.62), channel_id=1, source_target_pairs={{0,8},{4,12},{8,0},{12,4},{1,9},{5,13},{9,1},{13,5},{2,10},{6,14},... | collective-permute-start | bytes 215048 | tf_op jit(solution)/shard_map/ppermute | solution.py:17
  33.9 8.1 %collective-permute-start.7 = (bf16[56,640]{1,0:T(8,128)(2,1)S(1)}, bf16[56,640]{1,0:T(8,128)(2,1)S(1)}, u32[]{:S(2)}, u32[]{:S(2)}) collective-permute-start(bf16[56,640]{1,0:T(8,128)(2,1)S(1)} %get-tuple-element.63), channel_id=1, source_target_pairs={{0,12},{4,8},{8,4},{12,0},{1,13},{5,9},{9,5},{13,1},{2,14},{6,10},... | collective-permute-start | bytes 215048 | tf_op jit(solution)/shard_map/ppermute | solution.py:17
  36.2 8.3 %collective-permute-start.15 = (bf16[4,40,640]{2,1,0:T(8,128)(2,1)S(1)}, bf16[4,40,640]{2,1,0:T(8,128)(2,1)S(1)}, u32[]{:S(2)}, u32[]{:S(2)}) collective-permute-start(bf16[4,40,640]{2,1,0:T(8,128)(2,1)S(1)} %join.1.refs_4_), channel_id=1, source_target_pairs={{0,1},{1,0},{2,3},{3,2},{4,5},{5,4},{6,7},{7,6},{8,9},{9,8},{10,11... | collective-permute-start | bytes 614408 | tf_op jit(solution)/shard_map/ppermute | solution.py:17
  36.2 15.2 %collective-permute-start.16 = (bf16[4,40,640]{2,1,0:T(8,128)(2,1)S(1)}, bf16[4,40,640]{2,1,0:T(8,128)(2,1)S(1)}, u32[]{:S(2)}, u32[]{:S(2)}) collective-permute-start(bf16[4,40,640]{2,1,0:T(8,128)(2,1)S(1)} %collective-permute-done.14.refs_5_), channel_id=1, source_target_pairs={{0,1},{1,0},{2,3},{3,2},{4,5},{5,4},{6,7},{7,6},{8,9},{9,8},{10,11... | collective-permute-start | bytes 614408 | tf_op jit(solution)/shard_map/ppermute | solution.py:17
  42.0 6.9 %collective-permute-start.10 = (bf16[56,640]{1,0:T(8,128)(2,1)S(1)}, bf16[56,640]{1,0:T(8,128)(2,1)S(1)}, u32[]{:S(2)}, u32[]{:S(2)}) collective-permute-start(bf16[56,640]{1,0:T(8,128)(2,1)S(1)} %fusion.refs_0_), channel_id=1, source_target_pairs={{0,12},{4,8},{8,4},{12,0},{1,13},{5,9},{9,5},{13,1},{2,14},{6,10},... | collective-permute-start | bytes 215048 | tf_op jit(solution)/shard_map/ppermute | solution.py:17
  44.0 5.4 %collective-permute-start.8 = (bf16[56,640]{1,0:T(8,128)(2,1)S(1)}, bf16[56,640]{1,0:T(8,128)(2,1)S(1)}, u32[]{:S(2)}, u32[]{:S(2)}) collective-permute-start(bf16[56,640]{1,0:T(8,128)(2,1)S(1)} %fusion.refs_0_), channel_id=1, source_target_pairs={{0,4},{4,0},{8,12},{12,8},{1,5},{5,1},{9,13},{13,9},{2,6},{6,2},{1... | collective-permute-start | bytes 215048 | tf_op jit(solution)/shard_map/ppermute | solution.py:17
  44.5 6.8 %collective-permute-start.9 = (bf16[56,640]{1,0:T(8,128)(2,1)S(1)}, bf16[56,640]{1,0:T(8,128)(2,1)S(1)}, u32[]{:S(2)}, u32[]{:S(2)}) collective-permute-start(bf16[56,640]{1,0:T(8,128)(2,1)S(1)} %fusion.refs_0_), channel_id=1, source_target_pairs={{0,8},{4,12},{8,0},{12,4},{1,9},{5,13},{9,1},{13,5},{2,10},{6,14},... | collective-permute-start | bytes 215048 | tf_op jit(solution)/shard_map/ppermute | solution.py:17
  52.6 5.5 %collective-permute-start.21 = (bf16[224,320]{1,0:T(8,128)(2,1)S(1)}, bf16[224,320]{1,0:T(8,128)(2,1)S(1)}, u32[]{:S(2)}, u32[]{:S(2)}) collective-permute-start(bf16[224,320]{1,0:T(8,128)(2,1)S(1)} %get-tuple-element.74), channel_id=1, source_target_pairs={{0,2},{1,3},{2,0},{3,1},{4,6},{5,7},{6,4},{7,5},{8,10},{9,11},{10,... | collective-permute-start | bytes 430088 | tf_op jit(solution)/shard_map/ppermute | solution.py:17
  52.7 5.6 %collective-permute-start.22 = (bf16[224,320]{1,0:T(8,128)(2,1)S(1)}, bf16[224,320]{1,0:T(8,128)(2,1)S(1)}, u32[]{:S(2)}, u32[]{:S(2)}) collective-permute-start(bf16[224,320]{1,0:T(8,128)(2,1)S(1)} %get-tuple-element.73), channel_id=1, source_target_pairs={{0,1},{1,0},{2,3},{3,2},{4,5},{5,4},{6,7},{7,6},{8,9},{9,8},{10,11... | collective-permute-start | bytes 430088 | tf_op jit(solution)/shard_map/ppermute | solution.py:17
  58.1 1.4 %collective-permute-start.23 = (bf16[224,320]{1,0:T(8,128)(2,1)S(1)}, bf16[224,320]{1,0:T(8,128)(2,1)S(1)}, u32[]{:S(2)}, u32[]{:S(2)}) collective-permute-start(bf16[224,320]{1,0:T(8,128)(2,1)S(1)} %collective-permute-done.21), channel_id=1, source_target_pairs={{0,1},{1,0},{2,3},{3,2},{4,5},{5,4},{6,7},{7,6},{8,9},{9,8},{10,11... | collective-permute-start | bytes 430088 | tf_op jit(solution)/shard_map/ppermute | solution.py:17
  71.6 10.7 %collective-permute-start.31 = (bf16[224,768]{1,0:T(8,128)(2,1)S(1)}, bf16[224,768]{1,0:T(8,128)(2,1)S(1)}, u32[]{:S(2)}, u32[]{:S(2)}) collective-permute-start(bf16[224,768]{1,0:T(8,128)(2,1)S(1)} %get-tuple-element.90), channel_id=1, source_target_pairs={{0,2},{1,3},{2,0},{3,1},{4,6},{5,7},{6,4},{7,5},{8,10},{9,11},{10,... | collective-permute-start | bytes 1032200 | tf_op jit(solution)/shard_map/ppermute | solution.py:17
  71.7 12.7 %collective-permute-start.28 = (bf16[224,768]{1,0:T(8,128)(2,1)S(1)}, bf16[224,768]{1,0:T(8,128)(2,1)S(1)}, u32[]{:S(2)}, u32[]{:S(2)}) collective-permute-start(bf16[224,768]{1,0:T(8,128)(2,1)S(1)} %get-tuple-element.84), channel_id=1, source_target_pairs={{0,4},{4,0},{8,12},{12,8},{1,5},{5,1},{9,13},{13,9},{2,6},{6,2},{1... | collective-permute-start | bytes 1032200 | tf_op jit(solution)/shard_map/ppermute | solution.py:17
  75.0 18.5 %collective-permute-start.34 = (bf16[224,512]{1,0:T(8,128)(2,1)S(1)}, bf16[224,512]{1,0:T(8,128)(2,1)S(1)}, u32[]{:S(2)}, u32[]{:S(2)}) collective-permute-start(bf16[224,512]{1,0:T(8,128)(2,1)S(1)} %get-tuple-element.96), channel_id=1, source_target_pairs={{0,4},{4,0},{8,12},{12,8},{1,5},{5,1},{9,13},{13,9},{2,6},{6,2},{1... | collective-permute-start | bytes 688136 | tf_op jit(solution)/shard_map/ppermute | solution.py:17
  80.3 15.2 %collective-permute-start.25 = (bf16[224,512]{1,0:T(8,128)(2,1)S(1)}, bf16[224,512]{1,0:T(8,128)(2,1)S(1)}, u32[]{:S(2)}, u32[]{:S(2)}) collective-permute-start(bf16[224,512]{1,0:T(8,128)(2,1)S(1)} %get-tuple-element.78), channel_id=1, source_target_pairs={{0,2},{1,3},{2,0},{3,1},{4,6},{5,7},{6,4},{7,5},{8,10},{9,11},{10,... | collective-permute-start | bytes 688136 | tf_op jit(solution)/shard_map/ppermute | solution.py:17
  82.3 10.6 %collective-permute-start.17 = (bf16[56,640]{1,0:T(8,128)(2,1)S(1)}, bf16[56,640]{1,0:T(8,128)(2,1)S(1)}, u32[]{:S(2)}, u32[]{:S(2)}) collective-permute-start(bf16[56,640]{1,0:T(8,128)(2,1)S(1)} %get-tuple-element.70), channel_id=1, source_target_pairs={{0,4},{4,0},{8,12},{12,8},{1,5},{5,1},{9,13},{13,9},{2,6},{6,2},{1... | collective-permute-start | bytes 215048 | tf_op jit(solution)/shard_map/ppermute | solution.py:17
  82.4 23.1 %collective-permute-start.32 = (bf16[112,768]{1,0:T(8,128)(2,1)S(1)}, bf16[112,768]{1,0:T(8,128)(2,1)S(1)}, u32[]{:S(2)}, u32[]{:S(2)}) collective-permute-start(bf16[112,768]{1,0:T(8,128)(2,1)S(1)} %get-tuple-element.92), channel_id=1, source_target_pairs={{0,4},{4,0},{8,12},{12,8},{1,5},{5,1},{9,13},{13,9},{2,6},{6,2},{1... | collective-permute-start | bytes 516104 | tf_op jit(solution)/shard_map/ppermute | solution.py:17
  84.5 23.1 %collective-permute-start.29 = (bf16[112,768]{1,0:T(8,128)(2,1)S(1)}, bf16[112,768]{1,0:T(8,128)(2,1)S(1)}, u32[]{:S(2)}, u32[]{:S(2)}) collective-permute-start(bf16[112,768]{1,0:T(8,128)(2,1)S(1)} %get-tuple-element.86), channel_id=1, source_target_pairs={{0,8},{4,12},{8,0},{12,4},{1,9},{5,13},{9,1},{13,5},{2,10},{6,14},... | collective-permute-start | bytes 516104 | tf_op jit(solution)/shard_map/ppermute | solution.py:17
  92.9 10.6 %collective-permute-start.18 = (bf16[56,640]{1,0:T(8,128)(2,1)S(1)}, bf16[56,640]{1,0:T(8,128)(2,1)S(1)}, u32[]{:S(2)}, u32[]{:S(2)}) collective-permute-start(bf16[56,640]{1,0:T(8,128)(2,1)S(1)} %get-tuple-element.71), channel_id=1, source_target_pairs={{0,8},{4,12},{8,0},{12,4},{1,9},{5,13},{9,1},{13,5},{2,10},{6,14},... | collective-permute-start | bytes 215048 | tf_op jit(solution)/shard_map/ppermute | solution.py:17
  93.5 10.0 %collective-permute-start.19 = (bf16[56,640]{1,0:T(8,128)(2,1)S(1)}, bf16[56,640]{1,0:T(8,128)(2,1)S(1)}, u32[]{:S(2)}, u32[]{:S(2)}) collective-permute-start(bf16[56,640]{1,0:T(8,128)(2,1)S(1)} %get-tuple-element.72), channel_id=1, source_target_pairs={{0,12},{4,8},{8,4},{12,0},{1,13},{5,9},{9,5},{13,1},{2,14},{6,10},... | collective-permute-start | bytes 215048 | tf_op jit(solution)/shard_map/ppermute | solution.py:17
  95.5 13.9 %collective-permute-start.35 = (bf16[112,512]{1,0:T(8,128)(2,1)S(1)}, bf16[112,512]{1,0:T(8,128)(2,1)S(1)}, u32[]{:S(2)}, u32[]{:S(2)}) collective-permute-start(bf16[112,512]{1,0:T(8,128)(2,1)S(1)} %get-tuple-element.98), channel_id=1, source_target_pairs={{0,8},{4,12},{8,0},{12,4},{1,9},{5,13},{9,1},{13,5},{2,10},{6,14},... | collective-permute-start | bytes 344072 | tf_op jit(solution)/shard_map/ppermute | solution.py:17
  103.5 7.9 %collective-permute-start.26 = (bf16[112,512]{1,0:T(8,128)(2,1)S(1)}, bf16[112,512]{1,0:T(8,128)(2,1)S(1)}, u32[]{:S(2)}, u32[]{:S(2)}) collective-permute-start(bf16[112,512]{1,0:T(8,128)(2,1)S(1)} %get-tuple-element.80), channel_id=1, source_target_pairs={{0,4},{4,0},{8,12},{12,8},{1,5},{5,1},{9,13},{13,9},{2,6},{6,2},{1... | collective-permute-start | bytes 344072 | tf_op jit(solution)/shard_map/ppermute | solution.py:17
  104.1 15.7 %collective-permute-start.20 = (bf16[56,2560]{1,0:T(8,128)(2,1)S(1)}, bf16[56,2560]{1,0:T(8,128)(2,1)S(1)}, u32[]{:S(2)}, u32[]{:S(2)}) collective-permute-start(bf16[56,2560]{1,0:T(8,128)(2,1)S(1)} %spread.1.refs_4_.mine), channel_id=1, source_target_pairs={{16,0},{17,1},{18,2},{19,3},{20,4},{21,5},{22,6},{23,7},{24,8},{25... | collective-permute-start | bytes 860168 | tf_op jit(solution)/shard_map/ppermute | solution.py:578
  105.5 8.2 %collective-permute-start.33 = (bf16[56,768]{1,0:T(8,128)(2,1)S(1)}, bf16[56,768]{1,0:T(8,128)(2,1)S(1)}, u32[]{:S(2)}, u32[]{:S(2)}) collective-permute-start(bf16[56,768]{1,0:T(8,128)(2,1)S(1)} %get-tuple-element.94), channel_id=1, source_target_pairs={{0,8},{4,12},{8,0},{12,4},{1,9},{5,13},{9,1},{13,5},{2,10},{6,14},... | collective-permute-start | bytes 258056 | tf_op jit(solution)/shard_map/ppermute | solution.py:17
  107.7 10.7 %collective-permute-start.30 = (bf16[56,768]{1,0:T(8,128)(2,1)S(1)}, bf16[56,768]{1,0:T(8,128)(2,1)S(1)}, u32[]{:S(2)}, u32[]{:S(2)}) collective-permute-start(bf16[56,768]{1,0:T(8,128)(2,1)S(1)} %get-tuple-element.88), channel_id=1, source_target_pairs={{0,2},{1,3},{2,0},{3,1},{4,6},{5,7},{6,4},{7,5},{8,10},{9,11},{10,... | collective-permute-start | bytes 258056 | tf_op jit(solution)/shard_map/ppermute | solution.py:17
  109.4 4.2 %collective-permute-start.36 = (bf16[56,512]{1,0:T(8,128)(2,1)S(1)}, bf16[56,512]{1,0:T(8,128)(2,1)S(1)}, u32[]{:S(2)}, u32[]{:S(2)}) collective-permute-start(bf16[56,512]{1,0:T(8,128)(2,1)S(1)} %get-tuple-element.100), channel_id=1, source_target_pairs={{0,2},{1,3},{2,0},{3,1},{4,6},{5,7},{6,4},{7,5},{8,10},{9,11},{10,... | collective-permute-start | bytes 172040 | tf_op jit(solution)/shard_map/ppermute | solution.py:17
  111.4 6.9 %collective-permute-start.27 = (bf16[56,512]{1,0:T(8,128)(2,1)S(1)}, bf16[56,512]{1,0:T(8,128)(2,1)S(1)}, u32[]{:S(2)}, u32[]{:S(2)}) collective-permute-start(bf16[56,512]{1,0:T(8,128)(2,1)S(1)} %get-tuple-element.82), channel_id=1, source_target_pairs={{0,8},{4,12},{8,0},{12,4},{1,9},{5,13},{9,1},{13,5},{2,10},{6,14},... | collective-permute-start | bytes 172040 | tf_op jit(solution)/shard_map/ppermute | solution.py:17
  113.7 8.6 %collective-permute-start.38 = (bf16[56,1280]{1,0:T(8,128)(2,1)S(1)}, bf16[56,1280]{1,0:T(8,128)(2,1)S(1)}, u32[]{:S(2)}, u32[]{:S(2)}) collective-permute-start(bf16[56,1280]{1,0:T(8,128)(2,1)S(1)} %finish.3.refs_1_), channel_id=1, source_target_pairs={{0,16},{1,17},{2,18},{3,19},{4,20},{5,21},{6,22},{7,23},{8,24},{9,... | collective-permute-start | bytes 430088 | tf_op jit(solution)/shard_map/ppermute | solution.py:582
  118.4 5.6 %collective-permute-start.37 = (bf16[56,1280]{1,0:T(8,128)(2,1)S(1)}, bf16[56,1280]{1,0:T(8,128)(2,1)S(1)}, u32[]{:S(2)}, u32[]{:S(2)}) collective-permute-start(bf16[56,1280]{1,0:T(8,128)(2,1)S(1)} %finish.2.refs_0_), channel_id=1, source_target_pairs={{0,16},{1,17},{2,18},{3,19},{4,20},{5,21},{6,22},{7,23},{8,24},{9,... | collective-permute-start | bytes 430088 | tf_op jit(solution)/shard_map/ppermute | solution.py:582

commit v3 on v2

--- a/solution.py
+++ b/solution.py
@@ -25,7 +25,31 @@
     return pl.BlockSpec(memory_space=memory_space)
 
 
-def unfold_kernel(pairs, imgs, ocols, kd, ids, gains, shifts, *refs):
+def unfold_kernel(pairs, imgs, ocols, kd, rows, px, first, step, ids, gains, shifts, *refs):
+    w_own, w_other = refs[2 * pairs : 2 * pairs + 2]
+    a_own, a_other, sent, kept = refs[2 * pairs + 2 : 2 * pairs + 6]
+    held_own, held_other, sems = refs[2 * pairs + 9 :]
+    count = held_own.shape[1]
+    columns = pl.ds(first, count)
+    copies = [
+        pltpu.make_async_copy(w_own.at[:, columns], held_own, sems.at[0]),
+        pltpu.make_async_copy(w_other.at[:, columns], held_other, sems.at[1]),
+    ]
+    for copy in copies:
+        copy.start()
+    unfold_rows(pairs, imgs, ocols, kd, ids, gains, shifts, *refs[: 2 * pairs], *refs[2 * pairs + 2 : 2 * pairs + 4],
+                *refs[2 * pairs + 6 : 2 * pairs + 9])
+    for copy in copies:
+        copy.wait()
+    for at in range(0, count, step):
+        cut = slice(at, at + step)
+        value = jnp.dot(a_own[...], held_own[:, cut], preferred_element_type=F32)
+        value = value + jnp.dot(a_other[...], held_other[:, cut], preferred_element_type=F32)
+        copy_rows(sent.at[:, cut], value, rows[0], px)
+        copy_rows(kept.at[:, cut], value, rows[1], px)
+
+
+def unfold_rows(pairs, imgs, ocols, kd, ids, gains, shifts, *refs):
     own, other = refs[:pairs], refs[pairs : 2 * pairs]
     out_own, out_other, centre, border, strip = refs[2 * pairs :]
     y, core, group = ids[4], ids[5], ids[6]
@@ -73,28 +97,42 @@
                     out[row : row + 2 * px, tap * kd : (tap + 1) * kd] = jnp.concatenate(values).astype(BF16)
 
 
-def unfold(ids, gain, shift, own, other, ocols):
+def unfold(ids, gain, shift, own, other, ocols, w_own, w_other, first, count, step, split, block):
     pairs = len(own)
     imgs, px, kc = own[0].shape
     kd = kc // 2
     rows = pairs * imgs * px
     lanes = -(-kd // 128) * 128
+    deep = 9 * kd
     need = 8 * pairs * imgs * px * lanes + 256 * (pairs + 2) * imgs * lanes
     need += 36 * rows * kd + 8 * pairs * imgs * px * lanes
-    return pl.pallas_call(
-        functools.partial(unfold_kernel, pairs, imgs, ocols, kd),
-        out_shape=[pltpu.VMEM((rows, 9 * kd), BF16)] * 2,
-        in_specs=[whole(pltpu.SMEM)] + [whole()] * (2 + 2 * pairs),
-        out_specs=[whole()] * 2,
+    limit = (4 << 20) + 2 * need + 4 * deep * count + 8 * rows * count
+    sizes = [len(r) * block for r in split]
+    return pl.pallas_call(
+        functools.partial(unfold_kernel, pairs, imgs, ocols, kd, split, block, first, step),
+        out_shape=[pltpu.VMEM((rows, deep), BF16)] * 2
+        + [
+            jax.ShapeDtypeStruct((sizes[0], count), BF16),
+            jax.ShapeDtypeStruct((sizes[1], count), F32),
+        ],
+        in_specs=[whole(pltpu.SMEM)]
+        + [whole()] * (2 + 2 * pairs)
+        + [pl.BlockSpec(memory_space=pltpu.HBM)] * 2,
+        out_specs=[whole()] * 4,
         scratch_shapes=[
             pltpu.VMEM((pairs, imgs, 2, px, kd), F32),
             pltpu.VMEM((pairs + 2, imgs, 2, 2, ocols, kd), F32),
             pltpu.VMEM((2, 24 + px + 24, kd), F32),
+            pltpu.VMEM((deep, count), BF16),
+            pltpu.VMEM((deep, count), BF16),
+            pltpu.SemaphoreType.DMA((2,)),
         ],
         name="unfold",
-        compiler_params=pltpu.CompilerParams(vmem_limit_bytes=min(60 << 20, (2 << 20) + 2 * need)),
-        cost_estimate=pl.CostEstimate(flops=20 * rows * 9 * kd, bytes_accessed=8 * rows * 9 * kd, transcendentals=0),
-    )(ids, gain, shift, *own, *other)
+        compiler_params=pltpu.CompilerParams(vmem_limit_bytes=min(60 << 20, limit)),
+        cost_estimate=pl.CostEstimate(
+            flops=4 * rows * deep * count, bytes_accessed=4 * deep * count, transcendentals=0
+        ),
+    )(ids, gain, shift, *own, *other, w_own, w_other)
 
 
 def copy_rows(out, value, rows, px):
@@ -175,6 +213,24 @@
         compiler_params=pltpu.CompilerParams(vmem_limit_bytes=6 << 20),
         cost_estimate=pl.CostEstimate(flops=2 * px * wide, bytes_accessed=10 * px * wide, transcendentals=0),
     )(*flat, extra)
+
+
+def pool_kernel(total, mean, *refs):
+    value = total[...] + mean[...].reshape(total.shape)
+    for ref in refs[:-1]:
+        value = value + ref[...].astype(F32)
+    refs[-1][...] = value.astype(BF16)
+
+
+def pool(total, mean, came):
+    return pl.pallas_call(
+        pool_kernel,
+        out_shape=jax.ShapeDtypeStruct(total.shape, BF16),
+        in_specs=[whole()] * (2 + len(came)),
+        out_specs=whole(),
+        name="pool",
+        compiler_params=pltpu.CompilerParams(vmem_limit_bytes=4 << 20),
+    )(total, mean, *came)
 
 
 def join_kernel(*refs):
@@ -298,38 +354,39 @@
     )(ids, *backs)
 
 
-def final_kernel(parts, per, orows, ocols, ids, mine, far_mine, *refs):
-    own, far = refs[:parts], refs[parts : 2 * parts]
-    out, held = refs[2 * parts :]
+def final_kernel(per, orows, ocols, ids, mine, far_mine, own, far, *refs):
+    out, held = refs[-2:]
     first = ids[0] == 0
     for half in range(2):
-        at = 0
-        for i in range(parts):
-            count = own[i].shape[1]
-            for lane in range(0, count, 128):
-                here = slice(lane, lane + 128)
-                there = slice(at + lane, at + lane + 128)
-                a = mine[:, there] if half == 0 else far_mine[:, there]
-                b = far[i][:, here] if half == 0 else own[i][:, here]
-                held[...] = jnp.where(first, a.astype(F32), b.astype(F32))
-                for p in range(per):
-                    for c in range(ocols):
-                        some = held[pl.ds(p * orows * ocols + c, orows, stride=ocols), :]
-                        out[half * per + p, c, :, there] = some.astype(BF16)
-            at += count
-
-
-def final(ids, mine, far_mine, own, far, per, orows, ocols):
-    wide = mine.shape[1]
-    return pl.pallas_call(
-        functools.partial(final_kernel, len(own), per, orows, ocols),
+        for lane in range(0, own.shape[1], 128):
+            lanes = slice(lane, lane + 128)
+            a = mine if half == 0 else far_mine
+            b = far if half == 0 else own
+            held[...] = jnp.where(first, a[:, lanes].astype(F32), b[:, lanes].astype(F32))
+            for p in range(per):
+                for c in range(ocols):
+                    some = held[pl.ds(p * orows * ocols + c, orows, stride=ocols), :]
+                    out[half * per + p, c, :, lanes] = some.astype(BF16)
+
+
+def final(ids, mine, far_mine, own, far, so_far, first, step, per, orows, ocols):
+    px, wide = mine.shape
+    at = first // step
+    shared = pl.BlockSpec((px, step), lambda i: (0, at + i))
+    local = pl.BlockSpec((px, step), lambda i: (0, i))
+    more = [] if so_far is None else [so_far]
+    return pl.pallas_call(
+        functools.partial(final_kernel, per, orows, ocols),
+        grid=(own.shape[1] // step,),
         out_shape=jax.ShapeDtypeStruct((2 * per, ocols, orows, wide), BF16),
-        in_specs=[whole(pltpu.SMEM)] + [whole()] * (2 + 2 * len(own)),
-        out_specs=whole(),
-        scratch_shapes=[pltpu.VMEM((mine.shape[0], 128), F32)],
+        in_specs=[whole(pltpu.SMEM), shared, shared, local, local]
+        + [pl.BlockSpec(memory_space=pl.ANY)] * len(more),
+        out_specs=pl.BlockSpec((2 * per, ocols, orows, step), lambda i: (0, 0, 0, at + i)),
+        scratch_shapes=[pltpu.VMEM((px, 128), F32)],
+        input_output_aliases={5: 0} if more else {},
         name="final",
-        compiler_params=pltpu.CompilerParams(vmem_limit_bytes=10 << 20),
-    )(ids, mine, far_mine, *own, *far)
+        compiler_params=pltpu.CompilerParams(vmem_limit_bytes=6 << 20),
+    )(ids, mine, far_mine, own, far, *more)
 
 
 def pack_kernel(groups, per, c1, colp, ids, pixels, above, below, gain, shift, *refs):
@@ -523,9 +580,8 @@
     proj_twin = [swap(part, "ch", 1) for part in proj_own]
 
     total, *sent = stage(got, first_kernel.reshape(9, c1, depth), per, rows, cols, colp)
-    for k in range(1, groups):
-        total = total + swap(sent[k - 1], "img", k).astype(F32)
-    pooled = (total + mean.reshape(total.shape)).astype(BF16)
+    came = [swap(sent[k - 1], "img", k) for k in range(1, groups)]
+    pooled = pool(total, mean, came)
     pooled_all = [pooled] + [swap(pooled, "img", k) for k in range(1, groups)]
     px = per * orows * ocols
     imgs = groups * per
@@ -537,23 +593,15 @@
     twin = [swap(chip[0], "ch", 1)]
     twin += [swap(part, "ch", 1) for part in chip[1:]]
     back = [back[0]] + [swap(back[k], "img", k) for k in range(1, groups)]
-    a_own, a_other = unfold(
-        ids,
-        second_gain.reshape(groups * pairs, kc),
-        second_shift.reshape(groups * pairs, kc),
-        [c.reshape(imgs, out_px, kc) for c in chip],
-        [c.reshape(imgs, out_px, kc) for c in twin],
-        ocols,
-    )
     w_own = streamed(second_kernel.reshape(9 * kd, wide))
     w_other = streamed(other_kernel.reshape(9 * kd, wide))
 
     unit = wide // 10
-    plan = ((0, 2), (1, 3), (0, 3), (1, 2))
+    plan = ((0, 4), (1, 3), (0, 3))
     names = [("ch", 1 << i, 2) for i in range(pairs.bit_length() - 1)]
     names_z = [("img", 1 << i, 1) for i in range(groups.bit_length() - 1)]
     values, first = [], 0
-    for kind, n in plan:
+    for j, (kind, n) in enumerate(plan):
         hops = names_z + names if kind else names + names_z
         keys = [(a, b) for a in range(pairs) for b in range(groups)]
 
@@ -564,7 +612,24 @@
             return rows, [key for key, x in zip(keys, bit) if not x]
 
         rows, keys = split(keys, hops[0])
-        sent, kept = mix(a_own, a_other, w_own, w_other, first, n * unit, unit, rows, px)
+        if j == 0:
+            a_own, a_other, sent, kept = unfold(
+                ids,
+                second_gain.reshape(groups * pairs, kc),
+                second_shift.reshape(groups * pairs, kc),
+                [c.reshape(imgs, out_px, kc) for c in chip],
+                [c.reshape(imgs, out_px, kc) for c in twin],
+                ocols,
+                w_own,
+                w_other,
+                first,
+                n * unit,
+                unit,
+                rows,
+                px,
+            )
+        else:
+            sent, kept = mix(a_own, a_other, w_own, w_other, first, n * unit, unit, rows, px)
         for h, hop in enumerate(hops):
             axis, k, size = hop
             came = swap(sent, axis, k, size)
@@ -576,11 +641,12 @@
 
     mine_projected = spread(ids, back)
     far_projected = lax.ppermute(mine_projected, "section", [(1, 0)])
-    outs, fars = [], []
-    for j, some in enumerate((values[:2], values[2:])):
-        outs.append(finish([v[:2] for v in some], mine_projected, some[0][2]))
-        fars.append(lax.ppermute(outs[j], "section", [(0, 1)]))
-    block = final(ids, mine_projected, far_projected, outs, fars, per, orows, ocols)
+    block = None
+    for some in (values[:2], values[2:]):
+        at = some[0][2]
+        done = finish([v[:2] for v in some], mine_projected, at)
+        far = lax.ppermute(done, "section", [(0, 1)])
+        block = final(ids, mine_projected, far_projected, done, far, block, at, unit, per, orows, ocols)
     return block.transpose(0, 2, 1, 3)[None]
 
 

time: 126 us -> 122 us (0.968)
  starting transfers between devices: 53.3 us -> 49.9 us
  waiting for transfers between devices: 43.1 us -> 39.9 us
  Pallas kernels: 25.8 us -> 28.5 us
    pallas_call x2 -> x4, Pallas kernels: 4.87 us -> 14 us  [the longest x1 8.64 us: unfold(): pl.pallas_call(functools.partial(unfold_kernel, pairs, imgs, ocols, kd, s...]
    pallas_call x4 -> x2, Pallas kernels: 15.5 us -> 9.08 us  [mix(): pl.pallas_call(functools.partial(mix_kernel, rows, px), grid=(count // st...]
    ppermute x2, waiting for transfers between devices: 4.12 us -> 0.01 us  [body(): far = lax.ppermute(done, 'section', [(0, 1)])]
    ppermute x34 -> x31, starting transfers between devices: 42.6 us -> 40.8 us  [swap(): return lax.ppermute(array, axis, [(i, i ^ k * unit) for i in range(count)])]
    ppermute x2, starting transfers between devices: 6.03 us -> 4.71 us  [body(): far = lax.ppermute(done, 'section', [(0, 1)])]
    ppermute x34 -> x31, waiting for transfers between devices: 39 us -> 39.9 us  [swap(): return lax.ppermute(array, axis, [(i, i ^ k * unit) for i in range(count)])]
  transfers between devices with their start and end apart: 39 -> 36, of which waited for: 15 -> 19; matrix products, arithmetic and copies ran while one was open for 2% -> 2% of each run, Pallas kernels for 12% -> 15%
where the time goes in v3:
time: 122 us
  starting transfers between devices  49.9 us (41%)
  waiting for transfers between devices  39.9 us (33%)
  Pallas kernels  28.5 us (23%)
  local copies, waits for them, and re-layouts  3.13 us (3%)
    ppermute x31, starting transfers between devices, swap(): return lax.ppermute(array, axis, [(i, i ^ k * unit) for i in range(count)])  40.8 us
    ppermute x31, waiting for transfers between devices, swap(): return lax.ppermute(array, axis, [(i, i ^ k * unit) for i in range(count)])  39.9 us
    pallas_call x2, Pallas kernels, mix(): pl.pallas_call(functools.partial(mix_kernel, rows, px), grid=(count // st...  9.08 us
    pallas_call x1, Pallas kernels, unfold(): pl.pallas_call(functools.partial(unfold_kernel, pairs, imgs, ocols, kd, s...  8.64 us
    pallas_call x2, Pallas kernels, final(): pl.pallas_call(functools.partial(final_kernel, per, orows, ocols), grid=(...  5.27 us
    ppermute x2, starting transfers between devices, body(): far = lax.ppermute(done, 'section', [(0, 1)])  4.71 us
  transfers between devices with their start and end apart: 36, of which 19 were waited for; matrix products, arithmetic and copies ran while one was open for 2% of the time, Pallas kernels for 15%

profile of v3, /device:TPU:0, one launch (start us, length us, event | category | flops | bytes accessed | tf_op | source)
XLA Modules:
  0.0 121.7 jit_solution(1619139036874750637)
XLA Ops:
  0.6 1.1 copy-done.1
  2.4 2.7 %collective-permute-start.11 = (bf16[40,640]{1,0:T(8,128)(2,1)S(1)}, bf16[40,640]{1,0:T(8,128)(2,1)S(1)}, u32[]{:S(2)}, u32[]{:S(2)}) collective-permute-start(bf16[40,640]{1,0:T(8,128)(2,1)S(1)} %get-tuple-element.60), channel_id=1, source_target_pairs={{0,4},{4,0},{8,12},{12,8},{1,5},{5,1},{9,13},{13,9},{2,6},{6,2},{1... | collective-permute-start | bytes 153608 | tf_op jit(solution)/shard_map/ppermute | solution.py:17
  5.1 2.6 %collective-permute-start.12 = (bf16[40,640]{1,0:T(8,128)(2,1)S(1)}, bf16[40,640]{1,0:T(8,128)(2,1)S(1)}, u32[]{:S(2)}, u32[]{:S(2)}) collective-permute-start(bf16[40,640]{1,0:T(8,128)(2,1)S(1)} %get-tuple-element.61), channel_id=1, source_target_pairs={{0,8},{4,12},{8,0},{12,4},{1,9},{5,13},{9,1},{13,5},{2,10},{6,14},... | collective-permute-start | bytes 153608 | tf_op jit(solution)/shard_map/ppermute | solution.py:17
  7.7 1.5 %fusion = (bf16[2,1,28,640]{3,1,2,0:T(2,128)(2,1)S(1)}, bf16[2,1,28,640]{3,1,2,0:T(2,128)(2,1)S(1)}) fusion(bf16[2,8,28,640]{3,1,2,0:T(8,128)(2,1)} %param.8), kind=kLoop, calls=%fused_computation.2 | loop fusion | bytes 286720 | tf_op jit(solution)/shard_map/slice | solution.py:560
  9.3 1.8 %collective-permute-start = (bf16[1,1,28,640]{3,2,1,0:T(8,128)(2,1)S(1)}, bf16[1,1,28,640]{3,2,1,0:T(8,128)(2,1)S(1)}, u32[]{:S(2)}, u32[]{:S(2)}) collective-permute-start(bf16[1,1,28,640]{3,2,1,0:T(8,128)(2,1)S(1)} %copy.14), channel_id=1, source_target_pairs={{0,1},{1,2},{2,3},{4,5},{5,6},{6,7},{8,9},{9,10},{10,11},{12,13},{... | collective-permute-start | bytes 107528 | tf_op jit(solution)/shard_map/ppermute | solution.py:562
  11.2 1.3 %collective-permute-start.1 = (bf16[1,1,28,640]{3,2,1,0:T(8,128)(2,1)S(1)}, bf16[1,1,28,640]{3,2,1,0:T(8,128)(2,1)S(1)}, u32[]{:S(2)}, u32[]{:S(2)}) collective-permute-start(bf16[1,1,28,640]{3,2,1,0:T(8,128)(2,1)S(1)} %copy.16), channel_id=1, source_target_pairs={{1,0},{2,1},{3,2},{5,4},{6,5},{7,6},{9,8},{10,9},{11,10},{13,12},{... | collective-permute-start | bytes 107528 | tf_op jit(solution)/shard_map/ppermute | solution.py:563
  12.5 1.1 collective-permute-done.13.refs_3_
  13.6 3.2 %collective-permute-start.14 = (bf16[4,40,640]{2,1,0:T(8,128)(2,1)S(1)}, bf16[4,40,640]{2,1,0:T(8,128)(2,1)S(1)}, u32[]{:S(2)}, u32[]{:S(2)}) collective-permute-start(bf16[4,40,640]{2,1,0:T(8,128)(2,1)S(1)} %join.1.refs_4_), channel_id=1, source_target_pairs={{0,2},{1,3},{2,0},{3,1},{4,6},{5,7},{6,4},{7,5},{8,10},{9,11},{10,... | collective-permute-start | bytes 614408 | tf_op jit(solution)/shard_map/ppermute | solution.py:17
  16.9 0.9 pack.1
  18.6 3.5 %collective-permute-start.3 = (bf16[416,128]{1,0:T(8,128)(2,1)S(1)}, bf16[416,128]{1,0:T(8,128)(2,1)S(1)}, u32[]{:S(2)}, u32[]{:S(2)}) collective-permute-start(bf16[416,128]{1,0:T(8,128)(2,1)S(1)} %get-tuple-element.52), channel_id=1, source_target_pairs={{0,8},{4,12},{8,0},{12,4},{1,9},{5,13},{9,1},{13,5},{2,10},{6,14},... | collective-permute-start | bytes 319496 | tf_op jit(solution)/shard_map/ppermute | solution.py:17
  22.8 1.8 %collective-permute-start.15 = (bf16[4,40,640]{2,1,0:T(8,128)(2,1)S(1)}, bf16[4,40,640]{2,1,0:T(8,128)(2,1)S(1)}, u32[]{:S(2)}, u32[]{:S(2)}) collective-permute-start(bf16[4,40,640]{2,1,0:T(8,128)(2,1)S(1)} %join.1.refs_4_), channel_id=1, source_target_pairs={{0,1},{1,0},{2,3},{3,2},{4,5},{5,4},{6,7},{7,6},{8,9},{9,8},{10,11... | collective-permute-start | bytes 614408 | tf_op jit(solution)/shard_map/ppermute | solution.py:17
  24.6 1.7 %collective-permute-done.3.refs_2_ = bf16[416,128]{1,0:T(8,128)(2,1)S(1)} collective-permute-done((bf16[416,128]{1,0:T(8,128)(2,1)S(1)}, bf16[416,128]{1,0:T(8,128)(2,1)S(1)}, u32[]{:S(2)}, u32[]{:S(2)}) %collective-permute-start.3) | collective-permute-done | bytes 106528 | tf_op jit(solution)/shard_map/ppermute | solution.py:17
  26.3 3.4 %collective-permute-done.4.refs_3_ = bf16[416,128]{1,0:T(8,128)(2,1)S(1)} collective-permute-done((bf16[416,128]{1,0:T(8,128)(2,1)S(1)}, bf16[416,128]{1,0:T(8,128)(2,1)S(1)}, u32[]{:S(2)}, u32[]{:S(2)}) %collective-permute-start.4) | collective-permute-done | bytes 106528 | tf_op jit(solution)/shard_map/ppermute | solution.py:17
  29.7 1.5 %stage.1 = (f32[56,640]{1,0:T(8,128)S(1)}, bf16[56,640]{1,0:T(8,128)(2,1)S(1)}, bf16[56,640]{1,0:T(8,128)(2,1)S(1)}, bf16[56,640]{1,0:T(8,128)(2,1)S(1)}) custom-call(bf16[416,128]{1,0:T(8,128)(2,1)S(1)} %get-tuple-element.50.refs_0_, bf16[416,128]{1,0:T(8,128)(2,1)S(1)} %collective-permute-done.2.refs_1_, ...), custom_call_target="tpu_custom_call" | custom-call | flops 471859200 | bytes 573440 | tf_op jit(solution)/shard_map/stage/pallas_call | solution.py:517
  31.2 3.0 %collective-permute-start.5 = (bf16[56,640]{1,0:T(8,128)(2,1)S(1)}, bf16[56,640]{1,0:T(8,128)(2,1)S(1)}, u32[]{:S(2)}, u32[]{:S(2)}) collective-permute-start(bf16[56,640]{1,0:T(8,128)(2,1)S(1)} %get-tuple-element.56), channel_id=1, source_target_pairs={{0,4},{4,0},{8,12},{12,8},{1,5},{5,1},{9,13},{13,9},{2,6},{6,2},{1... | collective-permute-start | bytes 215048 | tf_op jit(solution)/shard_map/ppermute | solution.py:17
  34.5 1.4 %collective-permute-start.6 = (bf16[56,640]{1,0:T(8,128)(2,1)S(1)}, bf16[56,640]{1,0:T(8,128)(2,1)S(1)}, u32[]{:S(2)}, u32[]{:S(2)}) collective-permute-start(bf16[56,640]{1,0:T(8,128)(2,1)S(1)} %get-tuple-element.57), channel_id=1, source_target_pairs={{0,8},{4,12},{8,0},{12,4},{1,9},{5,13},{9,1},{13,5},{2,10},{6,14},... | collective-permute-start | bytes 215048 | tf_op jit(solution)/shard_map/ppermute | solution.py:17
  35.9 1.3 %collective-permute-done.5.refs_0_ = bf16[56,640]{1,0:T(8,128)(2,1)S(1)} collective-permute-done((bf16[56,640]{1,0:T(8,128)(2,1)S(1)}, bf16[56,640]{1,0:T(8,128)(2,1)S(1)}, u32[]{:S(2)}, u32[]{:S(2)}) %collective-permute-start.5) | collective-permute-done | bytes 71712 | tf_op jit(solution)/shard_map/ppermute | solution.py:17
  37.2 2.3 %collective-permute-start.7 = (bf16[56,640]{1,0:T(8,128)(2,1)S(1)}, bf16[56,640]{1,0:T(8,128)(2,1)S(1)}, u32[]{:S(2)}, u32[]{:S(2)}) collective-permute-start(bf16[56,640]{1,0:T(8,128)(2,1)S(1)} %get-tuple-element.58), channel_id=1, source_target_pairs={{0,12},{4,8},{8,4},{12,0},{1,13},{5,9},{9,5},{13,1},{2,14},{6,10},... | collective-permute-start | bytes 215048 | tf_op jit(solution)/shard_map/ppermute | solution.py:17
  39.5 2.2 %collective-permute-done.6.refs_1_ = bf16[56,640]{1,0:T(8,128)(2,1)S(1)} collective-permute-done((bf16[56,640]{1,0:T(8,128)(2,1)S(1)}, bf16[56,640]{1,0:T(8,128)(2,1)S(1)}, u32[]{:S(2)}, u32[]{:S(2)}) %collective-permute-start.6) | collective-permute-done | bytes 71712 | tf_op jit(solution)/shard_map/ppermute | solution.py:17
  41.6 1.7 %collective-permute-done.7.refs_2_ = bf16[56,640]{1,0:T(8,128)(2,1)S(1)} collective-permute-done((bf16[56,640]{1,0:T(8,128)(2,1)S(1)}, bf16[56,640]{1,0:T(8,128)(2,1)S(1)}, u32[]{:S(2)}, u32[]{:S(2)}) %collective-permute-start.7) | collective-permute-done | bytes 71712 | tf_op jit(solution)/shard_map/ppermute | solution.py:17
  43.4 2.4 %collective-permute-start.10 = (bf16[56,640]{1,0:T(8,128)(2,1)S(1)}, bf16[56,640]{1,0:T(8,128)(2,1)S(1)}, u32[]{:S(2)}, u32[]{:S(2)}) collective-permute-start(bf16[56,640]{1,0:T(8,128)(2,1)S(1)} %pool.1.refs_0_), channel_id=1, source_target_pairs={{0,12},{4,8},{8,4},{12,0},{1,13},{5,9},{9,5},{13,1},{2,14},{6,10},... | collective-permute-start | bytes 215048 | tf_op jit(solution)/shard_map/ppermute | solution.py:17
  46.5 1.3 %collective-permute-start.8 = (bf16[56,640]{1,0:T(8,128)(2,1)S(1)}, bf16[56,640]{1,0:T(8,128)(2,1)S(1)}, u32[]{:S(2)}, u32[]{:S(2)}) collective-permute-start(bf16[56,640]{1,0:T(8,128)(2,1)S(1)} %pool.1.refs_0_), channel_id=1, source_target_pairs={{0,4},{4,0},{8,12},{12,8},{1,5},{5,1},{9,13},{13,9},{2,6},{6,2},{1... | collective-permute-start | bytes 215048 | tf_op jit(solution)/shard_map/ppermute | solution.py:17
  47.8 2.6 %collective-permute-done.10.refs_3_ = bf16[56,640]{1,0:T(8,128)(2,1)S(1)} collective-permute-done((bf16[56,640]{1,0:T(8,128)(2,1)S(1)}, bf16[56,640]{1,0:T(8,128)(2,1)S(1)}, u32[]{:S(2)}, u32[]{:S(2)}) %collective-permute-start.10) | collective-permute-done | bytes 71712 | tf_op jit(solution)/shard_map/ppermute | solution.py:17
  50.4 2.5 %collective-permute-done.9.refs_2_ = bf16[56,640]{1,0:T(8,128)(2,1)S(1)} collective-permute-done((bf16[56,640]{1,0:T(8,128)(2,1)S(1)}, bf16[56,640]{1,0:T(8,128)(2,1)S(1)}, u32[]{:S(2)}, u32[]{:S(2)}) %collective-permute-start.9) | collective-permute-done | bytes 71712 | tf_op jit(solution)/shard_map/ppermute | solution.py:17
  52.9 1.2 %project.1 = (bf16[56,640]{1,0:T(8,128)(2,1)S(1)}, bf16[56,640]{1,0:T(8,128)(2,1)S(1)}, bf16[56,640]{1,0:T(8,128)(2,1)S(1)}, bf16[56,640]{1,0:T(8,128)(2,1)S(1)}...) custom-call(s32[7]{0:T(128)S(1)} %stack.27.ids, bf16[56,640]{1,0:T(8,128)(2,1)S(1)} %pool.1.refs_0_, ...), custom_call_target="tpu_custom_call" | custom-call | flops 183500800 | bytes 1638400 | tf_op jit(solution)/shard_map/project/pallas_call | solution.py:284
  54.3 5.7 %collective-permute-done.21 = bf16[224,320]{1,0:T(8,128)(2,1)S(1)} collective-permute-done((bf16[224,320]{1,0:T(8,128)(2,1)S(1)}, bf16[224,320]{1,0:T(8,128)(2,1)S(1)}, u32[]{:S(2)}, u32[]{:S(2)}) %collective-permute-start.21) | collective-permute-done | bytes 143392 | tf_op jit(solution)/shard_map/ppermute | solution.py:17
  60.2 1.2 %collective-permute-done.23 = bf16[224,320]{1,0:T(8,128)(2,1)S(1)} collective-permute-done((bf16[224,320]{1,0:T(8,128)(2,1)S(1)}, bf16[224,320]{1,0:T(8,128)(2,1)S(1)}, u32[]{:S(2)}, u32[]{:S(2)}) %collective-permute-start.23) | collective-permute-done | bytes 143392 | tf_op jit(solution)/shard_map/ppermute | solution.py:17
  61.4 8.6 %unfold.1 = (bf16[448,1440]{1,0:T(8,128)(2,1)S(1)}, bf16[448,1440]{1,0:T(8,128)(2,1)S(1)}, bf16[224,1024]{1,0:T(8,128)(2,1)S(1)}, f32[224,1024]{1,0:T(8,128)S(1)}) custom-call(s32[7]{0:T(128)S(1)} %stack.27.ids, f32[8,320]{1,0:T(8,128)S(1)} %reshape.36.gains, f32[8,320]{1,0:T(8,128)S(1)} %reshape.37.shifts, bf16[4,56,320]{2,1,0:T(8,128)(2,1)S(1)} %bitcast.17, ...), custom_call_target="tpu_custom_call" | custom-call | flops 2642411520 | bytes 5898240 | tf_op jit(solution)/shard_map/unfold/pallas_call | solution.py:111
  70.4 4.5 %mix.3 = (bf16[224,768]{1,0:T(8,128)(2,1)S(1)}, f32[224,768]{1,0:T(8,128)S(1)}) custom-call(bf16[448,1440]{1,0:T(8,128)(2,1)S(1)} %get-tuple-element.69.a_own, bf16[448,1440]{1,0:T(8,128)(2,1)S(1)} %get-tuple-element.70.a_other, bf16[1440,2560]{1,0:T(8,128)(2,1)} %bitcast.22, bf16[1440,2560]{1,0:T(8,128)(2,1)} %bitcast.12.refs_5_.w_other), custom_call_target="tpu_custom_call" | custom-call | flops 1981808640 | bytes 5455872 | tf_op jit(solution)/shard_map/mix/pallas_call | solution.py:154
  75.0 4.5 %mix.2 = (bf16[224,768]{1,0:T(8,128)(2,1)S(1)}, f32[224,768]{1,0:T(8,128)S(1)}) custom-call(bf16[448,1440]{1,0:T(8,128)(2,1)S(1)} %get-tuple-element.69.a_own, bf16[448,1440]{1,0:T(8,128)(2,1)S(1)} %get-tuple-element.70.a_other, bf16[1440,2560]{1,0:T(8,128)(2,1)} %bitcast.23, bf16[1440,2560]{1,0:T(8,128)(2,1)} %bitcast.12.refs_5_.w_other), custom_call_target="tpu_custom_call" | custom-call | flops 1981808640 | bytes 5455872 | tf_op jit(solution)/shard_map/mix/pallas_call | solution.py:154
  79.6 1.8 %collective-permute-start.25 = (bf16[224,768]{1,0:T(8,128)(2,1)S(1)}, bf16[224,768]{1,0:T(8,128)(2,1)S(1)}, u32[]{:S(2)}, u32[]{:S(2)}) collective-permute-start(bf16[224,768]{1,0:T(8,128)(2,1)S(1)} %get-tuple-element.72), channel_id=1, source_target_pairs={{0,2},{1,3},{2,0},{3,1},{4,6},{5,7},{6,4},{7,5},{8,10},{9,11},{10,... | collective-permute-start | bytes 1032200 | tf_op jit(solution)/shard_map/ppermute | solution.py:17
  81.4 1.9 %collective-permute-done.29.came = bf16[224,1024]{1,0:T(8,128)(2,1)S(1)} collective-permute-done((bf16[224,1024]{1,0:T(8,128)(2,1)S(1)}, bf16[224,1024]{1,0:T(8,128)(2,1)S(1)}, u32[]{:S(2)}, u32[]{:S(2)}) %collective-permute-start.29) | collective-permute-done | bytes 458784 | tf_op jit(solution)/shard_map/ppermute | solution.py:17
  83.5 1.5 %collective-permute-done.32.came = bf16[224,768]{1,0:T(8,128)(2,1)S(1)} collective-permute-done((bf16[224,768]{1,0:T(8,128)(2,1)S(1)}, bf16[224,768]{1,0:T(8,128)(2,1)S(1)}, u32[]{:S(2)}, u32[]{:S(2)}) %collective-permute-start.32) | collective-permute-done | bytes 344096 | tf_op jit(solution)/shard_map/ppermute | solution.py:17
  85.1 1.0 collective-permute-start.33
  86.1 1.6 %collective-permute-start.17 = (bf16[56,640]{1,0:T(8,128)(2,1)S(1)}, bf16[56,640]{1,0:T(8,128)(2,1)S(1)}, u32[]{:S(2)}, u32[]{:S(2)}) collective-permute-start(bf16[56,640]{1,0:T(8,128)(2,1)S(1)} %get-tuple-element.64), channel_id=1, source_target_pairs={{0,4},{4,0},{8,12},{12,8},{1,5},{5,1},{9,13},{13,9},{2,6},{6,2},{1... | collective-permute-start | bytes 215048 | tf_op jit(solution)/shard_map/ppermute | solution.py:17
  88.5 1.6 %collective-permute-done.25.came = bf16[224,768]{1,0:T(8,128)(2,1)S(1)} collective-permute-done((bf16[224,768]{1,0:T(8,128)(2,1)S(1)}, bf16[224,768]{1,0:T(8,128)(2,1)S(1)}, u32[]{:S(2)}, u32[]{:S(2)}) %collective-permute-start.25) | collective-permute-done | bytes 344096 | tf_op jit(solution)/shard_map/ppermute | solution.py:17
  90.1 2.0 %collective-permute-start.19 = (bf16[56,640]{1,0:T(8,128)(2,1)S(1)}, bf16[56,640]{1,0:T(8,128)(2,1)S(1)}, u32[]{:S(2)}, u32[]{:S(2)}) collective-permute-start(bf16[56,640]{1,0:T(8,128)(2,1)S(1)} %get-tuple-element.66), channel_id=1, source_target_pairs={{0,12},{4,8},{8,4},{12,0},{1,13},{5,9},{9,5},{13,1},{2,14},{6,10},... | collective-permute-start | bytes 215048 | tf_op jit(solution)/shard_map/ppermute | solution.py:17
  92.2 2.0 %collective-permute-done.30.came = bf16[112,1024]{1,0:T(8,128)(2,1)S(1)} collective-permute-done((bf16[112,1024]{1,0:T(8,128)(2,1)S(1)}, bf16[112,1024]{1,0:T(8,128)(2,1)S(1)}, u32[]{:S(2)}, u32[]{:S(2)}) %collective-permute-start.30) | collective-permute-done | bytes 229408 | tf_op jit(solution)/shard_map/ppermute | solution.py:17
  94.2 4.7 %collective-permute-done.33.came = bf16[112,768]{1,0:T(8,128)(2,1)S(1)} collective-permute-done((bf16[112,768]{1,0:T(8,128)(2,1)S(1)}, bf16[112,768]{1,0:T(8,128)(2,1)S(1)}, u32[]{:S(2)}, u32[]{:S(2)}) %collective-permute-start.33) | collective-permute-done | bytes 172064 | tf_op jit(solution)/shard_map/ppermute | solution.py:17
  98.9 3.3 %collective-permute-start.34 = (bf16[56,768]{1,0:T(8,128)(2,1)S(1)}, bf16[56,768]{1,0:T(8,128)(2,1)S(1)}, u32[]{:S(2)}, u32[]{:S(2)}) collective-permute-start(bf16[56,768]{1,0:T(8,128)(2,1)S(1)} %get-tuple-element.88), channel_id=1, source_target_pairs={{0,2},{1,3},{2,0},{3,1},{4,6},{5,7},{6,4},{7,5},{8,10},{9,11},{10,... | collective-permute-start | bytes 258056 | tf_op jit(solution)/shard_map/ppermute | solution.py:17
  102.8 1.3 %collective-permute-start.20 = (bf16[56,2560]{1,0:T(8,128)(2,1)S(1)}, bf16[56,2560]{1,0:T(8,128)(2,1)S(1)}, u32[]{:S(2)}, u32[]{:S(2)}) collective-permute-start(bf16[56,2560]{1,0:T(8,128)(2,1)S(1)} %spread.1.refs_2_.refs_4_.mine), channel_id=1, source_target_pairs={{16,0},{17,1},{18,2},{19,3},{20,4},{21,5},{22,6},{23,7},{24,8},{25... | collective-permute-start | bytes 860168 | tf_op jit(solution)/shard_map/ppermute | solution.py:643
  104.7 1.4 %collective-permute-done.31.refs_1_ = bf16[56,1024]{1,0:T(8,128)(2,1)S(1)} collective-permute-done((bf16[56,1024]{1,0:T(8,128)(2,1)S(1)}, bf16[56,1024]{1,0:T(8,128)(2,1)S(1)}, u32[]{:S(2)}, u32[]{:S(2)}) %collective-permute-start.31) | collective-permute-done | bytes 114720 | tf_op jit(solution)/shard_map/ppermute | solution.py:17
  106.1 3.4 %collective-permute-start.35 = (bf16[56,1792]{1,0:T(8,128)(2,1)S(1)}, bf16[56,1792]{1,0:T(8,128)(2,1)S(1)}, u32[]{:S(2)}, u32[]{:S(2)}) collective-permute-start(bf16[56,1792]{1,0:T(8,128)(2,1)S(1)} %finish.3.own), channel_id=1, source_target_pairs={{0,16},{1,17},{2,18},{3,19},{4,20},{5,21},{6,22},{7,23},{8,24},{9,... | collective-permute-start | bytes 602120 | tf_op jit(solution)/shard_map/ppermute | solution.py:648
  109.6 3.0 %collective-permute-start.27 = (bf16[56,768]{1,0:T(8,128)(2,1)S(1)}, bf16[56,768]{1,0:T(8,128)(2,1)S(1)}, u32[]{:S(2)}, u32[]{:S(2)}) collective-permute-start(bf16[56,768]{1,0:T(8,128)(2,1)S(1)} %get-tuple-element.76), channel_id=1, source_target_pairs={{0,8},{4,12},{8,0},{12,4},{1,9},{5,13},{9,1},{13,5},{2,10},{6,14},... | collective-permute-start | bytes 258056 | tf_op jit(solution)/shard_map/ppermute | solution.py:17
  112.6 2.5 %collective-permute-done.27.refs_1_ = bf16[56,768]{1,0:T(8,128)(2,1)S(1)} collective-permute-done((bf16[56,768]{1,0:T(8,128)(2,1)S(1)}, bf16[56,768]{1,0:T(8,128)(2,1)S(1)}, u32[]{:S(2)}, u32[]{:S(2)}) %collective-permute-start.27) | collective-permute-done | bytes 86048 | tf_op jit(solution)/shard_map/ppermute | solution.py:17
  115.1 1.3 %collective-permute-start.28 = (bf16[56,768]{1,0:T(8,128)(2,1)S(1)}, bf16[56,768]{1,0:T(8,128)(2,1)S(1)}, u32[]{:S(2)}, u32[]{:S(2)}) collective-permute-start(bf16[56,768]{1,0:T(8,128)(2,1)S(1)} %finish.2.own), channel_id=1, source_target_pairs={{0,16},{1,17},{2,18},{3,19},{4,20},{5,21},{6,22},{7,23},{8,24},{9,... | collective-permute-start | bytes 258056 | tf_op jit(solution)/shard_map/ppermute | solution.py:648
  116.4 3.3 %final.2.refs_0_ = bf16[2,14,4,2560]{3,2,1,0:T(4,128)(2,1)} custom-call(s32[7]{0:T(128)S(1)} %stack.27.ids, bf16[56,2560]{1,0:T(8,128)(2,1)S(1)} %spread.1.refs_2_.refs_4_.mine, bf16[56,2560]{1,0:T(8,128)(2,1)S(1)} %collective-permute-done.20.far_mine, bf16[56,1792]{1,0:T(8,128)(2,1)S(1)} %finish.3.own, bf16[56,1792]{1,0:T(8,128)(2,1)S(1)} %collective-permute-done.35.far), custom_call_target="tpu_custom_call" | custom-call | tf_op jit(solution)/shard_map/final/pallas_call | solution.py:378
  119.7 1.9 %final.3 = bf16[2,14,4,2560]{3,2,1,0:T(4,128)(2,1)} custom-call(s32[7]{0:T(128)S(1)} %stack.27.ids, bf16[56,2560]{1,0:T(8,128)(2,1)S(1)} %spread.1.refs_2_.refs_4_.mine, bf16[56,2560]{1,0:T(8,128)(2,1)S(1)} %collective-permute-done.20.far_mine, bf16[56,768]{1,0:T(8,128)(2,1)S(1)} %finish.2.own, ...), custom_call_target="tpu_custom_call", output_to_operand_aliasing={{}: (5, {})} | custom-call | tf_op jit(solution)/shard_map/final/pallas_call | solution.py:378
  (68 shorter events, 7.4 us)
Async XLA Ops:
  0.0 16.8 %copy-start.5 = (f32[640]{0:T(1024)S(1)}, f32[640]{0:T(1024)}, u32[]{:S(2)}) copy-start(f32[640]{0:T(1024)} %param.9) | copy-start | bytes 7684
  0.0 16.8 %copy-start.6 = (f32[640]{0:T(1024)S(1)}, f32[640]{0:T(1024)}, u32[]{:S(2)}) copy-start(f32[640]{0:T(1024)} %param.10) | copy-start | bytes 7684
  0.0 61.4 %collective-permute-start.24 = (bf16[3,3,160,2560]{3,2,1,0:T(8,128)(2,1)}, bf16[3,3,160,2560]{3,2,1,0:T(8,128)(2,1)}, u32[]{:S(2)}, u32[]{:S(2)}) collective-permute-start(bf16[3,3,160,2560]{3,2,1,0:T(8,128)(2,1)} %param.15), channel_id=1, source_target_pairs={{0,1},{1,0},{2,3},{3,2},{4,5},{5,4},{6,7},{7,6},{8,9},{9,8},{10,11... | collective-permute-start | bytes 22118408 | tf_op jit(solution)/shard_map/ppermute | solution.py:17
  0.6 1.1 copy-start.1
  1.7 15.1 %copy-start.2 = (bf16[2,8,28,640]{3,1,2,0:T(8,128)(2,1)S(1)}, bf16[2,8,28,640]{3,1,2,0:T(8,128)(2,1)}, u32[]{:S(2)}) copy-start(bf16[2,8,28,640]{3,1,2,0:T(8,128)(2,1)} %param.8) | copy-start | bytes 1720324
  2.4 27.3 %copy-start = (bf16[3,3,160,640]{3,2,1,0:T(8,128)(2,1)S(1)}, bf16[3,3,160,640]{3,2,1,0:T(8,128)(2,1)}, u32[]{:S(2)}) copy-start(bf16[3,3,160,640]{3,2,1,0:T(8,128)(2,1)} %param.11) | copy-start | bytes 5529604
  2.4 8.8 %collective-permute-start.11 = (bf16[40,640]{1,0:T(8,128)(2,1)S(1)}, bf16[40,640]{1,0:T(8,128)(2,1)S(1)}, u32[]{:S(2)}, u32[]{:S(2)}) collective-permute-start(bf16[40,640]{1,0:T(8,128)(2,1)S(1)} %get-tuple-element.60), channel_id=1, source_target_pairs={{0,4},{4,0},{8,12},{12,8},{1,5},{5,1},{9,13},{13,9},{2,6},{6,2},{1... | collective-permute-start | bytes 153608 | tf_op jit(solution)/shard_map/ppermute | solution.py:17
  5.1 7.4 %collective-permute-start.12 = (bf16[40,640]{1,0:T(8,128)(2,1)S(1)}, bf16[40,640]{1,0:T(8,128)(2,1)S(1)}, u32[]{:S(2)}, u32[]{:S(2)}) collective-permute-start(bf16[40,640]{1,0:T(8,128)(2,1)S(1)} %get-tuple-element.61), channel_id=1, source_target_pairs={{0,8},{4,12},{8,0},{12,4},{1,9},{5,13},{9,1},{13,5},{2,10},{6,14},... | collective-permute-start | bytes 153608 | tf_op jit(solution)/shard_map/ppermute | solution.py:17
  7.7 5.9 %collective-permute-start.13 = (bf16[40,640]{1,0:T(8,128)(2,1)S(1)}, bf16[40,640]{1,0:T(8,128)(2,1)S(1)}, u32[]{:S(2)}, u32[]{:S(2)}) collective-permute-start(bf16[40,640]{1,0:T(8,128)(2,1)S(1)} %get-tuple-element.62), channel_id=1, source_target_pairs={{0,12},{4,8},{8,4},{12,0},{1,13},{5,9},{9,5},{13,1},{2,14},{6,10},... | collective-permute-start | bytes 153608 | tf_op jit(solution)/shard_map/ppermute | solution.py:17
  9.3 7.6 %collective-permute-start = (bf16[1,1,28,640]{3,2,1,0:T(8,128)(2,1)S(1)}, bf16[1,1,28,640]{3,2,1,0:T(8,128)(2,1)S(1)}, u32[]{:S(2)}, u32[]{:S(2)}) collective-permute-start(bf16[1,1,28,640]{3,2,1,0:T(8,128)(2,1)S(1)} %copy.14), channel_id=1, source_target_pairs={{0,1},{1,2},{2,3},{4,5},{5,6},{6,7},{8,9},{9,10},{10,11},{12,13},{... | collective-permute-start | bytes 107528 | tf_op jit(solution)/shard_map/ppermute | solution.py:562
  11.2 5.7 %collective-permute-start.1 = (bf16[1,1,28,640]{3,2,1,0:T(8,128)(2,1)S(1)}, bf16[1,1,28,640]{3,2,1,0:T(8,128)(2,1)S(1)}, u32[]{:S(2)}, u32[]{:S(2)}) collective-permute-start(bf16[1,1,28,640]{3,2,1,0:T(8,128)(2,1)S(1)} %copy.16), channel_id=1, source_target_pairs={{1,0},{2,1},{3,2},{5,4},{6,5},{7,6},{9,8},{10,9},{11,10},{13,12},{... | collective-permute-start | bytes 107528 | tf_op jit(solution)/shard_map/ppermute | solution.py:563
  13.6 20.6 %collective-permute-start.14 = (bf16[4,40,640]{2,1,0:T(8,128)(2,1)S(1)}, bf16[4,40,640]{2,1,0:T(8,128)(2,1)S(1)}, u32[]{:S(2)}, u32[]{:S(2)}) collective-permute-start(bf16[4,40,640]{2,1,0:T(8,128)(2,1)S(1)} %join.1.refs_4_), channel_id=1, source_target_pairs={{0,2},{1,3},{2,0},{3,1},{4,6},{5,7},{6,4},{7,5},{8,10},{9,11},{10,... | collective-permute-start | bytes 614408 | tf_op jit(solution)/shard_map/ppermute | solution.py:17
  17.9 4.9 %collective-permute-start.2 = (bf16[416,128]{1,0:T(8,128)(2,1)S(1)}, bf16[416,128]{1,0:T(8,128)(2,1)S(1)}, u32[]{:S(2)}, u32[]{:S(2)}) collective-permute-start(bf16[416,128]{1,0:T(8,128)(2,1)S(1)} %get-tuple-element.51), channel_id=1, source_target_pairs={{0,4},{4,0},{8,12},{12,8},{1,5},{5,1},{9,13},{13,9},{2,6},{6,2},{1... | collective-permute-start | bytes 319496 | tf_op jit(solution)/shard_map/ppermute | solution.py:17
  18.6 7.7 %collective-permute-start.3 = (bf16[416,128]{1,0:T(8,128)(2,1)S(1)}, bf16[416,128]{1,0:T(8,128)(2,1)S(1)}, u32[]{:S(2)}, u32[]{:S(2)}) collective-permute-start(bf16[416,128]{1,0:T(8,128)(2,1)S(1)} %get-tuple-element.52), channel_id=1, source_target_pairs={{0,8},{4,12},{8,0},{12,4},{1,9},{5,13},{9,1},{13,5},{2,10},{6,14},... | collective-permute-start | bytes 319496 | tf_op jit(solution)/shard_map/ppermute | solution.py:17
  22.1 7.6 %collective-permute-start.4 = (bf16[416,128]{1,0:T(8,128)(2,1)S(1)}, bf16[416,128]{1,0:T(8,128)(2,1)S(1)}, u32[]{:S(2)}, u32[]{:S(2)}) collective-permute-start(bf16[416,128]{1,0:T(8,128)(2,1)S(1)} %get-tuple-element.53), channel_id=1, source_target_pairs={{0,12},{4,8},{8,4},{12,0},{1,13},{5,9},{9,5},{13,1},{2,14},{6,10},... | collective-permute-start | bytes 319496 | tf_op jit(solution)/shard_map/ppermute | solution.py:17
  22.8 23.7 %collective-permute-start.15 = (bf16[4,40,640]{2,1,0:T(8,128)(2,1)S(1)}, bf16[4,40,640]{2,1,0:T(8,128)(2,1)S(1)}, u32[]{:S(2)}, u32[]{:S(2)}) collective-permute-start(bf16[4,40,640]{2,1,0:T(8,128)(2,1)S(1)} %join.1.refs_4_), channel_id=1, source_target_pairs={{0,1},{1,0},{2,3},{3,2},{4,5},{5,4},{6,7},{7,6},{8,9},{9,8},{10,11... | collective-permute-start | bytes 614408 | tf_op jit(solution)/shard_map/ppermute | solution.py:17
  29.7 30.3 %copy-start.3 = (f32[2560]{0:T(1024)S(1)}, f32[2560]{0:T(1024)}, u32[]{:S(2)}) copy-start(f32[2560]{0:T(1024)} %param.13) | copy-start | bytes 30724
  29.7 30.4 %copy-start.4 = (f32[2560]{0:T(1024)S(1)}, f32[2560]{0:T(1024)}, u32[]{:S(2)}) copy-start(f32[2560]{0:T(1024)} %param.14) | copy-start | bytes 30724
  31.2 5.9 %collective-permute-start.5 = (bf16[56,640]{1,0:T(8,128)(2,1)S(1)}, bf16[56,640]{1,0:T(8,128)(2,1)S(1)}, u32[]{:S(2)}, u32[]{:S(2)}) collective-permute-start(bf16[56,640]{1,0:T(8,128)(2,1)S(1)} %get-tuple-element.56), channel_id=1, source_target_pairs={{0,4},{4,0},{8,12},{12,8},{1,5},{5,1},{9,13},{13,9},{2,6},{6,2},{1... | collective-permute-start | bytes 215048 | tf_op jit(solution)/shard_map/ppermute | solution.py:17
  34.2 18.6 %collective-permute-start.16 = (bf16[4,40,640]{2,1,0:T(8,128)(2,1)S(1)}, bf16[4,40,640]{2,1,0:T(8,128)(2,1)S(1)}, u32[]{:S(2)}, u32[]{:S(2)}) collective-permute-start(bf16[4,40,640]{2,1,0:T(8,128)(2,1)S(1)} %collective-permute-done.14.refs_5_), channel_id=1, source_target_pairs={{0,1},{1,0},{2,3},{3,2},{4,5},{5,4},{6,7},{7,6},{8,9},{9,8},{10,11... | collective-permute-start | bytes 614408 | tf_op jit(solution)/shard_map/ppermute | solution.py:17
  34.5 7.1 %collective-permute-start.6 = (bf16[56,640]{1,0:T(8,128)(2,1)S(1)}, bf16[56,640]{1,0:T(8,128)(2,1)S(1)}, u32[]{:S(2)}, u32[]{:S(2)}) collective-permute-start(bf16[56,640]{1,0:T(8,128)(2,1)S(1)} %get-tuple-element.57), channel_id=1, source_target_pairs={{0,8},{4,12},{8,0},{12,4},{1,9},{5,13},{9,1},{13,5},{2,10},{6,14},... | collective-permute-start | bytes 215048 | tf_op jit(solution)/shard_map/ppermute | solution.py:17
  37.2 6.1 %collective-permute-start.7 = (bf16[56,640]{1,0:T(8,128)(2,1)S(1)}, bf16[56,640]{1,0:T(8,128)(2,1)S(1)}, u32[]{:S(2)}, u32[]{:S(2)}) collective-permute-start(bf16[56,640]{1,0:T(8,128)(2,1)S(1)} %get-tuple-element.58), channel_id=1, source_target_pairs={{0,12},{4,8},{8,4},{12,0},{1,13},{5,9},{9,5},{13,1},{2,14},{6,10},... | collective-permute-start | bytes 215048 | tf_op jit(solution)/shard_map/ppermute | solution.py:17
  43.4 7.0 %collective-permute-start.10 = (bf16[56,640]{1,0:T(8,128)(2,1)S(1)}, bf16[56,640]{1,0:T(8,128)(2,1)S(1)}, u32[]{:S(2)}, u32[]{:S(2)}) collective-permute-start(bf16[56,640]{1,0:T(8,128)(2,1)S(1)} %pool.1.refs_0_), channel_id=1, source_target_pairs={{0,12},{4,8},{8,4},{12,0},{1,13},{5,9},{9,5},{13,1},{2,14},{6,10},... | collective-permute-start | bytes 215048 | tf_op jit(solution)/shard_map/ppermute | solution.py:17
  45.7 7.1 %collective-permute-start.9 = (bf16[56,640]{1,0:T(8,128)(2,1)S(1)}, bf16[56,640]{1,0:T(8,128)(2,1)S(1)}, u32[]{:S(2)}, u32[]{:S(2)}) collective-permute-start(bf16[56,640]{1,0:T(8,128)(2,1)S(1)} %pool.1.refs_0_), channel_id=1, source_target_pairs={{0,8},{4,12},{8,0},{12,4},{1,9},{5,13},{9,1},{13,5},{2,10},{6,14},... | collective-permute-start | bytes 215048 | tf_op jit(solution)/shard_map/ppermute | solution.py:17
  46.5 6.3 %collective-permute-start.8 = (bf16[56,640]{1,0:T(8,128)(2,1)S(1)}, bf16[56,640]{1,0:T(8,128)(2,1)S(1)}, u32[]{:S(2)}, u32[]{:S(2)}) collective-permute-start(bf16[56,640]{1,0:T(8,128)(2,1)S(1)} %pool.1.refs_0_), channel_id=1, source_target_pairs={{0,4},{4,0},{8,12},{12,8},{1,5},{5,1},{9,13},{13,9},{2,6},{6,2},{1... | collective-permute-start | bytes 215048 | tf_op jit(solution)/shard_map/ppermute | solution.py:17
  54.1 5.9 %collective-permute-start.21 = (bf16[224,320]{1,0:T(8,128)(2,1)S(1)}, bf16[224,320]{1,0:T(8,128)(2,1)S(1)}, u32[]{:S(2)}, u32[]{:S(2)}) collective-permute-start(bf16[224,320]{1,0:T(8,128)(2,1)S(1)} %get-tuple-element.68), channel_id=1, source_target_pairs={{0,2},{1,3},{2,0},{3,1},{4,6},{5,7},{6,4},{7,5},{8,10},{9,11},{10,... | collective-permute-start | bytes 430088 | tf_op jit(solution)/shard_map/ppermute | solution.py:17
  54.2 6.0 %collective-permute-start.22 = (bf16[224,320]{1,0:T(8,128)(2,1)S(1)}, bf16[224,320]{1,0:T(8,128)(2,1)S(1)}, u32[]{:S(2)}, u32[]{:S(2)}) collective-permute-start(bf16[224,320]{1,0:T(8,128)(2,1)S(1)} %get-tuple-element.67), channel_id=1, source_target_pairs={{0,1},{1,0},{2,3},{3,2},{4,5},{5,4},{6,7},{7,6},{8,9},{9,8},{10,11... | collective-permute-start | bytes 430088 | tf_op jit(solution)/shard_map/ppermute | solution.py:17
  60.0 1.4 %collective-permute-start.23 = (bf16[224,320]{1,0:T(8,128)(2,1)S(1)}, bf16[224,320]{1,0:T(8,128)(2,1)S(1)}, u32[]{:S(2)}, u32[]{:S(2)}) collective-permute-start(bf16[224,320]{1,0:T(8,128)(2,1)S(1)} %collective-permute-done.21), channel_id=1, source_target_pairs={{0,1},{1,0},{2,3},{3,2},{4,5},{5,4},{6,7},{7,6},{8,9},{9,8},{10,11... | collective-permute-start | bytes 430088 | tf_op jit(solution)/shard_map/ppermute | solution.py:17
  70.1 13.2 %collective-permute-start.29 = (bf16[224,1024]{1,0:T(8,128)(2,1)S(1)}, bf16[224,1024]{1,0:T(8,128)(2,1)S(1)}, u32[]{:S(2)}, u32[]{:S(2)}) collective-permute-start(bf16[224,1024]{1,0:T(8,128)(2,1)S(1)} %get-tuple-element.78), channel_id=1, source_target_pairs={{0,2},{1,3},{2,0},{3,1},{4,6},{5,7},{6,4},{7,5},{8,10},{9,11},{10,... | collective-permute-start | bytes 1376264 | tf_op jit(solution)/shard_map/ppermute | solution.py:17
  75.0 10.1 %collective-permute-start.32 = (bf16[224,768]{1,0:T(8,128)(2,1)S(1)}, bf16[224,768]{1,0:T(8,128)(2,1)S(1)}, u32[]{:S(2)}, u32[]{:S(2)}) collective-permute-start(bf16[224,768]{1,0:T(8,128)(2,1)S(1)} %get-tuple-element.84), channel_id=1, source_target_pairs={{0,4},{4,0},{8,12},{12,8},{1,5},{5,1},{9,13},{13,9},{2,6},{6,2},{1... | collective-permute-start | bytes 1032200 | tf_op jit(solution)/shard_map/ppermute | solution.py:17
  79.6 10.5 %collective-permute-start.25 = (bf16[224,768]{1,0:T(8,128)(2,1)S(1)}, bf16[224,768]{1,0:T(8,128)(2,1)S(1)}, u32[]{:S(2)}, u32[]{:S(2)}) collective-permute-start(bf16[224,768]{1,0:T(8,128)(2,1)S(1)} %get-tuple-element.72), channel_id=1, source_target_pairs={{0,2},{1,3},{2,0},{3,1},{4,6},{5,7},{6,4},{7,5},{8,10},{9,11},{10,... | collective-permute-start | bytes 1032200 | tf_op jit(solution)/shard_map/ppermute | solution.py:17
  83.3 10.8 %collective-permute-start.30 = (bf16[112,1024]{1,0:T(8,128)(2,1)S(1)}, bf16[112,1024]{1,0:T(8,128)(2,1)S(1)}, u32[]{:S(2)}, u32[]{:S(2)}) collective-permute-start(bf16[112,1024]{1,0:T(8,128)(2,1)S(1)} %get-tuple-element.80), channel_id=1, source_target_pairs={{0,4},{4,0},{8,12},{12,8},{1,5},{5,1},{9,13},{13,9},{2,6},{6,2},{1... | collective-permute-start | bytes 688136 | tf_op jit(solution)/shard_map/ppermute | solution.py:17
  85.1 13.8 %collective-permute-start.33 = (bf16[112,768]{1,0:T(8,128)(2,1)S(1)}, bf16[112,768]{1,0:T(8,128)(2,1)S(1)}, u32[]{:S(2)}, u32[]{:S(2)}) collective-permute-start(bf16[112,768]{1,0:T(8,128)(2,1)S(1)} %get-tuple-element.86), channel_id=1, source_target_pairs={{0,8},{4,12},{8,0},{12,4},{1,9},{5,13},{9,1},{13,5},{2,10},{6,14},... | collective-permute-start | bytes 516104 | tf_op jit(solution)/shard_map/ppermute | solution.py:17
  86.1 12.8 %collective-permute-start.17 = (bf16[56,640]{1,0:T(8,128)(2,1)S(1)}, bf16[56,640]{1,0:T(8,128)(2,1)S(1)}, u32[]{:S(2)}, u32[]{:S(2)}) collective-permute-start(bf16[56,640]{1,0:T(8,128)(2,1)S(1)} %get-tuple-element.64), channel_id=1, source_target_pairs={{0,4},{4,0},{8,12},{12,8},{1,5},{5,1},{9,13},{13,9},{2,6},{6,2},{1... | collective-permute-start | bytes 215048 | tf_op jit(solution)/shard_map/ppermute | solution.py:17
  87.7 14.4 %collective-permute-start.18 = (bf16[56,640]{1,0:T(8,128)(2,1)S(1)}, bf16[56,640]{1,0:T(8,128)(2,1)S(1)}, u32[]{:S(2)}, u32[]{:S(2)}) collective-permute-start(bf16[56,640]{1,0:T(8,128)(2,1)S(1)} %get-tuple-element.65), channel_id=1, source_target_pairs={{0,8},{4,12},{8,0},{12,4},{1,9},{5,13},{9,1},{13,5},{2,10},{6,14},... | collective-permute-start | bytes 215048 | tf_op jit(solution)/shard_map/ppermute | solution.py:17
  90.1 12.1 %collective-permute-start.19 = (bf16[56,640]{1,0:T(8,128)(2,1)S(1)}, bf16[56,640]{1,0:T(8,128)(2,1)S(1)}, u32[]{:S(2)}, u32[]{:S(2)}) collective-permute-start(bf16[56,640]{1,0:T(8,128)(2,1)S(1)} %get-tuple-element.66), channel_id=1, source_target_pairs={{0,12},{4,8},{8,4},{12,0},{1,13},{5,9},{9,5},{13,1},{2,14},{6,10},... | collective-permute-start | bytes 215048 | tf_op jit(solution)/shard_map/ppermute | solution.py:17
  94.1 15.4 %collective-permute-start.26 = (bf16[112,768]{1,0:T(8,128)(2,1)S(1)}, bf16[112,768]{1,0:T(8,128)(2,1)S(1)}, u32[]{:S(2)}, u32[]{:S(2)}) collective-permute-start(bf16[112,768]{1,0:T(8,128)(2,1)S(1)} %get-tuple-element.74), channel_id=1, source_target_pairs={{0,4},{4,0},{8,12},{12,8},{1,5},{5,1},{9,13},{13,9},{2,6},{6,2},{1... | collective-permute-start | bytes 516104 | tf_op jit(solution)/shard_map/ppermute | solution.py:17
  98.9 7.1 %collective-permute-start.31 = (bf16[56,1024]{1,0:T(8,128)(2,1)S(1)}, bf16[56,1024]{1,0:T(8,128)(2,1)S(1)}, u32[]{:S(2)}, u32[]{:S(2)}) collective-permute-start(bf16[56,1024]{1,0:T(8,128)(2,1)S(1)} %get-tuple-element.82), channel_id=1, source_target_pairs={{0,8},{4,12},{8,0},{12,4},{1,9},{5,13},{9,1},{13,5},{2,10},{6,14},... | collective-permute-start | bytes 344072 | tf_op jit(solution)/shard_map/ppermute | solution.py:17
  98.9 5.7 %collective-permute-start.34 = (bf16[56,768]{1,0:T(8,128)(2,1)S(1)}, bf16[56,768]{1,0:T(8,128)(2,1)S(1)}, u32[]{:S(2)}, u32[]{:S(2)}) collective-permute-start(bf16[56,768]{1,0:T(8,128)(2,1)S(1)} %get-tuple-element.88), channel_id=1, source_target_pairs={{0,2},{1,3},{2,0},{3,1},{4,6},{5,7},{6,4},{7,5},{8,10},{9,11},{10,... | collective-permute-start | bytes 258056 | tf_op jit(solution)/shard_map/ppermute | solution.py:17
  102.8 13.6 %collective-permute-start.20 = (bf16[56,2560]{1,0:T(8,128)(2,1)S(1)}, bf16[56,2560]{1,0:T(8,128)(2,1)S(1)}, u32[]{:S(2)}, u32[]{:S(2)}) collective-permute-start(bf16[56,2560]{1,0:T(8,128)(2,1)S(1)} %spread.1.refs_2_.refs_4_.mine), channel_id=1, source_target_pairs={{16,0},{17,1},{18,2},{19,3},{20,4},{21,5},{22,6},{23,7},{24,8},{25... | collective-permute-start | bytes 860168 | tf_op jit(solution)/shard_map/ppermute | solution.py:643
  106.1 10.3 %collective-permute-start.35 = (bf16[56,1792]{1,0:T(8,128)(2,1)S(1)}, bf16[56,1792]{1,0:T(8,128)(2,1)S(1)}, u32[]{:S(2)}, u32[]{:S(2)}) collective-permute-start(bf16[56,1792]{1,0:T(8,128)(2,1)S(1)} %finish.3.own), channel_id=1, source_target_pairs={{0,16},{1,17},{2,18},{3,19},{4,20},{5,21},{6,22},{7,23},{8,24},{9,... | collective-permute-start | bytes 602120 | tf_op jit(solution)/shard_map/ppermute | solution.py:648
  109.6 5.5 %collective-permute-start.27 = (bf16[56,768]{1,0:T(8,128)(2,1)S(1)}, bf16[56,768]{1,0:T(8,128)(2,1)S(1)}, u32[]{:S(2)}, u32[]{:S(2)}) collective-permute-start(bf16[56,768]{1,0:T(8,128)(2,1)S(1)} %get-tuple-element.76), channel_id=1, source_target_pairs={{0,8},{4,12},{8,0},{12,4},{1,9},{5,13},{9,1},{13,5},{2,10},{6,14},... | collective-permute-start | bytes 258056 | tf_op jit(solution)/shard_map/ppermute | solution.py:17
  115.1 4.7 %collective-permute-start.28 = (bf16[56,768]{1,0:T(8,128)(2,1)S(1)}, bf16[56,768]{1,0:T(8,128)(2,1)S(1)}, u32[]{:S(2)}, u32[]{:S(2)}) collective-permute-start(bf16[56,768]{1,0:T(8,128)(2,1)S(1)} %finish.2.own), channel_id=1, source_target_pairs={{0,16},{1,17},{2,18},{3,19},{4,20},{5,21},{6,22},{7,23},{8,24},{9,... | collective-permute-start | bytes 258056 | tf_op jit(solution)/shard_map/ppermute | solution.py:648

commit v4 on v3

--- a/solution.py
+++ b/solution.py
@@ -30,19 +30,23 @@
     a_own, a_other, sent, kept = refs[2 * pairs + 2 : 2 * pairs + 6]
     held_own, held_other, sems = refs[2 * pairs + 9 :]
     count = held_own.shape[1]
-    columns = pl.ds(first, count)
-    copies = [
-        pltpu.make_async_copy(w_own.at[:, columns], held_own, sems.at[0]),
-        pltpu.make_async_copy(w_other.at[:, columns], held_other, sems.at[1]),
-    ]
-    for copy in copies:
-        copy.start()
+    copies = []
+    for i in range(count // step):
+        here, there = pl.ds(i * step, step), pl.ds(first + i * step, step)
+        copies.append(
+            [
+                pltpu.make_async_copy(w_own.at[:, there], held_own.at[:, here], sems.at[2 * i]),
+                pltpu.make_async_copy(w_other.at[:, there], held_other.at[:, here], sems.at[2 * i + 1]),
+            ]
+        )
+        for copy in copies[i]:
+            copy.start()
     unfold_rows(pairs, imgs, ocols, kd, ids, gains, shifts, *refs[: 2 * pairs], *refs[2 * pairs + 2 : 2 * pairs + 4],
                 *refs[2 * pairs + 6 : 2 * pairs + 9])
-    for copy in copies:
-        copy.wait()
     for at in range(0, count, step):
         cut = slice(at, at + step)
+        for copy in copies[at // step]:
+            copy.wait()
         value = jnp.dot(a_own[...], held_own[:, cut], preferred_element_type=F32)
         value = value + jnp.dot(a_other[...], held_other[:, cut], preferred_element_type=F32)
         copy_rows(sent.at[:, cut], value, rows[0], px)
@@ -125,7 +129,7 @@
             pltpu.VMEM((2, 24 + px + 24, kd), F32),
             pltpu.VMEM((deep, count), BF16),
             pltpu.VMEM((deep, count), BF16),
-            pltpu.SemaphoreType.DMA((2,)),
+            pltpu.SemaphoreType.DMA((2 * (count // step),)),
         ],
         name="unfold",
         compiler_params=pltpu.CompilerParams(vmem_limit_bytes=min(60 << 20, limit)),
@@ -354,39 +358,38 @@
     )(ids, *backs)
 
 
-def final_kernel(per, orows, ocols, ids, mine, far_mine, own, far, *refs):
-    out, held = refs[-2:]
+def final_kernel(parts, per, orows, ocols, ids, mine, far_mine, *refs):
+    own, far = refs[:parts], refs[parts : 2 * parts]
+    out, held = refs[2 * parts :]
     first = ids[0] == 0
     for half in range(2):
-        for lane in range(0, own.shape[1], 128):
-            lanes = slice(lane, lane + 128)
-            a = mine if half == 0 else far_mine
-            b = far if half == 0 else own
-            held[...] = jnp.where(first, a[:, lanes].astype(F32), b[:, lanes].astype(F32))
-            for p in range(per):
-                for c in range(ocols):
-                    some = held[pl.ds(p * orows * ocols + c, orows, stride=ocols), :]
-                    out[half * per + p, c, :, lanes] = some.astype(BF16)
-
-
-def final(ids, mine, far_mine, own, far, so_far, first, step, per, orows, ocols):
-    px, wide = mine.shape
-    at = first // step
-    shared = pl.BlockSpec((px, step), lambda i: (0, at + i))
-    local = pl.BlockSpec((px, step), lambda i: (0, i))
-    more = [] if so_far is None else [so_far]
-    return pl.pallas_call(
-        functools.partial(final_kernel, per, orows, ocols),
-        grid=(own.shape[1] // step,),
+        at = 0
+        for i in range(parts):
+            count = own[i].shape[1]
+            for lane in range(0, count, 128):
+                here = slice(lane, lane + 128)
+                there = slice(at + lane, at + lane + 128)
+                a = mine[:, there] if half == 0 else far_mine[:, there]
+                b = far[i][:, here] if half == 0 else own[i][:, here]
+                held[...] = jnp.where(first, a.astype(F32), b.astype(F32))
+                for p in range(per):
+                    for c in range(ocols):
+                        some = held[pl.ds(p * orows * ocols + c, orows, stride=ocols), :]
+                        out[half * per + p, c, :, there] = some.astype(BF16)
+            at += count
+
+
+def final(ids, mine, far_mine, own, far, per, orows, ocols):
+    wide = mine.shape[1]
+    return pl.pallas_call(
+        functools.partial(final_kernel, len(own), per, orows, ocols),
         out_shape=jax.ShapeDtypeStruct((2 * per, ocols, orows, wide), BF16),
-        in_specs=[whole(pltpu.SMEM), shared, shared, local, local]
-        + [pl.BlockSpec(memory_space=pl.ANY)] * len(more),
-        out_specs=pl.BlockSpec((2 * per, ocols, orows, step), lambda i: (0, 0, 0, at + i)),
-        scratch_shapes=[pltpu.VMEM((px, 128), F32)],
-        input_output_aliases={5: 0} if more else {},
+        in_specs=[whole(pltpu.SMEM)] + [whole()] * (2 + 2 * len(own)),
+        out_specs=whole(),
+        scratch_shapes=[pltpu.VMEM((mine.shape[0], 128), F32)],
         name="final",
-        compiler_params=pltpu.CompilerParams(vmem_limit_bytes=6 << 20),
-    )(ids, mine, far_mine, own, far, *more)
+        compiler_params=pltpu.CompilerParams(vmem_limit_bytes=10 << 20),
+    )(ids, mine, far_mine, *own, *far)
 
 
 def pack_kernel(groups, per, c1, colp, ids, pixels, above, below, gain, shift, *refs):
@@ -554,7 +557,6 @@
     other_kernel = swap(second_kernel, "ch", 1)
 
     ids = jnp.stack([sec, z, ch, jnp.int32(shards - 1), y, core, z * pairs + y]).astype(jnp.int32)
-    cuts = cut(ids, projection, groups, shards)
     colp = -(-(cols + 2) // 16) * 16
     tails = lax.dynamic_slice_in_dim(pixels[:, -1:], sec * per, per, 0)
     heads = lax.dynamic_slice_in_dim(pixels[:, :1], sec * per, per, 0)
@@ -575,6 +577,7 @@
     blocks, mean = packed[:groups], packed[groups]
     got = [blocks[0]] + [swap(blocks[k], "img", k) for k in range(1, groups)]
 
+    cuts = cut(ids, projection, groups, shards)
     proj_z = join([cuts[0]] + [swap(cuts[k], "img", k) for k in range(1, groups)])
     proj_own = [proj_z] + [swap(proj_z, "ch", k, 2) for k in range(1, pairs)]
     proj_twin = [swap(part, "ch", 1) for part in proj_own]
@@ -641,12 +644,11 @@
 
     mine_projected = spread(ids, back)
     far_projected = lax.ppermute(mine_projected, "section", [(1, 0)])
-    block = None
-    for some in (values[:2], values[2:]):
-        at = some[0][2]
-        done = finish([v[:2] for v in some], mine_projected, at)
-        far = lax.ppermute(done, "section", [(0, 1)])
-        block = final(ids, mine_projected, far_projected, done, far, block, at, unit, per, orows, ocols)
+    outs, fars = [], []
+    for j, some in enumerate((values[:2], values[2:])):
+        outs.append(finish([v[:2] for v in some], mine_projected, some[0][2]))
+        fars.append(lax.ppermute(outs[j], "section", [(0, 1)]))
+    block = final(ids, mine_projected, far_projected, outs, fars, per, orows, ocols)
     return block.transpose(0, 2, 1, 3)[None]
 
 

time: 122 us -> 124 us (1.016)
  starting transfers between devices: 49.9 us -> 52 us
  Pallas kernels: 28.5 us -> 27 us
    pallas_call x2 -> x1, Pallas kernels: 5.27 us -> 1.84 us  [final(): pl.pallas_call(functools.partial(final_kernel, len(own), per, orows, ocol...]
    ppermute x31, starting transfers between devices: 40.8 us -> 42.9 us  [swap(): return lax.ppermute(array, axis, [(i, i ^ k * unit) for i in range(count)])]
    ppermute x2, waiting for transfers between devices: 0.01 us -> 2.07 us  [body(): fars.append(lax.ppermute(outs[j], 'section', [(0, 1)]))]
    pallas_call x1, Pallas kernels: 8.64 us -> 10.7 us  [unfold(): pl.pallas_call(functools.partial(unfold_kernel, pairs, imgs, ocols, kd, s...]
  transfers between devices with their start and end apart: 36 -> 36, of which waited for: 19 -> 18; matrix products, arithmetic and copies ran while one was open for 2% -> 2% of each run, Pallas kernels for 15% -> 12%
where the time goes in v4:
time: 124 us
  starting transfers between devices  52 us (42%)
  waiting for transfers between devices  41 us (33%)
  Pallas kernels  27 us (22%)
  local copies, waits for them, and re-layouts  3.13 us (3%)
    ppermute x31, starting transfers between devices, swap(): return lax.ppermute(array, axis, [(i, i ^ k * unit) for i in range(count)])  42.9 us
    ppermute x31, waiting for transfers between devices, swap(): return lax.ppermute(array, axis, [(i, i ^ k * unit) for i in range(count)])  39 us
    pallas_call x1, Pallas kernels, unfold(): pl.pallas_call(functools.partial(unfold_kernel, pairs, imgs, ocols, kd, s...  10.7 us
    pallas_call x2, Pallas kernels, mix(): pl.pallas_call(functools.partial(mix_kernel, rows, px), grid=(count // st...  9.08 us
    ppermute x2, starting transfers between devices, body(): fars.append(lax.ppermute(outs[j], 'section', [(0, 1)]))  4.71 us
  transfers between devices with their start and end apart: 36, of which 18 were waited for; matrix products, arithmetic and copies ran while one was open for 2% of the time, Pallas kernels for 12%

profile of v4, /device:TPU:0, one launch (start us, length us, event | category | flops | bytes accessed | tf_op | source)
XLA Modules:
  0.0 123.6 jit_solution(12346488720395479127)
XLA Ops:
  0.6 1.1 copy-done.1
  2.4 2.7 %collective-permute-start.11 = (bf16[40,640]{1,0:T(8,128)(2,1)S(1)}, bf16[40,640]{1,0:T(8,128)(2,1)S(1)}, u32[]{:S(2)}, u32[]{:S(2)}) collective-permute-start(bf16[40,640]{1,0:T(8,128)(2,1)S(1)} %get-tuple-element.60), channel_id=1, source_target_pairs={{0,4},{4,0},{8,12},{12,8},{1,5},{5,1},{9,13},{13,9},{2,6},{6,2},{1... | collective-permute-start | bytes 153608 | tf_op jit(solution)/shard_map/ppermute | solution.py:17
  5.1 2.6 %collective-permute-start.12 = (bf16[40,640]{1,0:T(8,128)(2,1)S(1)}, bf16[40,640]{1,0:T(8,128)(2,1)S(1)}, u32[]{:S(2)}, u32[]{:S(2)}) collective-permute-start(bf16[40,640]{1,0:T(8,128)(2,1)S(1)} %get-tuple-element.61), channel_id=1, source_target_pairs={{0,8},{4,12},{8,0},{12,4},{1,9},{5,13},{9,1},{13,5},{2,10},{6,14},... | collective-permute-start | bytes 153608 | tf_op jit(solution)/shard_map/ppermute | solution.py:17
  7.7 1.5 %fusion = (bf16[2,1,28,640]{3,1,2,0:T(2,128)(2,1)S(1)}, bf16[2,1,28,640]{3,1,2,0:T(2,128)(2,1)S(1)}) fusion(bf16[2,8,28,640]{3,1,2,0:T(8,128)(2,1)} %param.8), kind=kLoop, calls=%fused_computation.2 | loop fusion | bytes 286720 | tf_op jit(solution)/shard_map/slice | solution.py:562
  9.3 1.8 %collective-permute-start = (bf16[1,1,28,640]{3,2,1,0:T(8,128)(2,1)S(1)}, bf16[1,1,28,640]{3,2,1,0:T(8,128)(2,1)S(1)}, u32[]{:S(2)}, u32[]{:S(2)}) collective-permute-start(bf16[1,1,28,640]{3,2,1,0:T(8,128)(2,1)S(1)} %copy.13), channel_id=1, source_target_pairs={{0,1},{1,2},{2,3},{4,5},{5,6},{6,7},{8,9},{9,10},{10,11},{12,13},{... | collective-permute-start | bytes 107528 | tf_op jit(solution)/shard_map/ppermute | solution.py:564
  11.2 1.3 %collective-permute-start.1 = (bf16[1,1,28,640]{3,2,1,0:T(8,128)(2,1)S(1)}, bf16[1,1,28,640]{3,2,1,0:T(8,128)(2,1)S(1)}, u32[]{:S(2)}, u32[]{:S(2)}) collective-permute-start(bf16[1,1,28,640]{3,2,1,0:T(8,128)(2,1)S(1)} %copy.15), channel_id=1, source_target_pairs={{1,0},{2,1},{3,2},{5,4},{6,5},{7,6},{9,8},{10,9},{11,10},{13,12},{... | collective-permute-start | bytes 107528 | tf_op jit(solution)/shard_map/ppermute | solution.py:565
  12.5 1.1 collective-permute-done.13.refs_3_
  13.6 3.2 %collective-permute-start.14 = (bf16[4,40,640]{2,1,0:T(8,128)(2,1)S(1)}, bf16[4,40,640]{2,1,0:T(8,128)(2,1)S(1)}, u32[]{:S(2)}, u32[]{:S(2)}) collective-permute-start(bf16[4,40,640]{2,1,0:T(8,128)(2,1)S(1)} %join.1.refs_4_), channel_id=1, source_target_pairs={{0,2},{1,3},{2,0},{3,1},{4,6},{5,7},{6,4},{7,5},{8,10},{9,11},{10,... | collective-permute-start | bytes 614408 | tf_op jit(solution)/shard_map/ppermute | solution.py:17
  16.9 0.9 pack.1
  18.6 3.5 %collective-permute-start.3 = (bf16[416,128]{1,0:T(8,128)(2,1)S(1)}, bf16[416,128]{1,0:T(8,128)(2,1)S(1)}, u32[]{:S(2)}, u32[]{:S(2)}) collective-permute-start(bf16[416,128]{1,0:T(8,128)(2,1)S(1)} %get-tuple-element.52), channel_id=1, source_target_pairs={{0,8},{4,12},{8,0},{12,4},{1,9},{5,13},{9,1},{13,5},{2,10},{6,14},... | collective-permute-start | bytes 319496 | tf_op jit(solution)/shard_map/ppermute | solution.py:17
  22.8 1.8 %collective-permute-start.15 = (bf16[4,40,640]{2,1,0:T(8,128)(2,1)S(1)}, bf16[4,40,640]{2,1,0:T(8,128)(2,1)S(1)}, u32[]{:S(2)}, u32[]{:S(2)}) collective-permute-start(bf16[4,40,640]{2,1,0:T(8,128)(2,1)S(1)} %join.1.refs_4_), channel_id=1, source_target_pairs={{0,1},{1,0},{2,3},{3,2},{4,5},{5,4},{6,7},{7,6},{8,9},{9,8},{10,11... | collective-permute-start | bytes 614408 | tf_op jit(solution)/shard_map/ppermute | solution.py:17
  24.6 1.7 %collective-permute-done.3.refs_2_ = bf16[416,128]{1,0:T(8,128)(2,1)S(1)} collective-permute-done((bf16[416,128]{1,0:T(8,128)(2,1)S(1)}, bf16[416,128]{1,0:T(8,128)(2,1)S(1)}, u32[]{:S(2)}, u32[]{:S(2)}) %collective-permute-start.3) | collective-permute-done | bytes 106528 | tf_op jit(solution)/shard_map/ppermute | solution.py:17
  26.3 3.4 %collective-permute-done.4.refs_3_ = bf16[416,128]{1,0:T(8,128)(2,1)S(1)} collective-permute-done((bf16[416,128]{1,0:T(8,128)(2,1)S(1)}, bf16[416,128]{1,0:T(8,128)(2,1)S(1)}, u32[]{:S(2)}, u32[]{:S(2)}) %collective-permute-start.4) | collective-permute-done | bytes 106528 | tf_op jit(solution)/shard_map/ppermute | solution.py:17
  29.7 1.5 %stage.1 = (f32[56,640]{1,0:T(8,128)S(1)}, bf16[56,640]{1,0:T(8,128)(2,1)S(1)}, bf16[56,640]{1,0:T(8,128)(2,1)S(1)}, bf16[56,640]{1,0:T(8,128)(2,1)S(1)}) custom-call(bf16[416,128]{1,0:T(8,128)(2,1)S(1)} %get-tuple-element.50.refs_0_, bf16[416,128]{1,0:T(8,128)(2,1)S(1)} %collective-permute-done.2.refs_1_, ...), custom_call_target="tpu_custom_call" | custom-call | flops 471859200 | bytes 573440 | tf_op jit(solution)/shard_map/stage/pallas_call | solution.py:520
  31.3 3.0 %collective-permute-start.5 = (bf16[56,640]{1,0:T(8,128)(2,1)S(1)}, bf16[56,640]{1,0:T(8,128)(2,1)S(1)}, u32[]{:S(2)}, u32[]{:S(2)}) collective-permute-start(bf16[56,640]{1,0:T(8,128)(2,1)S(1)} %get-tuple-element.56), channel_id=1, source_target_pairs={{0,4},{4,0},{8,12},{12,8},{1,5},{5,1},{9,13},{13,9},{2,6},{6,2},{1... | collective-permute-start | bytes 215048 | tf_op jit(solution)/shard_map/ppermute | solution.py:17
  34.5 1.4 %collective-permute-start.6 = (bf16[56,640]{1,0:T(8,128)(2,1)S(1)}, bf16[56,640]{1,0:T(8,128)(2,1)S(1)}, u32[]{:S(2)}, u32[]{:S(2)}) collective-permute-start(bf16[56,640]{1,0:T(8,128)(2,1)S(1)} %get-tuple-element.57), channel_id=1, source_target_pairs={{0,8},{4,12},{8,0},{12,4},{1,9},{5,13},{9,1},{13,5},{2,10},{6,14},... | collective-permute-start | bytes 215048 | tf_op jit(solution)/shard_map/ppermute | solution.py:17
  35.9 1.3 %collective-permute-done.5.refs_0_ = bf16[56,640]{1,0:T(8,128)(2,1)S(1)} collective-permute-done((bf16[56,640]{1,0:T(8,128)(2,1)S(1)}, bf16[56,640]{1,0:T(8,128)(2,1)S(1)}, u32[]{:S(2)}, u32[]{:S(2)}) %collective-permute-start.5) | collective-permute-done | bytes 71712 | tf_op jit(solution)/shard_map/ppermute | solution.py:17
  37.2 2.3 %collective-permute-start.7 = (bf16[56,640]{1,0:T(8,128)(2,1)S(1)}, bf16[56,640]{1,0:T(8,128)(2,1)S(1)}, u32[]{:S(2)}, u32[]{:S(2)}) collective-permute-start(bf16[56,640]{1,0:T(8,128)(2,1)S(1)} %get-tuple-element.58), channel_id=1, source_target_pairs={{0,12},{4,8},{8,4},{12,0},{1,13},{5,9},{9,5},{13,1},{2,14},{6,10},... | collective-permute-start | bytes 215048 | tf_op jit(solution)/shard_map/ppermute | solution.py:17
  39.5 2.2 %collective-permute-done.6.refs_1_ = bf16[56,640]{1,0:T(8,128)(2,1)S(1)} collective-permute-done((bf16[56,640]{1,0:T(8,128)(2,1)S(1)}, bf16[56,640]{1,0:T(8,128)(2,1)S(1)}, u32[]{:S(2)}, u32[]{:S(2)}) %collective-permute-start.6) | collective-permute-done | bytes 71712 | tf_op jit(solution)/shard_map/ppermute | solution.py:17
  41.6 1.7 %collective-permute-done.7.refs_2_ = bf16[56,640]{1,0:T(8,128)(2,1)S(1)} collective-permute-done((bf16[56,640]{1,0:T(8,128)(2,1)S(1)}, bf16[56,640]{1,0:T(8,128)(2,1)S(1)}, u32[]{:S(2)}, u32[]{:S(2)}) %collective-permute-start.7) | collective-permute-done | bytes 71712 | tf_op jit(solution)/shard_map/ppermute | solution.py:17
  43.4 1.7 %collective-permute-start.8 = (bf16[56,640]{1,0:T(8,128)(2,1)S(1)}, bf16[56,640]{1,0:T(8,128)(2,1)S(1)}, u32[]{:S(2)}, u32[]{:S(2)}) collective-permute-start(bf16[56,640]{1,0:T(8,128)(2,1)S(1)} %pool.1.refs_0_), channel_id=1, source_target_pairs={{0,4},{4,0},{8,12},{12,8},{1,5},{5,1},{9,13},{13,9},{2,6},{6,2},{1... | collective-permute-start | bytes 215048 | tf_op jit(solution)/shard_map/ppermute | solution.py:17
  45.1 1.2 collective-permute-start.9
  46.3 1.5 %collective-permute-start.10 = (bf16[56,640]{1,0:T(8,128)(2,1)S(1)}, bf16[56,640]{1,0:T(8,128)(2,1)S(1)}, u32[]{:S(2)}, u32[]{:S(2)}) collective-permute-start(bf16[56,640]{1,0:T(8,128)(2,1)S(1)} %pool.1.refs_0_), channel_id=1, source_target_pairs={{0,12},{4,8},{8,4},{12,0},{1,13},{5,9},{9,5},{13,1},{2,14},{6,10},... | collective-permute-start | bytes 215048 | tf_op jit(solution)/shard_map/ppermute | solution.py:17
  47.8 5.5 %collective-permute-done.9.refs_2_ = bf16[56,640]{1,0:T(8,128)(2,1)S(1)} collective-permute-done((bf16[56,640]{1,0:T(8,128)(2,1)S(1)}, bf16[56,640]{1,0:T(8,128)(2,1)S(1)}, u32[]{:S(2)}, u32[]{:S(2)}) %collective-permute-start.9) | collective-permute-done | bytes 71712 | tf_op jit(solution)/shard_map/ppermute | solution.py:17
  53.4 1.2 %project.1 = (bf16[56,640]{1,0:T(8,128)(2,1)S(1)}, bf16[56,640]{1,0:T(8,128)(2,1)S(1)}, bf16[56,640]{1,0:T(8,128)(2,1)S(1)}, bf16[56,640]{1,0:T(8,128)(2,1)S(1)}...) custom-call(s32[7]{0:T(128)S(1)} %stack.27.ids, bf16[56,640]{1,0:T(8,128)(2,1)S(1)} %pool.1.refs_0_, ...), custom_call_target="tpu_custom_call" | custom-call | flops 183500800 | bytes 1638400 | tf_op jit(solution)/shard_map/project/pallas_call | solution.py:288
  54.8 5.3 %collective-permute-done.21 = bf16[224,320]{1,0:T(8,128)(2,1)S(1)} collective-permute-done((bf16[224,320]{1,0:T(8,128)(2,1)S(1)}, bf16[224,320]{1,0:T(8,128)(2,1)S(1)}, u32[]{:S(2)}, u32[]{:S(2)}) %collective-permute-start.21) | collective-permute-done | bytes 143392 | tf_op jit(solution)/shard_map/ppermute | solution.py:17
  60.3 1.2 %collective-permute-done.23 = bf16[224,320]{1,0:T(8,128)(2,1)S(1)} collective-permute-done((bf16[224,320]{1,0:T(8,128)(2,1)S(1)}, bf16[224,320]{1,0:T(8,128)(2,1)S(1)}, u32[]{:S(2)}, u32[]{:S(2)}) %collective-permute-start.23) | collective-permute-done | bytes 143392 | tf_op jit(solution)/shard_map/ppermute | solution.py:17
  61.5 10.7 %unfold.1 = (bf16[448,1440]{1,0:T(8,128)(2,1)S(1)}, bf16[448,1440]{1,0:T(8,128)(2,1)S(1)}, bf16[224,1024]{1,0:T(8,128)(2,1)S(1)}, f32[224,1024]{1,0:T(8,128)S(1)}) custom-call(s32[7]{0:T(128)S(1)} %stack.27.ids, f32[8,320]{1,0:T(8,128)S(1)} %reshape.36.gains, f32[8,320]{1,0:T(8,128)S(1)} %reshape.37.shifts, bf16[4,56,320]{2,1,0:T(8,128)(2,1)S(1)} %bitcast.17, ...), custom_call_target="tpu_custom_call" | custom-call | flops 2642411520 | bytes 5898240 | tf_op jit(solution)/shard_map/unfold/pallas_call | solution.py:115
  72.3 4.5 %mix.2 = (bf16[224,768]{1,0:T(8,128)(2,1)S(1)}, f32[224,768]{1,0:T(8,128)S(1)}) custom-call(bf16[448,1440]{1,0:T(8,128)(2,1)S(1)} %get-tuple-element.75.a_own, bf16[448,1440]{1,0:T(8,128)(2,1)S(1)} %get-tuple-element.76.a_other, bf16[1440,2560]{1,0:T(8,128)(2,1)} %bitcast.22, bf16[1440,2560]{1,0:T(8,128)(2,1)} %bitcast.12.refs_5_.w_other), custom_call_target="tpu_custom_call" | custom-call | flops 1981808640 | bytes 5455872 | tf_op jit(solution)/shard_map/mix/pallas_call | solution.py:158
  76.8 2.1 %collective-permute-start.28 = (bf16[224,768]{1,0:T(8,128)(2,1)S(1)}, bf16[224,768]{1,0:T(8,128)(2,1)S(1)}, u32[]{:S(2)}, u32[]{:S(2)}) collective-permute-start(bf16[224,768]{1,0:T(8,128)(2,1)S(1)} %get-tuple-element.78), channel_id=1, source_target_pairs={{0,4},{4,0},{8,12},{12,8},{1,5},{5,1},{9,13},{13,9},{2,6},{6,2},{1... | collective-permute-start | bytes 1032200 | tf_op jit(solution)/shard_map/ppermute | solution.py:17
  78.9 4.5 %mix.3 = (bf16[224,768]{1,0:T(8,128)(2,1)S(1)}, f32[224,768]{1,0:T(8,128)S(1)}) custom-call(bf16[448,1440]{1,0:T(8,128)(2,1)S(1)} %get-tuple-element.75.a_own, bf16[448,1440]{1,0:T(8,128)(2,1)S(1)} %get-tuple-element.76.a_other, bf16[1440,2560]{1,0:T(8,128)(2,1)} %bitcast.23, bf16[1440,2560]{1,0:T(8,128)(2,1)} %bitcast.12.refs_5_.w_other), custom_call_target="tpu_custom_call" | custom-call | flops 1981808640 | bytes 5455872 | tf_op jit(solution)/shard_map/mix/pallas_call | solution.py:158
  83.4 1.8 %collective-permute-start.31 = (bf16[224,768]{1,0:T(8,128)(2,1)S(1)}, bf16[224,768]{1,0:T(8,128)(2,1)S(1)}, u32[]{:S(2)}, u32[]{:S(2)}) collective-permute-start(bf16[224,768]{1,0:T(8,128)(2,1)S(1)} %get-tuple-element.84), channel_id=1, source_target_pairs={{0,2},{1,3},{2,0},{3,1},{4,6},{5,7},{6,4},{7,5},{8,10},{9,11},{10,... | collective-permute-start | bytes 1032200 | tf_op jit(solution)/shard_map/ppermute | solution.py:17
  85.3 1.9 %collective-permute-start.26 = (bf16[112,1024]{1,0:T(8,128)(2,1)S(1)}, bf16[112,1024]{1,0:T(8,128)(2,1)S(1)}, u32[]{:S(2)}, u32[]{:S(2)}) collective-permute-start(bf16[112,1024]{1,0:T(8,128)(2,1)S(1)} %get-tuple-element.72), channel_id=1, source_target_pairs={{0,4},{4,0},{8,12},{12,8},{1,5},{5,1},{9,13},{13,9},{2,6},{6,2},{1... | collective-permute-start | bytes 688136 | tf_op jit(solution)/shard_map/ppermute | solution.py:17
  87.3 1.9 %collective-permute-start.29 = (bf16[112,768]{1,0:T(8,128)(2,1)S(1)}, bf16[112,768]{1,0:T(8,128)(2,1)S(1)}, u32[]{:S(2)}, u32[]{:S(2)}) collective-permute-start(bf16[112,768]{1,0:T(8,128)(2,1)S(1)} %get-tuple-element.80), channel_id=1, source_target_pairs={{0,8},{4,12},{8,0},{12,4},{1,9},{5,13},{9,1},{13,5},{2,10},{6,14},... | collective-permute-start | bytes 516104 | tf_op jit(solution)/shard_map/ppermute | solution.py:17
  89.8 2.1 %collective-permute-start.18 = (bf16[56,640]{1,0:T(8,128)(2,1)S(1)}, bf16[56,640]{1,0:T(8,128)(2,1)S(1)}, u32[]{:S(2)}, u32[]{:S(2)}) collective-permute-start(bf16[56,640]{1,0:T(8,128)(2,1)S(1)} %get-tuple-element.65), channel_id=1, source_target_pairs={{0,8},{4,12},{8,0},{12,4},{1,9},{5,13},{9,1},{13,5},{2,10},{6,14},... | collective-permute-start | bytes 215048 | tf_op jit(solution)/shard_map/ppermute | solution.py:17
  92.0 1.1 collective-permute-done.31.came
  93.1 1.6 %collective-permute-start.19 = (bf16[56,640]{1,0:T(8,128)(2,1)S(1)}, bf16[56,640]{1,0:T(8,128)(2,1)S(1)}, u32[]{:S(2)}, u32[]{:S(2)}) collective-permute-start(bf16[56,640]{1,0:T(8,128)(2,1)S(1)} %get-tuple-element.66), channel_id=1, source_target_pairs={{0,12},{4,8},{8,4},{12,0},{1,13},{5,9},{9,5},{13,1},{2,14},{6,10},... | collective-permute-start | bytes 215048 | tf_op jit(solution)/shard_map/ppermute | solution.py:17
  94.8 2.6 %collective-permute-done.26.came = bf16[112,1024]{1,0:T(8,128)(2,1)S(1)} collective-permute-done((bf16[112,1024]{1,0:T(8,128)(2,1)S(1)}, bf16[112,1024]{1,0:T(8,128)(2,1)S(1)}, u32[]{:S(2)}, u32[]{:S(2)}) %collective-permute-start.26) | collective-permute-done | bytes 229408 | tf_op jit(solution)/shard_map/ppermute | solution.py:17
  97.4 3.7 %collective-permute-done.29.came = bf16[112,768]{1,0:T(8,128)(2,1)S(1)} collective-permute-done((bf16[112,768]{1,0:T(8,128)(2,1)S(1)}, bf16[112,768]{1,0:T(8,128)(2,1)S(1)}, u32[]{:S(2)}, u32[]{:S(2)}) %collective-permute-start.29) | collective-permute-done | bytes 172064 | tf_op jit(solution)/shard_map/ppermute | solution.py:17
  101.1 2.3 %collective-permute-start.30 = (bf16[56,768]{1,0:T(8,128)(2,1)S(1)}, bf16[56,768]{1,0:T(8,128)(2,1)S(1)}, u32[]{:S(2)}, u32[]{:S(2)}) collective-permute-start(bf16[56,768]{1,0:T(8,128)(2,1)S(1)} %get-tuple-element.82), channel_id=1, source_target_pairs={{0,2},{1,3},{2,0},{3,1},{4,6},{5,7},{6,4},{7,5},{8,10},{9,11},{10,... | collective-permute-start | bytes 258056 | tf_op jit(solution)/shard_map/ppermute | solution.py:17
  104.4 1.3 %collective-permute-start.20 = (bf16[56,2560]{1,0:T(8,128)(2,1)S(1)}, bf16[56,2560]{1,0:T(8,128)(2,1)S(1)}, u32[]{:S(2)}, u32[]{:S(2)}) collective-permute-start(bf16[56,2560]{1,0:T(8,128)(2,1)S(1)} %spread.1.refs_4_.refs_2_.mine), channel_id=1, source_target_pairs={{16,0},{17,1},{18,2},{19,3},{20,4},{21,5},{22,6},{23,7},{24,8},{25... | collective-permute-start | bytes 860168 | tf_op jit(solution)/shard_map/ppermute | solution.py:646
  105.9 2.5 %collective-permute-done.27.refs_1_ = bf16[56,1024]{1,0:T(8,128)(2,1)S(1)} collective-permute-done((bf16[56,1024]{1,0:T(8,128)(2,1)S(1)}, bf16[56,1024]{1,0:T(8,128)(2,1)S(1)}, u32[]{:S(2)}, u32[]{:S(2)}) %collective-permute-start.27) | collective-permute-done | bytes 114720 | tf_op jit(solution)/shard_map/ppermute | solution.py:17
  108.5 3.4 %collective-permute-start.34 = (bf16[56,1792]{1,0:T(8,128)(2,1)S(1)}, bf16[56,1792]{1,0:T(8,128)(2,1)S(1)}, u32[]{:S(2)}, u32[]{:S(2)}) collective-permute-start(bf16[56,1792]{1,0:T(8,128)(2,1)S(1)} %finish.2.refs_0_), channel_id=1, source_target_pairs={{0,16},{1,17},{2,18},{3,19},{4,20},{5,21},{6,22},{7,23},{8,24},{9,... | collective-permute-start | bytes 602120 | tf_op jit(solution)/shard_map/ppermute | solution.py:650
  111.9 1.8 %collective-permute-start.33 = (bf16[56,768]{1,0:T(8,128)(2,1)S(1)}, bf16[56,768]{1,0:T(8,128)(2,1)S(1)}, u32[]{:S(2)}, u32[]{:S(2)}) collective-permute-start(bf16[56,768]{1,0:T(8,128)(2,1)S(1)} %get-tuple-element.88), channel_id=1, source_target_pairs={{0,8},{4,12},{8,0},{12,4},{1,9},{5,13},{9,1},{13,5},{2,10},{6,14},... | collective-permute-start | bytes 258056 | tf_op jit(solution)/shard_map/ppermute | solution.py:17
  113.7 4.6 %collective-permute-done.33.refs_1_ = bf16[56,768]{1,0:T(8,128)(2,1)S(1)} collective-permute-done((bf16[56,768]{1,0:T(8,128)(2,1)S(1)}, bf16[56,768]{1,0:T(8,128)(2,1)S(1)}, u32[]{:S(2)}, u32[]{:S(2)}) %collective-permute-start.33) | collective-permute-done | bytes 86048 | tf_op jit(solution)/shard_map/ppermute | solution.py:17
  118.3 1.3 %collective-permute-start.35 = (bf16[56,768]{1,0:T(8,128)(2,1)S(1)}, bf16[56,768]{1,0:T(8,128)(2,1)S(1)}, u32[]{:S(2)}, u32[]{:S(2)}) collective-permute-start(bf16[56,768]{1,0:T(8,128)(2,1)S(1)} %finish.3.refs_1_), channel_id=1, source_target_pairs={{0,16},{1,17},{2,18},{3,19},{4,20},{5,21},{6,22},{7,23},{8,24},{9,... | collective-permute-start | bytes 258056 | tf_op jit(solution)/shard_map/ppermute | solution.py:650
  119.7 2.1 %collective-permute-done.35.refs_3_ = bf16[56,768]{1,0:T(8,128)(2,1)S(1)} collective-permute-done((bf16[56,768]{1,0:T(8,128)(2,1)S(1)}, bf16[56,768]{1,0:T(8,128)(2,1)S(1)}, u32[]{:S(2)}, u32[]{:S(2)}) %collective-permute-start.35) | collective-permute-done | bytes 86048 | tf_op jit(solution)/shard_map/ppermute | solution.py:650
  121.7 1.8 %final.1 = bf16[2,14,4,2560]{3,2,1,0:T(4,128)(2,1)} custom-call(s32[7]{0:T(128)S(1)} %stack.27.ids, bf16[56,2560]{1,0:T(8,128)(2,1)S(1)} %spread.1.refs_4_.refs_2_.mine, bf16[56,2560]{1,0:T(8,128)(2,1)S(1)} %collective-permute-done.20.far_mine, bf16[56,1792]{1,0:T(8,128)(2,1)S(1)} %finish.2.refs_0_, bf16[56,768]{1,0:T(8,128)(2,1)S(1)} %finish.3.refs_1_, ...), custom_call_target="tpu_custom_call" | custom-call | tf_op jit(solution)/shard_map/final/pallas_call | solution.py:384
  (67 shorter events, 5.9 us)
Async XLA Ops:
  0.0 16.9 %copy-start.5 = (f32[640]{0:T(1024)S(1)}, f32[640]{0:T(1024)}, u32[]{:S(2)}) copy-start(f32[640]{0:T(1024)} %param.9) | copy-start | bytes 7684
  0.0 16.9 %copy-start.6 = (f32[640]{0:T(1024)S(1)}, f32[640]{0:T(1024)}, u32[]{:S(2)}) copy-start(f32[640]{0:T(1024)} %param.10) | copy-start | bytes 7684
  0.0 61.5 %collective-permute-start.24 = (bf16[3,3,160,2560]{3,2,1,0:T(8,128)(2,1)}, bf16[3,3,160,2560]{3,2,1,0:T(8,128)(2,1)}, u32[]{:S(2)}, u32[]{:S(2)}) collective-permute-start(bf16[3,3,160,2560]{3,2,1,0:T(8,128)(2,1)} %param.15), channel_id=1, source_target_pairs={{0,1},{1,0},{2,3},{3,2},{4,5},{5,4},{6,7},{7,6},{8,9},{9,8},{10,11... | collective-permute-start | bytes 22118408 | tf_op jit(solution)/shard_map/ppermute | solution.py:17
  0.6 1.1 copy-start.1
  1.7 15.1 %copy-start.2 = (bf16[2,8,28,640]{3,1,2,0:T(8,128)(2,1)S(1)}, bf16[2,8,28,640]{3,1,2,0:T(8,128)(2,1)}, u32[]{:S(2)}) copy-start(bf16[2,8,28,640]{3,1,2,0:T(8,128)(2,1)} %param.8) | copy-start | bytes 1720324
  2.4 27.3 %copy-start = (bf16[3,3,160,640]{3,2,1,0:T(8,128)(2,1)S(1)}, bf16[3,3,160,640]{3,2,1,0:T(8,128)(2,1)}, u32[]{:S(2)}) copy-start(bf16[3,3,160,640]{3,2,1,0:T(8,128)(2,1)} %param.11) | copy-start | bytes 5529604
  2.4 8.8 %collective-permute-start.11 = (bf16[40,640]{1,0:T(8,128)(2,1)S(1)}, bf16[40,640]{1,0:T(8,128)(2,1)S(1)}, u32[]{:S(2)}, u32[]{:S(2)}) collective-permute-start(bf16[40,640]{1,0:T(8,128)(2,1)S(1)} %get-tuple-element.60), channel_id=1, source_target_pairs={{0,4},{4,0},{8,12},{12,8},{1,5},{5,1},{9,13},{13,9},{2,6},{6,2},{1... | collective-permute-start | bytes 153608 | tf_op jit(solution)/shard_map/ppermute | solution.py:17
  5.1 7.4 %collective-permute-start.12 = (bf16[40,640]{1,0:T(8,128)(2,1)S(1)}, bf16[40,640]{1,0:T(8,128)(2,1)S(1)}, u32[]{:S(2)}, u32[]{:S(2)}) collective-permute-start(bf16[40,640]{1,0:T(8,128)(2,1)S(1)} %get-tuple-element.61), channel_id=1, source_target_pairs={{0,8},{4,12},{8,0},{12,4},{1,9},{5,13},{9,1},{13,5},{2,10},{6,14},... | collective-permute-start | bytes 153608 | tf_op jit(solution)/shard_map/ppermute | solution.py:17
  7.7 5.9 %collective-permute-start.13 = (bf16[40,640]{1,0:T(8,128)(2,1)S(1)}, bf16[40,640]{1,0:T(8,128)(2,1)S(1)}, u32[]{:S(2)}, u32[]{:S(2)}) collective-permute-start(bf16[40,640]{1,0:T(8,128)(2,1)S(1)} %get-tuple-element.62), channel_id=1, source_target_pairs={{0,12},{4,8},{8,4},{12,0},{1,13},{5,9},{9,5},{13,1},{2,14},{6,10},... | collective-permute-start | bytes 153608 | tf_op jit(solution)/shard_map/ppermute | solution.py:17
  9.3 7.6 %collective-permute-start = (bf16[1,1,28,640]{3,2,1,0:T(8,128)(2,1)S(1)}, bf16[1,1,28,640]{3,2,1,0:T(8,128)(2,1)S(1)}, u32[]{:S(2)}, u32[]{:S(2)}) collective-permute-start(bf16[1,1,28,640]{3,2,1,0:T(8,128)(2,1)S(1)} %copy.13), channel_id=1, source_target_pairs={{0,1},{1,2},{2,3},{4,5},{5,6},{6,7},{8,9},{9,10},{10,11},{12,13},{... | collective-permute-start | bytes 107528 | tf_op jit(solution)/shard_map/ppermute | solution.py:564
  11.2 5.7 %collective-permute-start.1 = (bf16[1,1,28,640]{3,2,1,0:T(8,128)(2,1)S(1)}, bf16[1,1,28,640]{3,2,1,0:T(8,128)(2,1)S(1)}, u32[]{:S(2)}, u32[]{:S(2)}) collective-permute-start(bf16[1,1,28,640]{3,2,1,0:T(8,128)(2,1)S(1)} %copy.15), channel_id=1, source_target_pairs={{1,0},{2,1},{3,2},{5,4},{6,5},{7,6},{9,8},{10,9},{11,10},{13,12},{... | collective-permute-start | bytes 107528 | tf_op jit(solution)/shard_map/ppermute | solution.py:565
  13.6 20.6 %collective-permute-start.14 = (bf16[4,40,640]{2,1,0:T(8,128)(2,1)S(1)}, bf16[4,40,640]{2,1,0:T(8,128)(2,1)S(1)}, u32[]{:S(2)}, u32[]{:S(2)}) collective-permute-start(bf16[4,40,640]{2,1,0:T(8,128)(2,1)S(1)} %join.1.refs_4_), channel_id=1, source_target_pairs={{0,2},{1,3},{2,0},{3,1},{4,6},{5,7},{6,4},{7,5},{8,10},{9,11},{10,... | collective-permute-start | bytes 614408 | tf_op jit(solution)/shard_map/ppermute | solution.py:17
  17.9 4.9 %collective-permute-start.2 = (bf16[416,128]{1,0:T(8,128)(2,1)S(1)}, bf16[416,128]{1,0:T(8,128)(2,1)S(1)}, u32[]{:S(2)}, u32[]{:S(2)}) collective-permute-start(bf16[416,128]{1,0:T(8,128)(2,1)S(1)} %get-tuple-element.51), channel_id=1, source_target_pairs={{0,4},{4,0},{8,12},{12,8},{1,5},{5,1},{9,13},{13,9},{2,6},{6,2},{1... | collective-permute-start | bytes 319496 | tf_op jit(solution)/shard_map/ppermute | solution.py:17
  18.6 7.7 %collective-permute-start.3 = (bf16[416,128]{1,0:T(8,128)(2,1)S(1)}, bf16[416,128]{1,0:T(8,128)(2,1)S(1)}, u32[]{:S(2)}, u32[]{:S(2)}) collective-permute-start(bf16[416,128]{1,0:T(8,128)(2,1)S(1)} %get-tuple-element.52), channel_id=1, source_target_pairs={{0,8},{4,12},{8,0},{12,4},{1,9},{5,13},{9,1},{13,5},{2,10},{6,14},... | collective-permute-start | bytes 319496 | tf_op jit(solution)/shard_map/ppermute | solution.py:17
  22.1 7.6 %collective-permute-start.4 = (bf16[416,128]{1,0:T(8,128)(2,1)S(1)}, bf16[416,128]{1,0:T(8,128)(2,1)S(1)}, u32[]{:S(2)}, u32[]{:S(2)}) collective-permute-start(bf16[416,128]{1,0:T(8,128)(2,1)S(1)} %get-tuple-element.53), channel_id=1, source_target_pairs={{0,12},{4,8},{8,4},{12,0},{1,13},{5,9},{9,5},{13,1},{2,14},{6,10},... | collective-permute-start | bytes 319496 | tf_op jit(solution)/shard_map/ppermute | solution.py:17
  22.8 23.5 %collective-permute-start.15 = (bf16[4,40,640]{2,1,0:T(8,128)(2,1)S(1)}, bf16[4,40,640]{2,1,0:T(8,128)(2,1)S(1)}, u32[]{:S(2)}, u32[]{:S(2)}) collective-permute-start(bf16[4,40,640]{2,1,0:T(8,128)(2,1)S(1)} %join.1.refs_4_), channel_id=1, source_target_pairs={{0,1},{1,0},{2,3},{3,2},{4,5},{5,4},{6,7},{7,6},{8,9},{9,8},{10,11... | collective-permute-start | bytes 614408 | tf_op jit(solution)/shard_map/ppermute | solution.py:17
  29.7 30.4 %copy-start.3 = (f32[2560]{0:T(1024)S(1)}, f32[2560]{0:T(1024)}, u32[]{:S(2)}) copy-start(f32[2560]{0:T(1024)} %param.13) | copy-start | bytes 30724
  29.7 30.5 %copy-start.4 = (f32[2560]{0:T(1024)S(1)}, f32[2560]{0:T(1024)}, u32[]{:S(2)}) copy-start(f32[2560]{0:T(1024)} %param.14) | copy-start | bytes 30724
  31.3 5.9 %collective-permute-start.5 = (bf16[56,640]{1,0:T(8,128)(2,1)S(1)}, bf16[56,640]{1,0:T(8,128)(2,1)S(1)}, u32[]{:S(2)}, u32[]{:S(2)}) collective-permute-start(bf16[56,640]{1,0:T(8,128)(2,1)S(1)} %get-tuple-element.56), channel_id=1, source_target_pairs={{0,4},{4,0},{8,12},{12,8},{1,5},{5,1},{9,13},{13,9},{2,6},{6,2},{1... | collective-permute-start | bytes 215048 | tf_op jit(solution)/shard_map/ppermute | solution.py:17
  34.2 19.1 %collective-permute-start.16 = (bf16[4,40,640]{2,1,0:T(8,128)(2,1)S(1)}, bf16[4,40,640]{2,1,0:T(8,128)(2,1)S(1)}, u32[]{:S(2)}, u32[]{:S(2)}) collective-permute-start(bf16[4,40,640]{2,1,0:T(8,128)(2,1)S(1)} %collective-permute-done.14.refs_5_), channel_id=1, source_target_pairs={{0,1},{1,0},{2,3},{3,2},{4,5},{5,4},{6,7},{7,6},{8,9},{9,8},{10,11... | collective-permute-start | bytes 614408 | tf_op jit(solution)/shard_map/ppermute | solution.py:17
  34.5 7.1 %collective-permute-start.6 = (bf16[56,640]{1,0:T(8,128)(2,1)S(1)}, bf16[56,640]{1,0:T(8,128)(2,1)S(1)}, u32[]{:S(2)}, u32[]{:S(2)}) collective-permute-start(bf16[56,640]{1,0:T(8,128)(2,1)S(1)} %get-tuple-element.57), channel_id=1, source_target_pairs={{0,8},{4,12},{8,0},{12,4},{1,9},{5,13},{9,1},{13,5},{2,10},{6,14},... | collective-permute-start | bytes 215048 | tf_op jit(solution)/shard_map/ppermute | solution.py:17
  37.2 6.1 %collective-permute-start.7 = (bf16[56,640]{1,0:T(8,128)(2,1)S(1)}, bf16[56,640]{1,0:T(8,128)(2,1)S(1)}, u32[]{:S(2)}, u32[]{:S(2)}) collective-permute-start(bf16[56,640]{1,0:T(8,128)(2,1)S(1)} %get-tuple-element.58), channel_id=1, source_target_pairs={{0,12},{4,8},{8,4},{12,0},{1,13},{5,9},{9,5},{13,1},{2,14},{6,10},... | collective-permute-start | bytes 215048 | tf_op jit(solution)/shard_map/ppermute | solution.py:17
  43.4 4.5 %collective-permute-start.8 = (bf16[56,640]{1,0:T(8,128)(2,1)S(1)}, bf16[56,640]{1,0:T(8,128)(2,1)S(1)}, u32[]{:S(2)}, u32[]{:S(2)}) collective-permute-start(bf16[56,640]{1,0:T(8,128)(2,1)S(1)} %pool.1.refs_0_), channel_id=1, source_target_pairs={{0,4},{4,0},{8,12},{12,8},{1,5},{5,1},{9,13},{13,9},{2,6},{6,2},{1... | collective-permute-start | bytes 215048 | tf_op jit(solution)/shard_map/ppermute | solution.py:17
  45.1 8.3 %collective-permute-start.9 = (bf16[56,640]{1,0:T(8,128)(2,1)S(1)}, bf16[56,640]{1,0:T(8,128)(2,1)S(1)}, u32[]{:S(2)}, u32[]{:S(2)}) collective-permute-start(bf16[56,640]{1,0:T(8,128)(2,1)S(1)} %pool.1.refs_0_), channel_id=1, source_target_pairs={{0,8},{4,12},{8,0},{12,4},{1,9},{5,13},{9,1},{13,5},{2,10},{6,14},... | collective-permute-start | bytes 215048 | tf_op jit(solution)/shard_map/ppermute | solution.py:17
  46.3 7.1 %collective-permute-start.10 = (bf16[56,640]{1,0:T(8,128)(2,1)S(1)}, bf16[56,640]{1,0:T(8,128)(2,1)S(1)}, u32[]{:S(2)}, u32[]{:S(2)}) collective-permute-start(bf16[56,640]{1,0:T(8,128)(2,1)S(1)} %pool.1.refs_0_), channel_id=1, source_target_pairs={{0,12},{4,8},{8,4},{12,0},{1,13},{5,9},{9,5},{13,1},{2,14},{6,10},... | collective-permute-start | bytes 215048 | tf_op jit(solution)/shard_map/ppermute | solution.py:17
  54.6 5.5 %collective-permute-start.21 = (bf16[224,320]{1,0:T(8,128)(2,1)S(1)}, bf16[224,320]{1,0:T(8,128)(2,1)S(1)}, u32[]{:S(2)}, u32[]{:S(2)}) collective-permute-start(bf16[224,320]{1,0:T(8,128)(2,1)S(1)} %get-tuple-element.68), channel_id=1, source_target_pairs={{0,2},{1,3},{2,0},{3,1},{4,6},{5,7},{6,4},{7,5},{8,10},{9,11},{10,... | collective-permute-start | bytes 430088 | tf_op jit(solution)/shard_map/ppermute | solution.py:17
  54.7 5.6 %collective-permute-start.22 = (bf16[224,320]{1,0:T(8,128)(2,1)S(1)}, bf16[224,320]{1,0:T(8,128)(2,1)S(1)}, u32[]{:S(2)}, u32[]{:S(2)}) collective-permute-start(bf16[224,320]{1,0:T(8,128)(2,1)S(1)} %get-tuple-element.67), channel_id=1, source_target_pairs={{0,1},{1,0},{2,3},{3,2},{4,5},{5,4},{6,7},{7,6},{8,9},{9,8},{10,11... | collective-permute-start | bytes 430088 | tf_op jit(solution)/shard_map/ppermute | solution.py:17
  60.1 1.4 %collective-permute-start.23 = (bf16[224,320]{1,0:T(8,128)(2,1)S(1)}, bf16[224,320]{1,0:T(8,128)(2,1)S(1)}, u32[]{:S(2)}, u32[]{:S(2)}) collective-permute-start(bf16[224,320]{1,0:T(8,128)(2,1)S(1)} %collective-permute-done.21), channel_id=1, source_target_pairs={{0,1},{1,0},{2,3},{3,2},{4,5},{5,4},{6,7},{7,6},{8,9},{9,8},{10,11... | collective-permute-start | bytes 430088 | tf_op jit(solution)/shard_map/ppermute | solution.py:17
  72.2 13.0 %collective-permute-start.25 = (bf16[224,1024]{1,0:T(8,128)(2,1)S(1)}, bf16[224,1024]{1,0:T(8,128)(2,1)S(1)}, u32[]{:S(2)}, u32[]{:S(2)}) collective-permute-start(bf16[224,1024]{1,0:T(8,128)(2,1)S(1)} %get-tuple-element.70), channel_id=1, source_target_pairs={{0,2},{1,3},{2,0},{3,1},{4,6},{5,7},{6,4},{7,5},{8,10},{9,11},{10,... | collective-permute-start | bytes 1376264 | tf_op jit(solution)/shard_map/ppermute | solution.py:17
  76.8 10.4 %collective-permute-start.28 = (bf16[224,768]{1,0:T(8,128)(2,1)S(1)}, bf16[224,768]{1,0:T(8,128)(2,1)S(1)}, u32[]{:S(2)}, u32[]{:S(2)}) collective-permute-start(bf16[224,768]{1,0:T(8,128)(2,1)S(1)} %get-tuple-element.78), channel_id=1, source_target_pairs={{0,4},{4,0},{8,12},{12,8},{1,5},{5,1},{9,13},{13,9},{2,6},{6,2},{1... | collective-permute-start | bytes 1032200 | tf_op jit(solution)/shard_map/ppermute | solution.py:17
  83.4 9.6 %collective-permute-start.31 = (bf16[224,768]{1,0:T(8,128)(2,1)S(1)}, bf16[224,768]{1,0:T(8,128)(2,1)S(1)}, u32[]{:S(2)}, u32[]{:S(2)}) collective-permute-start(bf16[224,768]{1,0:T(8,128)(2,1)S(1)} %get-tuple-element.84), channel_id=1, source_target_pairs={{0,2},{1,3},{2,0},{3,1},{4,6},{5,7},{6,4},{7,5},{8,10},{9,11},{10,... | collective-permute-start | bytes 1032200 | tf_op jit(solution)/shard_map/ppermute | solution.py:17
  85.3 12.0 %collective-permute-start.26 = (bf16[112,1024]{1,0:T(8,128)(2,1)S(1)}, bf16[112,1024]{1,0:T(8,128)(2,1)S(1)}, u32[]{:S(2)}, u32[]{:S(2)}) collective-permute-start(bf16[112,1024]{1,0:T(8,128)(2,1)S(1)} %get-tuple-element.72), channel_id=1, source_target_pairs={{0,4},{4,0},{8,12},{12,8},{1,5},{5,1},{9,13},{13,9},{2,6},{6,2},{1... | collective-permute-start | bytes 688136 | tf_op jit(solution)/shard_map/ppermute | solution.py:17
  87.3 13.8 %collective-permute-start.29 = (bf16[112,768]{1,0:T(8,128)(2,1)S(1)}, bf16[112,768]{1,0:T(8,128)(2,1)S(1)}, u32[]{:S(2)}, u32[]{:S(2)}) collective-permute-start(bf16[112,768]{1,0:T(8,128)(2,1)S(1)} %get-tuple-element.80), channel_id=1, source_target_pairs={{0,8},{4,12},{8,0},{12,4},{1,9},{5,13},{9,1},{13,5},{2,10},{6,14},... | collective-permute-start | bytes 516104 | tf_op jit(solution)/shard_map/ppermute | solution.py:17
  89.2 11.9 %collective-permute-start.17 = (bf16[56,640]{1,0:T(8,128)(2,1)S(1)}, bf16[56,640]{1,0:T(8,128)(2,1)S(1)}, u32[]{:S(2)}, u32[]{:S(2)}) collective-permute-start(bf16[56,640]{1,0:T(8,128)(2,1)S(1)} %get-tuple-element.64), channel_id=1, source_target_pairs={{0,4},{4,0},{8,12},{12,8},{1,5},{5,1},{9,13},{13,9},{2,6},{6,2},{1... | collective-permute-start | bytes 215048 | tf_op jit(solution)/shard_map/ppermute | solution.py:17
  89.8 14.0 %collective-permute-start.18 = (bf16[56,640]{1,0:T(8,128)(2,1)S(1)}, bf16[56,640]{1,0:T(8,128)(2,1)S(1)}, u32[]{:S(2)}, u32[]{:S(2)}) collective-permute-start(bf16[56,640]{1,0:T(8,128)(2,1)S(1)} %get-tuple-element.65), channel_id=1, source_target_pairs={{0,8},{4,12},{8,0},{12,4},{1,9},{5,13},{9,1},{13,5},{2,10},{6,14},... | collective-permute-start | bytes 215048 | tf_op jit(solution)/shard_map/ppermute | solution.py:17
  93.1 10.8 %collective-permute-start.19 = (bf16[56,640]{1,0:T(8,128)(2,1)S(1)}, bf16[56,640]{1,0:T(8,128)(2,1)S(1)}, u32[]{:S(2)}, u32[]{:S(2)}) collective-permute-start(bf16[56,640]{1,0:T(8,128)(2,1)S(1)} %get-tuple-element.66), channel_id=1, source_target_pairs={{0,12},{4,8},{8,4},{12,0},{1,13},{5,9},{9,5},{13,1},{2,14},{6,10},... | collective-permute-start | bytes 215048 | tf_op jit(solution)/shard_map/ppermute | solution.py:17
  97.3 14.5 %collective-permute-start.32 = (bf16[112,768]{1,0:T(8,128)(2,1)S(1)}, bf16[112,768]{1,0:T(8,128)(2,1)S(1)}, u32[]{:S(2)}, u32[]{:S(2)}) collective-permute-start(bf16[112,768]{1,0:T(8,128)(2,1)S(1)} %get-tuple-element.86), channel_id=1, source_target_pairs={{0,4},{4,0},{8,12},{12,8},{1,5},{5,1},{9,13},{13,9},{2,6},{6,2},{1... | collective-permute-start | bytes 516104 | tf_op jit(solution)/shard_map/ppermute | solution.py:17
  101.1 7.3 %collective-permute-start.27 = (bf16[56,1024]{1,0:T(8,128)(2,1)S(1)}, bf16[56,1024]{1,0:T(8,128)(2,1)S(1)}, u32[]{:S(2)}, u32[]{:S(2)}) collective-permute-start(bf16[56,1024]{1,0:T(8,128)(2,1)S(1)} %get-tuple-element.74), channel_id=1, source_target_pairs={{0,8},{4,12},{8,0},{12,4},{1,9},{5,13},{9,1},{13,5},{2,10},{6,14},... | collective-permute-start | bytes 344072 | tf_op jit(solution)/shard_map/ppermute | solution.py:17
  101.1 4.7 %collective-permute-start.30 = (bf16[56,768]{1,0:T(8,128)(2,1)S(1)}, bf16[56,768]{1,0:T(8,128)(2,1)S(1)}, u32[]{:S(2)}, u32[]{:S(2)}) collective-permute-start(bf16[56,768]{1,0:T(8,128)(2,1)S(1)} %get-tuple-element.82), channel_id=1, source_target_pairs={{0,2},{1,3},{2,0},{3,1},{4,6},{5,7},{6,4},{7,5},{8,10},{9,11},{10,... | collective-permute-start | bytes 258056 | tf_op jit(solution)/shard_map/ppermute | solution.py:17
  104.4 15.2 %collective-permute-start.20 = (bf16[56,2560]{1,0:T(8,128)(2,1)S(1)}, bf16[56,2560]{1,0:T(8,128)(2,1)S(1)}, u32[]{:S(2)}, u32[]{:S(2)}) collective-permute-start(bf16[56,2560]{1,0:T(8,128)(2,1)S(1)} %spread.1.refs_4_.refs_2_.mine), channel_id=1, source_target_pairs={{16,0},{17,1},{18,2},{19,3},{20,4},{21,5},{22,6},{23,7},{24,8},{25... | collective-permute-start | bytes 860168 | tf_op jit(solution)/shard_map/ppermute | solution.py:646
  108.5 13.3 %collective-permute-start.34 = (bf16[56,1792]{1,0:T(8,128)(2,1)S(1)}, bf16[56,1792]{1,0:T(8,128)(2,1)S(1)}, u32[]{:S(2)}, u32[]{:S(2)}) collective-permute-start(bf16[56,1792]{1,0:T(8,128)(2,1)S(1)} %finish.2.refs_0_), channel_id=1, source_target_pairs={{0,16},{1,17},{2,18},{3,19},{4,20},{5,21},{6,22},{7,23},{8,24},{9,... | collective-permute-start | bytes 602120 | tf_op jit(solution)/shard_map/ppermute | solution.py:650
  111.9 6.4 %collective-permute-start.33 = (bf16[56,768]{1,0:T(8,128)(2,1)S(1)}, bf16[56,768]{1,0:T(8,128)(2,1)S(1)}, u32[]{:S(2)}, u32[]{:S(2)}) collective-permute-start(bf16[56,768]{1,0:T(8,128)(2,1)S(1)} %get-tuple-element.88), channel_id=1, source_target_pairs={{0,8},{4,12},{8,0},{12,4},{1,9},{5,13},{9,1},{13,5},{2,10},{6,14},... | collective-permute-start | bytes 258056 | tf_op jit(solution)/shard_map/ppermute | solution.py:17
  118.3 3.4 %collective-permute-start.35 = (bf16[56,768]{1,0:T(8,128)(2,1)S(1)}, bf16[56,768]{1,0:T(8,128)(2,1)S(1)}, u32[]{:S(2)}, u32[]{:S(2)}) collective-permute-start(bf16[56,768]{1,0:T(8,128)(2,1)S(1)} %finish.3.refs_1_), channel_id=1, source_target_pairs={{0,16},{1,17},{2,18},{3,19},{4,20},{5,21},{6,22},{7,23},{8,24},{9,... | collective-permute-start | bytes 258056 | tf_op jit(solution)/shard_map/ppermute | solution.py:650

commit v5 on v4

--- a/solution.py
+++ b/solution.py
@@ -27,30 +27,32 @@
 
 def unfold_kernel(pairs, imgs, ocols, kd, rows, px, first, step, ids, gains, shifts, *refs):
     w_own, w_other = refs[2 * pairs : 2 * pairs + 2]
-    a_own, a_other, sent, kept = refs[2 * pairs + 2 : 2 * pairs + 6]
-    held_own, held_other, sems = refs[2 * pairs + 9 :]
-    count = held_own.shape[1]
+    a_own, a_other, held_own, held_other, sent, kept = refs[2 * pairs + 2 : 2 * pairs + 8]
+    scratch, partial, sems = refs[2 * pairs + 8 : -2], refs[-2], refs[-1]
+    pieces = sems.shape[0] // 2
+    deep = w_own.shape[0] // pieces
     copies = []
-    for i in range(count // step):
-        here, there = pl.ds(i * step, step), pl.ds(first + i * step, step)
-        copies.append(
-            [
-                pltpu.make_async_copy(w_own.at[:, there], held_own.at[:, here], sems.at[2 * i]),
-                pltpu.make_async_copy(w_other.at[:, there], held_other.at[:, here], sems.at[2 * i + 1]),
-            ]
-        )
-        for copy in copies[i]:
-            copy.start()
-    unfold_rows(pairs, imgs, ocols, kd, ids, gains, shifts, *refs[: 2 * pairs], *refs[2 * pairs + 2 : 2 * pairs + 4],
-                *refs[2 * pairs + 6 : 2 * pairs + 9])
-    for at in range(0, count, step):
-        cut = slice(at, at + step)
-        for copy in copies[at // step]:
-            copy.wait()
-        value = jnp.dot(a_own[...], held_own[:, cut], preferred_element_type=F32)
-        value = value + jnp.dot(a_other[...], held_other[:, cut], preferred_element_type=F32)
-        copy_rows(sent.at[:, cut], value, rows[0], px)
-        copy_rows(kept.at[:, cut], value, rows[1], px)
+    for i in range(2 * pieces):
+        source, target = ((w_own, held_own), (w_other, held_other))[i // pieces]
+        if pieces > 1:
+            some = pl.ds((i % pieces) * deep, deep)
+            source, target = source.at[some], target.at[some]
+        copies.append(pltpu.make_async_copy(source, target, sems.at[i]))
+        copies[i].start()
+    unfold_rows(pairs, imgs, ocols, kd, ids, gains, shifts, *refs[: 2 * pairs], a_own, a_other, *scratch)
+    for copy in copies[:pieces]:
+        copy.wait()
+    count = sent.shape[1]
+    cuts = [slice(first + at, first + at + step) for at in range(0, count, step)]
+    for i, cut in enumerate(cuts):
+        partial[:, i * step : (i + 1) * step] = jnp.dot(a_own[...], held_own[:, cut], preferred_element_type=F32)
+    for copy in copies[pieces:]:
+        copy.wait()
+    for i, cut in enumerate(cuts):
+        here = slice(i * step, (i + 1) * step)
+        value = partial[:, here] + jnp.dot(a_other[...], held_other[:, cut], preferred_element_type=F32)
+        copy_rows(sent.at[:, here], value, rows[0], px)
+        copy_rows(kept.at[:, here], value, rows[1], px)
 
 
 def unfold_rows(pairs, imgs, ocols, kd, ids, gains, shifts, *refs):
@@ -110,11 +112,13 @@
     deep = 9 * kd
     need = 8 * pairs * imgs * px * lanes + 256 * (pairs + 2) * imgs * lanes
     need += 36 * rows * kd + 8 * pairs * imgs * px * lanes
-    limit = (4 << 20) + 2 * need + 4 * deep * count + 8 * rows * count
+    limit = (4 << 20) + need + need // 4 + 8 * rows * count
+    pieces = 3 if deep % 24 == 0 else 1
     sizes = [len(r) * block for r in split]
     return pl.pallas_call(
         functools.partial(unfold_kernel, pairs, imgs, ocols, kd, split, block, first, step),
         out_shape=[pltpu.VMEM((rows, deep), BF16)] * 2
+        + [pltpu.VMEM(w_own.shape, BF16)] * 2
         + [
             jax.ShapeDtypeStruct((sizes[0], count), BF16),
             jax.ShapeDtypeStruct((sizes[1], count), F32),
@@ -122,19 +126,18 @@
         in_specs=[whole(pltpu.SMEM)]
         + [whole()] * (2 + 2 * pairs)
         + [pl.BlockSpec(memory_space=pltpu.HBM)] * 2,
-        out_specs=[whole()] * 4,
+        out_specs=[whole()] * 6,
         scratch_shapes=[
             pltpu.VMEM((pairs, imgs, 2, px, kd), F32),
             pltpu.VMEM((pairs + 2, imgs, 2, 2, ocols, kd), F32),
             pltpu.VMEM((2, 24 + px + 24, kd), F32),
-            pltpu.VMEM((deep, count), BF16),
-            pltpu.VMEM((deep, count), BF16),
-            pltpu.SemaphoreType.DMA((2 * (count // step),)),
+            pltpu.VMEM((rows, count), F32),
+            pltpu.SemaphoreType.DMA((2 * pieces,)),
         ],
         name="unfold",
         compiler_params=pltpu.CompilerParams(vmem_limit_bytes=min(60 << 20, limit)),
         cost_estimate=pl.CostEstimate(
-            flops=4 * rows * deep * count, bytes_accessed=4 * deep * count, transcendentals=0
+            flops=4 * rows * deep * count, bytes_accessed=8 * deep * w_own.shape[1], transcendentals=0
         ),
     )(ids, gain, shift, *own, *other, w_own, w_other)
 
@@ -144,32 +147,31 @@
         out[i * px : (i + 1) * px, :] = value[row * px : (row + 1) * px].astype(out.dtype)
 
 
-def mix_kernel(rows, px, a_own, a_other, w_own, w_other, sent, kept):
-    value = jnp.dot(a_own[...], w_own[...], preferred_element_type=F32)
-    value = value + jnp.dot(a_other[...], w_other[...], preferred_element_type=F32)
-    copy_rows(sent, value, rows[0], px)
-    copy_rows(kept, value, rows[1], px)
+def mix_kernel(rows, px, first, step, a_own, a_other, w_own, w_other, sent, kept):
+    for at in range(0, sent.shape[1], step):
+        cut = slice(first + at, first + at + step)
+        value = jnp.dot(a_own[...], w_own[:, cut], preferred_element_type=F32)
+        value = value + jnp.dot(a_other[...], w_other[:, cut], preferred_element_type=F32)
+        here = slice(at, at + step)
+        copy_rows(sent.at[:, here], value, rows[0], px)
+        copy_rows(kept.at[:, here], value, rows[1], px)
 
 
 def mix(a_own, a_other, w_own, w_other, first, count, step, rows, px):
     total, deep = a_own.shape
-    weight = pl.BlockSpec((deep, step), lambda i: (0, first // step + i))
     sizes = [len(r) * px for r in rows]
     return pl.pallas_call(
-        functools.partial(mix_kernel, rows, px),
-        grid=(count // step,),
+        functools.partial(mix_kernel, rows, px, first, step),
         out_shape=[
             jax.ShapeDtypeStruct((sizes[0], count), BF16),
             jax.ShapeDtypeStruct((sizes[1], count), F32),
         ],
-        in_specs=[whole()] * 2 + [weight] * 2,
-        out_specs=[pl.BlockSpec((size, step), lambda i: (0, i)) for size in sizes],
+        in_specs=[whole()] * 4,
+        out_specs=[whole()] * 2,
         name="mix",
-        compiler_params=pltpu.CompilerParams(vmem_limit_bytes=16 << 20),
+        compiler_params=pltpu.CompilerParams(vmem_limit_bytes=12 << 20),
         cost_estimate=pl.CostEstimate(
-            flops=4 * total * deep * count,
-            bytes_accessed=4 * deep * count + 3 * total * count,
-            transcendentals=0,
+            flops=4 * total * deep * count, bytes_accessed=3 * total * count, transcendentals=0
         ),
     )(a_own, a_other, w_own, w_other)
 
@@ -616,7 +618,7 @@
 
         rows, keys = split(keys, hops[0])
         if j == 0:
-            a_own, a_other, sent, kept = unfold(
+            a_own, a_other, w_own, w_other, sent, kept = unfold(
                 ids,
                 second_gain.reshape(groups * pairs, kc),
                 second_shift.reshape(groups * pairs, kc),

time: 124 us -> 122 us (0.984)
  Pallas kernels: 27 us -> 20.6 us
  local copies, waits for them, and re-layouts: 3.13 us -> 7.05 us
  waiting for transfers between devices: 41 us -> 43.7 us
  starting transfers between devices: 52 us -> 49.7 us
    pallas_call x2, Pallas kernels: 9.08 us -> 4.64 us  [mix(): pl.pallas_call(functools.partial(mix_kernel, rows, px, first, step), out_...]
    ppermute x31, starting transfers between devices: 42.9 us -> 40.2 us  [swap(): return lax.ppermute(array, axis, [(i, i ^ k * unit) for i in range(count)])]
    ppermute x31, waiting for transfers between devices: 39 us -> 41.6 us  [swap(): return lax.ppermute(array, axis, [(i, i ^ k * unit) for i in range(count)])]
    pallas_call x1, Pallas kernels: 10.7 us -> 8.59 us  [unfold(): pl.pallas_call(functools.partial(unfold_kernel, pairs, imgs, ocols, kd, s...]
    unnamed x14 -> x8, local copies, waits for them, and re-layouts: 1.17 us -> 2.66 us
  transfers between devices with their start and end apart: 36 -> 36, of which waited for: 18 -> 19; matrix products, arithmetic and copies ran while one was open for 2% -> 4% of each run, Pallas kernels for 12% -> 8%
where the time goes in v5:
time: 122 us; the launch traced here: 121 us
  starting transfers between devices  49.7 us (41%)
  waiting for transfers between devices  43.7 us (36%)
  Pallas kernels  20.6 us (17%)
  local copies, waits for them, and re-layouts  7.05 us (6%)
    ppermute x31, waiting for transfers between devices, swap(): return lax.ppermute(array, axis, [(i, i ^ k * unit) for i in range(count)])  41.6 us
    ppermute x31, starting transfers between devices, swap(): return lax.ppermute(array, axis, [(i, i ^ k * unit) for i in range(count)])  40.2 us
    pallas_call x1, Pallas kernels, unfold(): pl.pallas_call(functools.partial(unfold_kernel, pairs, imgs, ocols, kd, s...  8.59 us
    ppermute x2, starting transfers between devices, body(): fars.append(lax.ppermute(outs[j], 'section', [(0, 1)]))  5.15 us
    pallas_call x2, Pallas kernels, mix(): pl.pallas_call(functools.partial(mix_kernel, rows, px, first, step), out_...  4.64 us
    unnamed x8, local copies, waits for them, and re-layouts  2.66 us
  transfers between devices with their start and end apart: 36, of which 19 were waited for; matrix products, arithmetic and copies ran while one was open for 4% of the time, Pallas kernels for 8%

profile of v5, /device:TPU:0, one launch (start us, length us, event | category | flops | bytes accessed | tf_op | source)
XLA Modules:
  0.0 121.3 jit_solution(703566072252279097)
XLA Ops:
  0.6 1.1 copy-done.1
  2.4 2.7 %collective-permute-start.11 = (bf16[40,640]{1,0:T(8,128)(2,1)S(1)}, bf16[40,640]{1,0:T(8,128)(2,1)S(1)}, u32[]{:S(2)}, u32[]{:S(2)}) collective-permute-start(bf16[40,640]{1,0:T(8,128)(2,1)S(1)} %get-tuple-element.62), channel_id=1, source_target_pairs={{0,4},{4,0},{8,12},{12,8},{1,5},{5,1},{9,13},{13,9},{2,6},{6,2},{1... | collective-permute-start | bytes 153608 | tf_op jit(solution)/shard_map/ppermute | solution.py:17
  5.1 2.6 %collective-permute-start.12 = (bf16[40,640]{1,0:T(8,128)(2,1)S(1)}, bf16[40,640]{1,0:T(8,128)(2,1)S(1)}, u32[]{:S(2)}, u32[]{:S(2)}) collective-permute-start(bf16[40,640]{1,0:T(8,128)(2,1)S(1)} %get-tuple-element.63), channel_id=1, source_target_pairs={{0,8},{4,12},{8,0},{12,4},{1,9},{5,13},{9,1},{13,5},{2,10},{6,14},... | collective-permute-start | bytes 153608 | tf_op jit(solution)/shard_map/ppermute | solution.py:17
  7.7 1.5 %fusion = (bf16[2,1,28,640]{3,1,2,0:T(2,128)(2,1)S(1)}, bf16[2,1,28,640]{3,1,2,0:T(2,128)(2,1)S(1)}) fusion(bf16[2,8,28,640]{3,1,2,0:T(8,128)(2,1)} %param.8), kind=kLoop, calls=%fused_computation.2 | loop fusion | bytes 286720 | tf_op jit(solution)/shard_map/slice | solution.py:564
  9.3 1.8 %collective-permute-start = (bf16[1,1,28,640]{3,2,1,0:T(8,128)(2,1)S(1)}, bf16[1,1,28,640]{3,2,1,0:T(8,128)(2,1)S(1)}, u32[]{:S(2)}, u32[]{:S(2)}) collective-permute-start(bf16[1,1,28,640]{3,2,1,0:T(8,128)(2,1)S(1)} %copy.13), channel_id=1, source_target_pairs={{0,1},{1,2},{2,3},{4,5},{5,6},{6,7},{8,9},{9,10},{10,11},{12,13},{... | collective-permute-start | bytes 107528 | tf_op jit(solution)/shard_map/ppermute | solution.py:566
  11.2 1.3 %collective-permute-start.1 = (bf16[1,1,28,640]{3,2,1,0:T(8,128)(2,1)S(1)}, bf16[1,1,28,640]{3,2,1,0:T(8,128)(2,1)S(1)}, u32[]{:S(2)}, u32[]{:S(2)}) collective-permute-start(bf16[1,1,28,640]{3,2,1,0:T(8,128)(2,1)S(1)} %copy.15), channel_id=1, source_target_pairs={{1,0},{2,1},{3,2},{5,4},{6,5},{7,6},{9,8},{10,9},{11,10},{13,12},{... | collective-permute-start | bytes 107528 | tf_op jit(solution)/shard_map/ppermute | solution.py:567
  12.5 1.1 collective-permute-done.13.refs_3_
  13.6 3.2 %collective-permute-start.14 = (bf16[4,40,640]{2,1,0:T(8,128)(2,1)S(1)}, bf16[4,40,640]{2,1,0:T(8,128)(2,1)S(1)}, u32[]{:S(2)}, u32[]{:S(2)}) collective-permute-start(bf16[4,40,640]{2,1,0:T(8,128)(2,1)S(1)} %join.1.refs_4_), channel_id=1, source_target_pairs={{0,2},{1,3},{2,0},{3,1},{4,6},{5,7},{6,4},{7,5},{8,10},{9,11},{10,... | collective-permute-start | bytes 614408 | tf_op jit(solution)/shard_map/ppermute | solution.py:17
  16.8 1.1 copy.11.pixels
  19.3 0.9 pack.1
  21.0 3.5 %collective-permute-start.3 = (bf16[416,128]{1,0:T(8,128)(2,1)S(1)}, bf16[416,128]{1,0:T(8,128)(2,1)S(1)}, u32[]{:S(2)}, u32[]{:S(2)}) collective-permute-start(bf16[416,128]{1,0:T(8,128)(2,1)S(1)} %get-tuple-element.54), channel_id=1, source_target_pairs={{0,8},{4,12},{8,0},{12,4},{1,9},{5,13},{9,1},{13,5},{2,10},{6,14},... | collective-permute-start | bytes 319496 | tf_op jit(solution)/shard_map/ppermute | solution.py:17
  24.7 1.5 %collective-permute-done.2.refs_1_ = bf16[416,128]{1,0:T(8,128)(2,1)S(1)} collective-permute-done((bf16[416,128]{1,0:T(8,128)(2,1)S(1)}, bf16[416,128]{1,0:T(8,128)(2,1)S(1)}, u32[]{:S(2)}, u32[]{:S(2)}) %collective-permute-start.2) | collective-permute-done | bytes 106528 | tf_op jit(solution)/shard_map/ppermute | solution.py:17
  26.2 6.4 %collective-permute-done.3.refs_2_ = bf16[416,128]{1,0:T(8,128)(2,1)S(1)} collective-permute-done((bf16[416,128]{1,0:T(8,128)(2,1)S(1)}, bf16[416,128]{1,0:T(8,128)(2,1)S(1)}, u32[]{:S(2)}, u32[]{:S(2)}) %collective-permute-start.3) | collective-permute-done | bytes 106528 | tf_op jit(solution)/shard_map/ppermute | solution.py:17
  32.6 1.5 %copy-done = bf16[3,3,160,640]{3,2,1,0:T(8,128)(2,1)S(1)} copy-done((bf16[3,3,160,640]{3,2,1,0:T(8,128)(2,1)S(1)}, bf16[3,3,160,640]{3,2,1,0:T(8,128)(2,1)}, u32[]{:S(2)}) %copy-start) | copy-done | bytes 1843224
  34.1 1.5 %stage.1 = (f32[56,640]{1,0:T(8,128)S(1)}, bf16[56,640]{1,0:T(8,128)(2,1)S(1)}, bf16[56,640]{1,0:T(8,128)(2,1)S(1)}, bf16[56,640]{1,0:T(8,128)(2,1)S(1)}) custom-call(bf16[416,128]{1,0:T(8,128)(2,1)S(1)} %get-tuple-element.52.refs_0_, bf16[416,128]{1,0:T(8,128)(2,1)S(1)} %collective-permute-done.2.refs_1_, ...), custom_call_target="tpu_custom_call" | custom-call | flops 471859200 | bytes 573440 | tf_op jit(solution)/shard_map/stage/pallas_call | solution.py:522
  35.7 1.8 %collective-permute-start.5 = (bf16[56,640]{1,0:T(8,128)(2,1)S(1)}, bf16[56,640]{1,0:T(8,128)(2,1)S(1)}, u32[]{:S(2)}, u32[]{:S(2)}) collective-permute-start(bf16[56,640]{1,0:T(8,128)(2,1)S(1)} %get-tuple-element.58), channel_id=1, source_target_pairs={{0,4},{4,0},{8,12},{12,8},{1,5},{5,1},{9,13},{13,9},{2,6},{6,2},{1... | collective-permute-start | bytes 215048 | tf_op jit(solution)/shard_map/ppermute | solution.py:17
  37.4 1.3 %collective-permute-start.6 = (bf16[56,640]{1,0:T(8,128)(2,1)S(1)}, bf16[56,640]{1,0:T(8,128)(2,1)S(1)}, u32[]{:S(2)}, u32[]{:S(2)}) collective-permute-start(bf16[56,640]{1,0:T(8,128)(2,1)S(1)} %get-tuple-element.59), channel_id=1, source_target_pairs={{0,8},{4,12},{8,0},{12,4},{1,9},{5,13},{9,1},{13,5},{2,10},{6,14},... | collective-permute-start | bytes 215048 | tf_op jit(solution)/shard_map/ppermute | solution.py:17
  38.8 1.3 %collective-permute-done.5.refs_0_ = bf16[56,640]{1,0:T(8,128)(2,1)S(1)} collective-permute-done((bf16[56,640]{1,0:T(8,128)(2,1)S(1)}, bf16[56,640]{1,0:T(8,128)(2,1)S(1)}, u32[]{:S(2)}, u32[]{:S(2)}) %collective-permute-start.5) | collective-permute-done | bytes 71712 | tf_op jit(solution)/shard_map/ppermute | solution.py:17
  40.1 2.5 %collective-permute-start.7 = (bf16[56,640]{1,0:T(8,128)(2,1)S(1)}, bf16[56,640]{1,0:T(8,128)(2,1)S(1)}, u32[]{:S(2)}, u32[]{:S(2)}) collective-permute-start(bf16[56,640]{1,0:T(8,128)(2,1)S(1)} %get-tuple-element.60), channel_id=1, source_target_pairs={{0,12},{4,8},{8,4},{12,0},{1,13},{5,9},{9,5},{13,1},{2,14},{6,10},... | collective-permute-start | bytes 215048 | tf_op jit(solution)/shard_map/ppermute | solution.py:17
  42.5 2.8 %collective-permute-done.6.refs_1_ = bf16[56,640]{1,0:T(8,128)(2,1)S(1)} collective-permute-done((bf16[56,640]{1,0:T(8,128)(2,1)S(1)}, bf16[56,640]{1,0:T(8,128)(2,1)S(1)}, u32[]{:S(2)}, u32[]{:S(2)}) %collective-permute-start.6) | collective-permute-done | bytes 71712 | tf_op jit(solution)/shard_map/ppermute | solution.py:17
  45.3 0.9 collective-permute-done.7.refs_2_
  46.3 2.5 %collective-permute-start.10 = (bf16[56,640]{1,0:T(8,128)(2,1)S(1)}, bf16[56,640]{1,0:T(8,128)(2,1)S(1)}, u32[]{:S(2)}, u32[]{:S(2)}) collective-permute-start(bf16[56,640]{1,0:T(8,128)(2,1)S(1)} %pool.1.refs_0_), channel_id=1, source_target_pairs={{0,12},{4,8},{8,4},{12,0},{1,13},{5,9},{9,5},{13,1},{2,14},{6,10},... | collective-permute-start | bytes 215048 | tf_op jit(solution)/shard_map/ppermute | solution.py:17
  49.6 1.2 collective-permute-start.9
  50.8 2.6 %collective-permute-done.10.refs_3_ = bf16[56,640]{1,0:T(8,128)(2,1)S(1)} collective-permute-done((bf16[56,640]{1,0:T(8,128)(2,1)S(1)}, bf16[56,640]{1,0:T(8,128)(2,1)S(1)}, u32[]{:S(2)}, u32[]{:S(2)}) %collective-permute-start.10) | collective-permute-done | bytes 71712 | tf_op jit(solution)/shard_map/ppermute | solution.py:17
  53.4 1.7 %collective-permute-done.8.refs_1_ = bf16[56,640]{1,0:T(8,128)(2,1)S(1)} collective-permute-done((bf16[56,640]{1,0:T(8,128)(2,1)S(1)}, bf16[56,640]{1,0:T(8,128)(2,1)S(1)}, u32[]{:S(2)}, u32[]{:S(2)}) %collective-permute-start.8) | collective-permute-done | bytes 71712 | tf_op jit(solution)/shard_map/ppermute | solution.py:17
  55.0 0.8 collective-permute-done.9.refs_2_
  55.8 1.2 %project.1 = (bf16[56,640]{1,0:T(8,128)(2,1)S(1)}, bf16[56,640]{1,0:T(8,128)(2,1)S(1)}, bf16[56,640]{1,0:T(8,128)(2,1)S(1)}, bf16[56,640]{1,0:T(8,128)(2,1)S(1)}...) custom-call(s32[7]{0:T(128)S(1)} %stack.27.ids, bf16[56,640]{1,0:T(8,128)(2,1)S(1)} %pool.1.refs_0_, ...), custom_call_target="tpu_custom_call" | custom-call | flops 183500800 | bytes 1638400 | tf_op jit(solution)/shard_map/project/pallas_call | solution.py:290
  57.6 4.9 %collective-permute-done.21 = bf16[224,320]{1,0:T(8,128)(2,1)S(1)} collective-permute-done((bf16[224,320]{1,0:T(8,128)(2,1)S(1)}, bf16[224,320]{1,0:T(8,128)(2,1)S(1)}, u32[]{:S(2)}, u32[]{:S(2)}) %collective-permute-start.21) | collective-permute-done | bytes 143392 | tf_op jit(solution)/shard_map/ppermute | solution.py:17
  62.7 1.2 %collective-permute-done.23 = bf16[224,320]{1,0:T(8,128)(2,1)S(1)} collective-permute-done((bf16[224,320]{1,0:T(8,128)(2,1)S(1)}, bf16[224,320]{1,0:T(8,128)(2,1)S(1)}, u32[]{:S(2)}, u32[]{:S(2)}) %collective-permute-start.23) | collective-permute-done | bytes 143392 | tf_op jit(solution)/shard_map/ppermute | solution.py:17
  63.9 8.6 %unfold.1 = (bf16[448,1440]{1,0:T(8,128)(2,1)S(1)}, bf16[448,1440]{1,0:T(8,128)(2,1)S(1)}, bf16[1440,2560]{1,0:T(8,128)(2,1)S(1)}, bf16[1440,2560]{1,0:T(8,128)(...) custom-call(s32[7]{0:T(128)S(1)} %stack.27.ids, f32[8,320]{1,0:T(8,128)S(1)} %reshape.36.gains, ...), custom_call_target="tpu_custom_call" | custom-call | flops 2642411520 | bytes 29491200 | tf_op jit(solution)/shard_map/unfold/pallas_call | solution.py:118
  73.1 2.3 %mix.2 = (bf16[224,768]{1,0:T(8,128)(2,1)S(1)}, f32[224,768]{1,0:T(8,128)S(1)}) custom-call(bf16[448,1440]{1,0:T(8,128)(2,1)S(1)} %get-tuple-element.77.a_own, bf16[448,1440]{1,0:T(8,128)(2,1)S(1)} %get-tuple-element.78.a_other, bf16[1440,2560]{1,0:T(8,128)(2,1)S(1)} %get-tuple-element.79.w_own, bf16[1440,2560]{1,0:T(8,128)(2,1)S(1)} %get-tuple-element.80.w_other), custom_call_target="tpu_custom_call" | custom-call | flops 1981808640 | bytes 1032192 | tf_op jit(solution)/shard_map/mix/pallas_call | solution.py:163
  75.8 2.3 %mix.3 = (bf16[224,768]{1,0:T(8,128)(2,1)S(1)}, f32[224,768]{1,0:T(8,128)S(1)}) custom-call(bf16[448,1440]{1,0:T(8,128)(2,1)S(1)} %get-tuple-element.77.a_own, bf16[448,1440]{1,0:T(8,128)(2,1)S(1)} %get-tuple-element.78.a_other, bf16[1440,2560]{1,0:T(8,128)(2,1)S(1)} %get-tuple-element.79.w_own, bf16[1440,2560]{1,0:T(8,128)(2,1)S(1)} %get-tuple-element.80.w_other), custom_call_target="tpu_custom_call" | custom-call | flops 1981808640 | bytes 1032192 | tf_op jit(solution)/shard_map/mix/pallas_call | solution.py:163
  78.1 1.7 %collective-permute-start.31 = (bf16[224,768]{1,0:T(8,128)(2,1)S(1)}, bf16[224,768]{1,0:T(8,128)(2,1)S(1)}, u32[]{:S(2)}, u32[]{:S(2)}) collective-permute-start(bf16[224,768]{1,0:T(8,128)(2,1)S(1)} %get-tuple-element.88), channel_id=1, source_target_pairs={{0,2},{1,3},{2,0},{3,1},{4,6},{5,7},{6,4},{7,5},{8,10},{9,11},{10,... | collective-permute-start | bytes 1032200 | tf_op jit(solution)/shard_map/ppermute | solution.py:17
  79.9 6.1 %collective-permute-done.25.came = bf16[224,1024]{1,0:T(8,128)(2,1)S(1)} collective-permute-done((bf16[224,1024]{1,0:T(8,128)(2,1)S(1)}, bf16[224,1024]{1,0:T(8,128)(2,1)S(1)}, u32[]{:S(2)}, u32[]{:S(2)}) %collective-permute-start.25) | collective-permute-done | bytes 458784 | tf_op jit(solution)/shard_map/ppermute | solution.py:17
  86.7 3.1 %collective-permute-start.29 = (bf16[112,768]{1,0:T(8,128)(2,1)S(1)}, bf16[112,768]{1,0:T(8,128)(2,1)S(1)}, u32[]{:S(2)}, u32[]{:S(2)}) collective-permute-start(bf16[112,768]{1,0:T(8,128)(2,1)S(1)} %get-tuple-element.84), channel_id=1, source_target_pairs={{0,8},{4,12},{8,0},{12,4},{1,9},{5,13},{9,1},{13,5},{2,10},{6,14},... | collective-permute-start | bytes 516104 | tf_op jit(solution)/shard_map/ppermute | solution.py:17
  89.8 1.5 %collective-permute-start.18 = (bf16[56,640]{1,0:T(8,128)(2,1)S(1)}, bf16[56,640]{1,0:T(8,128)(2,1)S(1)}, u32[]{:S(2)}, u32[]{:S(2)}) collective-permute-start(bf16[56,640]{1,0:T(8,128)(2,1)S(1)} %get-tuple-element.67), channel_id=1, source_target_pairs={{0,8},{4,12},{8,0},{12,4},{1,9},{5,13},{9,1},{13,5},{2,10},{6,14},... | collective-permute-start | bytes 215048 | tf_op jit(solution)/shard_map/ppermute | solution.py:17
  91.2 1.3 %collective-permute-done.31.came = bf16[224,768]{1,0:T(8,128)(2,1)S(1)} collective-permute-done((bf16[224,768]{1,0:T(8,128)(2,1)S(1)}, bf16[224,768]{1,0:T(8,128)(2,1)S(1)}, u32[]{:S(2)}, u32[]{:S(2)}) %collective-permute-start.31) | collective-permute-done | bytes 344096 | tf_op jit(solution)/shard_map/ppermute | solution.py:17
  92.5 2.9 %collective-permute-start.19 = (bf16[56,640]{1,0:T(8,128)(2,1)S(1)}, bf16[56,640]{1,0:T(8,128)(2,1)S(1)}, u32[]{:S(2)}, u32[]{:S(2)}) collective-permute-start(bf16[56,640]{1,0:T(8,128)(2,1)S(1)} %get-tuple-element.68), channel_id=1, source_target_pairs={{0,12},{4,8},{8,4},{12,0},{1,13},{5,9},{9,5},{13,1},{2,14},{6,10},... | collective-permute-start | bytes 215048 | tf_op jit(solution)/shard_map/ppermute | solution.py:17
  95.5 1.6 %collective-permute-done.26.came = bf16[112,1024]{1,0:T(8,128)(2,1)S(1)} collective-permute-done((bf16[112,1024]{1,0:T(8,128)(2,1)S(1)}, bf16[112,1024]{1,0:T(8,128)(2,1)S(1)}, u32[]{:S(2)}, u32[]{:S(2)}) %collective-permute-start.26) | collective-permute-done | bytes 229408 | tf_op jit(solution)/shard_map/ppermute | solution.py:17
  97.1 2.9 %collective-permute-done.29.came = bf16[112,768]{1,0:T(8,128)(2,1)S(1)} collective-permute-done((bf16[112,768]{1,0:T(8,128)(2,1)S(1)}, bf16[112,768]{1,0:T(8,128)(2,1)S(1)}, u32[]{:S(2)}, u32[]{:S(2)}) %collective-permute-start.29) | collective-permute-done | bytes 172064 | tf_op jit(solution)/shard_map/ppermute | solution.py:17
  100.7 2.6 %collective-permute-start.30 = (bf16[56,768]{1,0:T(8,128)(2,1)S(1)}, bf16[56,768]{1,0:T(8,128)(2,1)S(1)}, u32[]{:S(2)}, u32[]{:S(2)}) collective-permute-start(bf16[56,768]{1,0:T(8,128)(2,1)S(1)} %get-tuple-element.86), channel_id=1, source_target_pairs={{0,2},{1,3},{2,0},{3,1},{4,6},{5,7},{6,4},{7,5},{8,10},{9,11},{10,... | collective-permute-start | bytes 258056 | tf_op jit(solution)/shard_map/ppermute | solution.py:17
  104.5 1.3 %collective-permute-start.20 = (bf16[56,2560]{1,0:T(8,128)(2,1)S(1)}, bf16[56,2560]{1,0:T(8,128)(2,1)S(1)}, u32[]{:S(2)}, u32[]{:S(2)}) collective-permute-start(bf16[56,2560]{1,0:T(8,128)(2,1)S(1)} %spread.1.refs_4_.refs_2_.mine), channel_id=1, source_target_pairs={{16,0},{17,1},{18,2},{19,3},{20,4},{21,5},{22,6},{23,7},{24,8},{25... | collective-permute-start | bytes 860168 | tf_op jit(solution)/shard_map/ppermute | solution.py:648
  106.7 3.9 %collective-permute-start.34 = (bf16[56,1792]{1,0:T(8,128)(2,1)S(1)}, bf16[56,1792]{1,0:T(8,128)(2,1)S(1)}, u32[]{:S(2)}, u32[]{:S(2)}) collective-permute-start(bf16[56,1792]{1,0:T(8,128)(2,1)S(1)} %finish.2.refs_0_), channel_id=1, source_target_pairs={{0,16},{1,17},{2,18},{3,19},{4,20},{5,21},{6,22},{7,23},{8,24},{9,... | collective-permute-start | bytes 602120 | tf_op jit(solution)/shard_map/ppermute | solution.py:652
  110.6 2.4 %collective-permute-start.33 = (bf16[56,768]{1,0:T(8,128)(2,1)S(1)}, bf16[56,768]{1,0:T(8,128)(2,1)S(1)}, u32[]{:S(2)}, u32[]{:S(2)}) collective-permute-start(bf16[56,768]{1,0:T(8,128)(2,1)S(1)} %get-tuple-element.92), channel_id=1, source_target_pairs={{0,8},{4,12},{8,0},{12,4},{1,9},{5,13},{9,1},{13,5},{2,10},{6,14},... | collective-permute-start | bytes 258056 | tf_op jit(solution)/shard_map/ppermute | solution.py:17
  113.0 3.0 %collective-permute-done.33.refs_1_ = bf16[56,768]{1,0:T(8,128)(2,1)S(1)} collective-permute-done((bf16[56,768]{1,0:T(8,128)(2,1)S(1)}, bf16[56,768]{1,0:T(8,128)(2,1)S(1)}, u32[]{:S(2)}, u32[]{:S(2)}) %collective-permute-start.33) | collective-permute-done | bytes 86048 | tf_op jit(solution)/shard_map/ppermute | solution.py:17
  116.1 1.3 %collective-permute-start.35 = (bf16[56,768]{1,0:T(8,128)(2,1)S(1)}, bf16[56,768]{1,0:T(8,128)(2,1)S(1)}, u32[]{:S(2)}, u32[]{:S(2)}) collective-permute-start(bf16[56,768]{1,0:T(8,128)(2,1)S(1)} %finish.3.refs_1_), channel_id=1, source_target_pairs={{0,16},{1,17},{2,18},{3,19},{4,20},{5,21},{6,22},{7,23},{8,24},{9,... | collective-permute-start | bytes 258056 | tf_op jit(solution)/shard_map/ppermute | solution.py:652
  117.4 2.1 %collective-permute-done.35.refs_3_ = bf16[56,768]{1,0:T(8,128)(2,1)S(1)} collective-permute-done((bf16[56,768]{1,0:T(8,128)(2,1)S(1)}, bf16[56,768]{1,0:T(8,128)(2,1)S(1)}, u32[]{:S(2)}, u32[]{:S(2)}) %collective-permute-start.35) | collective-permute-done | bytes 86048 | tf_op jit(solution)/shard_map/ppermute | solution.py:652
  119.4 1.8 %final.1 = bf16[2,14,4,2560]{3,2,1,0:T(4,128)(2,1)} custom-call(s32[7]{0:T(128)S(1)} %stack.27.ids, bf16[56,2560]{1,0:T(8,128)(2,1)S(1)} %spread.1.refs_4_.refs_2_.mine, bf16[56,2560]{1,0:T(8,128)(2,1)S(1)} %collective-permute-done.20.far_mine, bf16[56,1792]{1,0:T(8,128)(2,1)S(1)} %finish.2.refs_0_, bf16[56,768]{1,0:T(8,128)(2,1)S(1)} %finish.3.refs_1_, ...), custom_call_target="tpu_custom_call" | custom-call | tf_op jit(solution)/shard_map/final/pallas_call | solution.py:386
  (61 shorter events, 9.8 us)
Async XLA Ops:
  0.0 62.5 %copy-start.2 = (f32[2560]{0:T(1024)S(1)}, f32[2560]{0:T(1024)}, u32[]{:S(2)}) copy-start(f32[2560]{0:T(1024)} %param.13) | copy-start | bytes 30724
  0.0 62.6 %copy-start.3 = (f32[2560]{0:T(1024)S(1)}, f32[2560]{0:T(1024)}, u32[]{:S(2)}) copy-start(f32[2560]{0:T(1024)} %param.14) | copy-start | bytes 30724
  0.0 63.9 %collective-permute-start.24 = (bf16[3,3,160,2560]{3,2,1,0:T(8,128)(2,1)}, bf16[3,3,160,2560]{3,2,1,0:T(8,128)(2,1)}, u32[]{:S(2)}, u32[]{:S(2)}) collective-permute-start(bf16[3,3,160,2560]{3,2,1,0:T(8,128)(2,1)} %param.15), channel_id=1, source_target_pairs={{0,1},{1,0},{2,3},{3,2},{4,5},{5,4},{6,7},{7,6},{8,9},{9,8},{10,11... | collective-permute-start | bytes 22118408 | tf_op jit(solution)/shard_map/ppermute | solution.py:17
  0.6 1.1 copy-start.1
  2.4 8.8 %collective-permute-start.11 = (bf16[40,640]{1,0:T(8,128)(2,1)S(1)}, bf16[40,640]{1,0:T(8,128)(2,1)S(1)}, u32[]{:S(2)}, u32[]{:S(2)}) collective-permute-start(bf16[40,640]{1,0:T(8,128)(2,1)S(1)} %get-tuple-element.62), channel_id=1, source_target_pairs={{0,4},{4,0},{8,12},{12,8},{1,5},{5,1},{9,13},{13,9},{2,6},{6,2},{1... | collective-permute-start | bytes 153608 | tf_op jit(solution)/shard_map/ppermute | solution.py:17
  5.1 7.4 %collective-permute-start.12 = (bf16[40,640]{1,0:T(8,128)(2,1)S(1)}, bf16[40,640]{1,0:T(8,128)(2,1)S(1)}, u32[]{:S(2)}, u32[]{:S(2)}) collective-permute-start(bf16[40,640]{1,0:T(8,128)(2,1)S(1)} %get-tuple-element.63), channel_id=1, source_target_pairs={{0,8},{4,12},{8,0},{12,4},{1,9},{5,13},{9,1},{13,5},{2,10},{6,14},... | collective-permute-start | bytes 153608 | tf_op jit(solution)/shard_map/ppermute | solution.py:17
  7.7 5.9 %collective-permute-start.13 = (bf16[40,640]{1,0:T(8,128)(2,1)S(1)}, bf16[40,640]{1,0:T(8,128)(2,1)S(1)}, u32[]{:S(2)}, u32[]{:S(2)}) collective-permute-start(bf16[40,640]{1,0:T(8,128)(2,1)S(1)} %get-tuple-element.64), channel_id=1, source_target_pairs={{0,12},{4,8},{8,4},{12,0},{1,13},{5,9},{9,5},{13,1},{2,14},{6,10},... | collective-permute-start | bytes 153608 | tf_op jit(solution)/shard_map/ppermute | solution.py:17
  9.3 10.0 %collective-permute-start = (bf16[1,1,28,640]{3,2,1,0:T(8,128)(2,1)S(1)}, bf16[1,1,28,640]{3,2,1,0:T(8,128)(2,1)S(1)}, u32[]{:S(2)}, u32[]{:S(2)}) collective-permute-start(bf16[1,1,28,640]{3,2,1,0:T(8,128)(2,1)S(1)} %copy.13), channel_id=1, source_target_pairs={{0,1},{1,2},{2,3},{4,5},{5,6},{6,7},{8,9},{9,10},{10,11},{12,13},{... | collective-permute-start | bytes 107528 | tf_op jit(solution)/shard_map/ppermute | solution.py:566
  11.2 8.1 %collective-permute-start.1 = (bf16[1,1,28,640]{3,2,1,0:T(8,128)(2,1)S(1)}, bf16[1,1,28,640]{3,2,1,0:T(8,128)(2,1)S(1)}, u32[]{:S(2)}, u32[]{:S(2)}) collective-permute-start(bf16[1,1,28,640]{3,2,1,0:T(8,128)(2,1)S(1)} %copy.15), channel_id=1, source_target_pairs={{1,0},{2,1},{3,2},{5,4},{6,5},{7,6},{9,8},{10,9},{11,10},{13,12},{... | collective-permute-start | bytes 107528 | tf_op jit(solution)/shard_map/ppermute | solution.py:567
  13.6 23.8 %collective-permute-start.14 = (bf16[4,40,640]{2,1,0:T(8,128)(2,1)S(1)}, bf16[4,40,640]{2,1,0:T(8,128)(2,1)S(1)}, u32[]{:S(2)}, u32[]{:S(2)}) collective-permute-start(bf16[4,40,640]{2,1,0:T(8,128)(2,1)S(1)} %join.1.refs_4_), channel_id=1, source_target_pairs={{0,2},{1,3},{2,0},{3,1},{4,6},{5,7},{6,4},{7,5},{8,10},{9,11},{10,... | collective-permute-start | bytes 614408 | tf_op jit(solution)/shard_map/ppermute | solution.py:17
  20.2 6.0 %collective-permute-start.2 = (bf16[416,128]{1,0:T(8,128)(2,1)S(1)}, bf16[416,128]{1,0:T(8,128)(2,1)S(1)}, u32[]{:S(2)}, u32[]{:S(2)}) collective-permute-start(bf16[416,128]{1,0:T(8,128)(2,1)S(1)} %get-tuple-element.53), channel_id=1, source_target_pairs={{0,4},{4,0},{8,12},{12,8},{1,5},{5,1},{9,13},{13,9},{2,6},{6,2},{1... | collective-permute-start | bytes 319496 | tf_op jit(solution)/shard_map/ppermute | solution.py:17
  21.0 11.6 %collective-permute-start.3 = (bf16[416,128]{1,0:T(8,128)(2,1)S(1)}, bf16[416,128]{1,0:T(8,128)(2,1)S(1)}, u32[]{:S(2)}, u32[]{:S(2)}) collective-permute-start(bf16[416,128]{1,0:T(8,128)(2,1)S(1)} %get-tuple-element.54), channel_id=1, source_target_pairs={{0,8},{4,12},{8,0},{12,4},{1,9},{5,13},{9,1},{13,5},{2,10},{6,14},... | collective-permute-start | bytes 319496 | tf_op jit(solution)/shard_map/ppermute | solution.py:17
  24.5 8.1 %collective-permute-start.4 = (bf16[416,128]{1,0:T(8,128)(2,1)S(1)}, bf16[416,128]{1,0:T(8,128)(2,1)S(1)}, u32[]{:S(2)}, u32[]{:S(2)}) collective-permute-start(bf16[416,128]{1,0:T(8,128)(2,1)S(1)} %get-tuple-element.55), channel_id=1, source_target_pairs={{0,12},{4,8},{8,4},{12,0},{1,13},{5,9},{9,5},{13,1},{2,14},{6,10},... | collective-permute-start | bytes 319496 | tf_op jit(solution)/shard_map/ppermute | solution.py:17
  26.2 23.4 %collective-permute-start.15 = (bf16[4,40,640]{2,1,0:T(8,128)(2,1)S(1)}, bf16[4,40,640]{2,1,0:T(8,128)(2,1)S(1)}, u32[]{:S(2)}, u32[]{:S(2)}) collective-permute-start(bf16[4,40,640]{2,1,0:T(8,128)(2,1)S(1)} %join.1.refs_4_), channel_id=1, source_target_pairs={{0,1},{1,0},{2,3},{3,2},{4,5},{5,4},{6,7},{7,6},{8,9},{9,8},{10,11... | collective-permute-start | bytes 614408 | tf_op jit(solution)/shard_map/ppermute | solution.py:17
  32.6 1.5 %copy-start = (bf16[3,3,160,640]{3,2,1,0:T(8,128)(2,1)S(1)}, bf16[3,3,160,640]{3,2,1,0:T(8,128)(2,1)}, u32[]{:S(2)}) copy-start(bf16[3,3,160,640]{3,2,1,0:T(8,128)(2,1)} %param.11) | copy-start | bytes 5529604
  35.7 4.4 %collective-permute-start.5 = (bf16[56,640]{1,0:T(8,128)(2,1)S(1)}, bf16[56,640]{1,0:T(8,128)(2,1)S(1)}, u32[]{:S(2)}, u32[]{:S(2)}) collective-permute-start(bf16[56,640]{1,0:T(8,128)(2,1)S(1)} %get-tuple-element.58), channel_id=1, source_target_pairs={{0,4},{4,0},{8,12},{12,8},{1,5},{5,1},{9,13},{13,9},{2,6},{6,2},{1... | collective-permute-start | bytes 215048 | tf_op jit(solution)/shard_map/ppermute | solution.py:17
  37.4 18.4 %collective-permute-start.16 = (bf16[4,40,640]{2,1,0:T(8,128)(2,1)S(1)}, bf16[4,40,640]{2,1,0:T(8,128)(2,1)S(1)}, u32[]{:S(2)}, u32[]{:S(2)}) collective-permute-start(bf16[4,40,640]{2,1,0:T(8,128)(2,1)S(1)} %collective-permute-done.14.refs_5_), channel_id=1, source_target_pairs={{0,1},{1,0},{2,3},{3,2},{4,5},{5,4},{6,7},{7,6},{8,9},{9,8},{10,11... | collective-permute-start | bytes 614408 | tf_op jit(solution)/shard_map/ppermute | solution.py:17
  37.4 7.9 %collective-permute-start.6 = (bf16[56,640]{1,0:T(8,128)(2,1)S(1)}, bf16[56,640]{1,0:T(8,128)(2,1)S(1)}, u32[]{:S(2)}, u32[]{:S(2)}) collective-permute-start(bf16[56,640]{1,0:T(8,128)(2,1)S(1)} %get-tuple-element.59), channel_id=1, source_target_pairs={{0,8},{4,12},{8,0},{12,4},{1,9},{5,13},{9,1},{13,5},{2,10},{6,14},... | collective-permute-start | bytes 215048 | tf_op jit(solution)/shard_map/ppermute | solution.py:17
  40.1 6.2 %collective-permute-start.7 = (bf16[56,640]{1,0:T(8,128)(2,1)S(1)}, bf16[56,640]{1,0:T(8,128)(2,1)S(1)}, u32[]{:S(2)}, u32[]{:S(2)}) collective-permute-start(bf16[56,640]{1,0:T(8,128)(2,1)S(1)} %get-tuple-element.60), channel_id=1, source_target_pairs={{0,12},{4,8},{8,4},{12,0},{1,13},{5,9},{9,5},{13,1},{2,14},{6,10},... | collective-permute-start | bytes 215048 | tf_op jit(solution)/shard_map/ppermute | solution.py:17
  46.3 7.1 %collective-permute-start.10 = (bf16[56,640]{1,0:T(8,128)(2,1)S(1)}, bf16[56,640]{1,0:T(8,128)(2,1)S(1)}, u32[]{:S(2)}, u32[]{:S(2)}) collective-permute-start(bf16[56,640]{1,0:T(8,128)(2,1)S(1)} %pool.1.refs_0_), channel_id=1, source_target_pairs={{0,12},{4,8},{8,4},{12,0},{1,13},{5,9},{9,5},{13,1},{2,14},{6,10},... | collective-permute-start | bytes 215048 | tf_op jit(solution)/shard_map/ppermute | solution.py:17
  48.9 6.2 %collective-permute-start.8 = (bf16[56,640]{1,0:T(8,128)(2,1)S(1)}, bf16[56,640]{1,0:T(8,128)(2,1)S(1)}, u32[]{:S(2)}, u32[]{:S(2)}) collective-permute-start(bf16[56,640]{1,0:T(8,128)(2,1)S(1)} %pool.1.refs_0_), channel_id=1, source_target_pairs={{0,4},{4,0},{8,12},{12,8},{1,5},{5,1},{9,13},{13,9},{2,6},{6,2},{1... | collective-permute-start | bytes 215048 | tf_op jit(solution)/shard_map/ppermute | solution.py:17
  49.6 6.2 %collective-permute-start.9 = (bf16[56,640]{1,0:T(8,128)(2,1)S(1)}, bf16[56,640]{1,0:T(8,128)(2,1)S(1)}, u32[]{:S(2)}, u32[]{:S(2)}) collective-permute-start(bf16[56,640]{1,0:T(8,128)(2,1)S(1)} %pool.1.refs_0_), channel_id=1, source_target_pairs={{0,8},{4,12},{8,0},{12,4},{1,9},{5,13},{9,1},{13,5},{2,10},{6,14},... | collective-permute-start | bytes 215048 | tf_op jit(solution)/shard_map/ppermute | solution.py:17
  57.1 5.5 %collective-permute-start.21 = (bf16[224,320]{1,0:T(8,128)(2,1)S(1)}, bf16[224,320]{1,0:T(8,128)(2,1)S(1)}, u32[]{:S(2)}, u32[]{:S(2)}) collective-permute-start(bf16[224,320]{1,0:T(8,128)(2,1)S(1)} %get-tuple-element.70), channel_id=1, source_target_pairs={{0,2},{1,3},{2,0},{3,1},{4,6},{5,7},{6,4},{7,5},{8,10},{9,11},{10,... | collective-permute-start | bytes 430088 | tf_op jit(solution)/shard_map/ppermute | solution.py:17
  57.6 5.1 %collective-permute-start.22 = (bf16[224,320]{1,0:T(8,128)(2,1)S(1)}, bf16[224,320]{1,0:T(8,128)(2,1)S(1)}, u32[]{:S(2)}, u32[]{:S(2)}) collective-permute-start(bf16[224,320]{1,0:T(8,128)(2,1)S(1)} %get-tuple-element.69), channel_id=1, source_target_pairs={{0,1},{1,0},{2,3},{3,2},{4,5},{5,4},{6,7},{7,6},{8,9},{9,8},{10,11... | collective-permute-start | bytes 430088 | tf_op jit(solution)/shard_map/ppermute | solution.py:17
  62.5 1.4 %collective-permute-start.23 = (bf16[224,320]{1,0:T(8,128)(2,1)S(1)}, bf16[224,320]{1,0:T(8,128)(2,1)S(1)}, u32[]{:S(2)}, u32[]{:S(2)}) collective-permute-start(bf16[224,320]{1,0:T(8,128)(2,1)S(1)} %collective-permute-done.21), channel_id=1, source_target_pairs={{0,1},{1,0},{2,3},{3,2},{4,5},{5,4},{6,7},{7,6},{8,9},{9,8},{10,11... | collective-permute-start | bytes 430088 | tf_op jit(solution)/shard_map/ppermute | solution.py:17
  72.5 13.5 %collective-permute-start.25 = (bf16[224,1024]{1,0:T(8,128)(2,1)S(1)}, bf16[224,1024]{1,0:T(8,128)(2,1)S(1)}, u32[]{:S(2)}, u32[]{:S(2)}) collective-permute-start(bf16[224,1024]{1,0:T(8,128)(2,1)S(1)} %get-tuple-element.72), channel_id=1, source_target_pairs={{0,2},{1,3},{2,0},{3,1},{4,6},{5,7},{6,4},{7,5},{8,10},{9,11},{10,... | collective-permute-start | bytes 1376264 | tf_op jit(solution)/shard_map/ppermute | solution.py:17
  75.4 11.2 %collective-permute-start.28 = (bf16[224,768]{1,0:T(8,128)(2,1)S(1)}, bf16[224,768]{1,0:T(8,128)(2,1)S(1)}, u32[]{:S(2)}, u32[]{:S(2)}) collective-permute-start(bf16[224,768]{1,0:T(8,128)(2,1)S(1)} %get-tuple-element.82), channel_id=1, source_target_pairs={{0,4},{4,0},{8,12},{12,8},{1,5},{5,1},{9,13},{13,9},{2,6},{6,2},{1... | collective-permute-start | bytes 1032200 | tf_op jit(solution)/shard_map/ppermute | solution.py:17
  78.1 14.4 %collective-permute-start.31 = (bf16[224,768]{1,0:T(8,128)(2,1)S(1)}, bf16[224,768]{1,0:T(8,128)(2,1)S(1)}, u32[]{:S(2)}, u32[]{:S(2)}) collective-permute-start(bf16[224,768]{1,0:T(8,128)(2,1)S(1)} %get-tuple-element.88), channel_id=1, source_target_pairs={{0,2},{1,3},{2,0},{3,1},{4,6},{5,7},{6,4},{7,5},{8,10},{9,11},{10,... | collective-permute-start | bytes 1032200 | tf_op jit(solution)/shard_map/ppermute | solution.py:17
  86.1 11.0 %collective-permute-start.26 = (bf16[112,1024]{1,0:T(8,128)(2,1)S(1)}, bf16[112,1024]{1,0:T(8,128)(2,1)S(1)}, u32[]{:S(2)}, u32[]{:S(2)}) collective-permute-start(bf16[112,1024]{1,0:T(8,128)(2,1)S(1)} %get-tuple-element.74), channel_id=1, source_target_pairs={{0,4},{4,0},{8,12},{12,8},{1,5},{5,1},{9,13},{13,9},{2,6},{6,2},{1... | collective-permute-start | bytes 688136 | tf_op jit(solution)/shard_map/ppermute | solution.py:17
  86.7 13.4 %collective-permute-start.29 = (bf16[112,768]{1,0:T(8,128)(2,1)S(1)}, bf16[112,768]{1,0:T(8,128)(2,1)S(1)}, u32[]{:S(2)}, u32[]{:S(2)}) collective-permute-start(bf16[112,768]{1,0:T(8,128)(2,1)S(1)} %get-tuple-element.84), channel_id=1, source_target_pairs={{0,8},{4,12},{8,0},{12,4},{1,9},{5,13},{9,1},{13,5},{2,10},{6,14},... | collective-permute-start | bytes 516104 | tf_op jit(solution)/shard_map/ppermute | solution.py:17
  89.7 10.9 %collective-permute-start.17 = (bf16[56,640]{1,0:T(8,128)(2,1)S(1)}, bf16[56,640]{1,0:T(8,128)(2,1)S(1)}, u32[]{:S(2)}, u32[]{:S(2)}) collective-permute-start(bf16[56,640]{1,0:T(8,128)(2,1)S(1)} %get-tuple-element.66), channel_id=1, source_target_pairs={{0,4},{4,0},{8,12},{12,8},{1,5},{5,1},{9,13},{13,9},{2,6},{6,2},{1... | collective-permute-start | bytes 215048 | tf_op jit(solution)/shard_map/ppermute | solution.py:17
  89.8 13.5 %collective-permute-start.18 = (bf16[56,640]{1,0:T(8,128)(2,1)S(1)}, bf16[56,640]{1,0:T(8,128)(2,1)S(1)}, u32[]{:S(2)}, u32[]{:S(2)}) collective-permute-start(bf16[56,640]{1,0:T(8,128)(2,1)S(1)} %get-tuple-element.67), channel_id=1, source_target_pairs={{0,8},{4,12},{8,0},{12,4},{1,9},{5,13},{9,1},{13,5},{2,10},{6,14},... | collective-permute-start | bytes 215048 | tf_op jit(solution)/shard_map/ppermute | solution.py:17
  92.5 11.4 %collective-permute-start.19 = (bf16[56,640]{1,0:T(8,128)(2,1)S(1)}, bf16[56,640]{1,0:T(8,128)(2,1)S(1)}, u32[]{:S(2)}, u32[]{:S(2)}) collective-permute-start(bf16[56,640]{1,0:T(8,128)(2,1)S(1)} %get-tuple-element.68), channel_id=1, source_target_pairs={{0,12},{4,8},{8,4},{12,0},{1,13},{5,9},{9,5},{13,1},{2,14},{6,10},... | collective-permute-start | bytes 215048 | tf_op jit(solution)/shard_map/ppermute | solution.py:17
  97.1 13.5 %collective-permute-start.32 = (bf16[112,768]{1,0:T(8,128)(2,1)S(1)}, bf16[112,768]{1,0:T(8,128)(2,1)S(1)}, u32[]{:S(2)}, u32[]{:S(2)}) collective-permute-start(bf16[112,768]{1,0:T(8,128)(2,1)S(1)} %get-tuple-element.90), channel_id=1, source_target_pairs={{0,4},{4,0},{8,12},{12,8},{1,5},{5,1},{9,13},{13,9},{2,6},{6,2},{1... | collective-permute-start | bytes 516104 | tf_op jit(solution)/shard_map/ppermute | solution.py:17
  100.0 6.5 %collective-permute-start.27 = (bf16[56,1024]{1,0:T(8,128)(2,1)S(1)}, bf16[56,1024]{1,0:T(8,128)(2,1)S(1)}, u32[]{:S(2)}, u32[]{:S(2)}) collective-permute-start(bf16[56,1024]{1,0:T(8,128)(2,1)S(1)} %get-tuple-element.76), channel_id=1, source_target_pairs={{0,8},{4,12},{8,0},{12,4},{1,9},{5,13},{9,1},{13,5},{2,10},{6,14},... | collective-permute-start | bytes 344072 | tf_op jit(solution)/shard_map/ppermute | solution.py:17
  100.7 5.2 %collective-permute-start.30 = (bf16[56,768]{1,0:T(8,128)(2,1)S(1)}, bf16[56,768]{1,0:T(8,128)(2,1)S(1)}, u32[]{:S(2)}, u32[]{:S(2)}) collective-permute-start(bf16[56,768]{1,0:T(8,128)(2,1)S(1)} %get-tuple-element.86), channel_id=1, source_target_pairs={{0,2},{1,3},{2,0},{3,1},{4,6},{5,7},{6,4},{7,5},{8,10},{9,11},{10,... | collective-permute-start | bytes 258056 | tf_op jit(solution)/shard_map/ppermute | solution.py:17
  104.5 12.8 %collective-permute-start.20 = (bf16[56,2560]{1,0:T(8,128)(2,1)S(1)}, bf16[56,2560]{1,0:T(8,128)(2,1)S(1)}, u32[]{:S(2)}, u32[]{:S(2)}) collective-permute-start(bf16[56,2560]{1,0:T(8,128)(2,1)S(1)} %spread.1.refs_4_.refs_2_.mine), channel_id=1, source_target_pairs={{16,0},{17,1},{18,2},{19,3},{20,4},{21,5},{22,6},{23,7},{24,8},{25... | collective-permute-start | bytes 860168 | tf_op jit(solution)/shard_map/ppermute | solution.py:648
  106.7 12.8 %collective-permute-start.34 = (bf16[56,1792]{1,0:T(8,128)(2,1)S(1)}, bf16[56,1792]{1,0:T(8,128)(2,1)S(1)}, u32[]{:S(2)}, u32[]{:S(2)}) collective-permute-start(bf16[56,1792]{1,0:T(8,128)(2,1)S(1)} %finish.2.refs_0_), channel_id=1, source_target_pairs={{0,16},{1,17},{2,18},{3,19},{4,20},{5,21},{6,22},{7,23},{8,24},{9,... | collective-permute-start | bytes 602120 | tf_op jit(solution)/shard_map/ppermute | solution.py:652
  110.6 5.4 %collective-permute-start.33 = (bf16[56,768]{1,0:T(8,128)(2,1)S(1)}, bf16[56,768]{1,0:T(8,128)(2,1)S(1)}, u32[]{:S(2)}, u32[]{:S(2)}) collective-permute-start(bf16[56,768]{1,0:T(8,128)(2,1)S(1)} %get-tuple-element.92), channel_id=1, source_target_pairs={{0,8},{4,12},{8,0},{12,4},{1,9},{5,13},{9,1},{13,5},{2,10},{6,14},... | collective-permute-start | bytes 258056 | tf_op jit(solution)/shard_map/ppermute | solution.py:17
  116.1 3.4 %collective-permute-start.35 = (bf16[56,768]{1,0:T(8,128)(2,1)S(1)}, bf16[56,768]{1,0:T(8,128)(2,1)S(1)}, u32[]{:S(2)}, u32[]{:S(2)}) collective-permute-start(bf16[56,768]{1,0:T(8,128)(2,1)S(1)} %finish.3.refs_1_), channel_id=1, source_target_pairs={{0,16},{1,17},{2,18},{3,19},{4,20},{5,21},{6,22},{7,23},{8,24},{9,... | collective-permute-start | bytes 258056 | tf_op jit(solution)/shard_map/ppermute | solution.py:652

commit v6 on v5

--- a/solution.py
+++ b/solution.py
@@ -465,9 +465,11 @@
 
 
 def stage_kernel(groups, per, rows, cols, colp, c1, *refs):
-    blocks, kernel = refs[:groups], refs[groups]
+    blocks, source = refs[:groups], refs[groups]
     outs = refs[groups + 1 : 2 * groups + 1]
-    flat, taps, squeezed = refs[2 * groups + 1 :]
+    flat, taps, squeezed, kernel, sem = refs[2 * groups + 1 :]
+    load = pltpu.make_async_copy(source, kernel, sem)
+    load.start()
     main, rest, deep, size = packing(rows + 2, colp, c1)
     tiles = main + (1 if rest else 0)
     orows, ocols = rows // 2, cols // 2
@@ -501,6 +503,7 @@
                         value = plane[pl.ds(q, half, stride=2), :].astype(BF16)
                         row = ((k * per + p) * orows + i) * half
                         taps[tap, row : row + half, t * 128 : t * 128 + lanes] = value[:, :lanes]
+    load.wait()
     total = jnp.dot(taps[0], kernel[0], preferred_element_type=F32)
     for tap in range(1, 9):
         total = total + jnp.dot(taps[tap], kernel[tap], preferred_element_type=F32)
@@ -523,19 +526,21 @@
         functools.partial(stage_kernel, groups, per, rows, cols, colp, c1),
         out_shape=[jax.ShapeDtypeStruct((px, depth), F32)]
         + [jax.ShapeDtypeStruct((px, depth), BF16)] * (groups - 1),
-        in_specs=[whole()] * (groups + 1),
+        in_specs=[whole()] * groups + [pl.BlockSpec(memory_space=pltpu.HBM)],
         out_specs=[whole()] * groups,
         scratch_shapes=[
             pltpu.VMEM((tiles + 2, (rows + 3) * colp + 32, 128), F32),
             pltpu.VMEM((taps, count, c1), BF16),
             pltpu.VMEM((px, depth), F32),
+            pltpu.VMEM(kernel.shape, BF16),
+            pltpu.SemaphoreType.DMA,
         ],
         name="stage",
         compiler_params=pltpu.CompilerParams(vmem_limit_bytes=12 << 20),
         cost_estimate=pl.CostEstimate(
             flops=2 * count * taps * c1 * depth, bytes_accessed=4 * groups * px * depth, transcendentals=0
         ),
-    )(*blocks, kernel)
+    )(*blocks, streamed(kernel))
 
 
 def body(pixels, first_gain, first_shift, first_kernel, projection, second_gain, second_shift, second_kernel):
@@ -602,11 +607,12 @@
     w_other = streamed(other_kernel.reshape(9 * kd, wide))
 
     unit = wide // 10
-    plan = ((0, 4), (1, 3), (0, 3))
+    plan = ((0, 4, 0), (1, 4, 6), (0, 2, 4))
     names = [("ch", 1 << i, 2) for i in range(pairs.bit_length() - 1)]
     names_z = [("img", 1 << i, 1) for i in range(groups.bit_length() - 1)]
-    values, first = [], 0
-    for j, (kind, n) in enumerate(plan):
+    values = []
+    for j, (kind, n, first) in enumerate(plan):
+        first *= unit
         hops = names_z + names if kind else names + names_z
         keys = [(a, b) for a in range(pairs) for b in range(groups)]
 
@@ -642,12 +648,11 @@
                 rows, keys = split(keys, hops[h + 1])
                 sent, kept = merge(kept, came, rows, px)
         values.append((kept, came, first, n * unit))
-        first += n * unit
 
     mine_projected = spread(ids, back)
     far_projected = lax.ppermute(mine_projected, "section", [(1, 0)])
     outs, fars = [], []
-    for j, some in enumerate((values[:2], values[2:])):
+    for j, some in enumerate(([values[0], values[2]], [values[1]])):
         outs.append(finish([v[:2] for v in some], mine_projected, some[0][2]))
         fars.append(lax.ppermute(outs[j], "section", [(0, 1)]))
     block = final(ids, mine_projected, far_projected, outs, fars, per, orows, ocols)

time: 122 us -> 129 us (1.057)
  waiting for transfers between devices: 43.7 us -> 48.3 us
  starting transfers between devices: 49.7 us -> 52.7 us
  local copies, waits for them, and re-layouts: 7.05 us -> 5.54 us
  Pallas kernels: 20.6 us -> 21.9 us
    ppermute x31, waiting for transfers between devices: 41.6 us -> 46 us  [swap(): return lax.ppermute(array, axis, [(i, i ^ k * unit) for i in range(count)])]
    ppermute x2, starting transfers between devices: 5.15 us -> 7.09 us  [body(): fars.append(lax.ppermute(outs[j], 'section', [(0, 1)]))]
    unnamed x8 -> x6, local copies, waits for them, and re-layouts: 2.66 us -> 1.15 us
    pallas_call x1, Pallas kernels: 1.55 us -> 2.98 us  [stage(): pl.pallas_call(functools.partial(stage_kernel, groups, per, rows, cols, c...]
  transfers between devices with their start and end apart: 36 -> 36, of which waited for: 19 -> 18; matrix products, arithmetic and copies ran while one was open for 4% -> 3% of each run, Pallas kernels for 8% -> 9%
where the time goes in v6:
time: 129 us
  starting transfers between devices  52.7 us (41%)
  waiting for transfers between devices  48.3 us (37%)
  Pallas kernels  21.9 us (17%)
  local copies, waits for them, and re-layouts  5.54 us (4%)
    ppermute x31, waiting for transfers between devices, swap(): return lax.ppermute(array, axis, [(i, i ^ k * unit) for i in range(count)])  46 us
    ppermute x31, starting transfers between devices, swap(): return lax.ppermute(array, axis, [(i, i ^ k * unit) for i in range(count)])  41.2 us
    pallas_call x1, Pallas kernels, unfold(): pl.pallas_call(functools.partial(unfold_kernel, pairs, imgs, ocols, kd, s...  8.59 us
    ppermute x2, starting transfers between devices, body(): fars.append(lax.ppermute(outs[j], 'section', [(0, 1)]))  7.09 us
    pallas_call x2, Pallas kernels, mix(): pl.pallas_call(functools.partial(mix_kernel, rows, px, first, step), out_...  4.57 us
    pallas_call x1, Pallas kernels, stage(): pl.pallas_call(functools.partial(stage_kernel, groups, per, rows, cols, c...  2.98 us
  transfers between devices with their start and end apart: 36, of which 18 were waited for; matrix products, arithmetic and copies ran while one was open for 3% of the time, Pallas kernels for 9%

profile of v6, /device:TPU:0, one launch (start us, length us, event | category | flops | bytes accessed | tf_op | source)
XLA Modules:
  0.0 128.7 jit_solution(10210927068719650328)
XLA Ops:
  0.6 1.1 copy-done
  2.4 2.7 %collective-permute-start.11 = (bf16[40,640]{1,0:T(8,128)(2,1)S(1)}, bf16[40,640]{1,0:T(8,128)(2,1)S(1)}, u32[]{:S(2)}, u32[]{:S(2)}) collective-permute-start(bf16[40,640]{1,0:T(8,128)(2,1)S(1)} %get-tuple-element.62), channel_id=1, source_target_pairs={{0,4},{4,0},{8,12},{12,8},{1,5},{5,1},{9,13},{13,9},{2,6},{6,2},{1... | collective-permute-start | bytes 153608 | tf_op jit(solution)/shard_map/ppermute | solution.py:17
  5.1 2.6 %collective-permute-start.12 = (bf16[40,640]{1,0:T(8,128)(2,1)S(1)}, bf16[40,640]{1,0:T(8,128)(2,1)S(1)}, u32[]{:S(2)}, u32[]{:S(2)}) collective-permute-start(bf16[40,640]{1,0:T(8,128)(2,1)S(1)} %get-tuple-element.63), channel_id=1, source_target_pairs={{0,8},{4,12},{8,0},{12,4},{1,9},{5,13},{9,1},{13,5},{2,10},{6,14},... | collective-permute-start | bytes 153608 | tf_op jit(solution)/shard_map/ppermute | solution.py:17
  7.7 1.5 %fusion = (bf16[2,1,28,640]{3,1,2,0:T(2,128)(2,1)S(1)}, bf16[2,1,28,640]{3,1,2,0:T(2,128)(2,1)S(1)}) fusion(bf16[2,8,28,640]{3,1,2,0:T(8,128)(2,1)} %param.8), kind=kLoop, calls=%fused_computation.2 | loop fusion | bytes 286720 | tf_op jit(solution)/shard_map/slice | solution.py:569
  9.3 1.8 %collective-permute-start = (bf16[1,1,28,640]{3,2,1,0:T(8,128)(2,1)S(1)}, bf16[1,1,28,640]{3,2,1,0:T(8,128)(2,1)S(1)}, u32[]{:S(2)}, u32[]{:S(2)}) collective-permute-start(bf16[1,1,28,640]{3,2,1,0:T(8,128)(2,1)S(1)} %copy.13), channel_id=1, source_target_pairs={{0,1},{1,2},{2,3},{4,5},{5,6},{6,7},{8,9},{9,10},{10,11},{12,13},{... | collective-permute-start | bytes 107528 | tf_op jit(solution)/shard_map/ppermute | solution.py:571
  11.2 1.3 %collective-permute-start.1 = (bf16[1,1,28,640]{3,2,1,0:T(8,128)(2,1)S(1)}, bf16[1,1,28,640]{3,2,1,0:T(8,128)(2,1)S(1)}, u32[]{:S(2)}, u32[]{:S(2)}) collective-permute-start(bf16[1,1,28,640]{3,2,1,0:T(8,128)(2,1)S(1)} %copy.15), channel_id=1, source_target_pairs={{1,0},{2,1},{3,2},{5,4},{6,5},{7,6},{9,8},{10,9},{11,10},{13,12},{... | collective-permute-start | bytes 107528 | tf_op jit(solution)/shard_map/ppermute | solution.py:572
  12.5 1.1 collective-permute-done.13.refs_3_
  13.6 3.2 %collective-permute-start.14 = (bf16[4,40,640]{2,1,0:T(8,128)(2,1)S(1)}, bf16[4,40,640]{2,1,0:T(8,128)(2,1)S(1)}, u32[]{:S(2)}, u32[]{:S(2)}) collective-permute-start(bf16[4,40,640]{2,1,0:T(8,128)(2,1)S(1)} %join.1.refs_4_), channel_id=1, source_target_pairs={{0,2},{1,3},{2,0},{3,1},{4,6},{5,7},{6,4},{7,5},{8,10},{9,11},{10,... | collective-permute-start | bytes 614408 | tf_op jit(solution)/shard_map/ppermute | solution.py:17
  16.8 1.1 copy.11.pixels
  19.3 0.9 pack.1
  21.0 3.5 %collective-permute-start.3 = (bf16[416,128]{1,0:T(8,128)(2,1)S(1)}, bf16[416,128]{1,0:T(8,128)(2,1)S(1)}, u32[]{:S(2)}, u32[]{:S(2)}) collective-permute-start(bf16[416,128]{1,0:T(8,128)(2,1)S(1)} %get-tuple-element.54), channel_id=1, source_target_pairs={{0,8},{4,12},{8,0},{12,4},{1,9},{5,13},{9,1},{13,5},{2,10},{6,14},... | collective-permute-start | bytes 319496 | tf_op jit(solution)/shard_map/ppermute | solution.py:17
  24.7 1.5 %collective-permute-done.2.refs_1_ = bf16[416,128]{1,0:T(8,128)(2,1)S(1)} collective-permute-done((bf16[416,128]{1,0:T(8,128)(2,1)S(1)}, bf16[416,128]{1,0:T(8,128)(2,1)S(1)}, u32[]{:S(2)}, u32[]{:S(2)}) %collective-permute-start.2) | collective-permute-done | bytes 106528 | tf_op jit(solution)/shard_map/ppermute | solution.py:17
  26.2 6.4 %collective-permute-done.3.refs_2_ = bf16[416,128]{1,0:T(8,128)(2,1)S(1)} collective-permute-done((bf16[416,128]{1,0:T(8,128)(2,1)S(1)}, bf16[416,128]{1,0:T(8,128)(2,1)S(1)}, u32[]{:S(2)}, u32[]{:S(2)}) %collective-permute-start.3) | collective-permute-done | bytes 106528 | tf_op jit(solution)/shard_map/ppermute | solution.py:17
  32.6 3.0 %stage.1 = (f32[56,640]{1,0:T(8,128)S(1)}, bf16[56,640]{1,0:T(8,128)(2,1)S(1)}, bf16[56,640]{1,0:T(8,128)(2,1)S(1)}, bf16[56,640]{1,0:T(8,128)(2,1)S(1)}) custom-call(bf16[416,128]{1,0:T(8,128)(2,1)S(1)} %get-tuple-element.52.refs_0_, bf16[416,128]{1,0:T(8,128)(2,1)S(1)} %collective-permute-done.2.refs_1_, ...), custom_call_target="tpu_custom_call" | custom-call | flops 471859200 | bytes 573440 | tf_op jit(solution)/shard_map/stage/pallas_call | solution.py:525
  35.6 1.8 %collective-permute-start.5 = (bf16[56,640]{1,0:T(8,128)(2,1)S(1)}, bf16[56,640]{1,0:T(8,128)(2,1)S(1)}, u32[]{:S(2)}, u32[]{:S(2)}) collective-permute-start(bf16[56,640]{1,0:T(8,128)(2,1)S(1)} %get-tuple-element.58), channel_id=1, source_target_pairs={{0,4},{4,0},{8,12},{12,8},{1,5},{5,1},{9,13},{13,9},{2,6},{6,2},{1... | collective-permute-start | bytes 215048 | tf_op jit(solution)/shard_map/ppermute | solution.py:17
  37.4 1.4 %collective-permute-start.6 = (bf16[56,640]{1,0:T(8,128)(2,1)S(1)}, bf16[56,640]{1,0:T(8,128)(2,1)S(1)}, u32[]{:S(2)}, u32[]{:S(2)}) collective-permute-start(bf16[56,640]{1,0:T(8,128)(2,1)S(1)} %get-tuple-element.59), channel_id=1, source_target_pairs={{0,8},{4,12},{8,0},{12,4},{1,9},{5,13},{9,1},{13,5},{2,10},{6,14},... | collective-permute-start | bytes 215048 | tf_op jit(solution)/shard_map/ppermute | solution.py:17
  38.7 1.3 collective-permute-done.5.refs_0_
  40.0 2.5 %collective-permute-start.7 = (bf16[56,640]{1,0:T(8,128)(2,1)S(1)}, bf16[56,640]{1,0:T(8,128)(2,1)S(1)}, u32[]{:S(2)}, u32[]{:S(2)}) collective-permute-start(bf16[56,640]{1,0:T(8,128)(2,1)S(1)} %get-tuple-element.60), channel_id=1, source_target_pairs={{0,12},{4,8},{8,4},{12,0},{1,13},{5,9},{9,5},{13,1},{2,14},{6,10},... | collective-permute-start | bytes 215048 | tf_op jit(solution)/shard_map/ppermute | solution.py:17
  42.5 2.8 %collective-permute-done.6.refs_1_ = bf16[56,640]{1,0:T(8,128)(2,1)S(1)} collective-permute-done((bf16[56,640]{1,0:T(8,128)(2,1)S(1)}, bf16[56,640]{1,0:T(8,128)(2,1)S(1)}, u32[]{:S(2)}, u32[]{:S(2)}) %collective-permute-start.6) | collective-permute-done | bytes 71712 | tf_op jit(solution)/shard_map/ppermute | solution.py:17
  45.3 0.9 collective-permute-done.7.refs_2_
  46.3 2.6 %collective-permute-start.10 = (bf16[56,640]{1,0:T(8,128)(2,1)S(1)}, bf16[56,640]{1,0:T(8,128)(2,1)S(1)}, u32[]{:S(2)}, u32[]{:S(2)}) collective-permute-start(bf16[56,640]{1,0:T(8,128)(2,1)S(1)} %pool.1.refs_0_), channel_id=1, source_target_pairs={{0,12},{4,8},{8,4},{12,0},{1,13},{5,9},{9,5},{13,1},{2,14},{6,10},... | collective-permute-start | bytes 215048 | tf_op jit(solution)/shard_map/ppermute | solution.py:17
  49.6 1.2 collective-permute-start.9
  50.7 2.6 %collective-permute-done.10.refs_3_ = bf16[56,640]{1,0:T(8,128)(2,1)S(1)} collective-permute-done((bf16[56,640]{1,0:T(8,128)(2,1)S(1)}, bf16[56,640]{1,0:T(8,128)(2,1)S(1)}, u32[]{:S(2)}, u32[]{:S(2)}) %collective-permute-start.10) | collective-permute-done | bytes 71712 | tf_op jit(solution)/shard_map/ppermute | solution.py:17
  53.3 1.7 %collective-permute-done.8.refs_1_ = bf16[56,640]{1,0:T(8,128)(2,1)S(1)} collective-permute-done((bf16[56,640]{1,0:T(8,128)(2,1)S(1)}, bf16[56,640]{1,0:T(8,128)(2,1)S(1)}, u32[]{:S(2)}, u32[]{:S(2)}) %collective-permute-start.8) | collective-permute-done | bytes 71712 | tf_op jit(solution)/shard_map/ppermute | solution.py:17
  55.0 0.8 collective-permute-done.9.refs_2_
  55.8 1.2 project.1
  57.6 4.9 %collective-permute-done.21 = bf16[224,320]{1,0:T(8,128)(2,1)S(1)} collective-permute-done((bf16[224,320]{1,0:T(8,128)(2,1)S(1)}, bf16[224,320]{1,0:T(8,128)(2,1)S(1)}, u32[]{:S(2)}, u32[]{:S(2)}) %collective-permute-start.21) | collective-permute-done | bytes 143392 | tf_op jit(solution)/shard_map/ppermute | solution.py:17
  62.6 1.2 collective-permute-done.23
  63.9 8.6 %unfold.1 = (bf16[448,1440]{1,0:T(8,128)(2,1)S(1)}, bf16[448,1440]{1,0:T(8,128)(2,1)S(1)}, bf16[1440,2560]{1,0:T(8,128)(2,1)S(1)}, bf16[1440,2560]{1,0:T(8,128)(...) custom-call(s32[7]{0:T(128)S(1)} %stack.27.ids, f32[8,320]{1,0:T(8,128)S(1)} %reshape.36.gains, ...), custom_call_target="tpu_custom_call" | custom-call | flops 2642411520 | bytes 29491200 | tf_op jit(solution)/shard_map/unfold/pallas_call | solution.py:118
  73.0 3.0 %mix.3 = (bf16[224,1024]{1,0:T(8,128)(2,1)S(1)}, f32[224,1024]{1,0:T(8,128)S(1)}) custom-call(bf16[448,1440]{1,0:T(8,128)(2,1)S(1)} %get-tuple-element.77.a_own, bf16[448,1440]{1,0:T(8,128)(2,1)S(1)} %get-tuple-element.78.a_other, bf16[1440,2560]{1,0:T(8,128)(2,1)S(1)} %get-tuple-element.79.w_own, bf16[1440,2560]{1,0:T(8,128)(2,1)S(1)} %get-tuple-element.80.w_other), custom_call_target="tpu_custom_call" | custom-call | flops 2642411520 | bytes 1376256 | tf_op jit(solution)/shard_map/mix/pallas_call | solution.py:163
  76.4 1.6 %mix.2 = (bf16[224,512]{1,0:T(8,128)(2,1)S(1)}, f32[224,512]{1,0:T(8,128)S(1)}) custom-call(bf16[448,1440]{1,0:T(8,128)(2,1)S(1)} %get-tuple-element.77.a_own, bf16[448,1440]{1,0:T(8,128)(2,1)S(1)} %get-tuple-element.78.a_other, bf16[1440,2560]{1,0:T(8,128)(2,1)S(1)} %get-tuple-element.79.w_own, bf16[1440,2560]{1,0:T(8,128)(2,1)S(1)} %get-tuple-element.80.w_other), custom_call_target="tpu_custom_call" | custom-call | flops 1321205760 | bytes 688128 | tf_op jit(solution)/shard_map/mix/pallas_call | solution.py:163
  78.0 1.7 %collective-permute-start.28 = (bf16[224,512]{1,0:T(8,128)(2,1)S(1)}, bf16[224,512]{1,0:T(8,128)(2,1)S(1)}, u32[]{:S(2)}, u32[]{:S(2)}) collective-permute-start(bf16[224,512]{1,0:T(8,128)(2,1)S(1)} %get-tuple-element.82), channel_id=1, source_target_pairs={{0,2},{1,3},{2,0},{3,1},{4,6},{5,7},{6,4},{7,5},{8,10},{9,11},{10,... | collective-permute-start | bytes 688136 | tf_op jit(solution)/shard_map/ppermute | solution.py:17
  79.7 6.2 %collective-permute-done.25.came = bf16[224,1024]{1,0:T(8,128)(2,1)S(1)} collective-permute-done((bf16[224,1024]{1,0:T(8,128)(2,1)S(1)}, bf16[224,1024]{1,0:T(8,128)(2,1)S(1)}, u32[]{:S(2)}, u32[]{:S(2)}) %collective-permute-start.25) | collective-permute-done | bytes 458784 | tf_op jit(solution)/shard_map/ppermute | solution.py:17
  86.6 3.0 %collective-permute-done.31.came = bf16[224,1024]{1,0:T(8,128)(2,1)S(1)} collective-permute-done((bf16[224,1024]{1,0:T(8,128)(2,1)S(1)}, bf16[224,1024]{1,0:T(8,128)(2,1)S(1)}, u32[]{:S(2)}, u32[]{:S(2)}) %collective-permute-start.31) | collective-permute-done | bytes 458784 | tf_op jit(solution)/shard_map/ppermute | solution.py:17
  89.6 1.5 %collective-permute-start.32 = (bf16[112,1024]{1,0:T(8,128)(2,1)S(1)}, bf16[112,1024]{1,0:T(8,128)(2,1)S(1)}, u32[]{:S(2)}, u32[]{:S(2)}) collective-permute-start(bf16[112,1024]{1,0:T(8,128)(2,1)S(1)} %get-tuple-element.90), channel_id=1, source_target_pairs={{0,8},{4,12},{8,0},{12,4},{1,9},{5,13},{9,1},{13,5},{2,10},{6,14},... | collective-permute-start | bytes 688136 | tf_op jit(solution)/shard_map/ppermute | solution.py:17
  91.1 2.0 %collective-permute-start.17 = (bf16[56,640]{1,0:T(8,128)(2,1)S(1)}, bf16[56,640]{1,0:T(8,128)(2,1)S(1)}, u32[]{:S(2)}, u32[]{:S(2)}) collective-permute-start(bf16[56,640]{1,0:T(8,128)(2,1)S(1)} %get-tuple-element.66), channel_id=1, source_target_pairs={{0,4},{4,0},{8,12},{12,8},{1,5},{5,1},{9,13},{13,9},{2,6},{6,2},{1... | collective-permute-start | bytes 215048 | tf_op jit(solution)/shard_map/ppermute | solution.py:17
  93.2 2.3 %collective-permute-start.19 = (bf16[56,640]{1,0:T(8,128)(2,1)S(1)}, bf16[56,640]{1,0:T(8,128)(2,1)S(1)}, u32[]{:S(2)}, u32[]{:S(2)}) collective-permute-start(bf16[56,640]{1,0:T(8,128)(2,1)S(1)} %get-tuple-element.68), channel_id=1, source_target_pairs={{0,12},{4,8},{8,4},{12,0},{1,13},{5,9},{9,5},{13,1},{2,14},{6,10},... | collective-permute-start | bytes 215048 | tf_op jit(solution)/shard_map/ppermute | solution.py:17
  95.6 1.8 %collective-permute-done.26.came = bf16[112,1024]{1,0:T(8,128)(2,1)S(1)} collective-permute-done((bf16[112,1024]{1,0:T(8,128)(2,1)S(1)}, bf16[112,1024]{1,0:T(8,128)(2,1)S(1)}, u32[]{:S(2)}, u32[]{:S(2)}) %collective-permute-start.26) | collective-permute-done | bytes 229408 | tf_op jit(solution)/shard_map/ppermute | solution.py:17
  97.4 1.6 %collective-permute-done.17.refs_1_ = bf16[56,640]{1,0:T(8,128)(2,1)S(1)} collective-permute-done((bf16[56,640]{1,0:T(8,128)(2,1)S(1)}, bf16[56,640]{1,0:T(8,128)(2,1)S(1)}, u32[]{:S(2)}, u32[]{:S(2)}) %collective-permute-start.17) | collective-permute-done | bytes 71712 | tf_op jit(solution)/shard_map/ppermute | solution.py:17
  99.0 3.4 %collective-permute-start.27 = (bf16[56,1024]{1,0:T(8,128)(2,1)S(1)}, bf16[56,1024]{1,0:T(8,128)(2,1)S(1)}, u32[]{:S(2)}, u32[]{:S(2)}) collective-permute-start(bf16[56,1024]{1,0:T(8,128)(2,1)S(1)} %get-tuple-element.76), channel_id=1, source_target_pairs={{0,8},{4,12},{8,0},{12,4},{1,9},{5,13},{9,1},{13,5},{2,10},{6,14},... | collective-permute-start | bytes 344072 | tf_op jit(solution)/shard_map/ppermute | solution.py:17
  102.5 7.7 %collective-permute-done.18.refs_2_ = bf16[56,640]{1,0:T(8,128)(2,1)S(1)} collective-permute-done((bf16[56,640]{1,0:T(8,128)(2,1)S(1)}, bf16[56,640]{1,0:T(8,128)(2,1)S(1)}, u32[]{:S(2)}, u32[]{:S(2)}) %collective-permute-start.18) | collective-permute-done | bytes 71712 | tf_op jit(solution)/shard_map/ppermute | solution.py:17
  110.8 1.3 %collective-permute-start.20 = (bf16[56,2560]{1,0:T(8,128)(2,1)S(1)}, bf16[56,2560]{1,0:T(8,128)(2,1)S(1)}, u32[]{:S(2)}, u32[]{:S(2)}) collective-permute-start(bf16[56,2560]{1,0:T(8,128)(2,1)S(1)} %spread.1.refs_4_.refs_2_.mine), channel_id=1, source_target_pairs={{16,0},{17,1},{18,2},{19,3},{20,4},{21,5},{22,6},{23,7},{24,8},{25... | collective-permute-start | bytes 860168 | tf_op jit(solution)/shard_map/ppermute | solution.py:653
  112.2 2.8 %collective-permute-start.30 = (bf16[56,512]{1,0:T(8,128)(2,1)S(1)}, bf16[56,512]{1,0:T(8,128)(2,1)S(1)}, u32[]{:S(2)}, u32[]{:S(2)}) collective-permute-start(bf16[56,512]{1,0:T(8,128)(2,1)S(1)} %get-tuple-element.86), channel_id=1, source_target_pairs={{0,8},{4,12},{8,0},{12,4},{1,9},{5,13},{9,1},{13,5},{2,10},{6,14},... | collective-permute-start | bytes 172040 | tf_op jit(solution)/shard_map/ppermute | solution.py:17
  115.1 1.8 %collective-permute-start.33 = (bf16[56,1024]{1,0:T(8,128)(2,1)S(1)}, bf16[56,1024]{1,0:T(8,128)(2,1)S(1)}, u32[]{:S(2)}, u32[]{:S(2)}) collective-permute-start(bf16[56,1024]{1,0:T(8,128)(2,1)S(1)} %get-tuple-element.92), channel_id=1, source_target_pairs={{0,2},{1,3},{2,0},{3,1},{4,6},{5,7},{6,4},{7,5},{8,10},{9,11},{10,... | collective-permute-start | bytes 344072 | tf_op jit(solution)/shard_map/ppermute | solution.py:17
  117.4 4.6 %collective-permute-start.34 = (bf16[56,1536]{1,0:T(8,128)(2,1)S(1)}, bf16[56,1536]{1,0:T(8,128)(2,1)S(1)}, u32[]{:S(2)}, u32[]{:S(2)}) collective-permute-start(bf16[56,1536]{1,0:T(8,128)(2,1)S(1)} %finish.2.refs_0_), channel_id=1, source_target_pairs={{0,16},{1,17},{2,18},{3,19},{4,20},{5,21},{6,22},{7,23},{8,24},{9,... | collective-permute-start | bytes 516104 | tf_op jit(solution)/shard_map/ppermute | solution.py:657
  122.0 2.5 %collective-permute-start.35 = (bf16[56,1024]{1,0:T(8,128)(2,1)S(1)}, bf16[56,1024]{1,0:T(8,128)(2,1)S(1)}, u32[]{:S(2)}, u32[]{:S(2)}) collective-permute-start(bf16[56,1024]{1,0:T(8,128)(2,1)S(1)} %finish.3.refs_1_), channel_id=1, source_target_pairs={{0,16},{1,17},{2,18},{3,19},{4,20},{5,21},{6,22},{7,23},{8,24},{9,... | collective-permute-start | bytes 344072 | tf_op jit(solution)/shard_map/ppermute | solution.py:657
  124.6 2.3 %collective-permute-done.35.refs_3_ = bf16[56,1024]{1,0:T(8,128)(2,1)S(1)} collective-permute-done((bf16[56,1024]{1,0:T(8,128)(2,1)S(1)}, bf16[56,1024]{1,0:T(8,128)(2,1)S(1)}, u32[]{:S(2)}, u32[]{:S(2)}) %collective-permute-start.35) | collective-permute-done | bytes 114720 | tf_op jit(solution)/shard_map/ppermute | solution.py:657
  126.9 1.8 %final.1 = bf16[2,14,4,2560]{3,2,1,0:T(4,128)(2,1)} custom-call(s32[7]{0:T(128)S(1)} %stack.27.ids, bf16[56,2560]{1,0:T(8,128)(2,1)S(1)} %spread.1.refs_4_.refs_2_.mine, bf16[56,2560]{1,0:T(8,128)(2,1)S(1)} %collective-permute-done.20.far_mine, bf16[56,1536]{1,0:T(8,128)(2,1)S(1)} %finish.2.refs_0_, bf16[56,1024]{1,0:T(8,128)(2,1)S(1)} %finish.3.refs_1_, ...), custom_call_target="tpu_custom_call" | custom-call | tf_op jit(solution)/shard_map/final/pallas_call | solution.py:386
  (59 shorter events, 8.4 us)
Async XLA Ops:
  0.0 62.5 %copy-start.1 = (f32[2560]{0:T(1024)S(1)}, f32[2560]{0:T(1024)}, u32[]{:S(2)}) copy-start(f32[2560]{0:T(1024)} %param.13) | copy-start | bytes 30724
  0.0 62.6 %copy-start.2 = (f32[2560]{0:T(1024)S(1)}, f32[2560]{0:T(1024)}, u32[]{:S(2)}) copy-start(f32[2560]{0:T(1024)} %param.14) | copy-start | bytes 30724
  0.0 63.9 %collective-permute-start.24 = (bf16[3,3,160,2560]{3,2,1,0:T(8,128)(2,1)}, bf16[3,3,160,2560]{3,2,1,0:T(8,128)(2,1)}, u32[]{:S(2)}, u32[]{:S(2)}) collective-permute-start(bf16[3,3,160,2560]{3,2,1,0:T(8,128)(2,1)} %param.15), channel_id=1, source_target_pairs={{0,1},{1,0},{2,3},{3,2},{4,5},{5,4},{6,7},{7,6},{8,9},{9,8},{10,11... | collective-permute-start | bytes 22118408 | tf_op jit(solution)/shard_map/ppermute | solution.py:17
  0.6 1.1 copy-start
  2.4 8.8 %collective-permute-start.11 = (bf16[40,640]{1,0:T(8,128)(2,1)S(1)}, bf16[40,640]{1,0:T(8,128)(2,1)S(1)}, u32[]{:S(2)}, u32[]{:S(2)}) collective-permute-start(bf16[40,640]{1,0:T(8,128)(2,1)S(1)} %get-tuple-element.62), channel_id=1, source_target_pairs={{0,4},{4,0},{8,12},{12,8},{1,5},{5,1},{9,13},{13,9},{2,6},{6,2},{1... | collective-permute-start | bytes 153608 | tf_op jit(solution)/shard_map/ppermute | solution.py:17
  5.1 7.4 %collective-permute-start.12 = (bf16[40,640]{1,0:T(8,128)(2,1)S(1)}, bf16[40,640]{1,0:T(8,128)(2,1)S(1)}, u32[]{:S(2)}, u32[]{:S(2)}) collective-permute-start(bf16[40,640]{1,0:T(8,128)(2,1)S(1)} %get-tuple-element.63), channel_id=1, source_target_pairs={{0,8},{4,12},{8,0},{12,4},{1,9},{5,13},{9,1},{13,5},{2,10},{6,14},... | collective-permute-start | bytes 153608 | tf_op jit(solution)/shard_map/ppermute | solution.py:17
  7.7 5.9 %collective-permute-start.13 = (bf16[40,640]{1,0:T(8,128)(2,1)S(1)}, bf16[40,640]{1,0:T(8,128)(2,1)S(1)}, u32[]{:S(2)}, u32[]{:S(2)}) collective-permute-start(bf16[40,640]{1,0:T(8,128)(2,1)S(1)} %get-tuple-element.64), channel_id=1, source_target_pairs={{0,12},{4,8},{8,4},{12,0},{1,13},{5,9},{9,5},{13,1},{2,14},{6,10},... | collective-permute-start | bytes 153608 | tf_op jit(solution)/shard_map/ppermute | solution.py:17
  9.3 10.0 %collective-permute-start = (bf16[1,1,28,640]{3,2,1,0:T(8,128)(2,1)S(1)}, bf16[1,1,28,640]{3,2,1,0:T(8,128)(2,1)S(1)}, u32[]{:S(2)}, u32[]{:S(2)}) collective-permute-start(bf16[1,1,28,640]{3,2,1,0:T(8,128)(2,1)S(1)} %copy.13), channel_id=1, source_target_pairs={{0,1},{1,2},{2,3},{4,5},{5,6},{6,7},{8,9},{9,10},{10,11},{12,13},{... | collective-permute-start | bytes 107528 | tf_op jit(solution)/shard_map/ppermute | solution.py:571
  11.2 8.1 %collective-permute-start.1 = (bf16[1,1,28,640]{3,2,1,0:T(8,128)(2,1)S(1)}, bf16[1,1,28,640]{3,2,1,0:T(8,128)(2,1)S(1)}, u32[]{:S(2)}, u32[]{:S(2)}) collective-permute-start(bf16[1,1,28,640]{3,2,1,0:T(8,128)(2,1)S(1)} %copy.15), channel_id=1, source_target_pairs={{1,0},{2,1},{3,2},{5,4},{6,5},{7,6},{9,8},{10,9},{11,10},{13,12},{... | collective-permute-start | bytes 107528 | tf_op jit(solution)/shard_map/ppermute | solution.py:572
  13.6 23.8 %collective-permute-start.14 = (bf16[4,40,640]{2,1,0:T(8,128)(2,1)S(1)}, bf16[4,40,640]{2,1,0:T(8,128)(2,1)S(1)}, u32[]{:S(2)}, u32[]{:S(2)}) collective-permute-start(bf16[4,40,640]{2,1,0:T(8,128)(2,1)S(1)} %join.1.refs_4_), channel_id=1, source_target_pairs={{0,2},{1,3},{2,0},{3,1},{4,6},{5,7},{6,4},{7,5},{8,10},{9,11},{10,... | collective-permute-start | bytes 614408 | tf_op jit(solution)/shard_map/ppermute | solution.py:17
  20.2 6.0 %collective-permute-start.2 = (bf16[416,128]{1,0:T(8,128)(2,1)S(1)}, bf16[416,128]{1,0:T(8,128)(2,1)S(1)}, u32[]{:S(2)}, u32[]{:S(2)}) collective-permute-start(bf16[416,128]{1,0:T(8,128)(2,1)S(1)} %get-tuple-element.53), channel_id=1, source_target_pairs={{0,4},{4,0},{8,12},{12,8},{1,5},{5,1},{9,13},{13,9},{2,6},{6,2},{1... | collective-permute-start | bytes 319496 | tf_op jit(solution)/shard_map/ppermute | solution.py:17
  21.0 11.6 %collective-permute-start.3 = (bf16[416,128]{1,0:T(8,128)(2,1)S(1)}, bf16[416,128]{1,0:T(8,128)(2,1)S(1)}, u32[]{:S(2)}, u32[]{:S(2)}) collective-permute-start(bf16[416,128]{1,0:T(8,128)(2,1)S(1)} %get-tuple-element.54), channel_id=1, source_target_pairs={{0,8},{4,12},{8,0},{12,4},{1,9},{5,13},{9,1},{13,5},{2,10},{6,14},... | collective-permute-start | bytes 319496 | tf_op jit(solution)/shard_map/ppermute | solution.py:17
  24.5 8.1 %collective-permute-start.4 = (bf16[416,128]{1,0:T(8,128)(2,1)S(1)}, bf16[416,128]{1,0:T(8,128)(2,1)S(1)}, u32[]{:S(2)}, u32[]{:S(2)}) collective-permute-start(bf16[416,128]{1,0:T(8,128)(2,1)S(1)} %get-tuple-element.55), channel_id=1, source_target_pairs={{0,12},{4,8},{8,4},{12,0},{1,13},{5,9},{9,5},{13,1},{2,14},{6,10},... | collective-permute-start | bytes 319496 | tf_op jit(solution)/shard_map/ppermute | solution.py:17
  26.2 23.4 %collective-permute-start.15 = (bf16[4,40,640]{2,1,0:T(8,128)(2,1)S(1)}, bf16[4,40,640]{2,1,0:T(8,128)(2,1)S(1)}, u32[]{:S(2)}, u32[]{:S(2)}) collective-permute-start(bf16[4,40,640]{2,1,0:T(8,128)(2,1)S(1)} %join.1.refs_4_), channel_id=1, source_target_pairs={{0,1},{1,0},{2,3},{3,2},{4,5},{5,4},{6,7},{7,6},{8,9},{9,8},{10,11... | collective-permute-start | bytes 614408 | tf_op jit(solution)/shard_map/ppermute | solution.py:17
  35.6 4.4 %collective-permute-start.5 = (bf16[56,640]{1,0:T(8,128)(2,1)S(1)}, bf16[56,640]{1,0:T(8,128)(2,1)S(1)}, u32[]{:S(2)}, u32[]{:S(2)}) collective-permute-start(bf16[56,640]{1,0:T(8,128)(2,1)S(1)} %get-tuple-element.58), channel_id=1, source_target_pairs={{0,4},{4,0},{8,12},{12,8},{1,5},{5,1},{9,13},{13,9},{2,6},{6,2},{1... | collective-permute-start | bytes 215048 | tf_op jit(solution)/shard_map/ppermute | solution.py:17
  37.4 18.4 %collective-permute-start.16 = (bf16[4,40,640]{2,1,0:T(8,128)(2,1)S(1)}, bf16[4,40,640]{2,1,0:T(8,128)(2,1)S(1)}, u32[]{:S(2)}, u32[]{:S(2)}) collective-permute-start(bf16[4,40,640]{2,1,0:T(8,128)(2,1)S(1)} %collective-permute-done.14.refs_5_), channel_id=1, source_target_pairs={{0,1},{1,0},{2,3},{3,2},{4,5},{5,4},{6,7},{7,6},{8,9},{9,8},{10,11... | collective-permute-start | bytes 614408 | tf_op jit(solution)/shard_map/ppermute | solution.py:17
  37.4 7.9 %collective-permute-start.6 = (bf16[56,640]{1,0:T(8,128)(2,1)S(1)}, bf16[56,640]{1,0:T(8,128)(2,1)S(1)}, u32[]{:S(2)}, u32[]{:S(2)}) collective-permute-start(bf16[56,640]{1,0:T(8,128)(2,1)S(1)} %get-tuple-element.59), channel_id=1, source_target_pairs={{0,8},{4,12},{8,0},{12,4},{1,9},{5,13},{9,1},{13,5},{2,10},{6,14},... | collective-permute-start | bytes 215048 | tf_op jit(solution)/shard_map/ppermute | solution.py:17
  40.0 6.2 %collective-permute-start.7 = (bf16[56,640]{1,0:T(8,128)(2,1)S(1)}, bf16[56,640]{1,0:T(8,128)(2,1)S(1)}, u32[]{:S(2)}, u32[]{:S(2)}) collective-permute-start(bf16[56,640]{1,0:T(8,128)(2,1)S(1)} %get-tuple-element.60), channel_id=1, source_target_pairs={{0,12},{4,8},{8,4},{12,0},{1,13},{5,9},{9,5},{13,1},{2,14},{6,10},... | collective-permute-start | bytes 215048 | tf_op jit(solution)/shard_map/ppermute | solution.py:17
  46.3 7.1 %collective-permute-start.10 = (bf16[56,640]{1,0:T(8,128)(2,1)S(1)}, bf16[56,640]{1,0:T(8,128)(2,1)S(1)}, u32[]{:S(2)}, u32[]{:S(2)}) collective-permute-start(bf16[56,640]{1,0:T(8,128)(2,1)S(1)} %pool.1.refs_0_), channel_id=1, source_target_pairs={{0,12},{4,8},{8,4},{12,0},{1,13},{5,9},{9,5},{13,1},{2,14},{6,10},... | collective-permute-start | bytes 215048 | tf_op jit(solution)/shard_map/ppermute | solution.py:17
  48.8 6.2 %collective-permute-start.8 = (bf16[56,640]{1,0:T(8,128)(2,1)S(1)}, bf16[56,640]{1,0:T(8,128)(2,1)S(1)}, u32[]{:S(2)}, u32[]{:S(2)}) collective-permute-start(bf16[56,640]{1,0:T(8,128)(2,1)S(1)} %pool.1.refs_0_), channel_id=1, source_target_pairs={{0,4},{4,0},{8,12},{12,8},{1,5},{5,1},{9,13},{13,9},{2,6},{6,2},{1... | collective-permute-start | bytes 215048 | tf_op jit(solution)/shard_map/ppermute | solution.py:17
  49.6 6.2 %collective-permute-start.9 = (bf16[56,640]{1,0:T(8,128)(2,1)S(1)}, bf16[56,640]{1,0:T(8,128)(2,1)S(1)}, u32[]{:S(2)}, u32[]{:S(2)}) collective-permute-start(bf16[56,640]{1,0:T(8,128)(2,1)S(1)} %pool.1.refs_0_), channel_id=1, source_target_pairs={{0,8},{4,12},{8,0},{12,4},{1,9},{5,13},{9,1},{13,5},{2,10},{6,14},... | collective-permute-start | bytes 215048 | tf_op jit(solution)/shard_map/ppermute | solution.py:17
  57.0 5.5 %collective-permute-start.21 = (bf16[224,320]{1,0:T(8,128)(2,1)S(1)}, bf16[224,320]{1,0:T(8,128)(2,1)S(1)}, u32[]{:S(2)}, u32[]{:S(2)}) collective-permute-start(bf16[224,320]{1,0:T(8,128)(2,1)S(1)} %get-tuple-element.70), channel_id=1, source_target_pairs={{0,2},{1,3},{2,0},{3,1},{4,6},{5,7},{6,4},{7,5},{8,10},{9,11},{10,... | collective-permute-start | bytes 430088 | tf_op jit(solution)/shard_map/ppermute | solution.py:17
  57.6 5.1 %collective-permute-start.22 = (bf16[224,320]{1,0:T(8,128)(2,1)S(1)}, bf16[224,320]{1,0:T(8,128)(2,1)S(1)}, u32[]{:S(2)}, u32[]{:S(2)}) collective-permute-start(bf16[224,320]{1,0:T(8,128)(2,1)S(1)} %get-tuple-element.69), channel_id=1, source_target_pairs={{0,1},{1,0},{2,3},{3,2},{4,5},{5,4},{6,7},{7,6},{8,9},{9,8},{10,11... | collective-permute-start | bytes 430088 | tf_op jit(solution)/shard_map/ppermute | solution.py:17
  62.5 1.4 %collective-permute-start.23 = (bf16[224,320]{1,0:T(8,128)(2,1)S(1)}, bf16[224,320]{1,0:T(8,128)(2,1)S(1)}, u32[]{:S(2)}, u32[]{:S(2)}) collective-permute-start(bf16[224,320]{1,0:T(8,128)(2,1)S(1)} %collective-permute-done.21), channel_id=1, source_target_pairs={{0,1},{1,0},{2,3},{3,2},{4,5},{5,4},{6,7},{7,6},{8,9},{9,8},{10,11... | collective-permute-start | bytes 430088 | tf_op jit(solution)/shard_map/ppermute | solution.py:17
  72.5 13.5 %collective-permute-start.25 = (bf16[224,1024]{1,0:T(8,128)(2,1)S(1)}, bf16[224,1024]{1,0:T(8,128)(2,1)S(1)}, u32[]{:S(2)}, u32[]{:S(2)}) collective-permute-start(bf16[224,1024]{1,0:T(8,128)(2,1)S(1)} %get-tuple-element.72), channel_id=1, source_target_pairs={{0,2},{1,3},{2,0},{3,1},{4,6},{5,7},{6,4},{7,5},{8,10},{9,11},{10,... | collective-permute-start | bytes 1376264 | tf_op jit(solution)/shard_map/ppermute | solution.py:17
  76.0 13.5 %collective-permute-start.31 = (bf16[224,1024]{1,0:T(8,128)(2,1)S(1)}, bf16[224,1024]{1,0:T(8,128)(2,1)S(1)}, u32[]{:S(2)}, u32[]{:S(2)}) collective-permute-start(bf16[224,1024]{1,0:T(8,128)(2,1)S(1)} %get-tuple-element.88), channel_id=1, source_target_pairs={{0,4},{4,0},{8,12},{12,8},{1,5},{5,1},{9,13},{13,9},{2,6},{6,2},{1... | collective-permute-start | bytes 1376264 | tf_op jit(solution)/shard_map/ppermute | solution.py:17
  78.0 15.2 %collective-permute-start.28 = (bf16[224,512]{1,0:T(8,128)(2,1)S(1)}, bf16[224,512]{1,0:T(8,128)(2,1)S(1)}, u32[]{:S(2)}, u32[]{:S(2)}) collective-permute-start(bf16[224,512]{1,0:T(8,128)(2,1)S(1)} %get-tuple-element.82), channel_id=1, source_target_pairs={{0,2},{1,3},{2,0},{3,1},{4,6},{5,7},{6,4},{7,5},{8,10},{9,11},{10,... | collective-permute-start | bytes 688136 | tf_op jit(solution)/shard_map/ppermute | solution.py:17
  86.0 11.3 %collective-permute-start.26 = (bf16[112,1024]{1,0:T(8,128)(2,1)S(1)}, bf16[112,1024]{1,0:T(8,128)(2,1)S(1)}, u32[]{:S(2)}, u32[]{:S(2)}) collective-permute-start(bf16[112,1024]{1,0:T(8,128)(2,1)S(1)} %get-tuple-element.74), channel_id=1, source_target_pairs={{0,4},{4,0},{8,12},{12,8},{1,5},{5,1},{9,13},{13,9},{2,6},{6,2},{1... | collective-permute-start | bytes 688136 | tf_op jit(solution)/shard_map/ppermute | solution.py:17
  89.6 25.4 %collective-permute-start.32 = (bf16[112,1024]{1,0:T(8,128)(2,1)S(1)}, bf16[112,1024]{1,0:T(8,128)(2,1)S(1)}, u32[]{:S(2)}, u32[]{:S(2)}) collective-permute-start(bf16[112,1024]{1,0:T(8,128)(2,1)S(1)} %get-tuple-element.90), channel_id=1, source_target_pairs={{0,8},{4,12},{8,0},{12,4},{1,9},{5,13},{9,1},{13,5},{2,10},{6,14},... | collective-permute-start | bytes 688136 | tf_op jit(solution)/shard_map/ppermute | solution.py:17
  91.1 7.9 %collective-permute-start.17 = (bf16[56,640]{1,0:T(8,128)(2,1)S(1)}, bf16[56,640]{1,0:T(8,128)(2,1)S(1)}, u32[]{:S(2)}, u32[]{:S(2)}) collective-permute-start(bf16[56,640]{1,0:T(8,128)(2,1)S(1)} %get-tuple-element.66), channel_id=1, source_target_pairs={{0,4},{4,0},{8,12},{12,8},{1,5},{5,1},{9,13},{13,9},{2,6},{6,2},{1... | collective-permute-start | bytes 215048 | tf_op jit(solution)/shard_map/ppermute | solution.py:17
  93.1 17.1 %collective-permute-start.18 = (bf16[56,640]{1,0:T(8,128)(2,1)S(1)}, bf16[56,640]{1,0:T(8,128)(2,1)S(1)}, u32[]{:S(2)}, u32[]{:S(2)}) collective-permute-start(bf16[56,640]{1,0:T(8,128)(2,1)S(1)} %get-tuple-element.67), channel_id=1, source_target_pairs={{0,8},{4,12},{8,0},{12,4},{1,9},{5,13},{9,1},{13,5},{2,10},{6,14},... | collective-permute-start | bytes 215048 | tf_op jit(solution)/shard_map/ppermute | solution.py:17
  93.2 17.0 %collective-permute-start.19 = (bf16[56,640]{1,0:T(8,128)(2,1)S(1)}, bf16[56,640]{1,0:T(8,128)(2,1)S(1)}, u32[]{:S(2)}, u32[]{:S(2)}) collective-permute-start(bf16[56,640]{1,0:T(8,128)(2,1)S(1)} %get-tuple-element.68), channel_id=1, source_target_pairs={{0,12},{4,8},{8,4},{12,0},{1,13},{5,9},{9,5},{13,1},{2,14},{6,10},... | collective-permute-start | bytes 215048 | tf_op jit(solution)/shard_map/ppermute | solution.py:17
  97.4 14.7 %collective-permute-start.29 = (bf16[112,512]{1,0:T(8,128)(2,1)S(1)}, bf16[112,512]{1,0:T(8,128)(2,1)S(1)}, u32[]{:S(2)}, u32[]{:S(2)}) collective-permute-start(bf16[112,512]{1,0:T(8,128)(2,1)S(1)} %get-tuple-element.84), channel_id=1, source_target_pairs={{0,4},{4,0},{8,12},{12,8},{1,5},{5,1},{9,13},{13,9},{2,6},{6,2},{1... | collective-permute-start | bytes 344072 | tf_op jit(solution)/shard_map/ppermute | solution.py:17
  99.0 18.3 %collective-permute-start.27 = (bf16[56,1024]{1,0:T(8,128)(2,1)S(1)}, bf16[56,1024]{1,0:T(8,128)(2,1)S(1)}, u32[]{:S(2)}, u32[]{:S(2)}) collective-permute-start(bf16[56,1024]{1,0:T(8,128)(2,1)S(1)} %get-tuple-element.76), channel_id=1, source_target_pairs={{0,8},{4,12},{8,0},{12,4},{1,9},{5,13},{9,1},{13,5},{2,10},{6,14},... | collective-permute-start | bytes 344072 | tf_op jit(solution)/shard_map/ppermute | solution.py:17
  110.8 13.7 %collective-permute-start.20 = (bf16[56,2560]{1,0:T(8,128)(2,1)S(1)}, bf16[56,2560]{1,0:T(8,128)(2,1)S(1)}, u32[]{:S(2)}, u32[]{:S(2)}) collective-permute-start(bf16[56,2560]{1,0:T(8,128)(2,1)S(1)} %spread.1.refs_4_.refs_2_.mine), channel_id=1, source_target_pairs={{16,0},{17,1},{18,2},{19,3},{20,4},{21,5},{22,6},{23,7},{24,8},{25... | collective-permute-start | bytes 860168 | tf_op jit(solution)/shard_map/ppermute | solution.py:653
  112.2 5.1 %collective-permute-start.30 = (bf16[56,512]{1,0:T(8,128)(2,1)S(1)}, bf16[56,512]{1,0:T(8,128)(2,1)S(1)}, u32[]{:S(2)}, u32[]{:S(2)}) collective-permute-start(bf16[56,512]{1,0:T(8,128)(2,1)S(1)} %get-tuple-element.86), channel_id=1, source_target_pairs={{0,8},{4,12},{8,0},{12,4},{1,9},{5,13},{9,1},{13,5},{2,10},{6,14},... | collective-permute-start | bytes 172040 | tf_op jit(solution)/shard_map/ppermute | solution.py:17
  115.1 6.9 %collective-permute-start.33 = (bf16[56,1024]{1,0:T(8,128)(2,1)S(1)}, bf16[56,1024]{1,0:T(8,128)(2,1)S(1)}, u32[]{:S(2)}, u32[]{:S(2)}) collective-permute-start(bf16[56,1024]{1,0:T(8,128)(2,1)S(1)} %get-tuple-element.92), channel_id=1, source_target_pairs={{0,2},{1,3},{2,0},{3,1},{4,6},{5,7},{6,4},{7,5},{8,10},{9,11},{10,... | collective-permute-start | bytes 344072 | tf_op jit(solution)/shard_map/ppermute | solution.py:17
  117.4 9.5 %collective-permute-start.34 = (bf16[56,1536]{1,0:T(8,128)(2,1)S(1)}, bf16[56,1536]{1,0:T(8,128)(2,1)S(1)}, u32[]{:S(2)}, u32[]{:S(2)}) collective-permute-start(bf16[56,1536]{1,0:T(8,128)(2,1)S(1)} %finish.2.refs_0_), channel_id=1, source_target_pairs={{0,16},{1,17},{2,18},{3,19},{4,20},{5,21},{6,22},{7,23},{8,24},{9,... | collective-permute-start | bytes 516104 | tf_op jit(solution)/shard_map/ppermute | solution.py:657
  122.0 4.9 %collective-permute-start.35 = (bf16[56,1024]{1,0:T(8,128)(2,1)S(1)}, bf16[56,1024]{1,0:T(8,128)(2,1)S(1)}, u32[]{:S(2)}, u32[]{:S(2)}) collective-permute-start(bf16[56,1024]{1,0:T(8,128)(2,1)S(1)} %finish.3.refs_1_), channel_id=1, source_target_pairs={{0,16},{1,17},{2,18},{3,19},{4,20},{5,21},{6,22},{7,23},{8,24},{9,... | collective-permute-start | bytes 344072 | tf_op jit(solution)/shard_map/ppermute | solution.py:657

commit v7 on v6

--- a/solution.py
+++ b/solution.py
@@ -29,30 +29,39 @@
     w_own, w_other = refs[2 * pairs : 2 * pairs + 2]
     a_own, a_other, held_own, held_other, sent, kept = refs[2 * pairs + 2 : 2 * pairs + 8]
     scratch, partial, sems = refs[2 * pairs + 8 : -2], refs[-2], refs[-1]
-    pieces = sems.shape[0] // 2
-    deep = w_own.shape[0] // pieces
+    bounds = row_pieces(w_own.shape[0])
+    pieces = len(bounds)
     copies = []
     for i in range(2 * pieces):
         source, target = ((w_own, held_own), (w_other, held_other))[i // pieces]
         if pieces > 1:
-            some = pl.ds((i % pieces) * deep, deep)
-            source, target = source.at[some], target.at[some]
+            low, high = bounds[i % pieces]
+            source, target = source.at[pl.ds(low, high - low)], target.at[pl.ds(low, high - low)]
         copies.append(pltpu.make_async_copy(source, target, sems.at[i]))
         copies[i].start()
     unfold_rows(pairs, imgs, ocols, kd, ids, gains, shifts, *refs[: 2 * pairs], a_own, a_other, *scratch)
     for copy in copies[:pieces]:
         copy.wait()
     count = sent.shape[1]
-    cuts = [slice(first + at, first + at + step) for at in range(0, count, step)]
-    for i, cut in enumerate(cuts):
-        partial[:, i * step : (i + 1) * step] = jnp.dot(a_own[...], held_own[:, cut], preferred_element_type=F32)
-    for copy in copies[pieces:]:
-        copy.wait()
-    for i, cut in enumerate(cuts):
-        here = slice(i * step, (i + 1) * step)
-        value = partial[:, here] + jnp.dot(a_other[...], held_other[:, cut], preferred_element_type=F32)
-        copy_rows(sent.at[:, here], value, rows[0], px)
-        copy_rows(kept.at[:, here], value, rows[1], px)
+    for at in range(0, count, step):
+        cut = slice(first + at, first + at + step)
+        partial[:, at : at + step] = jnp.dot(a_own[...], held_own[:, cut], preferred_element_type=F32)
+    for i, (low, high) in enumerate(bounds):
+        copies[pieces + i].wait()
+        for at in range(0, count, step):
+            here, cut = slice(at, at + step), slice(first + at, first + at + step)
+            more = jnp.dot(a_other[:, low:high], held_other[low:high, cut], preferred_element_type=F32)
+            if i + 1 < pieces:
+                partial[:, here] = partial[:, here] + more
+            else:
+                value = partial[:, here] + more
+                copy_rows(sent.at[:, here], value, rows[0], px)
+                copy_rows(kept.at[:, here], value, rows[1], px)
+
+
+def row_pieces(deep):
+    size = 512 if deep % 8 == 0 else deep
+    return [(low, min(low + size, deep)) for low in range(0, deep, size)]
 
 
 def unfold_rows(pairs, imgs, ocols, kd, ids, gains, shifts, *refs):
@@ -113,7 +122,7 @@
     need = 8 * pairs * imgs * px * lanes + 256 * (pairs + 2) * imgs * lanes
     need += 36 * rows * kd + 8 * pairs * imgs * px * lanes
     limit = (4 << 20) + need + need // 4 + 8 * rows * count
-    pieces = 3 if deep % 24 == 0 else 1
+    pieces = len(row_pieces(deep))
     sizes = [len(r) * block for r in split]
     return pl.pallas_call(
         functools.partial(unfold_kernel, pairs, imgs, ocols, kd, split, block, first, step),
@@ -607,7 +616,7 @@
     w_other = streamed(other_kernel.reshape(9 * kd, wide))
 
     unit = wide // 10
-    plan = ((0, 4, 0), (1, 4, 6), (0, 2, 4))
+    plan = ((0, 4, 0), (1, 3, 4), (0, 3, 7))
     names = [("ch", 1 << i, 2) for i in range(pairs.bit_length() - 1)]
     names_z = [("img", 1 << i, 1) for i in range(groups.bit_length() - 1)]
     values = []
@@ -652,7 +661,7 @@
     mine_projected = spread(ids, back)
     far_projected = lax.ppermute(mine_projected, "section", [(1, 0)])
     outs, fars = [], []
-    for j, some in enumerate(([values[0], values[2]], [values[1]])):
+    for j, some in enumerate((values[:2], values[2:])):
         outs.append(finish([v[:2] for v in some], mine_projected, some[0][2]))
         fars.append(lax.ppermute(outs[j], "section", [(0, 1)]))
     block = final(ids, mine_projected, far_projected, outs, fars, per, orows, ocols)

time: 129 us -> 121 us (0.938)
  waiting for transfers between devices: 48.3 us -> 43.7 us
  starting transfers between devices: 52.7 us -> 49.8 us
    ppermute x31, waiting for transfers between devices: 46 us -> 41.6 us  [swap(): return lax.ppermute(array, axis, [(i, i ^ k * unit) for i in range(count)])]
    ppermute x2, starting transfers between devices: 7.09 us -> 5.15 us  [body(): fars.append(lax.ppermute(outs[j], 'section', [(0, 1)]))]
  transfers between devices with their start and end apart: 36 -> 36, of which waited for: 18 -> 19; matrix products, arithmetic and copies ran while one was open for 3% -> 4% of each run, Pallas kernels for 9% -> 10%
where the time goes in v7:
time: 121 us
  starting transfers between devices  49.8 us (41%)
  waiting for transfers between devices  43.7 us (36%)
  Pallas kernels  21.3 us (18%)
  local copies, waits for them, and re-layouts  5.54 us (5%)
    ppermute x31, waiting for transfers between devices, swap(): return lax.ppermute(array, axis, [(i, i ^ k * unit) for i in range(count)])  41.6 us
    ppermute x31, starting transfers between devices, swap(): return lax.ppermute(array, axis, [(i, i ^ k * unit) for i in range(count)])  40.2 us
    pallas_call x1, Pallas kernels, unfold(): pl.pallas_call(functools.partial(unfold_kernel, pairs, imgs, ocols, kd, s...  7.93 us
    ppermute x2, starting transfers between devices, body(): fars.append(lax.ppermute(outs[j], 'section', [(0, 1)]))  5.15 us
    pallas_call x2, Pallas kernels, mix(): pl.pallas_call(functools.partial(mix_kernel, rows, px, first, step), out_...  4.64 us
    pallas_call x1, Pallas kernels, stage(): pl.pallas_call(functools.partial(stage_kernel, groups, per, rows, cols, c...  2.98 us
  transfers between devices with their start and end apart: 36, of which 19 were waited for; matrix products, arithmetic and copies ran while one was open for 4% of the time, Pallas kernels for 10%

profile of v7, /device:TPU:0, one launch (start us, length us, event | category | flops | bytes accessed | tf_op | source)
XLA Modules:
  0.0 120.6 jit_solution(9062458546280849167)
XLA Ops:
  0.6 1.1 copy-done
  2.4 2.7 %collective-permute-start.11 = (bf16[40,640]{1,0:T(8,128)(2,1)S(1)}, bf16[40,640]{1,0:T(8,128)(2,1)S(1)}, u32[]{:S(2)}, u32[]{:S(2)}) collective-permute-start(bf16[40,640]{1,0:T(8,128)(2,1)S(1)} %get-tuple-element.62), channel_id=1, source_target_pairs={{0,4},{4,0},{8,12},{12,8},{1,5},{5,1},{9,13},{13,9},{2,6},{6,2},{1... | collective-permute-start | bytes 153608 | tf_op jit(solution)/shard_map/ppermute | solution.py:17
  5.1 2.6 %collective-permute-start.12 = (bf16[40,640]{1,0:T(8,128)(2,1)S(1)}, bf16[40,640]{1,0:T(8,128)(2,1)S(1)}, u32[]{:S(2)}, u32[]{:S(2)}) collective-permute-start(bf16[40,640]{1,0:T(8,128)(2,1)S(1)} %get-tuple-element.63), channel_id=1, source_target_pairs={{0,8},{4,12},{8,0},{12,4},{1,9},{5,13},{9,1},{13,5},{2,10},{6,14},... | collective-permute-start | bytes 153608 | tf_op jit(solution)/shard_map/ppermute | solution.py:17
  7.7 1.5 %fusion = (bf16[2,1,28,640]{3,1,2,0:T(2,128)(2,1)S(1)}, bf16[2,1,28,640]{3,1,2,0:T(2,128)(2,1)S(1)}) fusion(bf16[2,8,28,640]{3,1,2,0:T(8,128)(2,1)} %param.8), kind=kLoop, calls=%fused_computation.2 | loop fusion | bytes 286720 | tf_op jit(solution)/shard_map/slice | solution.py:578
  9.3 1.8 %collective-permute-start = (bf16[1,1,28,640]{3,2,1,0:T(8,128)(2,1)S(1)}, bf16[1,1,28,640]{3,2,1,0:T(8,128)(2,1)S(1)}, u32[]{:S(2)}, u32[]{:S(2)}) collective-permute-start(bf16[1,1,28,640]{3,2,1,0:T(8,128)(2,1)S(1)} %copy.13), channel_id=1, source_target_pairs={{0,1},{1,2},{2,3},{4,5},{5,6},{6,7},{8,9},{9,10},{10,11},{12,13},{... | collective-permute-start | bytes 107528 | tf_op jit(solution)/shard_map/ppermute | solution.py:580
  11.2 1.3 %collective-permute-start.1 = (bf16[1,1,28,640]{3,2,1,0:T(8,128)(2,1)S(1)}, bf16[1,1,28,640]{3,2,1,0:T(8,128)(2,1)S(1)}, u32[]{:S(2)}, u32[]{:S(2)}) collective-permute-start(bf16[1,1,28,640]{3,2,1,0:T(8,128)(2,1)S(1)} %copy.15), channel_id=1, source_target_pairs={{1,0},{2,1},{3,2},{5,4},{6,5},{7,6},{9,8},{10,9},{11,10},{13,12},{... | collective-permute-start | bytes 107528 | tf_op jit(solution)/shard_map/ppermute | solution.py:581
  12.5 1.1 collective-permute-done.13.refs_3_
  13.6 3.2 %collective-permute-start.14 = (bf16[4,40,640]{2,1,0:T(8,128)(2,1)S(1)}, bf16[4,40,640]{2,1,0:T(8,128)(2,1)S(1)}, u32[]{:S(2)}, u32[]{:S(2)}) collective-permute-start(bf16[4,40,640]{2,1,0:T(8,128)(2,1)S(1)} %join.1.refs_4_), channel_id=1, source_target_pairs={{0,2},{1,3},{2,0},{3,1},{4,6},{5,7},{6,4},{7,5},{8,10},{9,11},{10,... | collective-permute-start | bytes 614408 | tf_op jit(solution)/shard_map/ppermute | solution.py:17
  16.8 1.1 copy.11.pixels
  19.3 0.9 pack.1
  20.2 0.7 collective-permute-start.2
  21.0 3.5 %collective-permute-start.3 = (bf16[416,128]{1,0:T(8,128)(2,1)S(1)}, bf16[416,128]{1,0:T(8,128)(2,1)S(1)}, u32[]{:S(2)}, u32[]{:S(2)}) collective-permute-start(bf16[416,128]{1,0:T(8,128)(2,1)S(1)} %get-tuple-element.54), channel_id=1, source_target_pairs={{0,8},{4,12},{8,0},{12,4},{1,9},{5,13},{9,1},{13,5},{2,10},{6,14},... | collective-permute-start | bytes 319496 | tf_op jit(solution)/shard_map/ppermute | solution.py:17
  24.7 1.5 %collective-permute-done.2.refs_1_ = bf16[416,128]{1,0:T(8,128)(2,1)S(1)} collective-permute-done((bf16[416,128]{1,0:T(8,128)(2,1)S(1)}, bf16[416,128]{1,0:T(8,128)(2,1)S(1)}, u32[]{:S(2)}, u32[]{:S(2)}) %collective-permute-start.2) | collective-permute-done | bytes 106528 | tf_op jit(solution)/shard_map/ppermute | solution.py:17
  26.2 6.4 %collective-permute-done.3.refs_2_ = bf16[416,128]{1,0:T(8,128)(2,1)S(1)} collective-permute-done((bf16[416,128]{1,0:T(8,128)(2,1)S(1)}, bf16[416,128]{1,0:T(8,128)(2,1)S(1)}, u32[]{:S(2)}, u32[]{:S(2)}) %collective-permute-start.3) | collective-permute-done | bytes 106528 | tf_op jit(solution)/shard_map/ppermute | solution.py:17
  32.6 3.0 %stage.1 = (f32[56,640]{1,0:T(8,128)S(1)}, bf16[56,640]{1,0:T(8,128)(2,1)S(1)}, bf16[56,640]{1,0:T(8,128)(2,1)S(1)}, bf16[56,640]{1,0:T(8,128)(2,1)S(1)}) custom-call(bf16[416,128]{1,0:T(8,128)(2,1)S(1)} %get-tuple-element.52.refs_0_, bf16[416,128]{1,0:T(8,128)(2,1)S(1)} %collective-permute-done.2.refs_1_, ...), custom_call_target="tpu_custom_call" | custom-call | flops 471859200 | bytes 573440 | tf_op jit(solution)/shard_map/stage/pallas_call | solution.py:534
  35.6 1.8 %collective-permute-start.5 = (bf16[56,640]{1,0:T(8,128)(2,1)S(1)}, bf16[56,640]{1,0:T(8,128)(2,1)S(1)}, u32[]{:S(2)}, u32[]{:S(2)}) collective-permute-start(bf16[56,640]{1,0:T(8,128)(2,1)S(1)} %get-tuple-element.58), channel_id=1, source_target_pairs={{0,4},{4,0},{8,12},{12,8},{1,5},{5,1},{9,13},{13,9},{2,6},{6,2},{1... | collective-permute-start | bytes 215048 | tf_op jit(solution)/shard_map/ppermute | solution.py:17
  37.4 1.4 %collective-permute-start.6 = (bf16[56,640]{1,0:T(8,128)(2,1)S(1)}, bf16[56,640]{1,0:T(8,128)(2,1)S(1)}, u32[]{:S(2)}, u32[]{:S(2)}) collective-permute-start(bf16[56,640]{1,0:T(8,128)(2,1)S(1)} %get-tuple-element.59), channel_id=1, source_target_pairs={{0,8},{4,12},{8,0},{12,4},{1,9},{5,13},{9,1},{13,5},{2,10},{6,14},... | collective-permute-start | bytes 215048 | tf_op jit(solution)/shard_map/ppermute | solution.py:17
  38.7 1.3 %collective-permute-done.5.refs_0_ = bf16[56,640]{1,0:T(8,128)(2,1)S(1)} collective-permute-done((bf16[56,640]{1,0:T(8,128)(2,1)S(1)}, bf16[56,640]{1,0:T(8,128)(2,1)S(1)}, u32[]{:S(2)}, u32[]{:S(2)}) %collective-permute-start.5) | collective-permute-done | bytes 71712 | tf_op jit(solution)/shard_map/ppermute | solution.py:17
  40.0 2.5 %collective-permute-start.7 = (bf16[56,640]{1,0:T(8,128)(2,1)S(1)}, bf16[56,640]{1,0:T(8,128)(2,1)S(1)}, u32[]{:S(2)}, u32[]{:S(2)}) collective-permute-start(bf16[56,640]{1,0:T(8,128)(2,1)S(1)} %get-tuple-element.60), channel_id=1, source_target_pairs={{0,12},{4,8},{8,4},{12,0},{1,13},{5,9},{9,5},{13,1},{2,14},{6,10},... | collective-permute-start | bytes 215048 | tf_op jit(solution)/shard_map/ppermute | solution.py:17
  42.5 2.8 %collective-permute-done.6.refs_1_ = bf16[56,640]{1,0:T(8,128)(2,1)S(1)} collective-permute-done((bf16[56,640]{1,0:T(8,128)(2,1)S(1)}, bf16[56,640]{1,0:T(8,128)(2,1)S(1)}, u32[]{:S(2)}, u32[]{:S(2)}) %collective-permute-start.6) | collective-permute-done | bytes 71712 | tf_op jit(solution)/shard_map/ppermute | solution.py:17
  45.3 0.9 collective-permute-done.7.refs_2_
  46.3 2.6 %collective-permute-start.10 = (bf16[56,640]{1,0:T(8,128)(2,1)S(1)}, bf16[56,640]{1,0:T(8,128)(2,1)S(1)}, u32[]{:S(2)}, u32[]{:S(2)}) collective-permute-start(bf16[56,640]{1,0:T(8,128)(2,1)S(1)} %pool.1.refs_0_), channel_id=1, source_target_pairs={{0,12},{4,8},{8,4},{12,0},{1,13},{5,9},{9,5},{13,1},{2,14},{6,10},... | collective-permute-start | bytes 215048 | tf_op jit(solution)/shard_map/ppermute | solution.py:17
  49.6 1.2 collective-permute-start.9
  50.7 2.6 %collective-permute-done.10.refs_3_ = bf16[56,640]{1,0:T(8,128)(2,1)S(1)} collective-permute-done((bf16[56,640]{1,0:T(8,128)(2,1)S(1)}, bf16[56,640]{1,0:T(8,128)(2,1)S(1)}, u32[]{:S(2)}, u32[]{:S(2)}) %collective-permute-start.10) | collective-permute-done | bytes 71712 | tf_op jit(solution)/shard_map/ppermute | solution.py:17
  53.3 1.7 %collective-permute-done.8.refs_1_ = bf16[56,640]{1,0:T(8,128)(2,1)S(1)} collective-permute-done((bf16[56,640]{1,0:T(8,128)(2,1)S(1)}, bf16[56,640]{1,0:T(8,128)(2,1)S(1)}, u32[]{:S(2)}, u32[]{:S(2)}) %collective-permute-start.8) | collective-permute-done | bytes 71712 | tf_op jit(solution)/shard_map/ppermute | solution.py:17
  55.0 0.8 collective-permute-done.9.refs_2_
  55.8 1.2 %project.1 = (bf16[56,640]{1,0:T(8,128)(2,1)S(1)}, bf16[56,640]{1,0:T(8,128)(2,1)S(1)}, bf16[56,640]{1,0:T(8,128)(2,1)S(1)}, bf16[56,640]{1,0:T(8,128)(2,1)S(1)}...) custom-call(s32[7]{0:T(128)S(1)} %stack.27.ids, bf16[56,640]{1,0:T(8,128)(2,1)S(1)} %pool.1.refs_0_, ...), custom_call_target="tpu_custom_call" | custom-call | flops 183500800 | bytes 1638400 | tf_op jit(solution)/shard_map/project/pallas_call | solution.py:299
  57.6 4.9 %collective-permute-done.21 = bf16[224,320]{1,0:T(8,128)(2,1)S(1)} collective-permute-done((bf16[224,320]{1,0:T(8,128)(2,1)S(1)}, bf16[224,320]{1,0:T(8,128)(2,1)S(1)}, u32[]{:S(2)}, u32[]{:S(2)}) %collective-permute-start.21) | collective-permute-done | bytes 143392 | tf_op jit(solution)/shard_map/ppermute | solution.py:17
  62.6 1.2 %collective-permute-done.23 = bf16[224,320]{1,0:T(8,128)(2,1)S(1)} collective-permute-done((bf16[224,320]{1,0:T(8,128)(2,1)S(1)}, bf16[224,320]{1,0:T(8,128)(2,1)S(1)}, u32[]{:S(2)}, u32[]{:S(2)}) %collective-permute-start.23) | collective-permute-done | bytes 143392 | tf_op jit(solution)/shard_map/ppermute | solution.py:17
  63.9 7.9 %unfold.1 = (bf16[448,1440]{1,0:T(8,128)(2,1)S(1)}, bf16[448,1440]{1,0:T(8,128)(2,1)S(1)}, bf16[1440,2560]{1,0:T(8,128)(2,1)S(1)}, bf16[1440,2560]{1,0:T(8,128)(...) custom-call(s32[7]{0:T(128)S(1)} %stack.27.ids, f32[8,320]{1,0:T(8,128)S(1)} %reshape.36.gains, ...), custom_call_target="tpu_custom_call" | custom-call | flops 2642411520 | bytes 29491200 | tf_op jit(solution)/shard_map/unfold/pallas_call | solution.py:127
  72.4 2.3 %mix.2 = (bf16[224,768]{1,0:T(8,128)(2,1)S(1)}, f32[224,768]{1,0:T(8,128)S(1)}) custom-call(bf16[448,1440]{1,0:T(8,128)(2,1)S(1)} %get-tuple-element.77.a_own, bf16[448,1440]{1,0:T(8,128)(2,1)S(1)} %get-tuple-element.78.a_other, bf16[1440,2560]{1,0:T(8,128)(2,1)S(1)} %get-tuple-element.79.w_own, bf16[1440,2560]{1,0:T(8,128)(2,1)S(1)} %get-tuple-element.80.w_other), custom_call_target="tpu_custom_call" | custom-call | flops 1981808640 | bytes 1032192 | tf_op jit(solution)/shard_map/mix/pallas_call | solution.py:172
  75.1 2.3 %mix.3 = (bf16[224,768]{1,0:T(8,128)(2,1)S(1)}, f32[224,768]{1,0:T(8,128)S(1)}) custom-call(bf16[448,1440]{1,0:T(8,128)(2,1)S(1)} %get-tuple-element.77.a_own, bf16[448,1440]{1,0:T(8,128)(2,1)S(1)} %get-tuple-element.78.a_other, bf16[1440,2560]{1,0:T(8,128)(2,1)S(1)} %get-tuple-element.79.w_own, bf16[1440,2560]{1,0:T(8,128)(2,1)S(1)} %get-tuple-element.80.w_other), custom_call_target="tpu_custom_call" | custom-call | flops 1981808640 | bytes 1032192 | tf_op jit(solution)/shard_map/mix/pallas_call | solution.py:172
  77.4 1.7 %collective-permute-start.31 = (bf16[224,768]{1,0:T(8,128)(2,1)S(1)}, bf16[224,768]{1,0:T(8,128)(2,1)S(1)}, u32[]{:S(2)}, u32[]{:S(2)}) collective-permute-start(bf16[224,768]{1,0:T(8,128)(2,1)S(1)} %get-tuple-element.88), channel_id=1, source_target_pairs={{0,2},{1,3},{2,0},{3,1},{4,6},{5,7},{6,4},{7,5},{8,10},{9,11},{10,... | collective-permute-start | bytes 1032200 | tf_op jit(solution)/shard_map/ppermute | solution.py:17
  79.1 6.1 %collective-permute-done.25.came = bf16[224,1024]{1,0:T(8,128)(2,1)S(1)} collective-permute-done((bf16[224,1024]{1,0:T(8,128)(2,1)S(1)}, bf16[224,1024]{1,0:T(8,128)(2,1)S(1)}, u32[]{:S(2)}, u32[]{:S(2)}) %collective-permute-start.25) | collective-permute-done | bytes 458784 | tf_op jit(solution)/shard_map/ppermute | solution.py:17
  86.0 3.0 %collective-permute-start.29 = (bf16[112,768]{1,0:T(8,128)(2,1)S(1)}, bf16[112,768]{1,0:T(8,128)(2,1)S(1)}, u32[]{:S(2)}, u32[]{:S(2)}) collective-permute-start(bf16[112,768]{1,0:T(8,128)(2,1)S(1)} %get-tuple-element.84), channel_id=1, source_target_pairs={{0,8},{4,12},{8,0},{12,4},{1,9},{5,13},{9,1},{13,5},{2,10},{6,14},... | collective-permute-start | bytes 516104 | tf_op jit(solution)/shard_map/ppermute | solution.py:17
  89.0 1.5 %collective-permute-start.18 = (bf16[56,640]{1,0:T(8,128)(2,1)S(1)}, bf16[56,640]{1,0:T(8,128)(2,1)S(1)}, u32[]{:S(2)}, u32[]{:S(2)}) collective-permute-start(bf16[56,640]{1,0:T(8,128)(2,1)S(1)} %get-tuple-element.67), channel_id=1, source_target_pairs={{0,8},{4,12},{8,0},{12,4},{1,9},{5,13},{9,1},{13,5},{2,10},{6,14},... | collective-permute-start | bytes 215048 | tf_op jit(solution)/shard_map/ppermute | solution.py:17
  90.5 1.3 %collective-permute-done.31.came = bf16[224,768]{1,0:T(8,128)(2,1)S(1)} collective-permute-done((bf16[224,768]{1,0:T(8,128)(2,1)S(1)}, bf16[224,768]{1,0:T(8,128)(2,1)S(1)}, u32[]{:S(2)}, u32[]{:S(2)}) %collective-permute-start.31) | collective-permute-done | bytes 344096 | tf_op jit(solution)/shard_map/ppermute | solution.py:17
  91.8 2.9 %collective-permute-start.19 = (bf16[56,640]{1,0:T(8,128)(2,1)S(1)}, bf16[56,640]{1,0:T(8,128)(2,1)S(1)}, u32[]{:S(2)}, u32[]{:S(2)}) collective-permute-start(bf16[56,640]{1,0:T(8,128)(2,1)S(1)} %get-tuple-element.68), channel_id=1, source_target_pairs={{0,12},{4,8},{8,4},{12,0},{1,13},{5,9},{9,5},{13,1},{2,14},{6,10},... | collective-permute-start | bytes 215048 | tf_op jit(solution)/shard_map/ppermute | solution.py:17
  94.8 1.6 %collective-permute-done.26.came = bf16[112,1024]{1,0:T(8,128)(2,1)S(1)} collective-permute-done((bf16[112,1024]{1,0:T(8,128)(2,1)S(1)}, bf16[112,1024]{1,0:T(8,128)(2,1)S(1)}, u32[]{:S(2)}, u32[]{:S(2)}) %collective-permute-start.26) | collective-permute-done | bytes 229408 | tf_op jit(solution)/shard_map/ppermute | solution.py:17
  96.4 2.9 %collective-permute-done.29.came = bf16[112,768]{1,0:T(8,128)(2,1)S(1)} collective-permute-done((bf16[112,768]{1,0:T(8,128)(2,1)S(1)}, bf16[112,768]{1,0:T(8,128)(2,1)S(1)}, u32[]{:S(2)}, u32[]{:S(2)}) %collective-permute-start.29) | collective-permute-done | bytes 172064 | tf_op jit(solution)/shard_map/ppermute | solution.py:17
  99.9 2.6 %collective-permute-start.30 = (bf16[56,768]{1,0:T(8,128)(2,1)S(1)}, bf16[56,768]{1,0:T(8,128)(2,1)S(1)}, u32[]{:S(2)}, u32[]{:S(2)}) collective-permute-start(bf16[56,768]{1,0:T(8,128)(2,1)S(1)} %get-tuple-element.86), channel_id=1, source_target_pairs={{0,2},{1,3},{2,0},{3,1},{4,6},{5,7},{6,4},{7,5},{8,10},{9,11},{10,... | collective-permute-start | bytes 258056 | tf_op jit(solution)/shard_map/ppermute | solution.py:17
  103.8 1.3 %collective-permute-start.20 = (bf16[56,2560]{1,0:T(8,128)(2,1)S(1)}, bf16[56,2560]{1,0:T(8,128)(2,1)S(1)}, u32[]{:S(2)}, u32[]{:S(2)}) collective-permute-start(bf16[56,2560]{1,0:T(8,128)(2,1)S(1)} %spread.1.refs_4_.refs_2_.mine), channel_id=1, source_target_pairs={{16,0},{17,1},{18,2},{19,3},{20,4},{21,5},{22,6},{23,7},{24,8},{25... | collective-permute-start | bytes 860168 | tf_op jit(solution)/shard_map/ppermute | solution.py:662
  105.9 3.9 %collective-permute-start.34 = (bf16[56,1792]{1,0:T(8,128)(2,1)S(1)}, bf16[56,1792]{1,0:T(8,128)(2,1)S(1)}, u32[]{:S(2)}, u32[]{:S(2)}) collective-permute-start(bf16[56,1792]{1,0:T(8,128)(2,1)S(1)} %finish.2.refs_0_), channel_id=1, source_target_pairs={{0,16},{1,17},{2,18},{3,19},{4,20},{5,21},{6,22},{7,23},{8,24},{9,... | collective-permute-start | bytes 602120 | tf_op jit(solution)/shard_map/ppermute | solution.py:666
  109.8 2.4 %collective-permute-start.33 = (bf16[56,768]{1,0:T(8,128)(2,1)S(1)}, bf16[56,768]{1,0:T(8,128)(2,1)S(1)}, u32[]{:S(2)}, u32[]{:S(2)}) collective-permute-start(bf16[56,768]{1,0:T(8,128)(2,1)S(1)} %get-tuple-element.92), channel_id=1, source_target_pairs={{0,8},{4,12},{8,0},{12,4},{1,9},{5,13},{9,1},{13,5},{2,10},{6,14},... | collective-permute-start | bytes 258056 | tf_op jit(solution)/shard_map/ppermute | solution.py:17
  112.2 3.0 %collective-permute-done.33.refs_1_ = bf16[56,768]{1,0:T(8,128)(2,1)S(1)} collective-permute-done((bf16[56,768]{1,0:T(8,128)(2,1)S(1)}, bf16[56,768]{1,0:T(8,128)(2,1)S(1)}, u32[]{:S(2)}, u32[]{:S(2)}) %collective-permute-start.33) | collective-permute-done | bytes 86048 | tf_op jit(solution)/shard_map/ppermute | solution.py:17
  115.3 1.3 %collective-permute-start.35 = (bf16[56,768]{1,0:T(8,128)(2,1)S(1)}, bf16[56,768]{1,0:T(8,128)(2,1)S(1)}, u32[]{:S(2)}, u32[]{:S(2)}) collective-permute-start(bf16[56,768]{1,0:T(8,128)(2,1)S(1)} %finish.3.refs_1_), channel_id=1, source_target_pairs={{0,16},{1,17},{2,18},{3,19},{4,20},{5,21},{6,22},{7,23},{8,24},{9,... | collective-permute-start | bytes 258056 | tf_op jit(solution)/shard_map/ppermute | solution.py:666
  116.6 2.1 %collective-permute-done.35.refs_3_ = bf16[56,768]{1,0:T(8,128)(2,1)S(1)} collective-permute-done((bf16[56,768]{1,0:T(8,128)(2,1)S(1)}, bf16[56,768]{1,0:T(8,128)(2,1)S(1)}, u32[]{:S(2)}, u32[]{:S(2)}) %collective-permute-start.35) | collective-permute-done | bytes 86048 | tf_op jit(solution)/shard_map/ppermute | solution.py:666
  118.7 1.8 %final.1 = bf16[2,14,4,2560]{3,2,1,0:T(4,128)(2,1)} custom-call(s32[7]{0:T(128)S(1)} %stack.27.ids, bf16[56,2560]{1,0:T(8,128)(2,1)S(1)} %spread.1.refs_4_.refs_2_.mine, bf16[56,2560]{1,0:T(8,128)(2,1)S(1)} %collective-permute-done.20.far_mine, bf16[56,1792]{1,0:T(8,128)(2,1)S(1)} %finish.2.refs_0_, bf16[56,768]{1,0:T(8,128)(2,1)S(1)} %finish.3.refs_1_, ...), custom_call_target="tpu_custom_call" | custom-call | tf_op jit(solution)/shard_map/final/pallas_call | solution.py:395
  (59 shorter events, 9.1 us)
Async XLA Ops:
  0.0 62.5 %copy-start.1 = (f32[2560]{0:T(1024)S(1)}, f32[2560]{0:T(1024)}, u32[]{:S(2)}) copy-start(f32[2560]{0:T(1024)} %param.13) | copy-start | bytes 30724
  0.0 62.6 %copy-start.2 = (f32[2560]{0:T(1024)S(1)}, f32[2560]{0:T(1024)}, u32[]{:S(2)}) copy-start(f32[2560]{0:T(1024)} %param.14) | copy-start | bytes 30724
  0.0 63.9 %collective-permute-start.24 = (bf16[3,3,160,2560]{3,2,1,0:T(8,128)(2,1)}, bf16[3,3,160,2560]{3,2,1,0:T(8,128)(2,1)}, u32[]{:S(2)}, u32[]{:S(2)}) collective-permute-start(bf16[3,3,160,2560]{3,2,1,0:T(8,128)(2,1)} %param.15), channel_id=1, source_target_pairs={{0,1},{1,0},{2,3},{3,2},{4,5},{5,4},{6,7},{7,6},{8,9},{9,8},{10,11... | collective-permute-start | bytes 22118408 | tf_op jit(solution)/shard_map/ppermute | solution.py:17
  0.6 1.1 copy-start
  2.4 8.8 %collective-permute-start.11 = (bf16[40,640]{1,0:T(8,128)(2,1)S(1)}, bf16[40,640]{1,0:T(8,128)(2,1)S(1)}, u32[]{:S(2)}, u32[]{:S(2)}) collective-permute-start(bf16[40,640]{1,0:T(8,128)(2,1)S(1)} %get-tuple-element.62), channel_id=1, source_target_pairs={{0,4},{4,0},{8,12},{12,8},{1,5},{5,1},{9,13},{13,9},{2,6},{6,2},{1... | collective-permute-start | bytes 153608 | tf_op jit(solution)/shard_map/ppermute | solution.py:17
  5.1 7.4 %collective-permute-start.12 = (bf16[40,640]{1,0:T(8,128)(2,1)S(1)}, bf16[40,640]{1,0:T(8,128)(2,1)S(1)}, u32[]{:S(2)}, u32[]{:S(2)}) collective-permute-start(bf16[40,640]{1,0:T(8,128)(2,1)S(1)} %get-tuple-element.63), channel_id=1, source_target_pairs={{0,8},{4,12},{8,0},{12,4},{1,9},{5,13},{9,1},{13,5},{2,10},{6,14},... | collective-permute-start | bytes 153608 | tf_op jit(solution)/shard_map/ppermute | solution.py:17
  7.7 5.9 %collective-permute-start.13 = (bf16[40,640]{1,0:T(8,128)(2,1)S(1)}, bf16[40,640]{1,0:T(8,128)(2,1)S(1)}, u32[]{:S(2)}, u32[]{:S(2)}) collective-permute-start(bf16[40,640]{1,0:T(8,128)(2,1)S(1)} %get-tuple-element.64), channel_id=1, source_target_pairs={{0,12},{4,8},{8,4},{12,0},{1,13},{5,9},{9,5},{13,1},{2,14},{6,10},... | collective-permute-start | bytes 153608 | tf_op jit(solution)/shard_map/ppermute | solution.py:17
  9.3 10.0 %collective-permute-start = (bf16[1,1,28,640]{3,2,1,0:T(8,128)(2,1)S(1)}, bf16[1,1,28,640]{3,2,1,0:T(8,128)(2,1)S(1)}, u32[]{:S(2)}, u32[]{:S(2)}) collective-permute-start(bf16[1,1,28,640]{3,2,1,0:T(8,128)(2,1)S(1)} %copy.13), channel_id=1, source_target_pairs={{0,1},{1,2},{2,3},{4,5},{5,6},{6,7},{8,9},{9,10},{10,11},{12,13},{... | collective-permute-start | bytes 107528 | tf_op jit(solution)/shard_map/ppermute | solution.py:580
  11.2 8.1 %collective-permute-start.1 = (bf16[1,1,28,640]{3,2,1,0:T(8,128)(2,1)S(1)}, bf16[1,1,28,640]{3,2,1,0:T(8,128)(2,1)S(1)}, u32[]{:S(2)}, u32[]{:S(2)}) collective-permute-start(bf16[1,1,28,640]{3,2,1,0:T(8,128)(2,1)S(1)} %copy.15), channel_id=1, source_target_pairs={{1,0},{2,1},{3,2},{5,4},{6,5},{7,6},{9,8},{10,9},{11,10},{13,12},{... | collective-permute-start | bytes 107528 | tf_op jit(solution)/shard_map/ppermute | solution.py:581
  13.6 23.8 %collective-permute-start.14 = (bf16[4,40,640]{2,1,0:T(8,128)(2,1)S(1)}, bf16[4,40,640]{2,1,0:T(8,128)(2,1)S(1)}, u32[]{:S(2)}, u32[]{:S(2)}) collective-permute-start(bf16[4,40,640]{2,1,0:T(8,128)(2,1)S(1)} %join.1.refs_4_), channel_id=1, source_target_pairs={{0,2},{1,3},{2,0},{3,1},{4,6},{5,7},{6,4},{7,5},{8,10},{9,11},{10,... | collective-permute-start | bytes 614408 | tf_op jit(solution)/shard_map/ppermute | solution.py:17
  20.2 6.0 %collective-permute-start.2 = (bf16[416,128]{1,0:T(8,128)(2,1)S(1)}, bf16[416,128]{1,0:T(8,128)(2,1)S(1)}, u32[]{:S(2)}, u32[]{:S(2)}) collective-permute-start(bf16[416,128]{1,0:T(8,128)(2,1)S(1)} %get-tuple-element.53), channel_id=1, source_target_pairs={{0,4},{4,0},{8,12},{12,8},{1,5},{5,1},{9,13},{13,9},{2,6},{6,2},{1... | collective-permute-start | bytes 319496 | tf_op jit(solution)/shard_map/ppermute | solution.py:17
  21.0 11.6 %collective-permute-start.3 = (bf16[416,128]{1,0:T(8,128)(2,1)S(1)}, bf16[416,128]{1,0:T(8,128)(2,1)S(1)}, u32[]{:S(2)}, u32[]{:S(2)}) collective-permute-start(bf16[416,128]{1,0:T(8,128)(2,1)S(1)} %get-tuple-element.54), channel_id=1, source_target_pairs={{0,8},{4,12},{8,0},{12,4},{1,9},{5,13},{9,1},{13,5},{2,10},{6,14},... | collective-permute-start | bytes 319496 | tf_op jit(solution)/shard_map/ppermute | solution.py:17
  24.5 8.1 %collective-permute-start.4 = (bf16[416,128]{1,0:T(8,128)(2,1)S(1)}, bf16[416,128]{1,0:T(8,128)(2,1)S(1)}, u32[]{:S(2)}, u32[]{:S(2)}) collective-permute-start(bf16[416,128]{1,0:T(8,128)(2,1)S(1)} %get-tuple-element.55), channel_id=1, source_target_pairs={{0,12},{4,8},{8,4},{12,0},{1,13},{5,9},{9,5},{13,1},{2,14},{6,10},... | collective-permute-start | bytes 319496 | tf_op jit(solution)/shard_map/ppermute | solution.py:17
  26.2 23.4 %collective-permute-start.15 = (bf16[4,40,640]{2,1,0:T(8,128)(2,1)S(1)}, bf16[4,40,640]{2,1,0:T(8,128)(2,1)S(1)}, u32[]{:S(2)}, u32[]{:S(2)}) collective-permute-start(bf16[4,40,640]{2,1,0:T(8,128)(2,1)S(1)} %join.1.refs_4_), channel_id=1, source_target_pairs={{0,1},{1,0},{2,3},{3,2},{4,5},{5,4},{6,7},{7,6},{8,9},{9,8},{10,11... | collective-permute-start | bytes 614408 | tf_op jit(solution)/shard_map/ppermute | solution.py:17
  35.6 4.4 %collective-permute-start.5 = (bf16[56,640]{1,0:T(8,128)(2,1)S(1)}, bf16[56,640]{1,0:T(8,128)(2,1)S(1)}, u32[]{:S(2)}, u32[]{:S(2)}) collective-permute-start(bf16[56,640]{1,0:T(8,128)(2,1)S(1)} %get-tuple-element.58), channel_id=1, source_target_pairs={{0,4},{4,0},{8,12},{12,8},{1,5},{5,1},{9,13},{13,9},{2,6},{6,2},{1... | collective-permute-start | bytes 215048 | tf_op jit(solution)/shard_map/ppermute | solution.py:17
  37.4 18.4 %collective-permute-start.16 = (bf16[4,40,640]{2,1,0:T(8,128)(2,1)S(1)}, bf16[4,40,640]{2,1,0:T(8,128)(2,1)S(1)}, u32[]{:S(2)}, u32[]{:S(2)}) collective-permute-start(bf16[4,40,640]{2,1,0:T(8,128)(2,1)S(1)} %collective-permute-done.14.refs_5_), channel_id=1, source_target_pairs={{0,1},{1,0},{2,3},{3,2},{4,5},{5,4},{6,7},{7,6},{8,9},{9,8},{10,11... | collective-permute-start | bytes 614408 | tf_op jit(solution)/shard_map/ppermute | solution.py:17
  37.4 7.9 %collective-permute-start.6 = (bf16[56,640]{1,0:T(8,128)(2,1)S(1)}, bf16[56,640]{1,0:T(8,128)(2,1)S(1)}, u32[]{:S(2)}, u32[]{:S(2)}) collective-permute-start(bf16[56,640]{1,0:T(8,128)(2,1)S(1)} %get-tuple-element.59), channel_id=1, source_target_pairs={{0,8},{4,12},{8,0},{12,4},{1,9},{5,13},{9,1},{13,5},{2,10},{6,14},... | collective-permute-start | bytes 215048 | tf_op jit(solution)/shard_map/ppermute | solution.py:17
  40.0 6.2 %collective-permute-start.7 = (bf16[56,640]{1,0:T(8,128)(2,1)S(1)}, bf16[56,640]{1,0:T(8,128)(2,1)S(1)}, u32[]{:S(2)}, u32[]{:S(2)}) collective-permute-start(bf16[56,640]{1,0:T(8,128)(2,1)S(1)} %get-tuple-element.60), channel_id=1, source_target_pairs={{0,12},{4,8},{8,4},{12,0},{1,13},{5,9},{9,5},{13,1},{2,14},{6,10},... | collective-permute-start | bytes 215048 | tf_op jit(solution)/shard_map/ppermute | solution.py:17
  46.3 7.1 %collective-permute-start.10 = (bf16[56,640]{1,0:T(8,128)(2,1)S(1)}, bf16[56,640]{1,0:T(8,128)(2,1)S(1)}, u32[]{:S(2)}, u32[]{:S(2)}) collective-permute-start(bf16[56,640]{1,0:T(8,128)(2,1)S(1)} %pool.1.refs_0_), channel_id=1, source_target_pairs={{0,12},{4,8},{8,4},{12,0},{1,13},{5,9},{9,5},{13,1},{2,14},{6,10},... | collective-permute-start | bytes 215048 | tf_op jit(solution)/shard_map/ppermute | solution.py:17
  48.8 6.2 %collective-permute-start.8 = (bf16[56,640]{1,0:T(8,128)(2,1)S(1)}, bf16[56,640]{1,0:T(8,128)(2,1)S(1)}, u32[]{:S(2)}, u32[]{:S(2)}) collective-permute-start(bf16[56,640]{1,0:T(8,128)(2,1)S(1)} %pool.1.refs_0_), channel_id=1, source_target_pairs={{0,4},{4,0},{8,12},{12,8},{1,5},{5,1},{9,13},{13,9},{2,6},{6,2},{1... | collective-permute-start | bytes 215048 | tf_op jit(solution)/shard_map/ppermute | solution.py:17
  49.6 6.2 %collective-permute-start.9 = (bf16[56,640]{1,0:T(8,128)(2,1)S(1)}, bf16[56,640]{1,0:T(8,128)(2,1)S(1)}, u32[]{:S(2)}, u32[]{:S(2)}) collective-permute-start(bf16[56,640]{1,0:T(8,128)(2,1)S(1)} %pool.1.refs_0_), channel_id=1, source_target_pairs={{0,8},{4,12},{8,0},{12,4},{1,9},{5,13},{9,1},{13,5},{2,10},{6,14},... | collective-permute-start | bytes 215048 | tf_op jit(solution)/shard_map/ppermute | solution.py:17
  57.0 5.5 %collective-permute-start.21 = (bf16[224,320]{1,0:T(8,128)(2,1)S(1)}, bf16[224,320]{1,0:T(8,128)(2,1)S(1)}, u32[]{:S(2)}, u32[]{:S(2)}) collective-permute-start(bf16[224,320]{1,0:T(8,128)(2,1)S(1)} %get-tuple-element.70), channel_id=1, source_target_pairs={{0,2},{1,3},{2,0},{3,1},{4,6},{5,7},{6,4},{7,5},{8,10},{9,11},{10,... | collective-permute-start | bytes 430088 | tf_op jit(solution)/shard_map/ppermute | solution.py:17
  57.6 5.1 %collective-permute-start.22 = (bf16[224,320]{1,0:T(8,128)(2,1)S(1)}, bf16[224,320]{1,0:T(8,128)(2,1)S(1)}, u32[]{:S(2)}, u32[]{:S(2)}) collective-permute-start(bf16[224,320]{1,0:T(8,128)(2,1)S(1)} %get-tuple-element.69), channel_id=1, source_target_pairs={{0,1},{1,0},{2,3},{3,2},{4,5},{5,4},{6,7},{7,6},{8,9},{9,8},{10,11... | collective-permute-start | bytes 430088 | tf_op jit(solution)/shard_map/ppermute | solution.py:17
  62.5 1.4 %collective-permute-start.23 = (bf16[224,320]{1,0:T(8,128)(2,1)S(1)}, bf16[224,320]{1,0:T(8,128)(2,1)S(1)}, u32[]{:S(2)}, u32[]{:S(2)}) collective-permute-start(bf16[224,320]{1,0:T(8,128)(2,1)S(1)} %collective-permute-done.21), channel_id=1, source_target_pairs={{0,1},{1,0},{2,3},{3,2},{4,5},{5,4},{6,7},{7,6},{8,9},{9,8},{10,11... | collective-permute-start | bytes 430088 | tf_op jit(solution)/shard_map/ppermute | solution.py:17
  71.8 13.5 %collective-permute-start.25 = (bf16[224,1024]{1,0:T(8,128)(2,1)S(1)}, bf16[224,1024]{1,0:T(8,128)(2,1)S(1)}, u32[]{:S(2)}, u32[]{:S(2)}) collective-permute-start(bf16[224,1024]{1,0:T(8,128)(2,1)S(1)} %get-tuple-element.72), channel_id=1, source_target_pairs={{0,2},{1,3},{2,0},{3,1},{4,6},{5,7},{6,4},{7,5},{8,10},{9,11},{10,... | collective-permute-start | bytes 1376264 | tf_op jit(solution)/shard_map/ppermute | solution.py:17
  74.7 11.2 %collective-permute-start.28 = (bf16[224,768]{1,0:T(8,128)(2,1)S(1)}, bf16[224,768]{1,0:T(8,128)(2,1)S(1)}, u32[]{:S(2)}, u32[]{:S(2)}) collective-permute-start(bf16[224,768]{1,0:T(8,128)(2,1)S(1)} %get-tuple-element.82), channel_id=1, source_target_pairs={{0,4},{4,0},{8,12},{12,8},{1,5},{5,1},{9,13},{13,9},{2,6},{6,2},{1... | collective-permute-start | bytes 1032200 | tf_op jit(solution)/shard_map/ppermute | solution.py:17
  77.4 14.4 %collective-permute-start.31 = (bf16[224,768]{1,0:T(8,128)(2,1)S(1)}, bf16[224,768]{1,0:T(8,128)(2,1)S(1)}, u32[]{:S(2)}, u32[]{:S(2)}) collective-permute-start(bf16[224,768]{1,0:T(8,128)(2,1)S(1)} %get-tuple-element.88), channel_id=1, source_target_pairs={{0,2},{1,3},{2,0},{3,1},{4,6},{5,7},{6,4},{7,5},{8,10},{9,11},{10,... | collective-permute-start | bytes 1032200 | tf_op jit(solution)/shard_map/ppermute | solution.py:17
  85.4 10.9 %collective-permute-start.26 = (bf16[112,1024]{1,0:T(8,128)(2,1)S(1)}, bf16[112,1024]{1,0:T(8,128)(2,1)S(1)}, u32[]{:S(2)}, u32[]{:S(2)}) collective-permute-start(bf16[112,1024]{1,0:T(8,128)(2,1)S(1)} %get-tuple-element.74), channel_id=1, source_target_pairs={{0,4},{4,0},{8,12},{12,8},{1,5},{5,1},{9,13},{13,9},{2,6},{6,2},{1... | collective-permute-start | bytes 688136 | tf_op jit(solution)/shard_map/ppermute | solution.py:17
  86.0 13.4 %collective-permute-start.29 = (bf16[112,768]{1,0:T(8,128)(2,1)S(1)}, bf16[112,768]{1,0:T(8,128)(2,1)S(1)}, u32[]{:S(2)}, u32[]{:S(2)}) collective-permute-start(bf16[112,768]{1,0:T(8,128)(2,1)S(1)} %get-tuple-element.84), channel_id=1, source_target_pairs={{0,8},{4,12},{8,0},{12,4},{1,9},{5,13},{9,1},{13,5},{2,10},{6,14},... | collective-permute-start | bytes 516104 | tf_op jit(solution)/shard_map/ppermute | solution.py:17
  89.0 10.9 %collective-permute-start.17 = (bf16[56,640]{1,0:T(8,128)(2,1)S(1)}, bf16[56,640]{1,0:T(8,128)(2,1)S(1)}, u32[]{:S(2)}, u32[]{:S(2)}) collective-permute-start(bf16[56,640]{1,0:T(8,128)(2,1)S(1)} %get-tuple-element.66), channel_id=1, source_target_pairs={{0,4},{4,0},{8,12},{12,8},{1,5},{5,1},{9,13},{13,9},{2,6},{6,2},{1... | collective-permute-start | bytes 215048 | tf_op jit(solution)/shard_map/ppermute | solution.py:17
  89.0 13.5 %collective-permute-start.18 = (bf16[56,640]{1,0:T(8,128)(2,1)S(1)}, bf16[56,640]{1,0:T(8,128)(2,1)S(1)}, u32[]{:S(2)}, u32[]{:S(2)}) collective-permute-start(bf16[56,640]{1,0:T(8,128)(2,1)S(1)} %get-tuple-element.67), channel_id=1, source_target_pairs={{0,8},{4,12},{8,0},{12,4},{1,9},{5,13},{9,1},{13,5},{2,10},{6,14},... | collective-permute-start | bytes 215048 | tf_op jit(solution)/shard_map/ppermute | solution.py:17
  91.8 11.4 %collective-permute-start.19 = (bf16[56,640]{1,0:T(8,128)(2,1)S(1)}, bf16[56,640]{1,0:T(8,128)(2,1)S(1)}, u32[]{:S(2)}, u32[]{:S(2)}) collective-permute-start(bf16[56,640]{1,0:T(8,128)(2,1)S(1)} %get-tuple-element.68), channel_id=1, source_target_pairs={{0,12},{4,8},{8,4},{12,0},{1,13},{5,9},{9,5},{13,1},{2,14},{6,10},... | collective-permute-start | bytes 215048 | tf_op jit(solution)/shard_map/ppermute | solution.py:17
  96.3 13.5 %collective-permute-start.32 = (bf16[112,768]{1,0:T(8,128)(2,1)S(1)}, bf16[112,768]{1,0:T(8,128)(2,1)S(1)}, u32[]{:S(2)}, u32[]{:S(2)}) collective-permute-start(bf16[112,768]{1,0:T(8,128)(2,1)S(1)} %get-tuple-element.90), channel_id=1, source_target_pairs={{0,4},{4,0},{8,12},{12,8},{1,5},{5,1},{9,13},{13,9},{2,6},{6,2},{1... | collective-permute-start | bytes 516104 | tf_op jit(solution)/shard_map/ppermute | solution.py:17
  99.3 6.5 %collective-permute-start.27 = (bf16[56,1024]{1,0:T(8,128)(2,1)S(1)}, bf16[56,1024]{1,0:T(8,128)(2,1)S(1)}, u32[]{:S(2)}, u32[]{:S(2)}) collective-permute-start(bf16[56,1024]{1,0:T(8,128)(2,1)S(1)} %get-tuple-element.76), channel_id=1, source_target_pairs={{0,8},{4,12},{8,0},{12,4},{1,9},{5,13},{9,1},{13,5},{2,10},{6,14},... | collective-permute-start | bytes 344072 | tf_op jit(solution)/shard_map/ppermute | solution.py:17
  99.9 5.2 %collective-permute-start.30 = (bf16[56,768]{1,0:T(8,128)(2,1)S(1)}, bf16[56,768]{1,0:T(8,128)(2,1)S(1)}, u32[]{:S(2)}, u32[]{:S(2)}) collective-permute-start(bf16[56,768]{1,0:T(8,128)(2,1)S(1)} %get-tuple-element.86), channel_id=1, source_target_pairs={{0,2},{1,3},{2,0},{3,1},{4,6},{5,7},{6,4},{7,5},{8,10},{9,11},{10,... | collective-permute-start | bytes 258056 | tf_op jit(solution)/shard_map/ppermute | solution.py:17
  103.8 12.8 %collective-permute-start.20 = (bf16[56,2560]{1,0:T(8,128)(2,1)S(1)}, bf16[56,2560]{1,0:T(8,128)(2,1)S(1)}, u32[]{:S(2)}, u32[]{:S(2)}) collective-permute-start(bf16[56,2560]{1,0:T(8,128)(2,1)S(1)} %spread.1.refs_4_.refs_2_.mine), channel_id=1, source_target_pairs={{16,0},{17,1},{18,2},{19,3},{20,4},{21,5},{22,6},{23,7},{24,8},{25... | collective-permute-start | bytes 860168 | tf_op jit(solution)/shard_map/ppermute | solution.py:662
  105.9 12.8 %collective-permute-start.34 = (bf16[56,1792]{1,0:T(8,128)(2,1)S(1)}, bf16[56,1792]{1,0:T(8,128)(2,1)S(1)}, u32[]{:S(2)}, u32[]{:S(2)}) collective-permute-start(bf16[56,1792]{1,0:T(8,128)(2,1)S(1)} %finish.2.refs_0_), channel_id=1, source_target_pairs={{0,16},{1,17},{2,18},{3,19},{4,20},{5,21},{6,22},{7,23},{8,24},{9,... | collective-permute-start | bytes 602120 | tf_op jit(solution)/shard_map/ppermute | solution.py:666
  109.8 5.4 %collective-permute-start.33 = (bf16[56,768]{1,0:T(8,128)(2,1)S(1)}, bf16[56,768]{1,0:T(8,128)(2,1)S(1)}, u32[]{:S(2)}, u32[]{:S(2)}) collective-permute-start(bf16[56,768]{1,0:T(8,128)(2,1)S(1)} %get-tuple-element.92), channel_id=1, source_target_pairs={{0,8},{4,12},{8,0},{12,4},{1,9},{5,13},{9,1},{13,5},{2,10},{6,14},... | collective-permute-start | bytes 258056 | tf_op jit(solution)/shard_map/ppermute | solution.py:17
  115.3 3.4 %collective-permute-start.35 = (bf16[56,768]{1,0:T(8,128)(2,1)S(1)}, bf16[56,768]{1,0:T(8,128)(2,1)S(1)}, u32[]{:S(2)}, u32[]{:S(2)}) collective-permute-start(bf16[56,768]{1,0:T(8,128)(2,1)S(1)} %finish.3.refs_1_), channel_id=1, source_target_pairs={{0,16},{1,17},{2,18},{3,19},{4,20},{5,21},{6,22},{7,23},{8,24},{9,... | collective-permute-start | bytes 258056 | tf_op jit(solution)/shard_map/ppermute | solution.py:666
